TPU v7x, 32 devices: a whole 2x2x4 slice. The times are simulated.
32 devices in a mesh: ulysses: 4 (over y, core), blk: 8 (over z, x).
Axes of the slice: x: 2, y: 2, z: 4, core: 2. Of those that a mesh axis runs over, the one named last changes fastest.
Arguments:
- tokens: bfloat16 [3, 2048, 768], P(None, ('ulysses', 'blk')), may hold values from -6 to 6
- cotangent: bfloat16 [3, 2048, 768], P(None, ('ulysses', 'blk')), may hold values from -6 to 6
- lengths: int32 [3, 32], replicated, may hold values from 1 to 512, 2048 in all within a row
- time_step: int32 [3], replicated, may hold values from 0 to 999
- modulate_weight: bfloat16 [4608, 128], P(('ulysses', 'blk')), may hold values from -0.5 to 0.5
- modulate_bias: bfloat16 [4608], P(('ulysses', 'blk')), may hold values from -3 to 3
- attend_gain: bfloat16 [768], P(('ulysses', 'blk')), may hold values from 0.099609375 to 1.8984375
- input_weight: bfloat16 [768, 2304], P(('ulysses', 'blk')), may hold values from -0.21875 to 0.21875
- output_weight: bfloat16 [768, 768], P(('ulysses', 'blk')), may hold values from -1.75 to 1.75
- feed_gain: bfloat16 [768], P(('ulysses', 'blk')), may hold values from 0.099609375 to 1.8984375
- expand_weight: bfloat16 [768, 3072], P(('ulysses', 'blk')), may hold values from -0.21875 to 0.21875
- expand_bias: bfloat16 [3072], P(('ulysses', 'blk')), may hold values from -3 to 3
- reduce_weight: bfloat16 [3072, 768], P(('ulysses', 'blk')), may hold values from -0.109375 to 0.109375
- reduce_bias: bfloat16 [768], P(('ulysses', 'blk')), may hold values from -3 to 3
Outputs:
- layer_output: bfloat16 [3, 2048, 768], P(None, ('ulysses', 'blk'))
- tokens_grad: bfloat16 [3, 2048, 768], P(None, ('ulysses', 'blk'))
- modulate_weight_grad: float32 [4608, 128], P(('ulysses', 'blk'))
- modulate_bias_grad: float32 [4608], P(('ulysses', 'blk'))
- attend_gain_grad: float32 [768], P(('ulysses', 'blk'))
- input_weight_grad: float32 [768, 2304], P(('ulysses', 'blk'))
- output_weight_grad: float32 [768, 768], P(('ulysses', 'blk'))
- feed_gain_grad: float32 [768], P(('ulysses', 'blk'))
- expand_weight_grad: float32 [768, 3072], P(('ulysses', 'blk'))
- expand_bias_grad: float32 [3072], P(('ulysses', 'blk'))
- reduce_weight_grad: float32 [3072, 768], P(('ulysses', 'blk'))
- reduce_bias_grad: float32 [768], P(('ulysses', 'blk'))
Inputs may be any that keep to these rules, and one draw needn't show every extreme that they name: Each row lists the lengths of the 32 documents that fill one sequence of 2048 tokens; the longest is exactly 512.
All inputs are finite; a program needn't handle non-finite values.
Results may differ from a plain program's by a relative error of at most 0.02.
Values may be sent and summed in bfloat16 or wider, within the bound.
No kernel may reach another device: no remote copies, remote signals or barrier semaphores. Data moves between devices by JAX's collectives and lax.ppermute only.
A program may use at most 512 MiB of HBM per device.

v0:
```python
import math

import jax
import jax.numpy as jnp
from jax import lax
from jax.sharding import PartitionSpec as P

HEADS = 12


def time_features(time_step, half):
    freqs = jnp.exp(-math.log(10000.0) * jnp.arange(half, dtype=jnp.float32) / half)
    angles = time_step.astype(jnp.float32)[:, None] * freqs[None, :]
    return jax.nn.silu(jnp.concatenate([jnp.cos(angles), jnp.sin(angles)], 1)).astype(jnp.bfloat16)


def doc_layout(index, lengths_row):
    ends = jnp.cumsum(lengths_row)
    over = index[:, None] >= ends[None, :]
    segment = jnp.sum(over.astype(jnp.int32), 1)
    place = index - jnp.sum(jnp.where(over, lengths_row[None, :], 0), 1)
    return (segment, place)


def rotary(values, place, flip):
    half = values.shape[-1] // 2
    freqs = jnp.exp(-math.log(10000.0) * jnp.arange(half, dtype=jnp.float32) / half)
    angles = place.astype(jnp.float32)[:, None] * freqs[None, :]
    cosine = jnp.cos(angles)[:, None, :]
    sine = flip * jnp.sin(angles)[:, None, :]
    first = values[..., :half]
    second = values[..., half:]
    return jnp.concatenate([first * cosine - second * sine, second * cosine + first * sine], -1)


def modulate(values, gain, shift, scale):
    centered = values - jnp.mean(values, -1, keepdims=True)
    spread = jnp.mean(centered * centered, -1, keepdims=True)
    return centered * lax.rsqrt(spread + 1e-05) * gain * (1.0 + scale) + shift


def gelu_tanh(values):
    return jax.nn.gelu(values, approximate=True)


def on_device(
    tokens,
    cotangent,
    lengths,
    time_step,
    modulate_weight,
    modulate_bias,
    attend_gain,
    input_weight,
    output_weight,
    feed_gain,
    expand_weight,
    expand_bias,
    reduce_weight,
    reduce_bias,
):
    gathered = (
        lax.all_gather(modulate_weight, ("ulysses", "blk"), axis=0, tiled=True),
        lax.all_gather(modulate_bias, ("ulysses", "blk"), axis=0, tiled=True),
        lax.all_gather(attend_gain, ("ulysses", "blk"), axis=0, tiled=True),
        lax.all_gather(input_weight, ("ulysses", "blk"), axis=0, tiled=True),
        lax.all_gather(output_weight, ("ulysses", "blk"), axis=0, tiled=True),
        lax.all_gather(feed_gain, ("ulysses", "blk"), axis=0, tiled=True),
        lax.all_gather(expand_weight, ("ulysses", "blk"), axis=0, tiled=True),
        lax.all_gather(expand_bias, ("ulysses", "blk"), axis=0, tiled=True),
        lax.all_gather(reduce_weight, ("ulysses", "blk"), axis=0, tiled=True),
        lax.all_gather(reduce_bias, ("ulysses", "blk"), axis=0, tiled=True),
    )
    (
        mod_full,
        mod_bias_full,
        gain_one_full,
        input_full,
        output_full,
        gain_two_full,
        expand_full,
        expand_bias_full,
        reduce_full,
        reduce_bias_full,
    ) = gathered
    groups = lax.axis_size("ulysses")
    blocks = lax.axis_size("blk")
    group_id = lax.axis_index("ulysses")
    block_id = lax.axis_index("blk")
    micro = tokens.shape[0]
    tokens_dev = tokens.shape[1]
    width = tokens.shape[2]
    span = groups * tokens_dev
    whole_rows = span * blocks
    sweep_rows = whole_rows
    while sweep_rows > 4096 and sweep_rows % (2 * span) == 0:
        sweep_rows = sweep_rows // 2
    local_heads = HEADS // groups
    head_width = width // HEADS
    shard_width = local_heads * head_width
    gain_one = gain_one_full.astype(jnp.float32)
    gain_two = gain_two_full.astype(jnp.float32)
    expand_bias_f = expand_bias_full.astype(jnp.float32)
    reduce_bias_f = reduce_bias_full.astype(jnp.float32)
    condition = time_features(time_step, mod_full.shape[1] // 2)
    modulations = jnp.einsum(
        "mc,fc->mf", condition, mod_full, preferred_element_type=jnp.float32
    ) + mod_bias_full.astype(jnp.float32)
    own_index = (group_id * blocks + block_id) * tokens_dev + jnp.arange(
        tokens_dev, dtype=jnp.int32
    )
    local_rows = jnp.arange(span, dtype=jnp.int32)
    query_index = (
        local_rows // tokens_dev * blocks + block_id
    ) * tokens_dev + local_rows % tokens_dev
    outputs = []
    input_grads = []
    totals = None
    shares = None
    for micro_index in range(micro):
        doc_lengths = lengths[micro_index]
        shift1, scale1, gate1, shift2, scale2, gate2 = jnp.split(modulations[micro_index], 6)
        values = tokens[micro_index].astype(jnp.float32)
        own_segment, own_place = doc_layout(own_index, doc_lengths)
        query_segment, unused_place = doc_layout(query_index, doc_lengths)

        def key_segments(start, count, doc_lengths=doc_lengths):
            rows = jnp.arange(count, dtype=jnp.int32)
            owner = rows // span
            within = rows % span
            index = (within // tokens_dev * blocks + owner) * tokens_dev + within % tokens_dev
            return doc_layout(index, doc_lengths)[0]

        normed, normed_back = jax.vjp(modulate, values, gain_one, shift1, scale1)
        normed_b = normed.astype(jnp.bfloat16)
        qkv = jnp.dot(normed_b, input_full, preferred_element_type=jnp.float32)
        query_b = (
            rotary(qkv[:, :width].reshape(tokens_dev, HEADS, head_width), own_place, 1.0)
            .reshape(tokens_dev, width)
            .astype(jnp.bfloat16)
        )
        key_b = (
            rotary(qkv[:, width : 2 * width].reshape(tokens_dev, HEADS, head_width), own_place, 1.0)
            .reshape(tokens_dev, width)
            .astype(jnp.bfloat16)
        )
        value_b = qkv[:, 2 * width :].astype(jnp.bfloat16)
        query_heads, key_heads, value_heads = (
            lax.all_to_all(query_b, "ulysses", split_axis=1, concat_axis=0, tiled=True),
            lax.all_to_all(key_b, "ulysses", split_axis=1, concat_axis=0, tiled=True),
            lax.all_to_all(value_b, "ulysses", split_axis=1, concat_axis=0, tiled=True),
        )
        query_three = query_heads.reshape(span, local_heads, head_width)
        key_three = key_heads.reshape(span, local_heads, head_width)
        value_three = value_heads.reshape(span, local_heads, head_width)

        def attend_core(
            carry,
            key_part,
            value_part,
            start,
            query_three=query_three,
            query_segment=query_segment,
            key_segments=key_segments,
        ):
            count = key_part.shape[0]
            piece_segment = key_segments(start, count)
            highest, weight_sum, accum = carry
            keys = key_part.reshape(count, local_heads, head_width)
            vals = value_part.reshape(count, local_heads, head_width)
            scores = (
                jnp.einsum("qhd,khd->hqk", query_three, keys, preferred_element_type=jnp.float32)
                * 0.125
            )
            allowed = (query_segment[:, None] == piece_segment[None, :])[None]
            new_high = jnp.maximum(highest, jnp.max(jnp.where(allowed, scores, -1e30), -1))
            weights = jnp.where(allowed, jnp.exp(scores - new_high[..., None]), 0.0)
            weight_sum = jnp.sum(weights, -1)
            accum = jnp.einsum(
                "hqk,khd->hqd",
                weights.astype(jnp.bfloat16),
                vals,
                preferred_element_type=jnp.float32,
            )
            return (new_high, weight_sum, accum)

        def attend(carry, piece, start, attend_core=attend_core):
            key_part, value_part = piece
            return attend_core(carry, key_part, value_part, start)

        start_state = (
            jnp.full((local_heads, span), -1e30, jnp.float32),
            jnp.zeros((local_heads, span), jnp.float32),
            jnp.zeros((local_heads, span, head_width), jnp.float32),
        )
        folded = attend(
            start_state,
            (
                lax.all_gather(key_heads, "blk", axis=0, tiled=True),
                lax.all_gather(value_heads, "blk", axis=0, tiled=True),
            ),
            jnp.int32(0),
        )
        highest, weight_sum, accum = (folded[0], folded[1], folded[2])
        log_total = highest + jnp.log(weight_sum)
        attended = (
            (accum / weight_sum[..., None])
            .transpose(1, 0, 2)
            .reshape(span, shard_width)
            .astype(jnp.bfloat16)
        )
        merged = lax.all_to_all(attended, "ulysses", split_axis=0, concat_axis=1, tiled=True)
        attn = jnp.dot(merged, output_full, preferred_element_type=jnp.float32)
        middle = values + gate1 * attn
        second, second_back = jax.vjp(modulate, middle, gain_two, shift2, scale2)
        second_b = second.astype(jnp.bfloat16)
        hidden = jnp.dot(second_b, expand_full, preferred_element_type=jnp.float32) + expand_bias_f
        active, active_back = jax.vjp(gelu_tanh, hidden)
        active_b = active.astype(jnp.bfloat16)
        branch = jnp.dot(active_b, reduce_full, preferred_element_type=jnp.float32) + reduce_bias_f
        outputs.append((middle + gate2 * branch).astype(jnp.bfloat16))
        grad_out = cotangent[micro_index].astype(jnp.float32)
        grad_gate2 = jnp.sum(grad_out * branch, 0)
        grad_branch = (gate2 * grad_out).astype(jnp.bfloat16)
        reduce_grad = jnp.einsum(
            "tf,td->fd", active_b, grad_branch, preferred_element_type=jnp.float32
        )
        reduce_bias_grad = jnp.sum(grad_branch.astype(jnp.float32), 0)
        grad_active = jnp.einsum(
            "td,fd->tf", grad_branch, reduce_full, preferred_element_type=jnp.float32
        )
        grad_hidden = active_back(grad_active)[0].astype(jnp.bfloat16)
        expand_grad = jnp.einsum(
            "td,tf->df", second_b, grad_hidden, preferred_element_type=jnp.float32
        )
        expand_bias_grad = jnp.sum(grad_hidden.astype(jnp.float32), 0)
        grad_second = jnp.einsum(
            "tf,df->td", grad_hidden, expand_full, preferred_element_type=jnp.float32
        )
        middle_part, gain_two_grad, grad_shift2, grad_scale2 = second_back(grad_second)
        grad_middle = grad_out + middle_part
        grad_gate1 = jnp.sum(grad_middle * attn, 0)
        grad_attn = (gate1 * grad_middle).astype(jnp.bfloat16)
        output_grad = jnp.einsum("ti,to->io", merged, grad_attn, preferred_element_type=jnp.float32)
        grad_merged = jnp.einsum(
            "to,io->ti", grad_attn, output_full, preferred_element_type=jnp.float32
        ).astype(jnp.bfloat16)
        grad_heads = lax.all_to_all(grad_merged, "ulysses", split_axis=1, concat_axis=0, tiled=True)
        grad_three = grad_heads.reshape(span, local_heads, head_width)
        delta = jnp.einsum(
            "qhd,qhd->hq",
            grad_three,
            attended.reshape(span, local_heads, head_width),
            preferred_element_type=jnp.float32,
        )
        log_all, delta_all = (
            lax.all_gather(log_total, "blk", axis=1, tiled=True),
            lax.all_gather(delta, "blk", axis=1, tiled=True),
        )

        def key_grads(
            carry,
            piece,
            start,
            key_three=key_three,
            value_three=value_three,
            query_segment=query_segment,
            key_segments=key_segments,
            log_all=log_all,
            delta_all=delta_all,
        ):
            query_part, grad_part = piece
            count = query_part.shape[0]
            piece_segment = key_segments(start, count)
            queries = query_part.reshape(count, local_heads, head_width)
            grads = grad_part.reshape(count, local_heads, head_width)
            scores = (
                jnp.einsum("qhd,khd->hqk", queries, key_three, preferred_element_type=jnp.float32)
                * 0.125
            )
            allowed = (piece_segment[:, None] == query_segment[None, :])[None]
            probs = jnp.where(allowed, jnp.exp(scores - log_all[..., None]), 0.0)
            grad_value = jnp.einsum(
                "hqk,qhd->hkd",
                probs.astype(jnp.bfloat16),
                grads,
                preferred_element_type=jnp.float32,
            )
            grad_probs = jnp.einsum(
                "qhd,khd->hqk", grads, value_three, preferred_element_type=jnp.float32
            )
            grad_scores = (probs * (grad_probs - delta_all[..., None])).astype(jnp.bfloat16)
            grad_key = jnp.einsum(
                "hqk,qhd->hkd", grad_scores, queries, preferred_element_type=jnp.float32
            )
            return (grad_key, grad_value)

        zero_heads = jnp.zeros((local_heads, span, head_width), jnp.float32)
        grad_key, grad_value = key_grads(
            (zero_heads, zero_heads),
            (
                lax.all_gather(query_heads, "blk", axis=0, tiled=True),
                lax.all_gather(grad_heads, "blk", axis=0, tiled=True),
            ),
            jnp.int32(0),
        )

        def query_core(
            grad_query,
            key_part,
            value_part,
            start,
            query_three=query_three,
            grad_three=grad_three,
            query_segment=query_segment,
            key_segments=key_segments,
            log_total=log_total,
            delta=delta,
        ):
            count = key_part.shape[0]
            piece_segment = key_segments(start, count)
            keys = key_part.reshape(count, local_heads, head_width)
            vals = value_part.reshape(count, local_heads, head_width)
            scores = (
                jnp.einsum("qhd,khd->hqk", query_three, keys, preferred_element_type=jnp.float32)
                * 0.125
            )
            allowed = (query_segment[:, None] == piece_segment[None, :])[None]
            probs = jnp.where(allowed, jnp.exp(scores - log_total[..., None]), 0.0)
            grad_probs = jnp.einsum(
                "qhd,khd->hqk", grad_three, vals, preferred_element_type=jnp.float32
            )
            grad_scores = (probs * (grad_probs - delta[..., None])).astype(jnp.bfloat16)
            return jnp.einsum("hqk,khd->hqd", grad_scores, keys, preferred_element_type=jnp.float32)

        def query_grads(state, piece, start, query_core=query_core):
            return query_core(state, piece[0], piece[1], start)

        grad_query = query_grads(
            zero_heads,
            (
                lax.all_gather(key_heads, "blk", axis=0, tiled=True),
                lax.all_gather(value_heads, "blk", axis=0, tiled=True),
            ),
            jnp.int32(0),
        )
        query_back = (
            (grad_query * 0.125).transpose(1, 0, 2).reshape(span, shard_width).astype(jnp.bfloat16)
        )
        key_back = (
            (grad_key * 0.125).transpose(1, 0, 2).reshape(span, shard_width).astype(jnp.bfloat16)
        )
        value_back = grad_value.transpose(1, 0, 2).reshape(span, shard_width).astype(jnp.bfloat16)
        query_tok, key_tok, value_tok = (
            lax.all_to_all(query_back, "ulysses", split_axis=0, concat_axis=1, tiled=True),
            lax.all_to_all(key_back, "ulysses", split_axis=0, concat_axis=1, tiled=True),
            lax.all_to_all(value_back, "ulysses", split_axis=0, concat_axis=1, tiled=True),
        )
        query_plain = rotary(
            query_tok.astype(jnp.float32).reshape(tokens_dev, HEADS, head_width), own_place, -1.0
        ).reshape(tokens_dev, width)
        key_plain = rotary(
            key_tok.astype(jnp.float32).reshape(tokens_dev, HEADS, head_width), own_place, -1.0
        ).reshape(tokens_dev, width)
        grad_qkv = jnp.concatenate(
            [query_plain, key_plain, value_tok.astype(jnp.float32)], 1
        ).astype(jnp.bfloat16)
        input_grad = jnp.einsum("td,tf->df", normed_b, grad_qkv, preferred_element_type=jnp.float32)
        grad_normed = jnp.einsum(
            "tf,df->td", grad_qkv, input_full, preferred_element_type=jnp.float32
        )
        values_part, gain_one_grad, grad_shift1, grad_scale1 = normed_back(grad_normed)
        input_grads.append((grad_middle + values_part).astype(jnp.bfloat16))
        grad_mods = jnp.concatenate(
            [grad_shift1, grad_scale1, grad_gate1, grad_shift2, grad_scale2, grad_gate2]
        )
        modulate_grad = grad_mods[:, None] * condition[micro_index].astype(jnp.float32)[None, :]
        micro_grads = (
            modulate_grad,
            grad_mods,
            gain_one_grad,
            input_grad,
            output_grad,
            gain_two_grad,
            expand_grad,
            expand_bias_grad,
            reduce_grad,
            reduce_bias_grad,
        )
        totals = (
            micro_grads
            if totals is None
            else tuple((left + right for left, right in zip(totals, micro_grads)))
        )
    shares = lax.psum_scatter(totals, ("ulysses", "blk"), scatter_dimension=0, tiled=True)
    return (
        jnp.stack(outputs),
        jnp.stack(input_grads),
        shares[0],
        shares[1],
        shares[2],
        shares[3],
        shares[4],
        shares[5],
        shares[6],
        shares[7],
        shares[8],
        shares[9],
    )


def solution(mesh):
    in_specs = (
        P(None, ("ulysses", "blk"), None),
        P(None, ("ulysses", "blk"), None),
        P(),
        P(),
        P(("ulysses", "blk"), None),
        P(("ulysses", "blk")),
        P(("ulysses", "blk")),
        P(("ulysses", "blk"), None),
        P(("ulysses", "blk"), None),
        P(("ulysses", "blk")),
        P(("ulysses", "blk"), None),
        P(("ulysses", "blk")),
        P(("ulysses", "blk"), None),
        P(("ulysses", "blk")),
    )
    out_specs = (
        P(None, ("ulysses", "blk"), None),
        P(None, ("ulysses", "blk"), None),
        P(("ulysses", "blk"), None),
        P(("ulysses", "blk")),
        P(("ulysses", "blk")),
        P(("ulysses", "blk"), None),
        P(("ulysses", "blk"), None),
        P(("ulysses", "blk")),
        P(("ulysses", "blk"), None),
        P(("ulysses", "blk")),
        P(("ulysses", "blk"), None),
        P(("ulysses", "blk")),
    )
    return jax.shard_map(
        on_device, mesh=mesh, in_specs=in_specs, out_specs=out_specs, check_vma=False
    )
```

profile of v0, /device:TPU:0, one launch (start us, length us, event | category | flops | bytes accessed | tf_op | source)
XLA Modules:
  0.0 1814.0 jit_solution(7308171736890220033)
XLA Ops:
  21.7 42.4 %all-reduce.11 = (bf16[4608]{0:T(1024)(128)(2,1)S(1)}, bf16[768]{0:T(1024)(128)(2,1)S(1)}, bf16[3072]{0:T(1024)(128)(2,1)S(1)}, bf16[768]{0:T(1024)(128)(2,1)S(1)}, bf16[768]{0:T(1024)(128)(2,1)S(1)}) all-reduce(bf16[4608]{0:T(1024)(128)(2,1)S(1)} %dynamic-update-slice, ...), channel_id=1, replica_groups=mesh['ulysses'=4,'blk'=8] {'ulysses','blk'}, use_global_device_ids=true, to_apply=%add | all-reduce | flops 9984 | bytes 39936
  74.9 55.2 %all-gather.8.cloned.1.call-done = bf16[768,2304]{1,0:T(8,128)(2,1)} async-done(((bf16[24,2304]{1,0:T(8,128)(2,1)}), bf16[768,2304]{1,0:T(8,128)(2,1)}) %all-gather.8.cloned.1.call-update) | async-done | bytes 3538960 | tf_op jit(solution)/shard_map/all_gather | solution.py:66
  153.0 33.3 %all_gather.95 = bf16[2048,192]{1,0:T(8,128)(2,1)S(1)} all-gather(bf16[256,192]{1,0:T(8,128)(2,1)S(1)} %bitcast.510), channel_id=1, replica_groups=mesh['ulysses'=4,'blk'=8] {'blk'}, dimensions={0}, use_global_device_ids=true | all-gather | bytes 884736 | tf_op jit(solution)/shard_map/all_gather | solution.py:200
  188.5 34.0 %all_gather.94 = bf16[2048,192]{1,0:T(8,128)(2,1)S(1)} all-gather(bf16[256,192]{1,0:T(8,128)(2,1)S(1)} %bitcast.514), channel_id=1, replica_groups=mesh['ulysses'=4,'blk'=8] {'blk'}, dimensions={0}, use_global_device_ids=true | all-gather | bytes 884736 | tf_op jit(solution)/shard_map/all_gather | solution.py:199
  233.6 37.6 %all_gather.106 = bf16[2048,192]{1,0:T(8,128)(2,1)S(1)} all-gather(bf16[256,192]{1,0:T(8,128)(2,1)S(1)} %bitcast.513), channel_id=1, replica_groups=mesh['ulysses'=4,'blk'=8] {'blk'}, dimensions={0}, use_global_device_ids=true | all-gather | bytes 884736 | tf_op jit(solution)/shard_map/all_gather | solution.py:302
  278.4 32.0 %all_gather.107 = f32[3,2048]{1,0:T(4,128)} all-gather(f32[3,256]{1,0:T(4,128)S(1)} %log_add_fusion.2), channel_id=1, replica_groups=mesh['ulysses'=4,'blk'=8] {'blk'}, dimensions={1}, use_global_device_ids=true | all-gather | bytes 27648 | tf_op jit(solution)/shard_map/all_gather | solution.py:257
  317.6 21.4 %all-gather.14.cloned.1.call-done = bf16[3072,768]{1,0:T(8,128)(2,1)} async-done(((bf16[96,768]{1,0:T(8,128)(2,1)}), bf16[3072,768]{1,0:T(8,128)(2,1)}) %all-gather.14.cloned.1.call-update) | async-done | bytes 4718608 | tf_op jit(solution)/shard_map/all_gather | solution.py:71
  339.1 4.7 convert_reduce_fusion.2
  358.5 31.8 %all_gather.109 = f32[3,2048]{1,0:T(4,128)} all-gather(f32[3,256]{1,0:T(4,128)S(1)} %fusion.173), channel_id=1, replica_groups=mesh['ulysses'=4,'blk'=8] {'blk'}, dimensions={1}, use_global_device_ids=true | all-gather | bytes 27648 | tf_op jit(solution)/shard_map/all_gather | solution.py:258
  390.3 6.5 fusion.74
  396.7 33.1 %all_gather.108 = bf16[2048,192]{1,0:T(8,128)(2,1)S(1)} all-gather(bf16[256,192]{1,0:T(8,128)(2,1)} %bitcast.517), channel_id=1, replica_groups=mesh['ulysses'=4,'blk'=8] {'blk'}, dimensions={0}, use_global_device_ids=true | all-gather | bytes 884736 | tf_op jit(solution)/shard_map/all_gather | solution.py:303
  430.3 5.7 fusion.77
  446.0 4.0 all-to-all-start.13
  511.1 4.1 all-to-all-start.8
  552.9 35.2 %all_gather.104 = bf16[2048,192]{1,0:T(8,128)(2,1)} all-gather(bf16[256,192]{1,0:T(8,128)(2,1)} %bitcast.45), channel_id=1, replica_groups=mesh['ulysses'=4,'blk'=8] {'blk'}, dimensions={0}, use_global_device_ids=true | all-gather | bytes 884736 | tf_op jit(solution)/shard_map/all_gather | solution.py:199
  602.1 34.9 %all_gather.105 = bf16[2048,192]{1,0:T(8,128)(2,1)} all-gather(bf16[256,192]{1,0:T(8,128)(2,1)} %bitcast.48), channel_id=1, replica_groups=mesh['ulysses'=4,'blk'=8] {'blk'}, dimensions={0}, use_global_device_ids=true | all-gather | bytes 884736 | tf_op jit(solution)/shard_map/all_gather | solution.py:200
  643.2 5.2 fusion.81
  648.4 4.0 all-to-all-start.5
  652.4 34.9 %all_gather.103 = bf16[2048,192]{1,0:T(8,128)(2,1)} all-gather(bf16[256,192]{1,0:T(8,128)(2,1)} %bitcast.32), channel_id=1, replica_groups=mesh['ulysses'=4,'blk'=8] {'blk'}, dimensions={0}, use_global_device_ids=true | all-gather | bytes 884736 | tf_op jit(solution)/shard_map/all_gather | solution.py:200
  700.5 34.8 %all_gather.102 = bf16[2048,192]{1,0:T(8,128)(2,1)} all-gather(bf16[256,192]{1,0:T(8,128)(2,1)} %bitcast.29), channel_id=1, replica_groups=mesh['ulysses'=4,'blk'=8] {'blk'}, dimensions={0}, use_global_device_ids=true | all-gather | bytes 884736 | tf_op jit(solution)/shard_map/all_gather | solution.py:199
  737.5 5.2 select_reduce_fusion.1
  743.9 35.4 %all_gather.114 = bf16[2048,192]{1,0:T(8,128)(2,1)} all-gather(bf16[256,192]{1,0:T(8,128)(2,1)} %bitcast.92), channel_id=1, replica_groups=mesh['ulysses'=4,'blk'=8] {'blk'}, dimensions={0}, use_global_device_ids=true | all-gather | bytes 884736 | tf_op jit(solution)/shard_map/all_gather | solution.py:302
  785.1 36.0 %all_gather.110 = bf16[2048,192]{1,0:T(8,128)(2,1)} all-gather(bf16[256,192]{1,0:T(8,128)(2,1)} %bitcast.76), channel_id=1, replica_groups=mesh['ulysses'=4,'blk'=8] {'blk'}, dimensions={0}, use_global_device_ids=true | all-gather | bytes 884736 | tf_op jit(solution)/shard_map/all_gather | solution.py:302
  826.8 4.8 fusion.2
  858.7 32.2 %all_gather.115 = f32[3,2048]{1,0:T(4,128)} all-gather(f32[3,256]{1,0:T(4,128)} %log_add_fusion), channel_id=1, replica_groups=mesh['ulysses'=4,'blk'=8] {'blk'}, dimensions={1}, use_global_device_ids=true | all-gather | bytes 27648 | tf_op jit(solution)/shard_map/all_gather | solution.py:257
  890.9 32.8 %all_gather.111 = f32[3,2048]{1,0:T(4,128)} all-gather(f32[3,256]{1,0:T(4,128)} %log_add_fusion.1), channel_id=1, replica_groups=mesh['ulysses'=4,'blk'=8] {'blk'}, dimensions={1}, use_global_device_ids=true | all-gather | bytes 27648 | tf_op jit(solution)/shard_map/all_gather | solution.py:257
  938.8 4.8 convert_reduce_fusion
  958.5 4.0 all-to-all-start.20
  977.4 4.1 all-to-all-start.16
  986.6 6.9 fusion.72
  993.5 32.2 %all_gather.117 = f32[3,2048]{1,0:T(4,128)} all-gather(f32[3,256]{1,0:T(4,128)} %fusion.171), channel_id=1, replica_groups=mesh['ulysses'=4,'blk'=8] {'blk'}, dimensions={1}, use_global_device_ids=true | all-gather | bytes 27648 | tf_op jit(solution)/shard_map/all_gather | solution.py:258
  1030.8 31.4 %all_gather.113 = f32[3,2048]{1,0:T(4,128)} all-gather(f32[3,256]{1,0:T(4,128)S(1)} %fusion.172), channel_id=1, replica_groups=mesh['ulysses'=4,'blk'=8] {'blk'}, dimensions={1}, use_global_device_ids=true | all-gather | bytes 27648 | tf_op jit(solution)/shard_map/all_gather | solution.py:258
  1062.3 6.8 fusion.73
  1069.1 35.5 %all_gather.116 = bf16[2048,192]{1,0:T(8,128)(2,1)} all-gather(bf16[256,192]{1,0:T(8,128)(2,1)} %bitcast.94), channel_id=1, replica_groups=mesh['ulysses'=4,'blk'=8] {'blk'}, dimensions={0}, use_global_device_ids=true | all-gather | bytes 884736 | tf_op jit(solution)/shard_map/all_gather | solution.py:303
  1106.8 5.2 fusion.63
  1111.9 6.7 fusion.75
  1126.1 35.2 %all_gather.112 = bf16[2048,192]{1,0:T(8,128)(2,1)} all-gather(bf16[256,192]{1,0:T(8,128)(2,1)} %bitcast.78), channel_id=1, replica_groups=mesh['ulysses'=4,'blk'=8] {'blk'}, dimensions={0}, use_global_device_ids=true | all-gather | bytes 884736 | tf_op jit(solution)/shard_map/all_gather | solution.py:303
  1163.4 6.8 fusion.76
  1170.2 5.2 fusion.66
  1250.2 4.0 all-to-all-start.19
  1301.2 4.1 add_add_fusion.2
  1309.6 5.1 add_add_fusion.1
  1318.9 5.1 add_add_fusion
  1324.9 41.2 %all-reduce.10 = (f32[4608]{0:T(1024)S(1)}, f32[768]{0:T(1024)S(1)}, f32[768]{0:T(1024)S(1)}, f32[3072]{0:T(1024)S(1)}, f32[768]{0:T(1024)S(1)}) all-reduce(f32[4608]{0:T(1024)S(1)} %add_add_fusion.10, f32[768]{0:T(1024)S(1)} %add_add_fusion.14, ...), channel_id=3, replica_groups=mesh['ulysses'=4,'blk'=8] {'ulysses','blk'}, use_global_device_ids=true, to_apply=%region_61.62.clone | all-reduce | flops 9984 | bytes 79872
  1370.9 28.4 %reduce-scatter.6.cloned.1.call-done = f32[144,128]{1,0:T(8,128)} async-done(((f32[4608,128]{1,0:T(8,128)}), f32[144,128]{1,0:T(8,128)}) %reduce-scatter.6.cloned.1.call-update) | async-done | bytes 73744 | tf_op jit(solution)/shard_map/reduce_scatter | solution.py:395
  1399.4 124.4 %reduce-scatter.8.cloned.1.call-done = f32[24,2304]{1,0:T(8,128)} async-done(((f32[768,2304]{1,0:T(8,128)}), f32[24,2304]{1,0:T(8,128)}) %reduce-scatter.8.cloned.1.call-update) | async-done | bytes 221200 | tf_op jit(solution)/shard_map/reduce_scatter | solution.py:395
  1523.8 142.2 %reduce-scatter.12.cloned.1.call-done = f32[24,3072]{1,0:T(8,128)} async-done(((f32[768,3072]{1,0:T(8,128)}), f32[24,3072]{1,0:T(8,128)}) %reduce-scatter.12.cloned.1.call-update) | async-done | bytes 294928 | tf_op jit(solution)/shard_map/reduce_scatter | solution.py:395
  1666.0 140.9 %reduce-scatter.14.cloned.1.call-done = f32[96,768]{1,0:T(8,128)} async-done(((f32[3072,768]{1,0:T(8,128)}), f32[96,768]{1,0:T(8,128)}) %reduce-scatter.14.cloned.1.call-update) | async-done | bytes 294928 | tf_op jit(solution)/shard_map/reduce_scatter | solution.py:395
  (777 shorter events, 475.2 us)
Async XLA Ops:
  7.2 122.9 %copy-start.8 = (bf16[3,64,768]{2,1,0:T(8,128)(2,1)S(1)}, bf16[3,64,768]{2,1,0:T(8,128)(2,1)}, u32[]{:S(2)}) copy-start(bf16[3,64,768]{2,1,0:T(8,128)(2,1)} %param.14) | copy-start | bytes 884740
  7.2 65.3 %all-gather.6.cloned.1.call-start = ((), (), s32[]{:S(2)}) async-start(), calls=%async_computation.29 | async-start | bytes 1216512 | tf_op jit(solution)/shard_map/all_gather | solution.py:63
  7.9 122.2 %all-gather.8.cloned.1.call-start = ((), (), s32[]{:S(2)}) async-start(), calls=%async_computation.30 | async-start | bytes 3649536 | tf_op jit(solution)/shard_map/all_gather | solution.py:66
  8.7 302.9 %all-gather.10.cloned.1.call-start = ((), (), s32[]{:S(2)}) async-start(), calls=%async_computation.31 | async-start | bytes 1216512 | tf_op jit(solution)/shard_map/all_gather | solution.py:67
  9.4 304.8 %all-gather.12.cloned.1.call-start = ((), (), s32[]{:S(2)}) async-start(), calls=%async_computation.32 | async-start | bytes 4866048 | tf_op jit(solution)/shard_map/all_gather | solution.py:69
  10.0 329.1 %all-gather.14.cloned.1.call-start = ((), (), s32[]{:S(2)}) async-start(), calls=%async_computation.33 | async-start | bytes 4866048 | tf_op jit(solution)/shard_map/all_gather | solution.py:71
  12.4 124.9 %copy-start.113 = (f32[64]{0:T(128)}, f32[64]{0:T(128)S(1)}, u32[]{:S(2)}) copy-start(f32[64]{0:T(128)S(1)} %broadcast_multiply_fusion.8) | copy-start | bytes 772
  17.4 120.5 %copy-start.124 = (f32[64]{0:T(128)}, f32[64]{0:T(128)S(1)}, u32[]{:S(2)}) copy-start(f32[64]{0:T(128)S(1)} %get-tuple-element.218) | copy-start | bytes 772
  66.3 71.5 %copy-start.65 = (f32[64,32]{1,0:T(8,128)}, f32[64,32]{1,0:T(8,128)S(1)}, u32[]{:S(2)}) copy-start(f32[64,32]{1,0:T(8,128)S(1)} %get-tuple-element.194) | copy-start | bytes 24580
  74.9 63.0 %copy-start.78 = (f32[768]{0:T(1024)}, f32[768]{0:T(1024)S(1)}, u32[]{:S(2)}) copy-start(f32[768]{0:T(1024)S(1)} %get-tuple-element.71) | copy-start | bytes 9220
  133.8 7.9 all-to-all-start.2
  141.7 46.2 %copy-start.54 = (bf16[64,4,192]{2,0,1:T(8,128)(2,1)}, bf16[64,4,192]{2,0,1:T(8,128)(2,1)S(1)}, u32[]{:S(2)}) copy-start(bf16[64,4,192]{2,0,1:T(8,128)(2,1)S(1)} %all-to-all-done.2) | copy-start | bytes 294916
  141.7 7.9 all-to-all-start
  149.6 38.2 %all-to-all-start.1 = ((bf16[64,4,192]{2,0,1:T(8,128)(2,1)}), bf16[64,4,192]{2,0,1:T(8,128)(2,1)S(1)}, u32[]{:S(2)}, u32[]{:S(2)}) async-start(bf16[64,4,192]{2,0,1:T(8,128)(2,1)} %copy.277), calls=%async_computation.1 | async-start | bytes 262144 | tf_op jit(solution)/shard_map/all_to_all | solution.py:150
  229.6 80.8 %all-to-all-start.3 = ((bf16[4,64,192]{2,1,0:T(8,128)(2,1)}), bf16[4,64,192]{2,1,0:T(8,128)(2,1)}, u32[]{:S(2)}, u32[]{:S(2)}) async-start(bf16[4,64,192]{2,1,0:T(8,128)(2,1)} %copy.281), calls=%async_computation.3 | async-start | bytes 262144 | tf_op jit(solution)/shard_map/all_to_all | solution.py:212
  273.0 66.0 %copy-start.22 = (bf16[3,64,768]{2,1,0:T(8,128)(2,1)S(1)}, bf16[3,64,768]{2,1,0:T(8,128)(2,1)}, u32[]{:S(2)}) copy-start(bf16[3,64,768]{2,1,0:T(8,128)(2,1)} %param.15) | copy-start | bytes 884740
  273.1 66.0 %copy-start.100 = (f32[768]{0:T(1024)S(1)}, f32[768]{0:T(1024)}, u32[]{:S(2)}) copy-start(f32[768]{0:T(1024)} %get-tuple-element.56) | copy-start | bytes 9220
  347.8 48.9 %copy-start.29 = (f32[64,768]{1,0:T(8,128)}, f32[64,768]{1,0:T(8,128)S(1)}, u32[]{:S(2)}) copy-start(f32[64,768]{1,0:T(8,128)S(1)} %get-tuple-element.102) | copy-start | bytes 589828
  347.9 48.9 %copy-start.161 = (f32[64]{0:T(128)}, f32[64]{0:T(128)S(1)}, u32[]{:S(2)}) copy-start(f32[64]{0:T(128)S(1)} %negate_multiply_fusion.5) | copy-start | bytes 772
  349.3 7.9 all-to-all-start.12
  437.0 9.0 all-to-all-start.14
  446.0 10.8 all-to-all-start.13
  456.8 23.7 %all-to-all-start.15 = ((bf16[4,64,192]{2,1,0:T(8,128)(2,1)}), bf16[4,64,192]{2,1,0:T(8,128)(2,1)}, u32[]{:S(2)}, u32[]{:S(2)}) async-start(bf16[4,64,192]{2,1,0:T(8,128)(2,1)} %copy.319), calls=%async_computation.15 | async-start | bytes 262144 | tf_op jit(solution)/shard_map/all_to_all | solution.py:357
  511.1 25.0 %all-to-all-start.8 = ((bf16[64,4,192]{2,0,1:T(8,128)(2,1)}), bf16[64,4,192]{2,0,1:T(8,128)(2,1)}, u32[]{:S(2)}, u32[]{:S(2)}) async-start(bf16[64,4,192]{2,0,1:T(8,128)(2,1)} %copy.296), calls=%async_computation.8 | async-start | bytes 262144 | tf_op jit(solution)/shard_map/all_to_all | solution.py:149
  536.0 12.9 all-to-all-start.9
  548.9 49.3 %all-to-all-start.10 = ((bf16[64,4,192]{2,0,1:T(8,128)(2,1)}), bf16[64,4,192]{2,0,1:T(8,128)(2,1)}, u32[]{:S(2)}, u32[]{:S(2)}) async-start(bf16[64,4,192]{2,0,1:T(8,128)(2,1)} %copy.301), calls=%async_computation.10 | async-start | bytes 262144 | tf_op jit(solution)/shard_map/all_to_all | solution.py:151
  598.2 41.1 %all-to-all-start.6 = ((bf16[64,4,192]{2,0,1:T(8,128)(2,1)}), bf16[64,4,192]{2,0,1:T(8,128)(2,1)}, u32[]{:S(2)}, u32[]{:S(2)}) async-start(bf16[64,4,192]{2,0,1:T(8,128)(2,1)} %copy.290), calls=%async_computation.6 | async-start | bytes 262144 | tf_op jit(solution)/shard_map/all_to_all | solution.py:151
  639.3 9.1 all-to-all-start.4
  648.4 48.1 %all-to-all-start.5 = ((bf16[64,4,192]{2,0,1:T(8,128)(2,1)}), bf16[64,4,192]{2,0,1:T(8,128)(2,1)}, u32[]{:S(2)}, u32[]{:S(2)}) async-start(bf16[64,4,192]{2,0,1:T(8,128)(2,1)} %copy.288), calls=%async_computation.5 | async-start | bytes 262144 | tf_op jit(solution)/shard_map/all_to_all | solution.py:150
  696.5 149.9 %all-to-all-start.11 = ((bf16[4,64,192]{2,1,0:T(8,128)(2,1)}), bf16[4,64,192]{2,1,0:T(8,128)(2,1)}, u32[]{:S(2)}, u32[]{:S(2)}) async-start(bf16[4,64,192]{2,1,0:T(8,128)(2,1)} %copy.303), calls=%async_computation.11 | async-start | bytes 262144 | tf_op jit(solution)/shard_map/all_to_all | solution.py:212
  846.4 80.7 %all-to-all-start.7 = ((bf16[4,64,192]{2,1,0:T(8,128)(2,1)}), bf16[4,64,192]{2,1,0:T(8,128)(2,1)}, u32[]{:S(2)}, u32[]{:S(2)}) async-start(bf16[4,64,192]{2,1,0:T(8,128)(2,1)} %copy.292), calls=%async_computation.7 | async-start | bytes 262144 | tf_op jit(solution)/shard_map/all_to_all | solution.py:212
  958.5 18.9 %all-to-all-start.20 = ((bf16[64,4,192]{2,0,1:T(8,128)(2,1)}), bf16[64,4,192]{2,0,1:T(8,128)(2,1)}, u32[]{:S(2)}, u32[]{:S(2)}) async-start(bf16[64,4,192]{2,0,1:T(8,128)(2,1)} %copy.337), calls=%async_computation.20 | async-start | bytes 262144 | tf_op jit(solution)/shard_map/all_to_all | solution.py:248
  962.5 408.4 %reduce-scatter.10.cloned.1.call-start = ((), (), s32[]{:S(2)}) async-start(), calls=%async_computation.36 | async-start | bytes 2433024 | tf_op jit(solution)/shard_map/reduce_scatter | solution.py:395
  977.4 48.3 %all-to-all-start.16 = ((bf16[64,4,192]{2,0,1:T(8,128)(2,1)}), bf16[64,4,192]{2,0,1:T(8,128)(2,1)}, u32[]{:S(2)}, u32[]{:S(2)}) async-start(bf16[64,4,192]{2,0,1:T(8,128)(2,1)} %copy.321), calls=%async_computation.16 | async-start | bytes 262144 | tf_op jit(solution)/shard_map/all_to_all | solution.py:248
  1122.1 70.5 %all-to-all-start.22 = ((bf16[4,64,192]{2,1,0:T(8,128)(2,1)}), bf16[4,64,192]{2,1,0:T(8,128)(2,1)}, u32[]{:S(2)}, u32[]{:S(2)}) async-start(bf16[4,64,192]{2,1,0:T(8,128)(2,1)} %copy.347), calls=%async_computation.22 | async-start | bytes 262144 | tf_op jit(solution)/shard_map/all_to_all | solution.py:356
  1192.6 13.3 all-to-all-start.21
  1205.9 18.5 %all-to-all-start.23 = ((bf16[4,64,192]{2,1,0:T(8,128)(2,1)}), bf16[4,64,192]{2,1,0:T(8,128)(2,1)}, u32[]{:S(2)}, u32[]{:S(2)}) async-start(bf16[4,64,192]{2,1,0:T(8,128)(2,1)} %copy.351), calls=%async_computation.23 | async-start | bytes 262144 | tf_op jit(solution)/shard_map/all_to_all | solution.py:357
  1224.4 11.0 all-to-all-start.18
  1235.4 14.8 all-to-all-start.17
  1250.2 24.2 %all-to-all-start.19 = ((bf16[4,64,192]{2,1,0:T(8,128)(2,1)}), bf16[4,64,192]{2,1,0:T(8,128)(2,1)}, u32[]{:S(2)}, u32[]{:S(2)}) async-start(bf16[4,64,192]{2,1,0:T(8,128)(2,1)} %copy.335), calls=%async_computation.19 | async-start | bytes 262144 | tf_op jit(solution)/shard_map/all_to_all | solution.py:357
  1254.2 145.2 %reduce-scatter.6.cloned.1.call-start = ((), (), s32[]{:S(2)}) async-start(), calls=%async_computation.34 | async-start | bytes 2433024 | tf_op jit(solution)/shard_map/reduce_scatter | solution.py:395
  1298.6 225.2 %reduce-scatter.8.cloned.1.call-start = ((), (), s32[]{:S(2)}) async-start(), calls=%async_computation.35 | async-start | bytes 7299072 | tf_op jit(solution)/shard_map/reduce_scatter | solution.py:395
  1305.4 360.6 %reduce-scatter.12.cloned.1.call-start = ((), (), s32[]{:S(2)}) async-start(), calls=%async_computation.37 | async-start | bytes 9732096 | tf_op jit(solution)/shard_map/reduce_scatter | solution.py:395
  1314.8 492.2 %reduce-scatter.14.cloned.1.call-start = ((), (), s32[]{:S(2)}) async-start(), calls=%async_computation.38 | async-start | bytes 9732096 | tf_op jit(solution)/shard_map/reduce_scatter | solution.py:395
  1324.2 45.8 %copy-start.30 = (f32[64,768]{1,0:T(8,128)S(1)}, f32[64,768]{1,0:T(8,128)}, u32[]{:S(2)}) copy-start(f32[64,768]{1,0:T(8,128)} %copy-done.29) | copy-start | bytes 589828
  1324.2 45.8 %copy-start.41 = (f32[64,768]{1,0:T(8,128)S(1)}, f32[64,768]{1,0:T(8,128)}, u32[]{:S(2)}) copy-start(f32[64,768]{1,0:T(8,128)} %get-tuple-element.201) | copy-start | bytes 589828
  1324.2 45.8 %copy-start.162 = (f32[64]{0:T(128)S(1)}, f32[64]{0:T(128)}, u32[]{:S(2)}) copy-start(f32[64]{0:T(128)} %copy-done.161) | copy-start | bytes 772
  1324.2 45.8 %copy-start.172 = (f32[64]{0:T(128)S(1)}, f32[64]{0:T(128)}, u32[]{:S(2)}) copy-start(f32[64]{0:T(128)} %multiply_multiply_fusion.10) | copy-start | bytes 772
  (172 other events, 1461.2 us)
Sparse Core Ops, SparseCore 0:
  11.0 57.0 all-gather.5
  71.1 58.9 all-gather.7
  133.1 56.6 all-gather.9
  192.7 79.6 all-gather.11
  275.2 63.7 all-gather.13
  969.3 100.3 reduce-scatter.9
  1298.6 100.6 reduce-scatter.5
  1405.6 118.1 reduce-scatter.7
  1531.3 134.7 reduce-scatter.11
  1672.4 134.5 reduce-scatter.13
where the time goes:
time: 1830 us; the launch traced here: 1810 us
  blocking collectives  696 us (38%)
  waiting for transfers between devices  525 us (29%)
  local copies, waits for them, and re-layouts  231 us (13%)
  matrix products  173 us (9%)
  starting transfers between devices  93 us (5%)
  other arithmetic  79.8 us (4%)
    reduce_scatter x5, waiting for transfers between devices, on_device(): lax.psum_scatter(totals, ('ulysses', 'blk'), scatter_dimension=0, tiled=T...  436 us
    all_gather x3, blocking collectives, on_device(): lax.all_gather(query_heads, 'blk', axis=0, tiled=True)  109 us
    all_gather x3, blocking collectives, on_device(): lax.all_gather(key_heads, 'blk', axis=0, tiled=True)  104 us
    all_gather x3, blocking collectives, on_device(): lax.all_gather(grad_heads, 'blk', axis=0, tiled=True)  104 us
    all_gather x3, blocking collectives, on_device(): lax.all_gather(value_heads, 'blk', axis=0, tiled=True)  103 us
    all_gather x3, blocking collectives, on_device(): lax.all_gather(log_total, 'blk', axis=1, tiled=True)  97 us
    all_gather x3, blocking collectives, on_device(): lax.all_gather(delta, 'blk', axis=1, tiled=True)  95.4 us
    unnamed x2, blocking collectives  83.5 us
  transfers between devices with their start and end apart: 34, of which 9 were waited for; matrix products, arithmetic and copies ran while one was open for 21% of the time, Pallas kernels for 0%

commit v1 on v0

v1 whole, which is shorter than its diff:
```python
import functools
import math

import jax
import jax.numpy as jnp
from jax import lax
from jax.experimental import pallas as pl
from jax.experimental.pallas import tpu as pltpu
from jax.sharding import PartitionSpec as P

HEADS = 12
ALL = ("ulysses", "blk")
BF = jnp.bfloat16
F32 = jnp.float32
NEG = -1e30


def exchange(x):
    return lax.all_to_all(x, ALL, split_axis=0, concat_axis=0, tiled=True)


def time_features(time_step, half):
    freqs = jnp.exp(-math.log(10000.0) * jnp.arange(half, dtype=F32) / half)
    angles = time_step.astype(F32)[:, None] * freqs[None, :]
    return jax.nn.silu(jnp.concatenate([jnp.cos(angles), jnp.sin(angles)], 1)).astype(BF)


def doc_layout(index, lengths_row):
    ends = jnp.cumsum(lengths_row)
    over = index[:, None] >= ends[None, :]
    segment = jnp.sum(over.astype(jnp.int32), 1)
    place = index - jnp.sum(jnp.where(over, lengths_row[None, :], 0), 1)
    return segment, place


def key_ranges(first, last, lengths_row, block):
    ends = jnp.cumsum(lengths_row)
    start = jnp.sum(jnp.where(first[:, None] >= ends[None, :], lengths_row[None, :], 0), 1)
    stop = jnp.min(jnp.where(ends[None, :] > last[:, None], ends[None, :], 1 << 30), 1)
    return jnp.stack([start // block, (stop + block - 1) // block], 1).reshape(-1)


def whole_vmem():
    return pl.BlockSpec(memory_space=pltpu.VMEM)


def project_body(slots, pairs, heads, extra, a_ref, w_ref, wz_ref, out_ref):
    groups, micro, rows, width = a_ref.shape
    last = a_ref[:, micro - 1].reshape(groups * rows, width)
    for m in range(micro):
        a = a_ref[:, m].reshape(groups * rows, width)
        for h in range(heads):
            slot = m * heads + h
            if slot >= slots:
                continue
            for c in range(0, out_ref.shape[2], 128):
                x = jnp.dot(a, w_ref[h, :, c : c + 128], preferred_element_type=F32)
                if extra and c > 0:
                    x = x + jnp.dot(last, wz_ref[:, c : c + 128], preferred_element_type=F32)
                out_ref[slot, :, c : c + 128] = x.astype(BF)
    for slot in range(pairs, slots):
        out_ref[slot] = jnp.zeros(out_ref.shape[1:], BF)


def turn_tables(cos_ref, sin_ref, extra):
    cos, sin = cos_ref[...], sin_ref[...]
    lane = lax.broadcasted_iota(jnp.int32, cos.shape, 1)
    low = lane < 64
    cos_r, sin_r = pltpu.roll(cos, 64, 1), pltpu.roll(sin, 64, 1)
    tables = [(jnp.where(low, cos, cos_r), jnp.where(low, sin, sin_r))]
    if extra:
        tables.append((jnp.where(low, 1.0, cos), jnp.where(low, 0.0, sin)))
        tables.append((jnp.where(low, cos_r, 1.0), jnp.where(low, sin_r, 0.0)))
    return tables


def turn(x, table):
    lane = lax.broadcasted_iota(jnp.int32, x.shape, 1)
    swapped = jnp.where(lane % 64 < 32, pltpu.roll(x, 96, 1), pltpu.roll(x, 32, 1))
    return x * table[0] + swapped * table[1]


def rotate_in_body(extra, x_ref, cos_ref, sin_ref, *outs):
    blocks, rows, lanes = x_ref.shape
    tables = turn_tables(cos_ref, sin_ref, extra)
    x = x_ref[...].reshape(blocks * rows, lanes)
    x0 = turn(x[:, :128].astype(F32), tables[0])
    outs[0][...] = (x0[:, :64] * 0.125).astype(BF)
    outs[1][...] = x0[:, 64:].astype(BF)
    x1 = x[:, 128:256].astype(F32)
    outs[2][...] = x1[:, :64].astype(BF)
    if extra:
        x1 = turn(x1, tables[1])
        outs[3][...] = (x1[:, 64:] * 0.125).astype(BF)
        x2 = turn(x[:, 256:].astype(F32), tables[2])
        outs[4][...] = x2[:, :64].astype(BF)
        outs[5][...] = x2[:, 64:].astype(BF)


def rotate_out_body(extra, cos_ref, sin_ref, *refs):
    out_ref = refs[-1]
    parts = [ref[...].astype(F32) for ref in refs[:-1]]
    tables = [(c, -s) for c, s in turn_tables(cos_ref, sin_ref, extra)]
    out_ref[:, :128] = turn(jnp.concatenate(parts[:2], 1), tables[0]).astype(BF)
    if extra:
        out_ref[:, 128:256] = turn(jnp.concatenate(parts[2:4], 1), tables[1]).astype(BF)
        out_ref[:, 256:] = turn(jnp.concatenate(parts[4:], 1), tables[2]).astype(BF)
    else:
        out_ref[:, 128:] = jnp.concatenate([parts[2], jnp.zeros_like(parts[2])], 1).astype(BF)


def attend_body(block, range_ref, q_ref, sq_ref, k_ref, v_ref, sk_ref, o_ref, lse_ref):
    i = pl.program_id(0)
    q, sq = q_ref[...], sq_ref[0]
    count, width = q.shape

    def step(j, carry):
        high, total, acc = carry
        at = pl.ds(pl.multiple_of(j * block, block), block)
        k, v, sk = k_ref[at, :], v_ref[at, :], sk_ref[at, :]
        s = lax.dot_general(k, q, (((1,), (1,)), ((), ())), preferred_element_type=F32)
        s = jnp.where(sk == sq, s, NEG)
        new = jnp.maximum(high, jnp.max(s, 0, keepdims=True))
        p = jnp.exp(s - new)
        fix = jnp.exp(high - new)
        total = total * fix + jnp.sum(p, 0, keepdims=True)
        acc = acc * fix + lax.dot_general(
            v, p.astype(BF), (((0,), (0,)), ((), ())), preferred_element_type=F32
        )
        return new, total, acc

    first = (
        jnp.full((1, count), NEG, F32),
        jnp.zeros((1, count), F32),
        jnp.zeros((width, count), F32),
    )
    high, total, acc = lax.fori_loop(range_ref[2 * i], range_ref[2 * i + 1], step, first)
    o_ref[...] = (acc / total).T.astype(BF)
    lse_ref[0] = high + jnp.log(total)


def attend_back_body(
    block, range_ref, q_ref, sq_ref, lse_ref, o_ref, do_ref, k_ref, v_ref, sk_ref,
    dq_ref, dk_ref, dv_ref, dk_sum, dv_sum,
):
    i = pl.program_id(0)

    @pl.when(i == 0)
    def _():
        dk_sum[...] = jnp.zeros_like(dk_sum)
        dv_sum[...] = jnp.zeros_like(dv_sum)

    q, sq, lse, do = q_ref[...], sq_ref[0], lse_ref[0], do_ref[...]
    count, width = q.shape
    delta = jnp.sum((do.astype(F32) * o_ref[...].astype(F32)).T, 0, keepdims=True)

    def step(j, dq):
        at = pl.ds(pl.multiple_of(j * block, block), block)
        k, v, sk = k_ref[at, :], v_ref[at, :], sk_ref[at, :]
        s = lax.dot_general(k, q, (((1,), (1,)), ((), ())), preferred_element_type=F32)
        p = jnp.where(sk == sq, jnp.exp(s - lse), 0.0)
        dp = lax.dot_general(v, do, (((1,), (1,)), ((), ())), preferred_element_type=F32)
        ds = (p * (dp - delta)).astype(BF)
        dv_sum[at, :] += jnp.dot(p.astype(BF), do, preferred_element_type=F32)
        dk_sum[at, :] += jnp.dot(ds, q, preferred_element_type=F32)
        return dq + lax.dot_general(
            k, ds, (((0,), (0,)), ((), ())), preferred_element_type=F32
        )

    dq = lax.fori_loop(
        range_ref[2 * i], range_ref[2 * i + 1], step, jnp.zeros((width, count), F32)
    )
    dq_ref[...] = (dq * 0.125).T.astype(BF)

    @pl.when(i == pl.num_programs(0) - 1)
    def _():
        dk_ref[...] = dk_sum[...].astype(BF)
        dv_ref[...] = dv_sum[...].astype(BF)


def attend(ranges, q, sq, k, v, sk, rows, block):
    count, width = q.shape
    steps = count // rows
    size = k.shape[0]
    by_row = pl.BlockSpec((rows, width), lambda i, r: (i, 0))
    as_row = pl.BlockSpec((1, 1, rows), lambda i, r: (i, 0, 0))
    return pl.pallas_call(
        functools.partial(attend_body, block),
        grid_spec=pltpu.PrefetchScalarGridSpec(
            num_scalar_prefetch=1,
            grid=(steps,),
            in_specs=[by_row, as_row, whole_vmem(), whole_vmem(), whole_vmem()],
            out_specs=[by_row, as_row],
        ),
        out_shape=[
            jax.ShapeDtypeStruct((count, width), BF),
            jax.ShapeDtypeStruct((steps, 1, rows), F32),
        ],
        cost_estimate=pl.CostEstimate(
            flops=count * size * width, transcendentals=count * size // 4, bytes_accessed=4 * size * width
        ),
        name="attend",
    )(ranges, q, sq.reshape(steps, 1, rows), k, v, sk)


def attend_back(ranges, q, sq, lse, o, do, k, v, sk, rows, block):
    count, width = q.shape
    steps = count // rows
    size = k.shape[0]
    by_row = pl.BlockSpec((rows, width), lambda i, r: (i, 0))
    as_row = pl.BlockSpec((1, 1, rows), lambda i, r: (i, 0, 0))
    return pl.pallas_call(
        functools.partial(attend_back_body, block),
        grid_spec=pltpu.PrefetchScalarGridSpec(
            num_scalar_prefetch=1,
            grid=(steps,),
            in_specs=[by_row, as_row, as_row, by_row, by_row, whole_vmem(), whole_vmem(), whole_vmem()],
            out_specs=[by_row, whole_vmem(), whole_vmem()],
            scratch_shapes=[pltpu.VMEM((size, width), F32)] * 2,
        ),
        out_shape=[
            jax.ShapeDtypeStruct((count, width), BF),
            jax.ShapeDtypeStruct((size, width), BF),
            jax.ShapeDtypeStruct((size, width), BF),
        ],
        cost_estimate=pl.CostEstimate(
            flops=3 * count * size * width, transcendentals=count * size // 4, bytes_accessed=8 * size * width
        ),
        name="attend_back",
    )(ranges, q, sq.reshape(steps, 1, rows), lse, o, do, k, v, sk)


def layer_norm(values):
    centered = values - jnp.mean(values, -1, keepdims=True)
    inverse = lax.rsqrt(jnp.mean(centered * centered, -1, keepdims=True) + 1e-05)
    return centered * inverse, inverse


def layer_norm_back(normed, inverse, grad):
    return inverse * (
        grad
        - jnp.mean(grad, -1, keepdims=True)
        - normed * jnp.mean(grad * normed, -1, keepdims=True)
    )


def gelu_tanh(values):
    return jax.nn.gelu(values, approximate=True)


def on_device(
    tokens,
    cotangent,
    lengths,
    time_step,
    modulate_weight,
    modulate_bias,
    attend_gain,
    input_weight,
    output_weight,
    feed_gain,
    expand_weight,
    expand_bias,
    reduce_weight,
    reduce_bias,
):
    groups, blocks = lax.axis_size("ulysses"), lax.axis_size("blk")
    group_id, block_id = lax.axis_index("ulysses"), lax.axis_index("blk")
    devices = groups * blocks
    me = group_id * blocks + block_id
    micro, rows, width = tokens.shape
    own = micro * rows
    size = devices * rows
    head_width = width // HEADS
    heads = HEADS // groups
    pairs = micro * heads
    extra = pairs > blocks
    assert pairs <= blocks + 1 and head_width == 64
    lanes = 384 if extra else 256
    stripe = rows // blocks if extra else 0
    mod_rows = modulate_weight.shape[0]
    gain_rows = attend_gain.shape[0]
    ff_rows = expand_bias.shape[0]
    ff = ff_rows * devices
    folds = ff // width
    pair_micro = jnp.minimum(block_id // heads, micro - 1)

    values = tokens.astype(F32)
    n1, r1 = layer_norm(values)
    weight_pack = jnp.concatenate(
        [
            output_weight,
            expand_weight.reshape(gain_rows, folds, width).transpose(1, 0, 2).reshape(-1, width),
            reduce_weight,
            n1.astype(BF).reshape(own, width),
            cotangent.reshape(own, width),
        ],
        0,
    )
    gathered = lax.all_gather(weight_pack, ALL, axis=0, tiled=False)
    at_expand = gain_rows
    at_reduce = at_expand + folds * gain_rows
    at_n1 = at_reduce + ff_rows
    at_dy = at_n1 + own
    output_full = gathered[:, :gain_rows].reshape(width, width)
    expand_full = (
        gathered[:, at_expand:at_reduce]
        .reshape(devices, folds, gain_rows, width)
        .transpose(0, 2, 1, 3)
        .reshape(width, ff)
    )
    reduce_full = gathered[:, at_reduce:at_n1].reshape(ff, width)

    condition = time_features(time_step, modulate_weight.shape[1] // 2)
    mod_own = jnp.einsum(
        "mc,fc->mf", condition, modulate_weight, preferred_element_type=F32
    ) + modulate_bias.astype(F32)
    small = jnp.concatenate(
        [
            mod_own.reshape(-1),
            attend_gain.astype(F32),
            feed_gain.astype(F32),
            reduce_bias.astype(F32),
            expand_bias.astype(F32),
        ]
    )
    small_size = -(-small.shape[0] // 1024) * 1024
    small = jnp.pad(small, (0, small_size - small.shape[0])).reshape(1, -1, 128)
    small_all = exchange(jnp.broadcast_to(small, (devices,) + small.shape[1:])).reshape(devices, -1)
    at = micro * mod_rows
    mods = small_all[:, :at].reshape(devices, micro, mod_rows).transpose(1, 0, 2).reshape(micro, -1)
    gain1 = small_all[:, at : at + gain_rows].reshape(-1)
    at += gain_rows
    gain2 = small_all[:, at : at + gain_rows].reshape(-1)
    at += gain_rows
    reduce_bias_f = small_all[:, at : at + gain_rows].reshape(-1)
    at += gain_rows
    expand_bias_f = small_all[:, at : at + ff_rows].reshape(-1)
    shift1, scale1, gate1, shift2, scale2, gate2 = [
        part[:, None, :] for part in jnp.split(mods, 6, 1)
    ]

    index = jnp.arange(size, dtype=jnp.int32)
    pair_lengths = lax.dynamic_index_in_dim(lengths, pair_micro, 0, keepdims=False)
    segment, place = doc_layout(index, pair_lengths)
    last_lengths = lengths[micro - 1]
    last_segment, last_place = doc_layout(index, last_lengths)
    half = head_width // 2
    freqs = jnp.exp(-math.log(10000.0) * jnp.arange(half, dtype=F32) / half)
    lane = jnp.arange(128)
    angles = jnp.where(
        (lane < 64)[None, :], place.astype(F32)[:, None], last_place.astype(F32)[:, None]
    ) * jnp.tile(freqs, 4)[None, :]
    cos_table = jnp.cos(angles)
    sin_table = jnp.where((lane % 64 < 32)[None, :], -1.0, 1.0) * jnp.sin(angles)
    query_rows = math.gcd(size, 256)
    key_block = math.gcd(size, 256)
    first = jnp.arange(size // query_rows, dtype=jnp.int32) * query_rows
    ranges = key_ranges(first, first + query_rows - 1, pair_lengths, key_block)
    segment_column = segment[:, None]

    a = (n1 * (gain1 * (1.0 + scale1)) + shift1).astype(BF)
    a_group = lax.all_to_all(
        jnp.broadcast_to(a[None], (groups,) + a.shape), "ulysses", split_axis=0, concat_axis=0, tiled=True
    )
    in_split = (
        input_weight.reshape(gain_rows, 3, groups, heads, head_width)
        .transpose(2, 0, 3, 1, 4)
        .reshape(groups, 1, gain_rows, heads * 3 * head_width)
    )
    in_own = exchange(
        jnp.broadcast_to(in_split, (groups, blocks) + in_split.shape[2:]).reshape(
            (devices,) + in_split.shape[2:]
        )
    ).reshape(width, heads, 3 * head_width)
    in_heads = jnp.pad(
        in_own.transpose(1, 0, 2), ((0, 0), (0, 0), (0, lanes - 3 * head_width))
    )
    in_last = jnp.pad(in_own[:, heads - 1], ((0, 0), (lanes - 3 * head_width, 0)))
    outgoing = pl.pallas_call(
        functools.partial(project_body, blocks, pairs, heads, extra),
        out_shape=jax.ShapeDtypeStruct((blocks, groups * rows, lanes), BF),
        in_specs=[whole_vmem()] * 3,
        out_specs=whole_vmem(),
        cost_estimate=pl.CostEstimate(
            flops=2 * own * groups * width * lanes * heads, transcendentals=0, bytes_accessed=4 * own * groups * width
        ),
        name="project",
    )(a_group, in_heads, in_last)
    incoming = lax.all_to_all(outgoing, "blk", split_axis=0, concat_axis=0, tiled=True)

    span = blocks * rows
    by_span = pl.BlockSpec((span, 64), lambda i: (i, 0))
    table_spec = pl.BlockSpec((span, 128), lambda i: (i, 0))
    parts = 6 if extra else 3
    turned = pl.pallas_call(
        functools.partial(rotate_in_body, extra),
        grid=(groups,),
        in_specs=[pl.BlockSpec((blocks, rows, lanes), lambda i: (0, i, 0)), table_spec, table_spec],
        out_specs=[by_span] * parts,
        out_shape=[jax.ShapeDtypeStruct((size, 64), BF)] * parts,
        name="rotate_in",
    )(incoming, cos_table, sin_table)
    query, key, value = turned[:3]
    attended, lse = attend(
        ranges, query, segment, key, value, segment_column, query_rows, key_block
    )
    message = attended.reshape(devices, rows, head_width)
    if extra:
        striped = lambda x: lax.dynamic_slice_in_dim(
            x.reshape((devices, rows) + x.shape[1:]), block_id * stripe, stripe, 1
        ).reshape((devices * stripe,) + x.shape[1:])
        last_key, last_value = turned[4:]
        last_query = striped(turned[3])
        last_query_segment = striped(last_segment)
        last_rows = math.gcd(devices * stripe, 128)
        chunk = last_rows // stripe
        last_first = jnp.arange(devices // chunk, dtype=jnp.int32) * (chunk * rows) + block_id * stripe
        last_ranges = key_ranges(
            last_first, last_first + (chunk - 1) * rows + stripe - 1, last_lengths, key_block
        )
        last_column = last_segment[:, None]
        last_attended, last_lse = attend(
            last_ranges, last_query, last_query_segment, last_key, last_value, last_column, last_rows, key_block
        )
        message = jnp.concatenate(
            [message, last_attended.reshape(devices, stripe, head_width)], 1
        )
    came = exchange(message)
    own_pairs = min(pairs, blocks)

    def to_heads(x):
        x = x.reshape((groups, blocks) + x.shape[1:])
        y = x[:, :own_pairs, :rows]
        if extra:
            y = jnp.concatenate([y, x[:, :, rows:].reshape(groups, 1, rows, head_width)], 1)
        return (
            y.reshape(groups, micro, heads, rows, head_width)
            .transpose(1, 3, 0, 2, 4)
            .reshape(own, width)
        )

    def from_heads(x):
        y = (
            x.reshape(micro, rows, groups, heads, head_width)
            .transpose(2, 0, 3, 1, 4)
            .reshape(groups, pairs, rows, head_width)
        )
        z = y[:, :own_pairs]
        if own_pairs < blocks:
            z = jnp.pad(z, ((0, 0), (0, blocks - own_pairs), (0, 0), (0, 0)))
        if extra:
            z = jnp.concatenate([z, y[:, own_pairs].reshape(groups, blocks, stripe, head_width)], 2)
        return z.reshape((devices,) + z.shape[2:])

    merged = to_heads(came)
    attn = jnp.dot(merged, output_full, preferred_element_type=F32).reshape(micro, rows, width)
    middle = values + gate1 * attn
    n2, r2 = layer_norm(middle)
    second = (n2 * (gain2 * (1.0 + scale2)) + shift2).astype(BF).reshape(own, width)
    late_pack = jnp.concatenate(
        [second, input_weight.reshape(gain_rows, 3, width).transpose(1, 0, 2).reshape(-1, width)], 0
    )
    late = lax.all_gather(late_pack, ALL, axis=0, tiled=False)

    hidden = jnp.dot(second, expand_full, preferred_element_type=F32) + expand_bias_f
    active, active_back = jax.vjp(gelu_tanh, hidden)
    branch = jnp.dot(active.astype(BF), reduce_full, preferred_element_type=F32) + reduce_bias_f
    branch = branch.reshape(micro, rows, width)
    layer_output = (middle + gate2 * branch).astype(BF)
    grad_out = cotangent.astype(F32)
    d_gate2 = jnp.sum(grad_out * branch, 1)
    grad_branch = (gate2 * grad_out).astype(BF)
    reduce_bias_part = jnp.sum(grad_branch.astype(F32), (0, 1))
    grad_active = lax.dot_general(
        grad_branch.reshape(own, width), reduce_full, (((1,), (1,)), ((), ())), preferred_element_type=F32
    )
    grad_hidden = active_back(grad_active)[0].astype(BF)
    grad_second = lax.dot_general(
        grad_hidden, expand_full, (((1,), (1,)), ((), ())), preferred_element_type=F32
    ).reshape(micro, rows, width)
    d_shift2 = jnp.sum(grad_second, 1)
    p2 = jnp.sum(grad_second * n2, 1)
    grad_middle = grad_out + layer_norm_back(n2, r2, grad_second * ((1.0 + scale2) * gain2))
    d_gate1 = jnp.sum(grad_middle * attn, 1)
    grad_attn = (gate1 * grad_middle).astype(BF).reshape(own, width)
    grad_merged = lax.dot_general(
        grad_attn, output_full, (((1,), (1,)), ((), ())), preferred_element_type=F32
    ).astype(BF)
    do_came = exchange(from_heads(grad_merged))
    output_part = lax.dot_general(
        merged, grad_attn, (((0,), (0,)), ((), ())), preferred_element_type=F32
    ).astype(BF)
    output_came = exchange(output_part.reshape(devices, gain_rows, width))

    do_pair = do_came[:, :rows].reshape(size, head_width)
    grads = list(
        attend_back(
            ranges, query, segment, lse, attended, do_pair, key, value, segment_column, query_rows, key_block
        )
    )
    if extra:
        dq_last, dk_last, dv_last = attend_back(
            last_ranges, last_query, last_query_segment, last_lse, last_attended,
            do_came[:, rows:].reshape(devices * stripe, head_width),
            last_key, last_value, last_column, last_rows, key_block,
        )
        dq_last = lax.dynamic_update_slice_in_dim(
            jnp.zeros((devices, rows, head_width), BF),
            dq_last.reshape(devices, stripe, head_width),
            block_id * stripe,
            1,
        ).reshape(size, head_width)
        grads += [dq_last, dk_last, dv_last]
    grad_heads = pl.pallas_call(
        functools.partial(rotate_out_body, extra),
        grid=(groups,),
        in_specs=[table_spec, table_spec] + [by_span] * parts,
        out_specs=pl.BlockSpec((span, lanes), lambda i: (i, 0)),
        out_shape=jax.ShapeDtypeStruct((size, lanes), BF),
        name="rotate_out",
    )(cos_table, sin_table, *grads)
    back = exchange(grad_heads.reshape(devices, rows, lanes))

    used = 3 * head_width

    def input_part(which, grad):
        normed = lax.dynamic_slice_in_dim(
            gathered[:, at_n1:at_dy], which * rows, rows, 1
        ).reshape(size, width)
        part = lax.dot_general(normed, grad, (((0,), (0,)), ((), ())), preferred_element_type=F32)
        total = jnp.sum(grad.astype(F32), 0)
        pick = lambda x: lax.dynamic_index_in_dim(x, which, 0, keepdims=False)[0]
        return (
            part * (gain1 * (1.0 + pick(scale1)))[:, None] + pick(shift1)[:, None] * total[None, :]
        )

    input_parts = [input_part(pair_micro, grad_heads[:, :used])]
    if extra:
        input_parts.append(input_part(micro - 1, grad_heads[:, used:]))
    input_came = exchange(
        jnp.concatenate(input_parts, 1).astype(BF).reshape(devices, gain_rows, -1)
    ).astype(F32)
    input_came = input_came.reshape(groups, blocks, gain_rows, -1)
    by_pair = input_came[:, :own_pairs, :, :used]
    if extra:
        by_pair = jnp.concatenate(
            [by_pair, jnp.sum(input_came[..., used:], 1, keepdims=True)], 1
        )
    input_grad = (
        jnp.sum(by_pair.reshape(groups, micro, heads, gain_rows, 3, head_width), 1)
        .transpose(2, 3, 0, 1, 4)
        .reshape(gain_rows, 3 * width)
    )

    second_all = late[:, :own].reshape(devices * own, width)
    dy_all = gathered[:, at_dy:].reshape(devices, micro, rows, width)
    dm_all = (dy_all.astype(F32) * gate2[None]).astype(BF).reshape(devices * own, width)
    expand_own = lax.dynamic_slice_in_dim(expand_full, me * ff_rows, ff_rows, 1)
    hidden_own = jnp.dot(second_all, expand_own, preferred_element_type=F32) + expand_bias.astype(F32)
    active_own, active_own_back = jax.vjp(gelu_tanh, hidden_own)
    reduce_grad = lax.dot_general(
        active_own.astype(BF), dm_all, (((0,), (0,)), ((), ())), preferred_element_type=F32
    )
    grad_active_own = lax.dot_general(
        dm_all, reduce_weight, (((1,), (1,)), ((), ())), preferred_element_type=F32
    )
    grad_hidden_own = active_own_back(grad_active_own)[0].astype(BF)
    expand_bias_grad = jnp.sum(grad_hidden_own.astype(F32), 0)
    expand_part = lax.dot_general(
        second_all, grad_hidden_own, (((0,), (0,)), ((), ())), preferred_element_type=F32
    )
    expand_grad = (
        exchange(expand_part.reshape(devices, gain_rows, ff_rows))
        .transpose(1, 0, 2)
        .reshape(gain_rows, ff)
    )

    back = back.reshape(groups, blocks, rows, lanes)
    grad_pairs = back[:, :own_pairs, :, :used]
    if extra:
        last = jnp.sum(back[..., used:].astype(F32), 1, keepdims=True).astype(BF)
        grad_pairs = jnp.concatenate([grad_pairs, last], 1)
    grad_qkv = (
        grad_pairs.reshape(groups, micro, heads, rows, 3, head_width)
        .transpose(4, 1, 3, 0, 2, 5)
        .reshape(3, own, width)
    )
    grad_first = jnp.zeros((own, width), F32)
    for part in range(3):
        weight = late[:, own + part * gain_rows : own + (part + 1) * gain_rows].reshape(width, width)
        grad_first += lax.dot_general(
            grad_qkv[part], weight, (((1,), (1,)), ((), ())), preferred_element_type=F32
        )
    grad_first = grad_first.reshape(micro, rows, width)
    d_shift1 = jnp.sum(grad_first, 1)
    p1 = jnp.sum(grad_first * n1, 1)
    tokens_grad = (
        grad_middle + layer_norm_back(n1, r1, grad_first * ((1.0 + scale1) * gain1))
    ).astype(BF)

    grad_mods = jnp.concatenate(
        [d_shift1, p1 * gain1, d_gate1, d_shift2, p2 * gain2, d_gate2], 1
    )
    gain1_part = jnp.sum((1.0 + scale1[:, 0]) * p1, 0)
    gain2_part = jnp.sum((1.0 + scale2[:, 0]) * p2, 0)
    small_parts = jnp.concatenate(
        [grad_mods.reshape(micro, devices, mod_rows).transpose(1, 0, 2).reshape(devices, -1)]
        + [x.reshape(devices, gain_rows) for x in (gain1_part, gain2_part, reduce_bias_part)],
        1,
    )
    count = small_parts.shape[1]
    padded = -(-count // 1024) * 1024
    small_sum = jnp.sum(
        exchange(
            jnp.pad(small_parts, ((0, 0), (0, padded - count))).reshape(devices, -1, 128)
        ),
        0,
    ).reshape(-1)
    at = micro * mod_rows
    mod_sum = small_sum[:at].reshape(micro, mod_rows)
    modulate_weight_grad = jnp.sum(
        mod_sum[:, :, None] * condition.astype(F32)[:, None, :], 0
    )
    output_grad = jnp.sum(output_came.astype(F32), 0)
    return (
        layer_output,
        tokens_grad,
        modulate_weight_grad,
        jnp.sum(mod_sum, 0),
        small_sum[at : at + gain_rows],
        input_grad,
        output_grad,
        small_sum[at + gain_rows : at + 2 * gain_rows],
        expand_grad,
        expand_bias_grad,
        reduce_grad,
        small_sum[at + 2 * gain_rows : at + 3 * gain_rows],
    )


def solution(mesh):
    both = P(("ulysses", "blk"))
    tall = P(("ulysses", "blk"), None)
    seq = P(None, ("ulysses", "blk"), None)
    in_specs = (
        seq, seq, P(), P(), tall, both, both, tall, tall, both, tall, both, tall, both,
    )
    out_specs = (seq, seq, tall, both, both, tall, tall, both, tall, both, tall, both)
    return jax.shard_map(
        on_device, mesh=mesh, in_specs=in_specs, out_specs=out_specs, check_vma=False
    )
```

time: 1830 us -> 559 us (0.31)
  blocking collectives: 696 us -> 46.6 us
  waiting for transfers between devices: 525 us -> 155 us
  matrix products: 173 us -> 54.2 us
  local copies, waits for them, and re-layouts: 231 us -> 126 us
  Pallas kernels: 0 us -> 63.9 us
  starting transfers between devices: 93 us -> 49.9 us
  other arithmetic: 79.8 us -> 39.1 us
    all_gather x18 -> x0, blocking collectives: 612 us -> none  [the longest x3 109 us: on_device(): lax.all_gather(query_heads, 'blk', axis=0, tiled=True)]
    reduce_scatter x5 -> x0, waiting for transfers between devices: 436 us -> none  [on_device(): lax.psum_scatter(totals, ('ulysses', 'blk'), scatter_dimension=0, tiled=T...]
    all_to_all x24 -> x10, waiting for transfers between devices: 8.7 us -> 153 us  [the longest x8 75.9 us: exchange(): return lax.all_to_all(x, ALL, split_axis=0, concat_axis=0, tiled=True)]
    dot_general x55 -> x17, matrix products: 173 us -> 54.2 us  [the longest x1 10.7 us: on_device(): jnp.dot(second_all, expand_own, preferred_element_type=F32)]
    unnamed x2 -> x0, blocking collectives: 83.5 us -> none
    all_gather x5 -> x2, waiting for transfers between devices: 76.7 us -> 2.28 us  [the longest x1 2.26 us: on_device(): gathered = lax.all_gather(weight_pack, ALL, axis=0, tiled=False)]
    pallas_call x0 -> x7, Pallas kernels: none -> 63.9 us  [the longest x2 23.2 us: attend_back(): pl.pallas_call(functools.partial(attend_back_body, block), grid_spec=pltp...]
    convert_element_type x42 -> x0, local copies, waits for them, and re-layouts: 60.3 us -> none  [the longest x6 10.1 us: on_device(): value_tok.astype(jnp.float32)]
  transfers between devices with their start and end apart: 34 -> 12, of which waited for: 9 -> 9; matrix products, arithmetic and copies ran while one was open for 21% -> 33% of each run, Pallas kernels for 0% -> 12%
where the time goes in v1:
time: 559 us; the launch traced here: 550 us
  waiting for transfers between devices  155 us (28%)
  local copies, waits for them, and re-layouts  126 us (23%)
  Pallas kernels  63.9 us (11%)
  matrix products  54.2 us (10%)
  starting transfers between devices  49.9 us (9%)
  blocking collectives  46.6 us (8%)
  other arithmetic  39.1 us (7%)
  between operations  15.4 us (3%)
    all_to_all x8, waiting for transfers between devices, exchange(): return lax.all_to_all(x, ALL, split_axis=0, concat_axis=0, tiled=True)  75.9 us
    all_to_all x1, waiting for transfers between devices, on_device(): lax.all_to_all(outgoing, 'blk', split_axis=0, concat_axis=0, tiled=True)  54.5 us
    all_to_all x1, blocking collectives, exchange(): return lax.all_to_all(x, ALL, split_axis=0, concat_axis=0, tiled=True)  46.6 us
    all_to_all x8, starting transfers between devices, exchange(): return lax.all_to_all(x, ALL, split_axis=0, concat_axis=0, tiled=True)  41.2 us
    pallas_call x2, Pallas kernels, attend_back(): pl.pallas_call(functools.partial(attend_back_body, block), grid_spec=pltp...  23.2 us
    all_to_all x1, waiting for transfers between devices, on_device(): lax.all_to_all(jnp.broadcast_to(a[None], (groups,) + a.shape), 'ulysses',...  22.1 us
    pallas_call x2, Pallas kernels, attend(): pl.pallas_call(functools.partial(attend_body, block), grid_spec=pltpu.Pre...  21.9 us
    slice x1, local copies, waits for them, and re-layouts, on_device(): dy_all = gathered[:, at_dy:].reshape(devices, micro, rows, width)  14.5 us
  transfers between devices with their start and end apart: 12, of which 9 were waited for; matrix products, arithmetic and copies ran while one was open for 33% of the time, Pallas kernels for 12%

profile of v1, /device:TPU:0, one launch (start us, length us, event | category | flops | bytes accessed | tf_op | source)
XLA Modules:
  0.0 549.8 jit_solution(8866818022234092199)
XLA Ops:
  9.6 2.8 concatenate.55
  13.0 7.3 %all-to-all-start = ((f32[32,8,128]{2,1,0:T(8,128)}), f32[32,8,128]{2,1,0:T(8,128)S(1)}, u32[]{:S(2)}, u32[]{:S(2)}) async-start(f32[32,8,128]{2,1,0:T(8,128)} %broadcast_in_dim.167), calls=%async_computation | async-start | bytes 262144 | tf_op jit(solution)/shard_map/all_to_all | solution.py:19
  25.5 2.5 all-to-all-done
  32.0 46.6 %all_to_all.55 = bf16[32,24,576]{2,1,0:T(8,128)(2,1)} all-to-all(bf16[32,24,576]{2,1,0:T(8,128)(2,1)S(1)} %bitcast.205), channel_id=1, replica_groups=mesh['ulysses'=4,'blk'=8] {'ulysses','blk'}, dimensions={0} | all-to-all | bytes 1769472 | tf_op jit(solution)/shard_map/all_to_all | solution.py:19
  79.7 3.5 all-to-all-start.1
  83.5 3.2 reshape.744
  89.6 22.1 %all-to-all-done.1.a_ref = bf16[4,3,64,768]{3,2,1,0:T(8,128)(2,1)S(1)} async-done(((bf16[4,3,64,768]{3,2,1,0:T(8,128)(2,1)}), bf16[4,3,64,768]{3,2,1,0:T(8,128)(2,1)S(1)}, u32[]{:S(2)}, u32[]{:S(2)}) %all-to-all-start.1) | async-done | bytes 1179680 | tf_op jit(solution)/shard_map/all_to_all | solution.py:363
  112.7 7.5 %project.1 = bf16[8,256,384]{2,1,0:T(8,128)(2,1)} custom-call(bf16[4,3,64,768]{3,2,1,0:T(8,128)(2,1)} %copy-done.9, bf16[3,768,384]{2,1,0:T(8,128)(2,1)} %pad.17.w_ref, bf16[768,384]{1,0:T(8,128)(2,1)} %pad.18.wz_ref), custom_call_target="tpu_custom_call" | custom-call | flops 1358954496 | bytes 2359296 | tf_op jit(solution)/shard_map/project/pallas_call | solution.py:380
  120.2 5.1 all-to-all-start.3
  131.4 5.7 %sine_multiply_fusion = (f32[2048,128]{1,0:T(8,128)}, f32[2048,128]{1,0:T(8,128)}) fusion(f32[128]{0:T(128)S(1)} %compare_select_fusion.2, f32[128]{0:T(128)S(1)} %mul.453, f32[2048]{0:T(1024)S(1)} %subtract_convert_fusion, f32[2048]{0:T(1024)S(1)} %subtract_convert_fusion.1, pred[128]{0:T(512)(128)(4,1)S(1)} %iota_compare_fusion.3), kind=kLoop, calls=%fused_computation.53 | loop fusion | flops 786432 | bytes 2114688 | tf_op jit(solution)/shard_map/mul | solution.py:355
  137.1 54.5 %all-to-all-done.3.x_ref = bf16[8,256,384]{2,1,0:T(8,128)(2,1)S(1)} async-done(((bf16[8,256,384]{2,1,0:T(8,128)(2,1)}), bf16[8,256,384]{2,1,0:T(8,128)(2,1)S(1)}, u32[]{:S(2)}, u32[]{:S(2)}) %all-to-all-start.3) | async-done | bytes 1572896 | tf_op jit(solution)/shard_map/all_to_all | solution.py:390
  192.8 5.6 %rotate_in.1 = (bf16[2048,64]{1,0:T(8,128)(2,1)}, bf16[2048,64]{1,0:T(8,128)(2,1)}, bf16[2048,64]{1,0:T(8,128)(2,1)}, bf16[2048,64]{1,0:T(8,128)(2,1)}, bf16[204...) custom-call(bf16[8,256,384]{2,1,0:T(8,128)(2,1)} %copy-done.6, f32[2048,128]{1,0:T(8,128)} %get-tuple-element.108.cos_ref, ...), custom_call_target="tpu_custom_call" | custom-call | tf_op jit(solution)/shard_map/rotate_in/pallas_call | solution.py:396
  199.8 6.8 %attend.3 = (bf16[256,64]{1,0:T(8,128)(2,1)}, f32[2,1,128]{2,1,0:T(1,128)}) custom-call(s32[4]{0:T(128)} %reshape.749.range_ref, bf16[256,64]{1,0:T(8,128)(2,1)} %dynamic-slice_bitcast_fusion.q_ref, s32[2,1,128]{2,1,0:T(1,128)} %bitcast.253, bf16[2048,64]{1,0:T(8,128)(2,1)} %get-tuple-element.33.k_ref, bf16[2048,64]{1,0:T(8,128)(2,1)} %get-tuple-element.34.v_ref, ...), custom_call_target="tpu_custom_call" | custom-call | flops 33554432 | bytes 524288 | tf_op jit(solution)/shard_map/attend/pallas_call | solution.py:187
  207.7 15.1 %attend.2 = (bf16[2048,64]{1,0:T(8,128)(2,1)}, f32[8,1,256]{2,1,0:T(1,128)}) custom-call(s32[16]{0:T(128)} %reshape.741.range_ref, bf16[2048,64]{1,0:T(8,128)(2,1)} %get-tuple-element.28.q_ref, s32[8,1,256]{2,1,0:T(1,128)} %bitcast.248, bf16[2048,64]{1,0:T(8,128)(2,1)} %get-tuple-element.29.k_ref, bf16[2048,64]{1,0:T(8,128)(2,1)} %get-tuple-element.30.v_ref, ...), custom_call_target="tpu_custom_call" | custom-call | flops 268435456 | bytes 524288 | tf_op jit(solution)/shard_map/attend/pallas_call | solution.py:187
  225.2 7.1 %all-to-all-start.4 = ((bf16[32,72,64]{1,2,0:T(8,128)(2,1)}), bf16[32,72,64]{1,2,0:T(8,128)(2,1)S(1)}, u32[]{:S(2)}, u32[]{:S(2)}) async-start(bf16[32,72,64]{1,2,0:T(8,128)(2,1)} %pad_maximum_fusion.4), calls=%async_computation.4 | async-start | bytes 1048576 | tf_op jit(solution)/shard_map/all_to_all | solution.py:19
  232.4 22.1 %all-to-all-done.4 = bf16[32,72,64]{1,2,0:T(8,128)(2,1)S(1)} async-done(((bf16[32,72,64]{1,2,0:T(8,128)(2,1)}), bf16[32,72,64]{1,2,0:T(8,128)(2,1)S(1)}, u32[]{:S(2)}, u32[]{:S(2)}) %all-to-all-start.4) | async-done | bytes 294944 | tf_op jit(solution)/shard_map/all_to_all | solution.py:19
  264.8 6.5 %fusion.75 = (bf16[32,96,768]{2,1,0:T(8,128)(2,1)S(1)}, bf16[32,96,768]{2,1,0:T(8,128)(2,1)}) fusion(bf16[32,600,768]{2,1,0:T(8,128)(2,1)} %bitcast.178), kind=kLoop, calls=%fused_computation.213 | loop fusion | bytes 18874368 | tf_op jit(solution)/shard_map/slice | solution.py:307
  273.7 3.8 copy.166
  277.4 9.5 %reshape.807 = bf16[768,3072,1]{1,0,2:T(8,128)(2,1)} reshape(bf16[32,24,4,768]{3,2,1,0:T(4,128)(2,1)} %bitcast.174) | data formatting | bytes 9437184 | tf_op jit(solution)/shard_map/reshape | solution.py:310
  286.9 4.5 fusion.84
  291.5 4.2 fusion.7
  295.7 2.4 multiply_reduce_fusion
  304.8 2.6 all-to-all-start.5
  309.4 19.2 %all-to-all-done.5 = bf16[32,72,64]{1,2,0:T(8,128)(2,1)S(1)} async-done(((bf16[32,72,64]{1,2,0:T(8,128)(2,1)}), bf16[32,72,64]{1,2,0:T(8,128)(2,1)S(1)}, u32[]{:S(2)}, u32[]{:S(2)}) %all-to-all-start.5) | async-done | bytes 294944 | tf_op jit(solution)/shard_map/all_to_all | solution.py:19
  328.6 6.3 %all-to-all-start.9 = ((bf16[32,24,768]{2,1,0:T(8,128)(2,1)}), bf16[32,24,768]{2,1,0:T(8,128)(2,1)S(1)}, u32[]{:S(2)}, u32[]{:S(2)}) async-start(bf16[32,24,768]{2,1,0:T(8,128)(2,1)} %bitcast.75), calls=%async_computation.9 | async-start | bytes 2359296 | tf_op jit(solution)/shard_map/all_to_all | solution.py:19
  336.9 7.4 %attend_back.3 = (bf16[256,64]{1,0:T(8,128)(2,1)}, bf16[2048,64]{1,0:T(8,128)(2,1)}, bf16[2048,64]{1,0:T(8,128)(2,1)}) custom-call(s32[4]{0:T(128)} %reshape.749.range_ref, bf16[256,64]{1,0:T(8,128)(2,1)} %dynamic-slice_bitcast_fusion.q_ref, s32[2,1,128]{2,1,0:T(1,128)} %bitcast.254, f32[2,1,128]{2,1,0:T(1,128)} %get-tuple-element.40.lse_ref, ...), custom_call_target="tpu_custom_call" | custom-call | flops 100663296 | bytes 1048576 | tf_op jit(solution)/shard_map/attend_back/pallas_call | solution.py:212
  344.4 15.8 %attend_back.2 = (bf16[2048,64]{1,0:T(8,128)(2,1)}, bf16[2048,64]{1,0:T(8,128)(2,1)}, bf16[2048,64]{1,0:T(8,128)(2,1)}) custom-call(s32[16]{0:T(128)} %reshape.741.range_ref, bf16[2048,64]{1,0:T(8,128)(2,1)} %get-tuple-element.28.q_ref, s32[8,1,256]{2,1,0:T(1,128)} %bitcast.249, f32[8,1,256]{2,1,0:T(1,128)} %get-tuple-element.36.lse_ref, ...), custom_call_target="tpu_custom_call" | custom-call | flops 805306368 | bytes 1048576 | tf_op jit(solution)/shard_map/attend_back/pallas_call | solution.py:212
  361.1 5.9 %rotate_out.1 = bf16[2048,384]{1,0:T(8,128)(2,1)} custom-call(f32[2048,128]{1,0:T(8,128)} %get-tuple-element.108.cos_ref, f32[2048,128]{1,0:T(8,128)} %get-tuple-element.107.sin_ref, bf16[2048,64]{1,0:T(8,128)(2,1)} %get-tuple-element.37.refs_0_, bf16[2048,64]{1,0:T(8,128)(2,1)} %get-tuple-element.38.refs_1_, bf16[2048,64]{1,0:T(8,128)(2,1)} %get-tuple-element.39.refs_2_, ...), custom_call_target="tpu_custom_call" | custom-call | tf_op jit(solution)/shard_map/rotate_out/pallas_call | solution.py:515
  367.0 17.6 %all-to-all-done.9 = bf16[32,24,768]{2,1,0:T(8,128)(2,1)S(1)} async-done(((bf16[32,24,768]{2,1,0:T(8,128)(2,1)}), bf16[32,24,768]{2,1,0:T(8,128)(2,1)S(1)}, u32[]{:S(2)}, u32[]{:S(2)}) %all-to-all-start.9) | async-done | bytes 1179680 | tf_op jit(solution)/shard_map/all_to_all | solution.py:19
  384.6 2.9 all-to-all-start.6
  390.7 3.9 dynamic_slice.31
  394.6 14.5 %fusion.74 = (bf16[32,192,768]{2,1,0:T(8,128)(2,1)}, bf16[32,192,768]{2,1,0:T(8,128)(2,1)}) fusion(bf16[32,600,768]{2,1,0:T(8,128)(2,1)} %bitcast.180), kind=kLoop, calls=%fused_computation.212 | loop fusion | bytes 37748736 | tf_op jit(solution)/shard_map/slice | solution.py:557
  409.1 9.2 %fusion = bf16[6144,768]{1,0:T(8,128)(2,1)} fusion(bf16[32,192,768]{2,1,0:T(8,128)(2,1)} %get-tuple-element.75, f32[3,768]{1,0:T(4,128)S(1)} %get-tuple-element.101), kind=kLoop, calls=%fused_computation.1 | loop fusion | flops 14155776 | bytes 18883584 | tf_op jit(solution)/shard_map/convert_element_type | solution.py:558
  418.3 4.0 constant_dynamic-slice_fusion
  422.3 8.2 %fusion.86 = f32[6144,96]{0,1:T(8,128)} fusion(bf16[6144,768]{1,0:T(8,128)(2,1)} %fusion, bf16[96,768]{1,0:T(8,128)(2,1)S(1)} %copy-done.22), kind=kOutput, calls=%fused_computation.224 | convolution fusion | flops 905969664 | bytes 11943936 | tf_op jit(solution)/shard_map/dot_general | solution.py:565
  432.6 2.9 copy.153
  446.2 3.7 fusion.76
  449.9 8.2 %slice.185 = bf16[32,192,768]{2,1,0:T(8,128)(2,1)} slice(bf16[32,264,768]{2,1,0:T(8,128)(2,1)} %bitcast.188), slice={[0:32], [0:192], [0:768]} | slice | bytes 18874368 | tf_op jit(solution)/shard_map/slice | solution.py:556
  464.7 6.3 %all-to-all-start.7 = ((f32[32,8,128]{2,1,0:T(8,128)}), f32[32,8,128]{2,1,0:T(8,128)S(1)}, u32[]{:S(2)}, u32[]{:S(2)}) async-start(f32[32,8,128]{2,1,0:T(8,128)} %bitcast.92), calls=%async_computation.7 | async-start | bytes 262144 | tf_op jit(solution)/shard_map/all_to_all | solution.py:19
  471.1 12.7 %copy.163 = bf16[768,6144]{1,0:T(8,128)(2,1)} copy(bf16[768,6144]{0,1:T(8,128)(2,1)} %bitcast.175) | data formatting | bytes 18874368 | tf_op jit(solution)/shard_map/dot_general | solution.py:570
  483.7 10.7 %convert_reduce_fusion = (f32[96]{0:T(128)}, bf16[6144,96]{0,1:T(8,128)(2,1)S(1)}, f32[6144,96]{0,1:T(8,128)}) fusion(f32[6144,96]{0,1:T(8,128)} %fusion.86, f32[96]{0:T(128)S(1)} %copy-done.41, bf16[6144,768]{1,0:T(8,128)(2,1)} %bitcast.176, bf16[768,3072]{1,0:T(8,128)(2,1)} %bitcast.199, s32[]{:T(128)S(6)} %select_n.131), kind=kOutput, calls=%fused_computation.23 | convolution fusion | flops 919535488 | bytes 15532804 | tf_op jit(solution)/shard_map/dot_general | solution.py:560
  494.5 3.5 fusion.20
  499.6 5.9 %all-to-all-start.10 = ((f32[32,24,96]{2,1,0:T(8,128)}), f32[32,24,96]{2,1,0:T(8,128)S(1)}, u32[]{:S(2)}, u32[]{:S(2)}) async-start(f32[32,24,96]{2,1,0:T(8,128)} %fusion.20), calls=%async_computation.10 | async-start | bytes 786432 | tf_op jit(solution)/shard_map/all_to_all | solution.py:19
  505.6 3.4 fusion.17
  511.2 7.8 %all-to-all-done.10 = f32[32,24,96]{2,1,0:T(8,128)S(1)} async-done(((f32[32,24,96]{2,1,0:T(8,128)}), f32[32,24,96]{2,1,0:T(8,128)S(1)}, u32[]{:S(2)}, u32[]{:S(2)}) %all-to-all-start.10) | async-done | bytes 294944 | tf_op jit(solution)/shard_map/all_to_all | solution.py:19
  519.1 2.8 all-to-all-start.8
  522.9 7.0 %fusion.19 = f32[96,768]{1,0:T(8,128)} fusion(bf16[6144,768]{1,0:T(8,128)(2,1)} %fusion, f32[6144,96]{0,1:T(8,128)} %get-tuple-element.127), kind=kOutput, calls=%fused_computation.41 | convolution fusion | flops 911278080 | bytes 12091392 | tf_op jit(solution)/shard_map/dot_general | solution.py:562
  532.9 6.7 %all-to-all-done.8 = bf16[32,24,384]{2,1,0:T(8,128)(2,1)S(1)} async-done(((bf16[32,24,384]{2,1,0:T(8,128)(2,1)}), bf16[32,24,384]{2,1,0:T(8,128)(2,1)S(1)}, u32[]{:S(2)}, u32[]{:S(2)}) %all-to-all-start.8) | async-done | bytes 589856 | tf_op jit(solution)/shard_map/all_to_all | solution.py:19
  (278 shorter events, 86.8 us)
Async XLA Ops:
  7.2 2.2 copy-start
  7.2 22.7 %copy-start.4 = (bf16[3,64,768]{2,1,0:T(8,128)(2,1)S(1)}, bf16[3,64,768]{2,1,0:T(8,128)(2,1)}, u32[]{:S(2)}) copy-start(bf16[3,64,768]{2,1,0:T(8,128)(2,1)} %param.14) | copy-start | bytes 884740
  13.0 15.0 %all-to-all-start = ((f32[32,8,128]{2,1,0:T(8,128)}), f32[32,8,128]{2,1,0:T(8,128)S(1)}, u32[]{:S(2)}, u32[]{:S(2)}) async-start(f32[32,8,128]{2,1,0:T(8,128)} %broadcast_in_dim.167), calls=%async_computation | async-start | bytes 262144 | tf_op jit(solution)/shard_map/all_to_all | solution.py:19
  20.4 9.8 %copy-start.15 = (bf16[3,64,768]{2,1,0:T(8,128)(2,1)S(1)}, bf16[3,64,768]{2,1,0:T(8,128)(2,1)}, u32[]{:S(2)}) copy-start(bf16[3,64,768]{2,1,0:T(8,128)(2,1)} %param.15) | copy-start | bytes 884740
  20.4 238.7 %all-gather.5.cloned.1.call-start = ((), (), s32[]{:S(2)}) async-start(), calls=%async_computation.11 | async-start | bytes 30412800 | tf_op jit(solution)/shard_map/all_gather | solution.py:300
  24.5 6.7 %copy-start.23 = (bf16[24,2304]{1,0:T(8,128)(2,1)S(1)}, bf16[24,2304]{1,0:T(8,128)(2,1)}, u32[]{:S(2)}) copy-start(bf16[24,2304]{1,0:T(8,128)(2,1)} %param.21) | copy-start | bytes 331780
  25.5 6.0 %copy-start.30 = (f32[3,64]{1,0:T(4,128)}, f32[3,64]{1,0:T(4,128)S(1)}, u32[]{:S(2)}) copy-start(f32[3,64]{1,0:T(4,128)S(1)} %add_rsqrt_fusion.1) | copy-start | bytes 2308
  29.1 2.8 copy-start.24
  29.9 2.0 copy-start.28
  78.5 4.7 copy-start.39
  79.7 32.0 %all-to-all-start.1 = ((bf16[4,3,64,768]{3,2,1,0:T(8,128)(2,1)}), bf16[4,3,64,768]{3,2,1,0:T(8,128)(2,1)S(1)}, u32[]{:S(2)}, u32[]{:S(2)}) async-start(bf16[4,3,64,768]{3,2,1,0:T(8,128)(2,1)} %broadcast_in_dim.172), calls=%async_computation.1 | async-start | bytes 2359296 | tf_op jit(solution)/shard_map/all_to_all | solution.py:363
  120.2 71.4 %all-to-all-start.3 = ((bf16[8,256,384]{2,1,0:T(8,128)(2,1)}), bf16[8,256,384]{2,1,0:T(8,128)(2,1)S(1)}, u32[]{:S(2)}, u32[]{:S(2)}) async-start(bf16[8,256,384]{2,1,0:T(8,128)(2,1)} %project.1), calls=%async_computation.3 | async-start | bytes 3145728 | tf_op jit(solution)/shard_map/all_to_all | solution.py:390
  126.9 71.4 %copy-start.25 = (s32[2048]{0:T(1024)}, s32[2048]{0:T(1024)S(1)}, u32[]{:S(2)}) copy-start(s32[2048]{0:T(1024)S(1)} %get-tuple-element.133) | copy-start | bytes 24580
  225.2 29.3 %all-to-all-start.4 = ((bf16[32,72,64]{1,2,0:T(8,128)(2,1)}), bf16[32,72,64]{1,2,0:T(8,128)(2,1)S(1)}, u32[]{:S(2)}, u32[]{:S(2)}) async-start(bf16[32,72,64]{1,2,0:T(8,128)(2,1)} %pad_maximum_fusion.4), calls=%async_computation.4 | async-start | bytes 1048576 | tf_op jit(solution)/shard_map/all_to_all | solution.py:19
  232.3 213.9 %all-gather.7.cloned.1.call-start = ((), (), s32[]{:S(2)}) async-start(), calls=%async_computation.12 | async-start | bytes 13381632 | tf_op jit(solution)/shard_map/all_gather | solution.py:464
  259.1 1.4 copy-start.20
  260.5 1.5 copy-start.29
  260.5 3.4 copy-start.27
  260.5 3.5 copy-start.16
  273.7 3.8 copy-start.2
  286.9 8.8 %slice-start.2 = ((s8[4718592]{0:T(1024)(128)(4,1)}), s8[4194304]{0:T(1024)(128)(4,1)S(1)}, s32[]{:S(2)}) async-start(s8[4718592]{0:T(1024)(128)(4,1)} %bitcast.200), calls=%async_computation.15 | async-start | bytes 8388608
  286.9 11.2 %slice-start = ((s8[4718592]{0:T(1024)(128)(4,1)}), s8[4194304]{0:T(1024)(128)(4,1)S(1)}, s32[]{:S(2)}) async-start(s8[4718592]{0:T(1024)(128)(4,1)} %bitcast.183), calls=%async_computation.13 | async-start | bytes 8388608
  291.5 4.3 slice-start.3
  291.5 6.7 %slice-start.1 = ((s8[4718592]{0:T(1024)(128)(4,1)}), s8[524288]{0:T(1024)(128)(4,1)S(1)}, s32[]{:S(2)}) async-start(s8[4718592]{0:T(1024)(128)(4,1)} %bitcast.183), calls=%async_computation.14 | async-start | bytes 1048576
  298.2 1.5 copy-start.17
  304.8 23.8 %all-to-all-start.5 = ((bf16[32,72,64]{1,2,0:T(8,128)(2,1)}), bf16[32,72,64]{1,2,0:T(8,128)(2,1)S(1)}, u32[]{:S(2)}, u32[]{:S(2)}) async-start(bf16[32,72,64]{1,2,0:T(8,128)(2,1)} %pad_maximum_fusion.5), calls=%async_computation.5 | async-start | bytes 1048576 | tf_op jit(solution)/shard_map/all_to_all | solution.py:19
  328.6 56.0 %all-to-all-start.9 = ((bf16[32,24,768]{2,1,0:T(8,128)(2,1)}), bf16[32,24,768]{2,1,0:T(8,128)(2,1)S(1)}, u32[]{:S(2)}, u32[]{:S(2)}) async-start(bf16[32,24,768]{2,1,0:T(8,128)(2,1)} %bitcast.75), calls=%async_computation.9 | async-start | bytes 2359296 | tf_op jit(solution)/shard_map/all_to_all | solution.py:19
  344.4 15.9 %copy-start.26 = (bf16[256,64]{1,0:T(8,128)(2,1)S(1)}, bf16[256,64]{1,0:T(8,128)(2,1)}, u32[]{:S(2)}) copy-start(bf16[256,64]{1,0:T(8,128)(2,1)} %get-tuple-element.41) | copy-start | bytes 98308
  367.0 20.5 %copy-start.40 = (bf16[96]{0:T(256)(128)(2,1)S(1)}, bf16[96]{0:T(256)(128)(2,1)}, u32[]{:S(2)}) copy-start(bf16[96]{0:T(256)(128)(2,1)} %param.25) | copy-start | bytes 580
  384.5 10.0 %copy-start.11 = (bf16[32,24,768]{2,1,0:T(8,128)(2,1)}, bf16[32,24,768]{2,1,0:T(8,128)(2,1)S(1)}, u32[]{:S(2)}) copy-start(bf16[32,24,768]{2,1,0:T(8,128)(2,1)S(1)} %all-to-all-done.9) | copy-start | bytes 3538948
  384.6 48.0 %all-to-all-start.6 = ((bf16[32,64,384]{2,1,0:T(8,128)(2,1)}), bf16[32,64,384]{2,1,0:T(8,128)(2,1)S(1)}, u32[]{:S(2)}, u32[]{:S(2)}) async-start(bf16[32,64,384]{2,1,0:T(8,128)(2,1)} %bitcast.186), calls=%async_computation.6 | async-start | bytes 3145728 | tf_op jit(solution)/shard_map/all_to_all | solution.py:19
  418.3 4.0 copy-start.22
  422.3 8.2 %copy-start.3 = (bf16[2048,384]{1,0:T(8,128)(2,1)S(1)}, bf16[2048,384]{1,0:T(8,128)(2,1)}, u32[]{:S(2)}) copy-start(bf16[2048,384]{1,0:T(8,128)(2,1)} %rotate_out.1) | copy-start | bytes 4718596
  458.1 1.7 copy-start.13
  458.1 3.3 copy-start.10
  464.7 34.9 %all-to-all-start.7 = ((f32[32,8,128]{2,1,0:T(8,128)}), f32[32,8,128]{2,1,0:T(8,128)S(1)}, u32[]{:S(2)}, u32[]{:S(2)}) async-start(f32[32,8,128]{2,1,0:T(8,128)} %bitcast.92), calls=%async_computation.7 | async-start | bytes 262144 | tf_op jit(solution)/shard_map/all_to_all | solution.py:19
  471.0 12.7 %copy-start.41 = (f32[96]{0:T(128)S(1)}, f32[96]{0:T(128)}, u32[]{:S(2)}) copy-start(f32[96]{0:T(128)} %convert_element_type.155) | copy-start | bytes 1156
  483.7 10.7 %copy-start.5 = (bf16[768,6144]{1,0:T(8,128)(2,1)S(1)}, bf16[768,6144]{1,0:T(8,128)(2,1)}, u32[]{:S(2)}) copy-start(bf16[768,6144]{1,0:T(8,128)(2,1)} %copy.163) | copy-start | bytes 28311556
  494.5 3.5 copy-start.14
  494.5 3.5 copy-start.35
  494.5 3.5 copy-start.38
  498.0 7.5 %copy-start.36 = (f32[768]{0:T(1024)S(1)}, f32[768]{0:T(1024)}, u32[]{:S(2)}) copy-start(f32[768]{0:T(1024)} %dynamic-slice_reduce_fusion) | copy-start | bytes 9220
  498.0 7.5 %copy-start.37 = (f32[192]{0:T(256)S(1)}, f32[192]{0:T(256)}, u32[]{:S(2)}) copy-start(f32[192]{0:T(256)} %get-tuple-element.44) | copy-start | bytes 2308
  499.6 19.5 %all-to-all-start.10 = ((f32[32,24,96]{2,1,0:T(8,128)}), f32[32,24,96]{2,1,0:T(8,128)S(1)}, u32[]{:S(2)}, u32[]{:S(2)}) async-start(f32[32,24,96]{2,1,0:T(8,128)} %fusion.20), calls=%async_computation.10 | async-start | bytes 786432 | tf_op jit(solution)/shard_map/all_to_all | solution.py:19
  509.0 12.9 %copy-start.8 = (f32[3,64,768]{2,1,0:T(8,128)S(1)}, f32[3,64,768]{2,1,0:T(8,128)}, u32[]{:S(2)}) copy-start(f32[3,64,768]{2,1,0:T(8,128)} %copy-done.7) | copy-start | bytes 1769476
  519.1 20.5 %all-to-all-start.8 = ((bf16[32,24,384]{2,1,0:T(8,128)(2,1)}), bf16[32,24,384]{2,1,0:T(8,128)(2,1)S(1)}, u32[]{:S(2)}, u32[]{:S(2)}) async-start(bf16[32,24,384]{2,1,0:T(8,128)(2,1)} %pad_maximum_fusion.3), calls=%async_computation.8 | async-start | bytes 1179648 | tf_op jit(solution)/shard_map/all_to_all | solution.py:19
  522.9 7.7 %copy-start.34 = (f32[3,128]{1,0:T(4,128)S(1)}, f32[3,128]{1,0:T(4,128)}, u32[]{:S(2)}) copy-start(f32[3,128]{1,0:T(4,128)} %get-tuple-element.71) | copy-start | bytes 4612
  540.1 2.7 copy-start.1
  (10 other events, 10.1 us)
Sparse Core Ops, SparseCore 0:
  31.4 227.6 all-gather.4
  263.9 120.1 all-gather.6

commit v2 on v1

v2 whole, which is shorter than its diff:
```python
import functools
import math

import jax
import jax.numpy as jnp
from jax import lax
from jax.experimental import pallas as pl
from jax.experimental.pallas import tpu as pltpu
from jax.sharding import PartitionSpec as P

HEADS = 12
ALL = ("ulysses", "blk")
BF = jnp.bfloat16
F32 = jnp.float32
NEG = -1e30


def exchange(x):
    return lax.all_to_all(x, ALL, split_axis=0, concat_axis=0, tiled=True)


def time_features(time_step, half):
    freqs = jnp.exp(-math.log(10000.0) * jnp.arange(half, dtype=F32) / half)
    angles = time_step.astype(F32)[:, None] * freqs[None, :]
    return jax.nn.silu(jnp.concatenate([jnp.cos(angles), jnp.sin(angles)], 1)).astype(BF)


def doc_layout(index, lengths_row):
    ends = jnp.cumsum(lengths_row)
    over = index[:, None] >= ends[None, :]
    segment = jnp.sum(over.astype(jnp.int32), 1)
    place = index - jnp.sum(jnp.where(over, lengths_row[None, :], 0), 1)
    return segment, place


def key_ranges(first, last, lengths_row, block):
    ends = jnp.cumsum(lengths_row)
    start = jnp.sum(jnp.where(first[:, None] >= ends[None, :], lengths_row[None, :], 0), 1)
    stop = jnp.min(jnp.where(ends[None, :] > last[:, None], ends[None, :], 1 << 30), 1)
    return jnp.stack([start // block, (stop + block - 1) // block], 1).reshape(-1)


def whole_vmem():
    return pl.BlockSpec(memory_space=pltpu.VMEM)


def swap(blocks, axis):
    size = lax.axis_size(axis)
    return [
        x if k == 0 else lax.ppermute(x, axis, [(i, i ^ k) for i in range(size)])
        for k, x in enumerate(blocks)
    ]


def project_body(blocks, pairs, heads, extra, place_ref, c_ref, shift_ref, w_ref, *refs):
    groups = len(refs) - blocks - 1
    tokens, outs, kept = refs[:groups], refs[groups:-1], refs[-1]
    micro, rows, width = tokens[0].shape
    two = 128 * heads
    weights = [w_ref[:, c : min(c + 128, w_ref.shape[1])] for c in range(0, w_ref.shape[1], 128)]
    order = list(range(micro))[::-1]
    z_qk = z_v = None
    for m in order:
        a = jnp.concatenate(
            [(x[m].astype(F32) * c_ref[m][None] + shift_ref[m][None]).astype(BF) for x in tokens], 0
        )
        parts = [jnp.dot(a, w, preferred_element_type=F32).astype(BF) for w in weights]
        v = jnp.concatenate(parts[heads:], 1)
        if extra and m == micro - 1:
            z_qk = parts[heads - 1]
            z_v = v[:, (heads - 1) * 64 : heads * 64]
        for h in range(heads):
            pair = m * heads + h
            if pair >= blocks:
                continue
            kept[pair, :, :128] = parts[h]
            own_v = v[:, h * 64 : (h + 1) * 64]
            if extra:
                kept[pair, :, 128:256] = z_qk
                kept[pair, :, 256:] = jnp.concatenate([own_v, z_v], 1)
            else:
                kept[pair, :, 128:] = jnp.concatenate([own_v, jnp.zeros_like(own_v)], 1)
    for pair in range(pairs, blocks):
        kept[pair] = jnp.zeros(kept.shape[1:], BF)
    for j in range(blocks):
        outs[j][...] = kept[place_ref[1] ^ j]


def turn_tables(cos_ref, sin_ref, extra):
    cos, sin = cos_ref[...], sin_ref[...]
    lane = lax.broadcasted_iota(jnp.int32, cos.shape, 1)
    low = lane < 64
    cos_r, sin_r = pltpu.roll(cos, 64, 1), pltpu.roll(sin, 64, 1)
    tables = [(jnp.where(low, cos, cos_r), jnp.where(low, sin, sin_r))]
    if extra:
        tables.append((jnp.where(low, cos_r, cos), jnp.where(low, sin_r, sin)))
    return tables


def turn(x, table):
    lane = lax.broadcasted_iota(jnp.int32, x.shape, 1)
    swapped = jnp.where(lane % 64 < 32, pltpu.roll(x, 96, 1), pltpu.roll(x, 32, 1))
    return x * table[0] + swapped * table[1]


def rotate_in_body(blocks, extra, place_ref, cos_ref, sin_ref, *refs):
    ins, outs = refs[:blocks], refs[blocks : 2 * blocks - blocks + (6 if extra else 3)]
    kept = refs[-1]
    rows = ins[0].shape[0]
    for j in range(blocks):
        at = pl.multiple_of((place_ref[1] ^ j) * rows, rows)
        kept[pl.ds(at, rows), :] = ins[j][...]
    tables = turn_tables(cos_ref, sin_ref, extra)
    x0 = turn(kept[:, :128].astype(F32), tables[0])
    outs[0][...] = (x0[:, :64] * 0.125).astype(BF)
    outs[1][...] = x0[:, 64:].astype(BF)
    if extra:
        outs[2][...] = kept[:, 256:320]
        x1 = turn(kept[:, 128:256].astype(F32), tables[1])
        outs[3][...] = (x1[:, :64] * 0.125).astype(BF)
        outs[4][...] = x1[:, 64:].astype(BF)
        outs[5][...] = kept[:, 320:]
    else:
        outs[2][...] = kept[:, 128:192]


def rotate_out_body(blocks, extra, place_ref, cos_ref, sin_ref, *refs):
    count = 6 if extra else 3
    ins, outs, kept = refs[:count], refs[count:-1], refs[-1]
    rows = outs[0].shape[0]
    parts = [ref[...].astype(F32) for ref in ins]
    tables = [(c, -s) for c, s in turn_tables(cos_ref, sin_ref, extra)]
    kept[:, :128] = turn(jnp.concatenate(parts[:2], 1), tables[0]).astype(BF)
    if extra:
        kept[:, 128:256] = turn(jnp.concatenate(parts[3:5], 1), tables[1]).astype(BF)
        kept[:, 256:] = jnp.concatenate([parts[2], parts[5]], 1).astype(BF)
    else:
        kept[:, 128:] = jnp.concatenate([parts[2], jnp.zeros_like(parts[2])], 1).astype(BF)
    for j in range(blocks):
        at = pl.multiple_of((place_ref[1] ^ j) * rows, rows)
        outs[j][...] = kept[pl.ds(at, rows), :]


def project_back_body(blocks, pairs, heads, extra, place_ref, c_ref, shift_ref, w_ref, *refs):
    kept = refs[-1]
    groups = (len(refs) - blocks - 4) // 2
    tokens, ins = refs[:groups], refs[groups : groups + blocks]
    outs = refs[groups + blocks : 2 * groups + blocks]
    grad_ref, sum_ref, dot_ref = refs[2 * groups + blocks : -1]
    micro, rows, width = tokens[0].shape
    count = groups * rows
    for j in range(blocks):
        kept[place_ref[1] ^ j] = ins[j][...]
    last = None
    if extra:
        last = jnp.zeros((count, 256), F32)
        for j in range(blocks):
            last = last + kept[j, :, 128:].astype(F32)
        last = last.astype(BF)
    all_a, all_g = [], []
    for m in range(micro):
        n = jnp.concatenate([x[m] for x in tokens], 0).astype(F32)
        a = (n * c_ref[m][None] + shift_ref[m][None]).astype(BF)
        qk, v = [], []
        for h in range(heads):
            pair = m * heads + h
            if pair < blocks:
                qk.append(kept[pair, :, :128])
                at = 256 if extra else 128
                v.append(kept[pair, :, at : at + 64])
            else:
                qk.append(last[:, :128])
                v.append(last[:, 192:])
        g = jnp.concatenate(qk + v, 1)
        da = lax.dot_general(g, w_ref[...], (((1,), (1,)), ((), ())), preferred_element_type=F32)
        for k in range(groups):
            outs[k][m] = da[k * rows : (k + 1) * rows].astype(BF)
        sum_ref[m : m + 1] = jnp.sum(da, 0, keepdims=True)
        dot_ref[m : m + 1] = jnp.sum(da * n, 0, keepdims=True)
        all_a.append(a)
        all_g.append(g)
    grad_ref[...] = lax.dot_general(
        jnp.concatenate(all_a, 0), jnp.concatenate(all_g, 0), (((0,), (0,)), ((), ())),
        preferred_element_type=F32,
    ).astype(BF)


def norm(values):
    centered = values - jnp.mean(values, -1, keepdims=True)
    inverse = lax.rsqrt(jnp.mean(centered * centered, -1, keepdims=True) + 1e-05)
    return centered * inverse, inverse


def by_micro(ref, rows):
    return jnp.concatenate(
        [jnp.broadcast_to(ref[m][None], (rows, ref.shape[1])) for m in range(ref.shape[0])], 0
    )


def middle_body(
    groups, blocks, heads, micro, rows, stripe,
    came_ref, out_ref, x_ref, gate_ref, c_ref, shift_ref,
    merged_ref, attn_ref, middle_ref, second_ref,
):
    width = x_ref.shape[1]
    for u in range(groups):
        for m in range(micro):
            for h in range(heads):
                pair = m * heads + h
                lanes = slice((u * heads + h) * 64, (u * heads + h + 1) * 64)
                if pair < blocks:
                    merged_ref[m * rows : (m + 1) * rows, lanes] = came_ref[u * blocks + pair, :rows]
                else:
                    for b in range(blocks):
                        at = m * rows + b * stripe
                        merged_ref[at : at + stripe, lanes] = came_ref[u * blocks + b, rows:]
    attn = jnp.dot(merged_ref[...], out_ref[...].reshape(width, width), preferred_element_type=F32)
    attn_ref[...] = attn
    middle = x_ref[...].astype(F32) + by_micro(gate_ref, rows) * attn
    middle_ref[...] = middle
    normed, _ = norm(middle)
    second_ref[...] = (normed * by_micro(c_ref, rows) + by_micro(shift_ref, rows)).astype(BF)


def gelu_pair(u):
    t = jnp.tanh(0.7978845608028654 * (u + 0.044715 * u * u * u))
    value = 0.5 * u * (1.0 + t)
    slope = 0.5 * (1.0 + t) + 0.5 * u * (1.0 - t * t) * (
        0.7978845608028654 * (1.0 + 0.134145 * u * u)
    )
    return value, slope


NT = (((1,), (1,)), ((), ()))
TN = (((0,), (0,)), ((), ()))


def feed_body(
    groups, blocks, heads, micro, rows, stripe,
    ex_ref, re_ref, out_w_ref, ex_bias_ref, re_bias_ref, second_ref, middle_ref, attn_ref, dy_ref,
    gate1_ref, gate2_ref, c_ref,
    layer_ref, grad_ref, dattn_ref, do_ref, sums_ref,
    branch_sum, back_sum, dm_sum, do_sum,
):
    step = pl.program_id(0)
    width = middle_ref.shape[1]

    @pl.when(step == 0)
    def _():
        branch_sum[...] = jnp.zeros_like(branch_sum)
        back_sum[...] = jnp.zeros_like(back_sum)
        dm_sum[...] = (by_micro(gate2_ref, rows) * dy_ref[...].astype(F32)).astype(BF)

    expand = ex_ref[...].reshape(width, width)
    reduce = re_ref[...].reshape(width, width)
    u = jnp.dot(second_ref[...], expand, preferred_element_type=F32) + ex_bias_ref[0]
    g, slope = gelu_pair(u)
    branch_sum[...] += jnp.dot(g.astype(BF), reduce, preferred_element_type=F32)
    dg = lax.dot_general(dm_sum[...], reduce, NT, preferred_element_type=F32)
    du = (dg * slope).astype(BF)
    back_sum[...] += lax.dot_general(du, expand, NT, preferred_element_type=F32)

    @pl.when(step == pl.num_programs(0) - 1)
    def _():
        def total(at, x):
            for m in range(micro):
                sums_ref[at * micro + m : at * micro + m + 1] = jnp.sum(
                    x[m * rows : (m + 1) * rows], 0, keepdims=True
                )

        branch = branch_sum[...] + re_bias_ref[...]
        middle = middle_ref[...]
        dy = dy_ref[...].astype(F32)
        layer_ref[...] = (middle + by_micro(gate2_ref, rows) * branch).astype(BF)
        total(0, dy * branch)
        normed, inverse = norm(middle)
        db = back_sum[...]
        total(1, db)
        total(2, db * normed)
        e = db * by_micro(c_ref, rows)
        grad = dy + inverse * (
            e
            - jnp.mean(e, -1, keepdims=True)
            - normed * jnp.mean(e * normed, -1, keepdims=True)
        )
        grad_ref[...] = grad
        total(3, grad * attn_ref[...])
        total(4, dm_sum[...].astype(F32))
        dattn = (by_micro(gate1_ref, rows) * grad).astype(BF)
        dattn_ref[...] = dattn
        do_sum[...] = lax.dot_general(
            dattn, out_w_ref[...].reshape(width, width), NT, preferred_element_type=F32
        ).astype(BF)
        for at in range(groups):
            for m in range(micro):
                for h in range(heads):
                    pair = m * heads + h
                    lanes = slice((at * heads + h) * 64, (at * heads + h + 1) * 64)
                    if pair < blocks:
                        do_ref[at * blocks + pair, :rows] = do_sum[m * rows : (m + 1) * rows, lanes]
                    else:
                        for b in range(blocks):
                            top = m * rows + b * stripe
                            do_ref[at * blocks + b, rows:] = do_sum[top : top + stripe, lanes]
            for b in range(micro * heads, blocks):
                do_ref[at * blocks + b, :rows] = jnp.zeros((rows, 64), BF)


def feed_weights_body(rows, place_ref, ex_ref, re_ref, bias_ref, gate_ref, *refs):
    groups = (len(refs) - 3) // 2
    reduce_ref, expand_ref, sum_ref = refs[2 * groups :]
    width = refs[0].shape[-1]
    second = jnp.concatenate([x[...] for x in refs[:groups]], 0)
    gate = by_micro(gate_ref, rows)
    dm = jnp.concatenate(
        [(gate * x[...].astype(F32)).astype(BF) for x in refs[groups : 2 * groups]], 0
    )
    expand = ex_ref[...].reshape(width, width)
    reduce = re_ref[...].reshape(width, width)
    u = jnp.dot(second, expand, preferred_element_type=F32) + bias_ref[0]
    g, slope = gelu_pair(u)
    du = lax.dot_general(dm, reduce, NT, preferred_element_type=F32) * slope
    du = du.astype(BF)
    sum_ref[...] = jnp.sum(du.astype(F32), 0, keepdims=True)
    reduce_ref[...] = lax.dot_general(g.astype(BF), dm, TN, preferred_element_type=F32).astype(BF)
    expand_ref[...] = lax.dot_general(second, du, TN, preferred_element_type=F32).astype(BF)


def attend_body(block, range_ref, q_ref, sq_ref, k_ref, v_ref, sk_ref, o_ref, lse_ref):
    i = pl.program_id(0)
    q, sq = q_ref[...], sq_ref[0]
    count, width = q.shape

    def step(j, carry):
        high, total, acc = carry
        at = pl.ds(pl.multiple_of(j * block, block), block)
        k, v, sk = k_ref[at, :], v_ref[at, :], sk_ref[at, :]
        s = lax.dot_general(k, q, (((1,), (1,)), ((), ())), preferred_element_type=F32)
        s = jnp.where(sk == sq, s, NEG)
        new = jnp.maximum(high, jnp.max(s, 0, keepdims=True))
        p = jnp.exp(s - new)
        fix = jnp.exp(high - new)
        total = total * fix + jnp.sum(p, 0, keepdims=True)
        acc = acc * fix + lax.dot_general(
            v, p.astype(BF), (((0,), (0,)), ((), ())), preferred_element_type=F32
        )
        return new, total, acc

    first = (
        jnp.full((1, count), NEG, F32),
        jnp.zeros((1, count), F32),
        jnp.zeros((width, count), F32),
    )
    high, total, acc = lax.fori_loop(range_ref[2 * i], range_ref[2 * i + 1], step, first)
    o_ref[...] = (acc / total).T.astype(BF)
    lse_ref[0] = high + jnp.log(total)


def attend_back_body(
    block, range_ref, q_ref, sq_ref, lse_ref, o_ref, do_ref, k_ref, v_ref, sk_ref,
    dq_ref, dk_ref, dv_ref, dk_sum, dv_sum,
):
    i = pl.program_id(0)

    @pl.when(i == 0)
    def _():
        dk_sum[...] = jnp.zeros_like(dk_sum)
        dv_sum[...] = jnp.zeros_like(dv_sum)

    q, sq, lse, do = q_ref[...], sq_ref[0], lse_ref[0], do_ref[...]
    count, width = q.shape
    delta = jnp.sum((do.astype(F32) * o_ref[...].astype(F32)).T, 0, keepdims=True)

    def step(j, dq):
        at = pl.ds(pl.multiple_of(j * block, block), block)
        k, v, sk = k_ref[at, :], v_ref[at, :], sk_ref[at, :]
        s = lax.dot_general(k, q, (((1,), (1,)), ((), ())), preferred_element_type=F32)
        p = jnp.where(sk == sq, jnp.exp(s - lse), 0.0)
        dp = lax.dot_general(v, do, (((1,), (1,)), ((), ())), preferred_element_type=F32)
        ds = (p * (dp - delta)).astype(BF)
        dv_sum[at, :] += jnp.dot(p.astype(BF), do, preferred_element_type=F32)
        dk_sum[at, :] += jnp.dot(ds, q, preferred_element_type=F32)
        return dq + lax.dot_general(
            k, ds, (((0,), (0,)), ((), ())), preferred_element_type=F32
        )

    dq = lax.fori_loop(
        range_ref[2 * i], range_ref[2 * i + 1], step, jnp.zeros((width, count), F32)
    )
    dq_ref[...] = (dq * 0.125).T.astype(BF)

    @pl.when(i == pl.num_programs(0) - 1)
    def _():
        dk_ref[...] = dk_sum[...].astype(BF)
        dv_ref[...] = dv_sum[...].astype(BF)


def attend(ranges, q, sq, k, v, sk, rows, block):
    count, width = q.shape
    steps = count // rows
    size = k.shape[0]
    by_row = pl.BlockSpec((rows, width), lambda i, r: (i, 0))
    as_row = pl.BlockSpec((1, 1, rows), lambda i, r: (i, 0, 0))
    return pl.pallas_call(
        functools.partial(attend_body, block),
        grid_spec=pltpu.PrefetchScalarGridSpec(
            num_scalar_prefetch=1,
            grid=(steps,),
            in_specs=[by_row, as_row, whole_vmem(), whole_vmem(), whole_vmem()],
            out_specs=[by_row, as_row],
        ),
        out_shape=[
            jax.ShapeDtypeStruct((count, width), BF),
            jax.ShapeDtypeStruct((steps, 1, rows), F32),
        ],
        cost_estimate=pl.CostEstimate(
            flops=count * size * width, transcendentals=count * size // 4, bytes_accessed=4 * size * width
        ),
        name="attend",
    )(ranges, q, sq.reshape(steps, 1, rows), k, v, sk)


def attend_back(ranges, q, sq, lse, o, do, k, v, sk, rows, block):
    count, width = q.shape
    steps = count // rows
    size = k.shape[0]
    by_row = pl.BlockSpec((rows, width), lambda i, r: (i, 0))
    as_row = pl.BlockSpec((1, 1, rows), lambda i, r: (i, 0, 0))
    return pl.pallas_call(
        functools.partial(attend_back_body, block),
        grid_spec=pltpu.PrefetchScalarGridSpec(
            num_scalar_prefetch=1,
            grid=(steps,),
            in_specs=[by_row, as_row, as_row, by_row, by_row, whole_vmem(), whole_vmem(), whole_vmem()],
            out_specs=[by_row, whole_vmem(), whole_vmem()],
            scratch_shapes=[pltpu.VMEM((size, width), F32)] * 2,
        ),
        out_shape=[
            jax.ShapeDtypeStruct((count, width), BF),
            jax.ShapeDtypeStruct((size, width), BF),
            jax.ShapeDtypeStruct((size, width), BF),
        ],
        cost_estimate=pl.CostEstimate(
            flops=3 * count * size * width, transcendentals=count * size // 4, bytes_accessed=8 * size * width
        ),
        name="attend_back",
    )(ranges, q, sq.reshape(steps, 1, rows), lse, o, do, k, v, sk)


def on_device(
    tokens,
    cotangent,
    lengths,
    time_step,
    modulate_weight,
    modulate_bias,
    attend_gain,
    input_weight,
    output_weight,
    feed_gain,
    expand_weight,
    expand_bias,
    reduce_weight,
    reduce_bias,
):
    groups, blocks = lax.axis_size("ulysses"), lax.axis_size("blk")
    group_id, block_id = lax.axis_index("ulysses"), lax.axis_index("blk")
    devices = groups * blocks
    micro, rows, width = tokens.shape
    own = micro * rows
    size = devices * rows
    head_width = width // HEADS
    heads = HEADS // groups
    pairs = micro * heads
    extra = pairs > blocks
    lanes = 384 if extra else 256
    stripe = rows // blocks if extra else 0
    mod_rows = modulate_weight.shape[0]
    gain_rows = attend_gain.shape[0]
    ff_rows = expand_bias.shape[0]
    ff = ff_rows * devices
    folds = ff // width
    assert pairs <= blocks + 1 and head_width == 64 and folds == groups and heads == 3
    place = jnp.stack([group_id, block_id]).astype(jnp.int32)
    pair_micro = jnp.minimum(block_id // heads, micro - 1)

    values = tokens.astype(F32)
    n1, r1 = norm(values)
    n1_b = n1.astype(BF)
    n1_group = swap([n1_b] * groups, "ulysses")
    gathered = lax.all_gather(
        jnp.concatenate(
            [
                reduce_weight,
                output_weight,
                expand_weight.reshape(gain_rows, folds, width).transpose(1, 0, 2).reshape(-1, width),
            ],
            0,
        ),
        ALL,
        axis=0,
        tiled=False,
    )
    unit = gain_rows
    while unit % 8:
        unit *= 2
    units = width // unit
    if unit != gain_rows:
        gathered = jnp.concatenate(
            [gathered[:, :ff_rows].reshape(units, -1, width)]
            + [
                gathered[:, at : at + gain_rows].reshape(units, unit, width)
                for at in range(ff_rows, ff_rows + (folds + 1) * gain_rows, gain_rows)
            ],
            1,
        )
    wide = unit * folds

    in_split = input_weight.reshape(gain_rows, 3, groups, heads, head_width)
    in_split = jnp.concatenate(
        [
            in_split[:, :2].transpose(2, 0, 3, 1, 4).reshape(groups, 1, gain_rows, -1),
            in_split[:, 2].transpose(1, 0, 2, 3).reshape(groups, 1, gain_rows, -1),
        ],
        3,
    )
    in_own = exchange(
        jnp.broadcast_to(in_split, (groups, blocks) + in_split.shape[2:]).reshape(
            (devices,) + in_split.shape[2:]
        )
    ).reshape(width, heads * 3 * head_width)

    condition = time_features(time_step, modulate_weight.shape[1] // 2)
    mod_own = jnp.einsum(
        "mc,fc->mf", condition, modulate_weight, preferred_element_type=F32
    ) + modulate_bias.astype(F32)
    small = jnp.concatenate(
        [
            mod_own.reshape(-1),
            attend_gain.astype(F32),
            feed_gain.astype(F32),
            reduce_bias.astype(F32),
            expand_bias.astype(F32),
        ]
    )
    small_size = -(-small.shape[0] // 1024) * 1024
    small = jnp.pad(small, (0, small_size - small.shape[0])).reshape(1, -1, 128)
    small_all = exchange(jnp.broadcast_to(small, (devices,) + small.shape[1:])).reshape(devices, -1)
    at = micro * mod_rows
    mods = small_all[:, :at].reshape(devices, micro, mod_rows).transpose(1, 0, 2).reshape(micro, -1)
    gain1 = small_all[:, at : at + gain_rows].reshape(-1)
    at += gain_rows
    gain2 = small_all[:, at : at + gain_rows].reshape(-1)
    at += gain_rows
    reduce_bias_f = small_all[:, at : at + gain_rows].reshape(1, -1)
    at += gain_rows
    expand_bias_f = small_all[:, at : at + ff_rows].reshape(folds, 1, width)
    shift1, scale1, gate1, shift2, scale2, gate2 = jnp.split(mods, 6, 1)
    c1 = gain1 * (1.0 + scale1)
    c2 = gain2 * (1.0 + scale2)

    index = jnp.arange(size, dtype=jnp.int32)
    pair_lengths = lax.dynamic_index_in_dim(lengths, pair_micro, 0, keepdims=False)
    segment, position = doc_layout(index, pair_lengths)
    last_lengths = lengths[micro - 1]
    last_segment, last_position = doc_layout(index, last_lengths)
    half = head_width // 2
    freqs = jnp.exp(-math.log(10000.0) * jnp.arange(half, dtype=F32) / half)
    lane = jnp.arange(128)
    angles = jnp.where(
        (lane < 64)[None, :], position.astype(F32)[:, None], last_position.astype(F32)[:, None]
    ) * jnp.tile(freqs, 4)[None, :]
    cos_table = jnp.cos(angles)
    sin_table = jnp.where((lane % 64 < 32)[None, :], -1.0, 1.0) * jnp.sin(angles)
    query_rows = math.gcd(size, 256)
    key_block = math.gcd(size, 256)
    first = jnp.arange(size // query_rows, dtype=jnp.int32) * query_rows
    ranges = key_ranges(first, first + query_rows - 1, pair_lengths, key_block)
    segment_column = segment[:, None]

    count = groups * rows
    smem = pl.BlockSpec(memory_space=pltpu.SMEM)
    outgoing = pl.pallas_call(
        functools.partial(project_body, blocks, pairs, heads, extra),
        out_shape=[jax.ShapeDtypeStruct((count, lanes), BF)] * blocks,
        in_specs=[smem] + [whole_vmem()] * (3 + groups),
        out_specs=[whole_vmem()] * blocks,
        scratch_shapes=[pltpu.VMEM((blocks, count, lanes), BF)],
        cost_estimate=pl.CostEstimate(
            flops=2 * micro * count * width * 3 * 64 * heads, transcendentals=0, bytes_accessed=8 * own * width
        ),
        name="project",
    )(place, c1, shift1, in_own, *n1_group)
    incoming = swap(outgoing, "blk")

    span = blocks * rows
    by_span = pl.BlockSpec((span, 64), lambda i, p: (i ^ p[0], 0))
    table_spec = pl.BlockSpec((span, 128), lambda i, p: (i ^ p[0], 0))
    by_rows = pl.BlockSpec((rows, lanes), lambda i, p: (i, 0))
    parts = 6 if extra else 3
    turned = pl.pallas_call(
        functools.partial(rotate_in_body, blocks, extra),
        grid_spec=pltpu.PrefetchScalarGridSpec(
            num_scalar_prefetch=1,
            grid=(groups,),
            in_specs=[table_spec, table_spec] + [by_rows] * blocks,
            out_specs=[by_span] * parts,
            scratch_shapes=[pltpu.VMEM((span, lanes), BF)],
        ),
        out_shape=[jax.ShapeDtypeStruct((size, 64), BF)] * parts,
        name="rotate_in",
    )(place, cos_table, sin_table, *incoming)
    query, key, value = turned[:3]
    attended, lse = attend(
        ranges, query, segment, key, value, segment_column, query_rows, key_block
    )
    message = attended.reshape(devices, rows, head_width)
    if extra:
        striped = lambda x: lax.dynamic_slice_in_dim(
            x.reshape((devices, rows) + x.shape[1:]), block_id * stripe, stripe, 1
        ).reshape((devices * stripe,) + x.shape[1:])
        last_key, last_value = turned[4:]
        last_query = striped(turned[3])
        last_query_segment = striped(last_segment)
        last_rows = math.gcd(devices * stripe, 128)
        chunk = last_rows // stripe
        last_first = jnp.arange(devices // chunk, dtype=jnp.int32) * (chunk * rows) + block_id * stripe
        last_ranges = key_ranges(
            last_first, last_first + (chunk - 1) * rows + stripe - 1, last_lengths, key_block
        )
        last_column = last_segment[:, None]
        last_attended, last_lse = attend(
            last_ranges, last_query, last_query_segment, last_key, last_value, last_column, last_rows, key_block
        )
        message = jnp.concatenate(
            [message, last_attended.reshape(devices, stripe, head_width)], 1
        )
    came = exchange(message)

    ex_spec = lambda f: pl.BlockSpec((units, unit, width), f)
    flat = pl.BlockSpec((own, width), lambda i: (0, 0))
    vec = lambda n: pl.BlockSpec((n, width), lambda i: (0, 0))
    message_spec = pl.BlockSpec((devices, rows + stripe, head_width), lambda i: (0, 0, 0))
    sizes = (groups, blocks, heads, micro, rows, stripe)
    own_f32 = jax.ShapeDtypeStruct((own, width), F32)
    own_bf = jax.ShapeDtypeStruct((own, width), BF)
    merged, attn, middle, second = pl.pallas_call(
        functools.partial(middle_body, *sizes),
        grid=(1,),
        in_specs=[message_spec, ex_spec(lambda i: (0, folds, 0)), flat, vec(micro), vec(micro), vec(micro)],
        out_specs=[flat] * 4,
        out_shape=[own_bf, own_f32, own_f32, own_bf],
        name="middle",
    )(came, gathered, tokens.reshape(own, width), gate1, c2, shift2)
    second_group = swap([second] * groups, "ulysses")
    dy = cotangent.reshape(own, width)
    dy_group = swap([dy] * groups, "ulysses")

    per = width // wide
    layer_output, grad_middle, grad_attn, do_message, sums = pl.pallas_call(
        functools.partial(feed_body, *sizes),
        grid=(folds,),
        in_specs=[
            ex_spec(lambda i: (0, folds + 1 + i, 0)),
            pl.BlockSpec((per, wide, width), lambda i: (i, 0, 0)),
            ex_spec(lambda i: (0, folds, 0)),
            pl.BlockSpec((1, 1, width), lambda i: (i, 0, 0)),
            vec(1),
            flat, flat, flat, flat,
            vec(micro), vec(micro), vec(micro),
        ],
        out_specs=[flat, flat, flat, message_spec, vec(5 * micro)],
        out_shape=[
            own_bf, own_f32, own_bf,
            jax.ShapeDtypeStruct((devices, rows + stripe, head_width), BF),
            jax.ShapeDtypeStruct((5 * micro, width), F32),
        ],
        scratch_shapes=[
            pltpu.VMEM((own, width), F32), pltpu.VMEM((own, width), F32),
            pltpu.VMEM((own, width), BF), pltpu.VMEM((own, width), BF),
        ],
        cost_estimate=pl.CostEstimate(
            flops=8 * own * width * ff, transcendentals=own * ff, bytes_accessed=4 * width * ff
        ),
        name="feed",
    )(gathered, gathered, gathered, expand_bias_f, reduce_bias_f, second, middle, attn, dy, gate1, gate2, c2)
    do_came = exchange(do_message)
    d_gate2, d_shift2, p2, d_gate1, dm_sums = [
        sums[i * micro : (i + 1) * micro] for i in range(5)
    ]

    flat_p = pl.BlockSpec((own, width), lambda i, p: (0, 0))
    square = pl.BlockSpec((width, width), lambda i, p: (0, 0))
    reduce_part, expand_part, bias_part = pl.pallas_call(
        functools.partial(feed_weights_body, rows),
        grid_spec=pltpu.PrefetchScalarGridSpec(
            num_scalar_prefetch=1,
            grid=(1,),
            in_specs=[
                pl.BlockSpec((units, unit, width), lambda i, p: (0, folds + 1 + p[0], 0)),
                pl.BlockSpec((per, wide, width), lambda i, p: (p[0], 0, 0)),
                pl.BlockSpec((1, 1, width), lambda i, p: (p[0], 0, 0)),
                pl.BlockSpec((micro, width), lambda i, p: (0, 0)),
            ]
            + [flat_p] * (2 * groups),
            out_specs=[square, square, pl.BlockSpec((1, width), lambda i, p: (0, 0))],
        ),
        out_shape=[
            jax.ShapeDtypeStruct((width, width), BF),
            jax.ShapeDtypeStruct((width, width), BF),
            jax.ShapeDtypeStruct((1, width), F32),
        ],
        cost_estimate=pl.CostEstimate(
            flops=10 * own * groups * width * width, transcendentals=own * ff, bytes_accessed=16 * width * width
        ),
        name="feed_weights",
    )(place, gathered, gathered, expand_bias_f, gate2, *second_group, *dy_group)
    feed_part = jnp.concatenate(
        [
            reduce_part.reshape(blocks, ff_rows, width),
            expand_part.reshape(groups, blocks, gain_rows, width)
            .transpose(1, 0, 2, 3)
            .reshape(blocks, groups * gain_rows, width),
        ],
        1,
    )
    feed_sum = lax.psum_scatter(feed_part, "blk", scatter_dimension=0, tiled=True)[0]
    reduce_grad = feed_sum[:ff_rows].astype(F32)
    expand_rows = feed_sum[ff_rows:].reshape(groups, gain_rows, width)
    expand_came = jnp.stack(
        swap(
            [
                lax.dynamic_index_in_dim(expand_rows, group_id ^ k, 0, keepdims=False)
                for k in range(groups)
            ],
            "ulysses",
        )
    )
    expand_grad = jnp.concatenate(
        [
            lax.dynamic_index_in_dim(expand_came, group_id ^ k, 0, keepdims=False)
            for k in range(groups)
        ],
        1,
    ).astype(F32)

    output_part = lax.dot_general(merged, grad_attn, TN, preferred_element_type=F32).astype(BF)
    output_part = output_part.reshape(groups, width // groups, width)
    output_part = sum(
        x.astype(F32)
        for x in swap(
            [
                lax.dynamic_index_in_dim(output_part, group_id ^ k, 0, keepdims=False)
                for k in range(groups)
            ],
            "ulysses",
        )
    )
    output_part = output_part.astype(BF).reshape(blocks, gain_rows, width)
    output_grad = sum(
        x.astype(F32)
        for x in swap(
            [
                lax.dynamic_index_in_dim(output_part, block_id ^ k, 0, keepdims=False)
                for k in range(blocks)
            ],
            "blk",
        )
    )

    do_pair = do_came[:, :rows].reshape(size, head_width)
    grads = list(
        attend_back(
            ranges, query, segment, lse, attended, do_pair, key, value, segment_column, query_rows, key_block
        )
    )
    if extra:
        dq_last, dk_last, dv_last = attend_back(
            last_ranges, last_query, last_query_segment, last_lse, last_attended,
            do_came[:, rows:].reshape(devices * stripe, head_width),
            last_key, last_value, last_column, last_rows, key_block,
        )
        dq_last = lax.dynamic_update_slice_in_dim(
            jnp.zeros((devices, rows, head_width), BF),
            dq_last.reshape(devices, stripe, head_width),
            block_id * stripe,
            1,
        ).reshape(size, head_width)
        grads += [dq_last, dk_last, dv_last]
    leaving = pl.pallas_call(
        functools.partial(rotate_out_body, blocks, extra),
        grid_spec=pltpu.PrefetchScalarGridSpec(
            num_scalar_prefetch=1,
            grid=(groups,),
            in_specs=[table_spec, table_spec] + [by_span] * parts,
            out_specs=[by_rows] * blocks,
            scratch_shapes=[pltpu.VMEM((span, lanes), BF)],
        ),
        out_shape=[jax.ShapeDtypeStruct((count, lanes), BF)] * blocks,
        name="rotate_out",
    )(place, cos_table, sin_table, *grads)
    back = swap(leaving, "blk")

    returned = pl.pallas_call(
        functools.partial(project_back_body, blocks, pairs, heads, extra),
        out_shape=[jax.ShapeDtypeStruct((micro, rows, width), BF)] * groups
        + [
            jax.ShapeDtypeStruct((width, heads * 3 * head_width), BF),
            jax.ShapeDtypeStruct((micro, width), F32),
            jax.ShapeDtypeStruct((micro, width), F32),
        ],
        in_specs=[smem] + [whole_vmem()] * (3 + groups + blocks),
        out_specs=[whole_vmem()] * (groups + 3),
        scratch_shapes=[pltpu.VMEM((blocks, count, lanes), BF)],
        cost_estimate=pl.CostEstimate(
            flops=4 * micro * count * width * 3 * 64 * heads, transcendentals=0, bytes_accessed=8 * own * width
        ),
        name="project_back",
    )(place, c1, shift1, in_own, *n1_group, *back)
    input_part, d_shift1, p1 = returned[groups:]
    grad_first = sum(x.astype(F32) for x in swap(returned[:groups], "ulysses"))
    e = grad_first * c1[:, None]
    tokens_grad = (
        grad_middle.reshape(micro, rows, width)
        + r1
        * (
            e
            - jnp.mean(e, -1, keepdims=True)
            - n1 * jnp.mean(e * n1, -1, keepdims=True)
        )
    ).astype(BF)

    grad_mods = jnp.concatenate(
        [d_shift1, p1 * gain1, d_gate1, d_shift2, p2 * gain2, d_gate2], 1
    )
    gain1_part = jnp.sum((1.0 + scale1) * p1, 0)
    gain2_part = jnp.sum((1.0 + scale2) * p2, 0)
    own_units = jnp.where(
        (jnp.arange(groups) == group_id)[:, None], bias_part.reshape(1, width), 0.0
    )
    small_parts = jnp.concatenate(
        [grad_mods.reshape(micro, devices, mod_rows).transpose(1, 0, 2).reshape(devices, -1)]
        + [
            x.reshape(devices, -1)
            for x in (gain1_part, gain2_part, jnp.sum(dm_sums, 0), own_units)
        ],
        1,
    ).astype(BF)
    in_lanes = heads * 3 * head_width
    taken = small_parts.shape[1]
    small_rows = 8 * -(-taken // (8 * in_lanes))
    small_parts = jnp.pad(small_parts, ((0, 0), (0, small_rows * in_lanes - taken)))
    final = exchange(
        jnp.concatenate(
            [
                input_part.reshape(devices, gain_rows, in_lanes),
                small_parts.reshape(devices, small_rows, in_lanes),
            ],
            1,
        )
    )
    small_sum = jnp.sum(final[:, gain_rows:].astype(F32), 0).reshape(-1)
    input_sum = jnp.sum(
        final[:, :gain_rows].astype(F32).reshape(groups, blocks, gain_rows, in_lanes), 1
    )
    two = heads * 2 * head_width
    input_grad = jnp.concatenate(
        [
            input_sum[:, :, :two]
            .reshape(groups, gain_rows, heads, 2, head_width)
            .transpose(1, 3, 0, 2, 4)
            .reshape(gain_rows, 2 * width),
            input_sum[:, :, two:].transpose(1, 0, 2).reshape(gain_rows, width),
        ],
        1,
    )
    at = micro * mod_rows
    mod_sum = small_sum[:at].reshape(micro, mod_rows)
    modulate_weight_grad = jnp.sum(
        mod_sum[:, :, None] * condition.astype(F32)[:, None, :], 0
    )
    cuts = []
    for length in (gain_rows, gain_rows, gain_rows, ff_rows):
        cuts.append(small_sum[at : at + length])
        at += length
    return (
        layer_output.reshape(micro, rows, width),
        tokens_grad,
        modulate_weight_grad,
        jnp.sum(mod_sum, 0),
        cuts[0],
        input_grad,
        output_grad,
        cuts[1],
        expand_grad,
        cuts[3],
        reduce_grad,
        cuts[2],
    )


def solution(mesh):
    both = P(("ulysses", "blk"))
    tall = P(("ulysses", "blk"), None)
    seq = P(None, ("ulysses", "blk"), None)
    in_specs = (
        seq, seq, P(), P(), tall, both, both, tall, tall, both, tall, both, tall, both,
    )
    out_specs = (seq, seq, tall, both, both, tall, tall, both, tall, both, tall, both)
    return jax.shard_map(
        on_device, mesh=mesh, in_specs=in_specs, out_specs=out_specs, check_vma=False
    )
```

time: 559 us -> 436 us (0.78)
  local copies, waits for them, and re-layouts: 126 us -> 32.1 us
  matrix products: 54.2 us -> 0.66 us
  blocking collectives: 46.6 us -> 0 us
  starting transfers between devices: 49.9 us -> 82.5 us
  waiting for transfers between devices: 155 us -> 182 us
  Pallas kernels: 63.9 us -> 88.5 us
  other arithmetic: 39.1 us -> 27.4 us
    ppermute x0 -> x39, waiting for transfers between devices: none -> 115 us  [swap(): lax.ppermute(x, axis, [(i, i ^ k) for i in range(size)])]
    all_to_all x2 -> x0, waiting for transfers between devices: 76.6 us -> none  [the longest x1 54.5 us: on_device(): lax.all_to_all(outgoing, 'blk', split_axis=0, concat_axis=0, tiled=True)]
    dot_general x16 -> x1, matrix products: 54 us -> 0.52 us  [on_device(): lax.dot_general(merged, grad_attn, TN, preferred_element_type=F32)]
    all_to_all x1 -> x0, blocking collectives: 46.6 us -> none  [exchange(): return lax.all_to_all(x, ALL, split_axis=0, concat_axis=0, tiled=True)]
    ppermute x0 -> x39, starting transfers between devices: none -> 43.4 us  [swap(): lax.ppermute(x, axis, [(i, i ^ k) for i in range(size)])]
    slice x15 -> x5, local copies, waits for them, and re-layouts: 40.8 us -> 1.33 us  [the longest x2 1.17 us: on_device(): cuts.append(small_sum[at:at + length])]
    pallas_call x2 -> x6, Pallas kernels: 11.4 us -> 40.8 us  [the longest x1 11.5 us: on_device(): pl.pallas_call(functools.partial(feed_body, *sizes), grid=(folds,), in_sp...]
    reshape x16 -> x14, local copies, waits for them, and re-layouts: 19.5 us -> 3.07 us  [the longest x1 0.69 us: on_device(): expand_bias_f = small_all[:, at:at + ff_rows].reshape(folds, 1, width)]
  transfers between devices with their start and end apart: 12 -> 46, of which waited for: 9 -> 20; matrix products, arithmetic and copies ran while one was open for 33% -> 11% of each run, Pallas kernels for 12% -> 17%
where the time goes in v2:
time: 436 us; the launch traced here: 428 us
  waiting for transfers between devices  182 us (42%)
  Pallas kernels  88.5 us (20%)
  starting transfers between devices  82.5 us (19%)
  local copies, waits for them, and re-layouts  32.1 us (7%)
  other arithmetic  27.4 us (6%)
  between operations  15.1 us (3%)
    ppermute x39, waiting for transfers between devices, swap(): lax.ppermute(x, axis, [(i, i ^ k) for i in range(size)])  115 us
    all_to_all x5, waiting for transfers between devices, exchange(): return lax.all_to_all(x, ALL, split_axis=0, concat_axis=0, tiled=True)  66.9 us
    ppermute x39, starting transfers between devices, swap(): lax.ppermute(x, axis, [(i, i ^ k) for i in range(size)])  43.4 us
    all_to_all x5, starting transfers between devices, exchange(): return lax.all_to_all(x, ALL, split_axis=0, concat_axis=0, tiled=True)  38.9 us
    pallas_call x2, Pallas kernels, attend_back(): pl.pallas_call(functools.partial(attend_back_body, block), grid_spec=pltp...  22.1 us
    pallas_call x2, Pallas kernels, attend(): pl.pallas_call(functools.partial(attend_body, block), grid_spec=pltpu.Pre...  20.6 us
    pallas_call x1, Pallas kernels, on_device(): pl.pallas_call(functools.partial(feed_body, *sizes), grid=(folds,), in_sp...  11.5 us
  transfers between devices with their start and end apart: 46, of which 20 were waited for; matrix products, arithmetic and copies ran while one was open for 11% of the time, Pallas kernels for 17%

profile of v2, /device:TPU:0, one launch (start us, length us, event | category | flops | bytes accessed | tf_op | source)
XLA Modules:
  0.0 428.3 jit_solution(4701269716727811478)
XLA Ops:
  8.3 1.7 pad_maximum_fusion.3
  11.1 2.6 collective-permute-start.1
  15.0 6.1 %all-to-all-start = ((f32[32,8,128]{2,1,0:T(8,128)}), f32[32,8,128]{2,1,0:T(8,128)S(1)}, u32[]{:S(2)}, u32[]{:S(2)}) async-start(f32[32,8,128]{2,1,0:T(8,128)} %broadcast_in_dim.172), calls=%async_computation | async-start | bytes 262144 | tf_op jit(solution)/shard_map/all_to_all | solution.py:19
  23.9 7.5 %all-to-all-done = f32[32,8,128]{2,1,0:T(8,128)S(1)} async-done(((f32[32,8,128]{2,1,0:T(8,128)}), f32[32,8,128]{2,1,0:T(8,128)S(1)}, u32[]{:S(2)}, u32[]{:S(2)}) %all-to-all-start) | async-done | bytes 131104 | tf_op jit(solution)/shard_map/all_to_all | solution.py:19
  32.4 6.1 %all-to-all-start.1 = ((bf16[32,24,576]{2,1,0:T(8,128)(2,1)}), bf16[32,24,576]{2,1,0:T(8,128)(2,1)S(1)}, u32[]{:S(2)}, u32[]{:S(2)}) async-start(bf16[32,24,576]{2,1,0:T(8,128)(2,1)} %bitcast.17), calls=%async_computation.1 | async-start | bytes 1966080 | tf_op jit(solution)/shard_map/all_to_all | solution.py:19
  39.4 5.7 %sine_multiply_fusion = (f32[2048,128]{1,0:T(8,128)}, f32[2048,128]{1,0:T(8,128)}) fusion(f32[128]{0:T(128)S(1)} %compare_select_fusion.2, f32[128]{0:T(128)S(1)} %mul.173, f32[2048]{0:T(1024)S(1)} %subtract_convert_fusion, f32[2048]{0:T(1024)S(1)} %subtract_convert_fusion.1, pred[128]{0:T(512)(128)(4,1)S(1)} %iota_compare_fusion.3), kind=kLoop, calls=%fused_computation.5 | loop fusion | flops 786432 | bytes 2114688 | tf_op jit(solution)/shard_map/mul | solution.py:574
  46.3 32.6 %all-to-all-done.1 = bf16[32,24,576]{2,1,0:T(8,128)(2,1)S(1)} async-done(((bf16[32,24,576]{2,1,0:T(8,128)(2,1)}), bf16[32,24,576]{2,1,0:T(8,128)(2,1)S(1)}, u32[]{:S(2)}, u32[]{:S(2)}) %all-to-all-start.1) | async-done | bytes 884768 | tf_op jit(solution)/shard_map/all_to_all | solution.py:19
  79.9 5.0 %project.1 = (bf16[256,384]{1,0:T(8,128)(2,1)}, bf16[256,384]{1,0:T(8,128)(2,1)}, bf16[256,384]{1,0:T(8,128)(2,1)}, bf16[256,384]{1,0:T(8,128)(2,1)}, bf16[256,3...) custom-call(s32[2]{0:T(128)} %pad_add_fusion.2.place_ref, ...), custom_call_target="tpu_custom_call" | custom-call | flops 679477248 | bytes 1179648 | tf_op jit(solution)/shard_map/project/pallas_call | solution.py:583
  85.0 3.4 collective-permute-start.5
  88.5 2.5 collective-permute-start.7
  90.9 5.5 %collective-permute-done.3.refs_1_ = bf16[256,384]{1,0:T(8,128)(2,1)S(1)} collective-permute-done((bf16[256,384]{1,0:T(8,128)(2,1)}, bf16[256,384]{1,0:T(8,128)(2,1)S(1)}, u32[]{:S(2)}, u32[]{:S(2)}) %collective-permute-start.3) | collective-permute-done | bytes 196640 | tf_op jit(solution)/shard_map/ppermute | solution.py:50
  97.2 13.5 %collective-permute-done.4.refs_2_ = bf16[256,384]{1,0:T(8,128)(2,1)S(1)} collective-permute-done((bf16[256,384]{1,0:T(8,128)(2,1)}, bf16[256,384]{1,0:T(8,128)(2,1)S(1)}, u32[]{:S(2)}, u32[]{:S(2)}) %collective-permute-start.4) | collective-permute-done | bytes 196640 | tf_op jit(solution)/shard_map/ppermute | solution.py:50
  110.7 2.3 collective-permute-start.9
  117.1 4.9 %collective-permute-done.5.refs_3_ = bf16[256,384]{1,0:T(8,128)(2,1)S(1)} collective-permute-done((bf16[256,384]{1,0:T(8,128)(2,1)}, bf16[256,384]{1,0:T(8,128)(2,1)S(1)}, u32[]{:S(2)}, u32[]{:S(2)}) %collective-permute-start.5) | collective-permute-done | bytes 196640 | tf_op jit(solution)/shard_map/ppermute | solution.py:50
  122.0 2.1 collective-permute-done.7.refs_5_
  124.2 6.0 %collective-permute-done.8.refs_6_ = bf16[256,384]{1,0:T(8,128)(2,1)S(1)} collective-permute-done((bf16[256,384]{1,0:T(8,128)(2,1)}, bf16[256,384]{1,0:T(8,128)(2,1)S(1)}, u32[]{:S(2)}, u32[]{:S(2)}) %collective-permute-start.8) | collective-permute-done | bytes 196640 | tf_op jit(solution)/shard_map/ppermute | solution.py:50
  130.2 8.6 %collective-permute-done.9.refs_7_ = bf16[256,384]{1,0:T(8,128)(2,1)S(1)} collective-permute-done((bf16[256,384]{1,0:T(8,128)(2,1)}, bf16[256,384]{1,0:T(8,128)(2,1)S(1)}, u32[]{:S(2)}, u32[]{:S(2)}) %collective-permute-start.9) | collective-permute-done | bytes 196640 | tf_op jit(solution)/shard_map/ppermute | solution.py:50
  139.4 6.0 %rotate_in.1 = (bf16[2048,64]{1,0:T(8,128)(2,1)}, bf16[2048,64]{1,0:T(8,128)(2,1)}, bf16[2048,64]{1,0:T(8,128)(2,1)}, bf16[2048,64]{1,0:T(8,128)(2,1)}, bf16[204...) custom-call(s32[2]{0:T(128)} %pad_add_fusion.2.place_ref, f32[2048,128]{1,0:T(8,128)} %get-tuple-element.163.cos_ref, ...), custom_call_target="tpu_custom_call" | custom-call | tf_op jit(solution)/shard_map/rotate_in/pallas_call | solution.py:601
  146.9 6.4 %attend.3 = (bf16[256,64]{1,0:T(8,128)(2,1)}, f32[2,1,128]{2,1,0:T(1,128)}) custom-call(s32[4]{0:T(128)} %reshape.611.range_ref, bf16[256,64]{1,0:T(8,128)(2,1)} %dynamic-slice_bitcast_fusion.3.q_ref, s32[2,1,128]{2,1,0:T(1,128)} %bitcast.211, bf16[2048,64]{1,0:T(8,128)(2,1)} %get-tuple-element.76.k_ref, bf16[2048,64]{1,0:T(8,128)(2,1)} %get-tuple-element.77.v_ref, ...), custom_call_target="tpu_custom_call" | custom-call | flops 33554432 | bytes 524288 | tf_op jit(solution)/shard_map/attend/pallas_call | solution.py:404
  154.4 14.2 %attend.2 = (bf16[2048,64]{1,0:T(8,128)(2,1)}, f32[8,1,256]{2,1,0:T(1,128)}) custom-call(s32[16]{0:T(128)} %reshape.599.range_ref, bf16[2048,64]{1,0:T(8,128)(2,1)} %get-tuple-element.71.q_ref, s32[8,1,256]{2,1,0:T(1,128)} %bitcast.205, bf16[2048,64]{1,0:T(8,128)(2,1)} %get-tuple-element.72.k_ref, bf16[2048,64]{1,0:T(8,128)(2,1)} %get-tuple-element.73.v_ref, ...), custom_call_target="tpu_custom_call" | custom-call | flops 268435456 | bytes 524288 | tf_op jit(solution)/shard_map/attend/pallas_call | solution.py:404
  171.1 10.1 %all-to-all-start.2 = ((bf16[32,72,64]{1,2,0:T(8,128)(2,1)}), bf16[32,72,64]{1,2,0:T(8,128)(2,1)S(1)}, u32[]{:S(2)}, u32[]{:S(2)}) async-start(bf16[32,72,64]{1,2,0:T(8,128)(2,1)} %pad_maximum_fusion.2), calls=%async_computation.2 | async-start | bytes 1048576 | tf_op jit(solution)/shard_map/all_to_all | solution.py:19
  182.6 14.7 %all-to-all-done.2 = bf16[32,72,64]{1,2,0:T(8,128)(2,1)S(1)} async-done(((bf16[32,72,64]{1,2,0:T(8,128)(2,1)}), bf16[32,72,64]{1,2,0:T(8,128)(2,1)S(1)}, u32[]{:S(2)}, u32[]{:S(2)}) %all-to-all-start.2) | async-done | bytes 294944 | tf_op jit(solution)/shard_map/all_to_all | solution.py:19
  198.5 3.2 middle.1
  201.7 11.5 %feed.1 = (bf16[192,768]{1,0:T(8,128)(2,1)}, f32[192,768]{1,0:T(8,128)}, bf16[192,768]{1,0:T(8,128)(2,1)}, bf16[32,72,64]{2,1,0:T(8,128)(2,1)}, f32[15,768]{1,0:T(8,128)}) custom-call(bf16[32,216,768]{2,1,0:T(8,128)(2,1)} %bitcast.166, bf16[32,216,768]{2,1,0:T(8,128)(2,1)} %bitcast.167, bf16[32,216,768]{2,1,0:T(8,128)(2,1)} %bitcast.168, ...), custom_call_target="tpu_custom_call" | custom-call | flops 3623878656 | bytes 9437184 | tf_op jit(solution)/shard_map/feed/pallas_call | solution.py:660
  213.2 2.1 copy.106
  215.4 2.6 all-to-all-start.3
  218.2 1.7 collective-permute-start.24
  220.5 1.7 collective-permute-start.21
  222.2 12.1 %all-to-all-done.3 = bf16[32,72,64]{1,2,0:T(8,128)(2,1)S(1)} async-done(((bf16[32,72,64]{1,2,0:T(8,128)(2,1)}), bf16[32,72,64]{1,2,0:T(8,128)(2,1)S(1)}, u32[]{:S(2)}, u32[]{:S(2)}) %all-to-all-start.3) | async-done | bytes 294944 | tf_op jit(solution)/shard_map/all_to_all | solution.py:19
  236.4 7.1 %attend_back.3 = (bf16[256,64]{1,0:T(8,128)(2,1)}, bf16[2048,64]{1,0:T(8,128)(2,1)}, bf16[2048,64]{1,0:T(8,128)(2,1)}) custom-call(s32[4]{0:T(128)} %reshape.611.range_ref, bf16[256,64]{1,0:T(8,128)(2,1)} %dynamic-slice_bitcast_fusion.3.q_ref, s32[2,1,128]{2,1,0:T(1,128)} %bitcast.212, f32[2,1,128]{2,1,0:T(1,128)} %get-tuple-element.89.lse_ref, ...), custom_call_target="tpu_custom_call" | custom-call | flops 100663296 | bytes 1048576 | tf_op jit(solution)/shard_map/attend_back/pallas_call | solution.py:429
  244.1 15.0 %attend_back.2 = (bf16[2048,64]{1,0:T(8,128)(2,1)}, bf16[2048,64]{1,0:T(8,128)(2,1)}, bf16[2048,64]{1,0:T(8,128)(2,1)}) custom-call(s32[16]{0:T(128)} %reshape.599.range_ref, bf16[2048,64]{1,0:T(8,128)(2,1)} %get-tuple-element.71.q_ref, s32[8,1,256]{2,1,0:T(1,128)} %bitcast.206, f32[8,1,256]{2,1,0:T(1,128)} %get-tuple-element.84.lse_ref, ...), custom_call_target="tpu_custom_call" | custom-call | flops 805306368 | bytes 1048576 | tf_op jit(solution)/shard_map/attend_back/pallas_call | solution.py:429
  260.0 6.3 %rotate_out.1 = (bf16[256,384]{1,0:T(8,128)(2,1)}, bf16[256,384]{1,0:T(8,128)(2,1)}, bf16[256,384]{1,0:T(8,128)(2,1)}, bf16[256,384]{1,0:T(8,128)(2,1)}, bf16[25...) custom-call(s32[2]{0:T(128)} %pad_add_fusion.2.place_ref, ...), custom_call_target="tpu_custom_call" | custom-call | tf_op jit(solution)/shard_map/rotate_out/pallas_call | solution.py:790
  268.7 8.5 %feed_weights.1 = (bf16[768,768]{1,0:T(8,128)(2,1)}, bf16[768,768]{1,0:T(8,128)(2,1)}, f32[1,768]{1,0:T(1,128)}) custom-call(s32[2]{0:T(128)} %pad_add_fusion.2.place_ref, bf16[32,216,768]{2,1,0:T(8,128)(2,1)} %bitcast.169, bf16[32,216,768]{2,1,0:T(8,128)(2,1)} %bitcast.170, f32[4,1,768]{2,1,0:T(1,128)} %reshape.595.ex_bias_ref.bias_ref, ...), custom_call_target="tpu_custom_call" | custom-call | flops 4529848320 | bytes 9437184 | tf_op jit(solution)/shard_map/feed_weights/pallas_call | solution.py:694
  279.4 1.6 pad_maximum_fusion
  281.9 2.8 collective-permute-start.12
  284.7 3.0 collective-permute-start.14
  288.9 3.6 collective-permute-start.16
  292.5 2.1 collective-permute-done.12.refs_7_
  294.6 23.3 %collective-permute-done.13.refs_8_ = bf16[256,384]{1,0:T(8,128)(2,1)S(1)} collective-permute-done((bf16[256,384]{1,0:T(8,128)(2,1)S(1)}, bf16[256,384]{1,0:T(8,128)(2,1)S(1)}, u32[]{:S(2)}, u32[]{:S(2)}) %collective-permute-start.13) | collective-permute-done | bytes 196640 | tf_op jit(solution)/shard_map/ppermute | solution.py:50
  317.9 11.2 %collective-permute-done.14.refs_9_ = bf16[256,384]{1,0:T(8,128)(2,1)S(1)} collective-permute-done((bf16[256,384]{1,0:T(8,128)(2,1)S(1)}, bf16[256,384]{1,0:T(8,128)(2,1)S(1)}, u32[]{:S(2)}, u32[]{:S(2)}) %collective-permute-start.14) | collective-permute-done | bytes 196640 | tf_op jit(solution)/shard_map/ppermute | solution.py:50
  330.0 5.4 %project_back.1 = (bf16[3,64,768]{2,1,0:T(8,128)(2,1)}, bf16[3,64,768]{2,1,0:T(8,128)(2,1)}, bf16[3,64,768]{2,1,0:T(8,128)(2,1)}, bf16[3,64,768]{2,1,0:T(8,128)(...) custom-call(s32[2]{0:T(128)} %pad_add_fusion.2.place_ref, f32[3,768]{1,0:T(4,128)} %get-tuple-element.158.c_ref, ...), custom_call_target="tpu_custom_call" | custom-call | flops 1358954496 | bytes 1179648 | tf_op jit(solution)/shard_map/project_back/pallas_call | solution.py:804
  339.9 14.1 %all-to-all-start.4 = ((bf16[32,32,576]{2,1,0:T(8,128)(2,1)}), bf16[32,32,576]{2,1,0:T(8,128)(2,1)S(1)}, u32[]{:S(2)}, u32[]{:S(2)}) async-start(bf16[32,32,576]{2,1,0:T(8,128)(2,1)} %pad_maximum_fusion.1), calls=%async_computation.4 | async-start | bytes 2621440 | tf_op jit(solution)/shard_map/all_to_all | solution.py:19
  357.2 14.7 %collective-permute-done.28 = bf16[192,768]{1,0:T(8,128)(2,1)} collective-permute-done((bf16[192,768]{1,0:T(8,128)(2,1)}, bf16[192,768]{1,0:T(8,128)(2,1)}, u32[]{:S(2)}, u32[]{:S(2)}) %collective-permute-start.28) | collective-permute-done | bytes 294944 | tf_op jit(solution)/shard_map/ppermute | solution.py:50
  371.9 9.7 %collective-permute-done.27 = bf16[192,768]{1,0:T(8,128)(2,1)} collective-permute-done((bf16[192,768]{1,0:T(8,128)(2,1)S(1)}, bf16[192,768]{1,0:T(8,128)(2,1)}, u32[]{:S(2)}, u32[]{:S(2)}) %collective-permute-start.27) | collective-permute-done | bytes 294944 | tf_op jit(solution)/shard_map/ppermute | solution.py:50
  384.3 1.6 collective-permute-start.34
  385.9 4.8 %collective-permute-start.32 = (bf16[24,768]{1,0:T(8,128)(2,1)S(1)}, bf16[24,768]{1,0:T(8,128)(2,1)}, u32[]{:S(2)}, u32[]{:S(2)}) collective-permute-start(bf16[24,768]{1,0:T(8,128)(2,1)S(1)} %get-tuple-element.139), channel_id=1, source_target_pairs={{0,4},{1,5},{2,6},{3,7},{4,0},{5,1},{6,2},{7,3},{8,12},{9,13},{10,... | collective-permute-start | bytes 110600 | tf_op jit(solution)/shard_map/ppermute | solution.py:50
  392.6 9.4 %collective-permute-done.33 = bf16[24,768]{1,0:T(8,128)(2,1)} collective-permute-done((bf16[24,768]{1,0:T(8,128)(2,1)S(1)}, bf16[24,768]{1,0:T(8,128)(2,1)}, u32[]{:S(2)}, u32[]{:S(2)}) %collective-permute-start.33) | collective-permute-done | bytes 36896 | tf_op jit(solution)/shard_map/ppermute | solution.py:50
  414.7 1.7 fusion.15
  (310 shorter events, 65.1 us)
Async XLA Ops:
  7.3 191.2 %all-gather.3.cloned.1.call-start = ((), (), s32[]{:S(2)}) async-start(), calls=%async_computation.7 | async-start | bytes 10948608 | tf_op jit(solution)/shard_map/all_gather | solution.py:491
  10.6 35.7 %collective-permute-start = (bf16[3,64,768]{2,1,0:T(8,128)(2,1)S(1)}, bf16[3,64,768]{2,1,0:T(8,128)(2,1)S(1)}, u32[]{:S(2)}, u32[]{:S(2)}) collective-permute-start(bf16[3,64,768]{2,1,0:T(8,128)(2,1)S(1)} %fusion.5.refs_0_), channel_id=1, source_target_pairs={{0,8},{8,0},{16,24},{24,16},{1,9},{9,1},{17,25},{25,17},{2,10},{10... | collective-permute-start | bytes 884744 | tf_op jit(solution)/shard_map/ppermute | solution.py:50
  11.1 35.2 %collective-permute-start.1 = (bf16[3,64,768]{2,1,0:T(8,128)(2,1)S(1)}, bf16[3,64,768]{2,1,0:T(8,128)(2,1)S(1)}, u32[]{:S(2)}, u32[]{:S(2)}) collective-permute-start(bf16[3,64,768]{2,1,0:T(8,128)(2,1)S(1)} %fusion.5.refs_0_), channel_id=1, source_target_pairs={{0,16},{8,24},{16,0},{24,8},{1,17},{9,25},{17,1},{25,9},{2,18},{10... | collective-permute-start | bytes 884744 | tf_op jit(solution)/shard_map/ppermute | solution.py:50
  13.7 32.6 %collective-permute-start.2 = (bf16[3,64,768]{2,1,0:T(8,128)(2,1)S(1)}, bf16[3,64,768]{2,1,0:T(8,128)(2,1)S(1)}, u32[]{:S(2)}, u32[]{:S(2)}) collective-permute-start(bf16[3,64,768]{2,1,0:T(8,128)(2,1)S(1)} %fusion.5.refs_0_), channel_id=1, source_target_pairs={{0,24},{8,16},{16,8},{24,0},{1,25},{9,17},{17,9},{25,1},{2,26},{10... | collective-permute-start | bytes 884744 | tf_op jit(solution)/shard_map/ppermute | solution.py:50
  15.0 16.4 %all-to-all-start = ((f32[32,8,128]{2,1,0:T(8,128)}), f32[32,8,128]{2,1,0:T(8,128)S(1)}, u32[]{:S(2)}, u32[]{:S(2)}) async-start(f32[32,8,128]{2,1,0:T(8,128)} %broadcast_in_dim.172), calls=%async_computation | async-start | bytes 262144 | tf_op jit(solution)/shard_map/all_to_all | solution.py:19
  22.5 93.3 %copy-start.28 = (s32[2048]{0:T(1024)}, s32[2048]{0:T(1024)S(1)}, u32[]{:S(2)}) copy-start(s32[2048]{0:T(1024)S(1)} %get-tuple-element.175) | copy-start | bytes 24580
  32.4 46.5 %all-to-all-start.1 = ((bf16[32,24,576]{2,1,0:T(8,128)(2,1)}), bf16[32,24,576]{2,1,0:T(8,128)(2,1)S(1)}, u32[]{:S(2)}, u32[]{:S(2)}) async-start(bf16[32,24,576]{2,1,0:T(8,128)(2,1)} %bitcast.17), calls=%async_computation.1 | async-start | bytes 1966080 | tf_op jit(solution)/shard_map/all_to_all | solution.py:19
  84.9 11.5 %collective-permute-start.3 = (bf16[256,384]{1,0:T(8,128)(2,1)}, bf16[256,384]{1,0:T(8,128)(2,1)S(1)}, u32[]{:S(2)}, u32[]{:S(2)}) collective-permute-start(bf16[256,384]{1,0:T(8,128)(2,1)} %get-tuple-element.64), channel_id=1, source_target_pairs={{0,1},{1,0},{2,3},{3,2},{4,5},{5,4},{6,7},{7,6},{8,9},{9,8},{10,11... | collective-permute-start | bytes 589832 | tf_op jit(solution)/shard_map/ppermute | solution.py:50
  85.0 25.7 %collective-permute-start.4 = (bf16[256,384]{1,0:T(8,128)(2,1)}, bf16[256,384]{1,0:T(8,128)(2,1)S(1)}, u32[]{:S(2)}, u32[]{:S(2)}) collective-permute-start(bf16[256,384]{1,0:T(8,128)(2,1)} %get-tuple-element.65), channel_id=1, source_target_pairs={{0,2},{1,3},{2,0},{3,1},{4,6},{5,7},{6,4},{7,5},{8,10},{9,11},{10,... | collective-permute-start | bytes 589832 | tf_op jit(solution)/shard_map/ppermute | solution.py:50
  85.0 37.0 %collective-permute-start.5 = (bf16[256,384]{1,0:T(8,128)(2,1)}, bf16[256,384]{1,0:T(8,128)(2,1)S(1)}, u32[]{:S(2)}, u32[]{:S(2)}) collective-permute-start(bf16[256,384]{1,0:T(8,128)(2,1)} %get-tuple-element.66), channel_id=1, source_target_pairs={{0,3},{1,2},{2,1},{3,0},{4,7},{5,6},{6,5},{7,4},{8,11},{9,10},{10,... | collective-permute-start | bytes 589832 | tf_op jit(solution)/shard_map/ppermute | solution.py:50
  88.5 33.6 %collective-permute-start.6 = (bf16[256,384]{1,0:T(8,128)(2,1)}, bf16[256,384]{1,0:T(8,128)(2,1)S(1)}, u32[]{:S(2)}, u32[]{:S(2)}) collective-permute-start(bf16[256,384]{1,0:T(8,128)(2,1)} %get-tuple-element.67), channel_id=1, source_target_pairs={{0,4},{1,5},{2,6},{3,7},{4,0},{5,1},{6,2},{7,3},{8,12},{9,13},{10,... | collective-permute-start | bytes 589832 | tf_op jit(solution)/shard_map/ppermute | solution.py:50
  88.5 35.7 %collective-permute-start.7 = (bf16[256,384]{1,0:T(8,128)(2,1)}, bf16[256,384]{1,0:T(8,128)(2,1)S(1)}, u32[]{:S(2)}, u32[]{:S(2)}) collective-permute-start(bf16[256,384]{1,0:T(8,128)(2,1)} %get-tuple-element.68), channel_id=1, source_target_pairs={{0,5},{1,4},{2,7},{3,6},{4,1},{5,0},{6,3},{7,2},{8,13},{9,12},{10,... | collective-permute-start | bytes 589832 | tf_op jit(solution)/shard_map/ppermute | solution.py:50
  96.4 33.8 %collective-permute-start.8 = (bf16[256,384]{1,0:T(8,128)(2,1)}, bf16[256,384]{1,0:T(8,128)(2,1)S(1)}, u32[]{:S(2)}, u32[]{:S(2)}) collective-permute-start(bf16[256,384]{1,0:T(8,128)(2,1)} %get-tuple-element.69), channel_id=1, source_target_pairs={{0,6},{1,7},{2,4},{3,5},{4,2},{5,3},{6,0},{7,1},{8,14},{9,15},{10,... | collective-permute-start | bytes 589832 | tf_op jit(solution)/shard_map/ppermute | solution.py:50
  110.7 28.0 %collective-permute-start.9 = (bf16[256,384]{1,0:T(8,128)(2,1)}, bf16[256,384]{1,0:T(8,128)(2,1)S(1)}, u32[]{:S(2)}, u32[]{:S(2)}) collective-permute-start(bf16[256,384]{1,0:T(8,128)(2,1)} %get-tuple-element.70), channel_id=1, source_target_pairs={{0,7},{1,6},{2,5},{3,4},{4,3},{5,2},{6,1},{7,0},{8,15},{9,14},{10,... | collective-permute-start | bytes 589832 | tf_op jit(solution)/shard_map/ppermute | solution.py:50
  171.1 26.3 %all-to-all-start.2 = ((bf16[32,72,64]{1,2,0:T(8,128)(2,1)}), bf16[32,72,64]{1,2,0:T(8,128)(2,1)S(1)}, u32[]{:S(2)}, u32[]{:S(2)}) async-start(bf16[32,72,64]{1,2,0:T(8,128)(2,1)} %pad_maximum_fusion.2), calls=%async_computation.2 | async-start | bytes 1048576 | tf_op jit(solution)/shard_map/all_to_all | solution.py:19
  215.4 19.0 %all-to-all-start.3 = ((bf16[32,72,64]{1,2,0:T(8,128)(2,1)}), bf16[32,72,64]{1,2,0:T(8,128)(2,1)S(1)}, u32[]{:S(2)}, u32[]{:S(2)}) async-start(bf16[32,72,64]{1,2,0:T(8,128)(2,1)} %copy.106), calls=%async_computation.3 | async-start | bytes 1048576 | tf_op jit(solution)/shard_map/all_to_all | solution.py:19
  218.0 196.8 %reduce-scatter.2.cloned.1.call-start = ((), (), s32[]{:S(2)}) async-start(), calls=%async_computation.6 | async-start | bytes 2654208 | tf_op jit(solution)/shard_map/reduce_scatter | solution.py:727
  218.0 25.5 %collective-permute-start.23 = (bf16[192,768]{1,0:T(8,128)(2,1)S(1)}, bf16[192,768]{1,0:T(8,128)(2,1)S(1)}, u32[]{:S(2)}, u32[]{:S(2)}) collective-permute-start(bf16[192,768]{1,0:T(8,128)(2,1)S(1)} %bitcast.186), channel_id=1, source_target_pairs={{0,8},{8,0},{16,24},{24,16},{1,9},{9,1},{17,25},{25,17},{2,10},{10... | collective-permute-start | bytes 884744 | tf_op jit(solution)/shard_map/ppermute | solution.py:50
  218.2 48.1 %collective-permute-start.24 = (bf16[192,768]{1,0:T(8,128)(2,1)S(1)}, bf16[192,768]{1,0:T(8,128)(2,1)S(1)}, u32[]{:S(2)}, u32[]{:S(2)}) collective-permute-start(bf16[192,768]{1,0:T(8,128)(2,1)S(1)} %bitcast.187), channel_id=1, source_target_pairs={{0,16},{8,24},{16,0},{24,8},{1,17},{9,25},{17,1},{25,9},{2,18},{10... | collective-permute-start | bytes 884744 | tf_op jit(solution)/shard_map/ppermute | solution.py:50
  219.9 47.1 %collective-permute-start.25 = (bf16[192,768]{1,0:T(8,128)(2,1)S(1)}, bf16[192,768]{1,0:T(8,128)(2,1)S(1)}, u32[]{:S(2)}, u32[]{:S(2)}) collective-permute-start(bf16[192,768]{1,0:T(8,128)(2,1)S(1)} %bitcast.188), channel_id=1, source_target_pairs={{0,24},{8,16},{16,8},{24,0},{1,25},{9,17},{17,9},{25,1},{2,26},{10... | collective-permute-start | bytes 884744 | tf_op jit(solution)/shard_map/ppermute | solution.py:50
  220.2 46.9 %collective-permute-start.20 = (bf16[192,768]{1,0:T(8,128)(2,1)S(1)}, bf16[192,768]{1,0:T(8,128)(2,1)S(1)}, u32[]{:S(2)}, u32[]{:S(2)}) collective-permute-start(bf16[192,768]{1,0:T(8,128)(2,1)S(1)} %copy-done.6), channel_id=1, source_target_pairs={{0,8},{8,0},{16,24},{24,16},{1,9},{9,1},{17,25},{25,17},{2,10},{10... | collective-permute-start | bytes 884744 | tf_op jit(solution)/shard_map/ppermute | solution.py:50
  220.5 46.5 %collective-permute-start.21 = (bf16[192,768]{1,0:T(8,128)(2,1)S(1)}, bf16[192,768]{1,0:T(8,128)(2,1)S(1)}, u32[]{:S(2)}, u32[]{:S(2)}) collective-permute-start(bf16[192,768]{1,0:T(8,128)(2,1)S(1)} %copy-done.6), channel_id=1, source_target_pairs={{0,16},{8,24},{16,0},{24,8},{1,17},{9,25},{17,1},{25,9},{2,18},{10... | collective-permute-start | bytes 884744 | tf_op jit(solution)/shard_map/ppermute | solution.py:50
  243.5 23.5 %collective-permute-start.22 = (bf16[192,768]{1,0:T(8,128)(2,1)S(1)}, bf16[192,768]{1,0:T(8,128)(2,1)S(1)}, u32[]{:S(2)}, u32[]{:S(2)}) collective-permute-start(bf16[192,768]{1,0:T(8,128)(2,1)S(1)} %copy-done.6), channel_id=1, source_target_pairs={{0,24},{8,16},{16,8},{24,0},{1,25},{9,17},{17,9},{25,1},{2,26},{10... | collective-permute-start | bytes 884744 | tf_op jit(solution)/shard_map/ppermute | solution.py:50
  266.3 21.4 %collective-permute-start.10 = (bf16[256,384]{1,0:T(8,128)(2,1)}, bf16[256,384]{1,0:T(8,128)(2,1)S(1)}, u32[]{:S(2)}, u32[]{:S(2)}) collective-permute-start(bf16[256,384]{1,0:T(8,128)(2,1)} %get-tuple-element.94), channel_id=1, source_target_pairs={{0,1},{1,0},{2,3},{3,2},{4,5},{5,4},{6,7},{7,6},{8,9},{9,8},{10,11... | collective-permute-start | bytes 589832 | tf_op jit(solution)/shard_map/ppermute | solution.py:50
  267.0 21.8 %collective-permute-start.11 = (bf16[256,384]{1,0:T(8,128)(2,1)}, bf16[256,384]{1,0:T(8,128)(2,1)S(1)}, u32[]{:S(2)}, u32[]{:S(2)}) collective-permute-start(bf16[256,384]{1,0:T(8,128)(2,1)} %get-tuple-element.95), channel_id=1, source_target_pairs={{0,2},{1,3},{2,0},{3,1},{4,6},{5,7},{6,4},{7,5},{8,10},{9,11},{10,... | collective-permute-start | bytes 589832 | tf_op jit(solution)/shard_map/ppermute | solution.py:50
  281.9 12.7 %collective-permute-start.12 = (bf16[256,384]{1,0:T(8,128)(2,1)S(1)}, bf16[256,384]{1,0:T(8,128)(2,1)S(1)}, u32[]{:S(2)}, u32[]{:S(2)}) collective-permute-start(bf16[256,384]{1,0:T(8,128)(2,1)S(1)} %copy-done.47), channel_id=1, source_target_pairs={{0,3},{1,2},{2,1},{3,0},{4,7},{5,6},{6,5},{7,4},{8,11},{9,10},{10,... | collective-permute-start | bytes 589832 | tf_op jit(solution)/shard_map/ppermute | solution.py:50
  284.7 33.3 %collective-permute-start.13 = (bf16[256,384]{1,0:T(8,128)(2,1)S(1)}, bf16[256,384]{1,0:T(8,128)(2,1)S(1)}, u32[]{:S(2)}, u32[]{:S(2)}) collective-permute-start(bf16[256,384]{1,0:T(8,128)(2,1)S(1)} %copy-done.46), channel_id=1, source_target_pairs={{0,4},{1,5},{2,6},{3,7},{4,0},{5,1},{6,2},{7,3},{8,12},{9,13},{10,... | collective-permute-start | bytes 589832 | tf_op jit(solution)/shard_map/ppermute | solution.py:50
  284.7 44.5 %collective-permute-start.14 = (bf16[256,384]{1,0:T(8,128)(2,1)S(1)}, bf16[256,384]{1,0:T(8,128)(2,1)S(1)}, u32[]{:S(2)}, u32[]{:S(2)}) collective-permute-start(bf16[256,384]{1,0:T(8,128)(2,1)S(1)} %copy-done.45), channel_id=1, source_target_pairs={{0,5},{1,4},{2,7},{3,6},{4,1},{5,0},{6,3},{7,2},{8,13},{9,12},{10,... | collective-permute-start | bytes 589832 | tf_op jit(solution)/shard_map/ppermute | solution.py:50
  287.7 41.5 %collective-permute-start.15 = (bf16[256,384]{1,0:T(8,128)(2,1)S(1)}, bf16[256,384]{1,0:T(8,128)(2,1)S(1)}, u32[]{:S(2)}, u32[]{:S(2)}) collective-permute-start(bf16[256,384]{1,0:T(8,128)(2,1)S(1)} %copy-done.44), channel_id=1, source_target_pairs={{0,6},{1,7},{2,4},{3,5},{4,2},{5,3},{6,0},{7,1},{8,14},{9,15},{10,... | collective-permute-start | bytes 589832 | tf_op jit(solution)/shard_map/ppermute | solution.py:50
  288.9 40.3 %collective-permute-start.16 = (bf16[256,384]{1,0:T(8,128)(2,1)S(1)}, bf16[256,384]{1,0:T(8,128)(2,1)S(1)}, u32[]{:S(2)}, u32[]{:S(2)}) collective-permute-start(bf16[256,384]{1,0:T(8,128)(2,1)S(1)} %copy-done.42), channel_id=1, source_target_pairs={{0,7},{1,6},{2,5},{3,4},{4,3},{5,2},{6,1},{7,0},{8,15},{9,14},{10,... | collective-permute-start | bytes 589832 | tf_op jit(solution)/shard_map/ppermute | solution.py:50
  339.9 71.5 %all-to-all-start.4 = ((bf16[32,32,576]{2,1,0:T(8,128)(2,1)}), bf16[32,32,576]{2,1,0:T(8,128)(2,1)S(1)}, u32[]{:S(2)}, u32[]{:S(2)}) async-start(bf16[32,32,576]{2,1,0:T(8,128)(2,1)} %pad_maximum_fusion.1), calls=%async_computation.4 | async-start | bytes 2621440 | tf_op jit(solution)/shard_map/all_to_all | solution.py:19
  355.3 53.8 %copy-start.31 = (f32[3,768]{1,0:T(4,128)S(1)}, f32[3,768]{1,0:T(4,128)}, u32[]{:S(2)}) copy-start(f32[3,768]{1,0:T(4,128)} %get-tuple-element.158.c_ref) | copy-start | bytes 27652
  355.3 16.6 %collective-permute-start.28 = (bf16[192,768]{1,0:T(8,128)(2,1)}, bf16[192,768]{1,0:T(8,128)(2,1)}, u32[]{:S(2)}, u32[]{:S(2)}) collective-permute-start(bf16[192,768]{1,0:T(8,128)(2,1)} %get-tuple-element.131), channel_id=1, source_target_pairs={{0,24},{8,16},{16,8},{24,0},{1,25},{9,17},{17,9},{25,1},{2,26},{10... | collective-permute-start | bytes 884744 | tf_op jit(solution)/shard_map/ppermute | solution.py:50
  356.6 25.0 %collective-permute-start.27 = (bf16[192,768]{1,0:T(8,128)(2,1)S(1)}, bf16[192,768]{1,0:T(8,128)(2,1)}, u32[]{:S(2)}, u32[]{:S(2)}) collective-permute-start(bf16[192,768]{1,0:T(8,128)(2,1)S(1)} %get-tuple-element.132), channel_id=1, source_target_pairs={{0,16},{8,24},{16,0},{24,8},{1,17},{9,25},{17,1},{25,9},{2,18},{10... | collective-permute-start | bytes 884744 | tf_op jit(solution)/shard_map/ppermute | solution.py:50
  357.0 24.6 %collective-permute-start.26 = (bf16[192,768]{1,0:T(8,128)(2,1)S(1)}, bf16[192,768]{1,0:T(8,128)(2,1)}, u32[]{:S(2)}, u32[]{:S(2)}) collective-permute-start(bf16[192,768]{1,0:T(8,128)(2,1)S(1)} %get-tuple-element.130), channel_id=1, source_target_pairs={{0,8},{8,0},{16,24},{24,16},{1,9},{9,1},{17,25},{25,17},{2,10},{10... | collective-permute-start | bytes 884744 | tf_op jit(solution)/shard_map/ppermute | solution.py:50
  383.0 8.2 %collective-permute-start.35 = (bf16[24,768]{1,0:T(8,128)(2,1)S(1)}, bf16[24,768]{1,0:T(8,128)(2,1)S(1)}, u32[]{:S(2)}, u32[]{:S(2)}) collective-permute-start(bf16[24,768]{1,0:T(8,128)(2,1)S(1)} %get-tuple-element.136), channel_id=1, source_target_pairs={{0,7},{1,6},{2,5},{3,4},{4,3},{5,2},{6,1},{7,0},{8,15},{9,14},{10,... | collective-permute-start | bytes 110600 | tf_op jit(solution)/shard_map/ppermute | solution.py:50
  384.3 6.8 %collective-permute-start.34 = (bf16[24,768]{1,0:T(8,128)(2,1)S(1)}, bf16[24,768]{1,0:T(8,128)(2,1)}, u32[]{:S(2)}, u32[]{:S(2)}) collective-permute-start(bf16[24,768]{1,0:T(8,128)(2,1)S(1)} %get-tuple-element.137), channel_id=1, source_target_pairs={{0,6},{1,7},{2,4},{3,5},{4,2},{5,3},{6,0},{7,1},{8,14},{9,15},{10,... | collective-permute-start | bytes 110600 | tf_op jit(solution)/shard_map/ppermute | solution.py:50
  385.9 16.1 %collective-permute-start.33 = (bf16[24,768]{1,0:T(8,128)(2,1)S(1)}, bf16[24,768]{1,0:T(8,128)(2,1)}, u32[]{:S(2)}, u32[]{:S(2)}) collective-permute-start(bf16[24,768]{1,0:T(8,128)(2,1)S(1)} %get-tuple-element.138), channel_id=1, source_target_pairs={{0,5},{1,4},{2,7},{3,6},{4,1},{5,0},{6,3},{7,2},{8,13},{9,12},{10,... | collective-permute-start | bytes 110600 | tf_op jit(solution)/shard_map/ppermute | solution.py:50
  385.9 16.1 %collective-permute-start.32 = (bf16[24,768]{1,0:T(8,128)(2,1)S(1)}, bf16[24,768]{1,0:T(8,128)(2,1)}, u32[]{:S(2)}, u32[]{:S(2)}) collective-permute-start(bf16[24,768]{1,0:T(8,128)(2,1)S(1)} %get-tuple-element.139), channel_id=1, source_target_pairs={{0,4},{1,5},{2,6},{3,7},{4,0},{5,1},{6,2},{7,3},{8,12},{9,13},{10,... | collective-permute-start | bytes 110600 | tf_op jit(solution)/shard_map/ppermute | solution.py:50
  390.7 12.1 %collective-permute-start.31 = (bf16[24,768]{1,0:T(8,128)(2,1)S(1)}, bf16[24,768]{1,0:T(8,128)(2,1)S(1)}, u32[]{:S(2)}, u32[]{:S(2)}) collective-permute-start(bf16[24,768]{1,0:T(8,128)(2,1)S(1)} %get-tuple-element.140), channel_id=1, source_target_pairs={{0,3},{1,2},{2,1},{3,0},{4,7},{5,6},{6,5},{7,4},{8,11},{9,10},{10,... | collective-permute-start | bytes 110600 | tf_op jit(solution)/shard_map/ppermute | solution.py:50
  391.1 17.9 %collective-permute-start.19 = (bf16[3,64,768]{2,1,0:T(8,128)(2,1)}, bf16[3,64,768]{2,1,0:T(8,128)(2,1)S(1)}, u32[]{:S(2)}, u32[]{:S(2)}) collective-permute-start(bf16[3,64,768]{2,1,0:T(8,128)(2,1)} %get-tuple-element.104), channel_id=1, source_target_pairs={{0,24},{8,16},{16,8},{24,0},{1,25},{9,17},{17,9},{25,1},{2,26},{10... | collective-permute-start | bytes 884744 | tf_op jit(solution)/shard_map/ppermute | solution.py:50
  391.2 17.9 %collective-permute-start.18 = (bf16[3,64,768]{2,1,0:T(8,128)(2,1)}, bf16[3,64,768]{2,1,0:T(8,128)(2,1)S(1)}, u32[]{:S(2)}, u32[]{:S(2)}) collective-permute-start(bf16[3,64,768]{2,1,0:T(8,128)(2,1)} %get-tuple-element.103), channel_id=1, source_target_pairs={{0,16},{8,24},{16,0},{24,8},{1,17},{9,25},{17,1},{25,9},{2,18},{10... | collective-permute-start | bytes 884744 | tf_op jit(solution)/shard_map/ppermute | solution.py:50
  402.0 7.1 %collective-permute-start.17 = (bf16[3,64,768]{2,1,0:T(8,128)(2,1)}, bf16[3,64,768]{2,1,0:T(8,128)(2,1)}, u32[]{:S(2)}, u32[]{:S(2)}) collective-permute-start(bf16[3,64,768]{2,1,0:T(8,128)(2,1)} %get-tuple-element.102), channel_id=1, source_target_pairs={{0,8},{8,0},{16,24},{24,16},{1,9},{9,1},{17,25},{25,17},{2,10},{10... | collective-permute-start | bytes 884744 | tf_op jit(solution)/shard_map/ppermute | solution.py:50
  402.0 4.1 collective-permute-start.30
  403.5 4.1 collective-permute-start.29
  416.5 3.8 collective-permute-start.38
  416.6 4.2 collective-permute-start.37
  418.1 2.6 collective-permute-start.36
  (53 other events, 669.1 us)
Sparse Core Ops, SparseCore 0:
  11.1 133.7 all-gather.2
  281.2 102.0 reduce-scatter.1

commit v3 on v2

--- a/solution.py
+++ b/solution.py
@@ -52,12 +52,23 @@
     ]
 
 
+def unscramble(x, index, axis):
+    count, bit = x.shape[axis], 1
+    while bit < count:
+        shape = x.shape
+        y = x.reshape(shape[:axis] + (count // (2 * bit), 2, bit) + shape[axis + 1 :])
+        flipped = jnp.flip(y, axis + 1)
+        x = jnp.where((index & bit) != 0, flipped, y).reshape(shape)
+        bit *= 2
+    return x
+
+
 def project_body(blocks, pairs, heads, extra, place_ref, c_ref, shift_ref, w_ref, *refs):
     groups = len(refs) - blocks - 1
     tokens, outs, kept = refs[:groups], refs[groups:-1], refs[-1]
     micro, rows, width = tokens[0].shape
-    two = 128 * heads
-    weights = [w_ref[:, c : min(c + 128, w_ref.shape[1])] for c in range(0, w_ref.shape[1], 128)]
+    end = 192 * heads
+    weights = [w_ref[:, c : min(c + 128, end)] for c in range(0, end, 128)]
     order = list(range(micro))[::-1]
     z_qk = z_v = None
     for m in order:
@@ -86,8 +97,7 @@
         outs[j][...] = kept[place_ref[1] ^ j]
 
 
-def turn_tables(cos_ref, sin_ref, extra):
-    cos, sin = cos_ref[...], sin_ref[...]
+def turn_tables(cos, sin, extra):
     lane = lax.broadcasted_iota(jnp.int32, cos.shape, 1)
     low = lane < 64
     cos_r, sin_r = pltpu.roll(cos, 64, 1), pltpu.roll(sin, 64, 1)
@@ -110,7 +120,7 @@
     for j in range(blocks):
         at = pl.multiple_of((place_ref[1] ^ j) * rows, rows)
         kept[pl.ds(at, rows), :] = ins[j][...]
-    tables = turn_tables(cos_ref, sin_ref, extra)
+    tables = turn_tables(cos_ref[...], sin_ref[...], extra)
     x0 = turn(kept[:, :128].astype(F32), tables[0])
     outs[0][...] = (x0[:, :64] * 0.125).astype(BF)
     outs[1][...] = x0[:, 64:].astype(BF)
@@ -129,7 +139,7 @@
     ins, outs, kept = refs[:count], refs[count:-1], refs[-1]
     rows = outs[0].shape[0]
     parts = [ref[...].astype(F32) for ref in ins]
-    tables = [(c, -s) for c, s in turn_tables(cos_ref, sin_ref, extra)]
+    tables = [(c, -s) for c, s in turn_tables(cos_ref[...], sin_ref[...], extra)]
     kept[:, :128] = turn(jnp.concatenate(parts[:2], 1), tables[0]).astype(BF)
     if extra:
         kept[:, 128:256] = turn(jnp.concatenate(parts[3:5], 1), tables[1]).astype(BF)
@@ -172,7 +182,7 @@
                 qk.append(last[:, :128])
                 v.append(last[:, 192:])
         g = jnp.concatenate(qk + v, 1)
-        da = lax.dot_general(g, w_ref[...], (((1,), (1,)), ((), ())), preferred_element_type=F32)
+        da = lax.dot_general(g, w_ref[:, : 192 * heads], (((1,), (1,)), ((), ())), preferred_element_type=F32)
         for k in range(groups):
             outs[k][m] = da[k * rows : (k + 1) * rows].astype(BF)
         sum_ref[m : m + 1] = jnp.sum(da, 0, keepdims=True)
@@ -208,12 +218,17 @@
             for h in range(heads):
                 pair = m * heads + h
                 lanes = slice((u * heads + h) * 64, (u * heads + h + 1) * 64)
-                if pair < blocks:
-                    merged_ref[m * rows : (m + 1) * rows, lanes] = came_ref[u * blocks + pair, :rows]
+                half = rows // 2
+                if pair < blocks and stripe:
+                    at = m * rows
+                    merged_ref[at : at + half, lanes] = came_ref[u * blocks + pair, :half, :64]
+                    merged_ref[at + half : at + rows, lanes] = came_ref[u * blocks + pair, :half, 64:]
+                elif pair < blocks:
+                    merged_ref[m * rows : (m + 1) * rows, lanes] = came_ref[u * blocks + pair]
                 else:
                     for b in range(blocks):
                         at = m * rows + b * stripe
-                        merged_ref[at : at + stripe, lanes] = came_ref[u * blocks + b, rows:]
+                        merged_ref[at : at + stripe, lanes] = came_ref[u * blocks + b, half:, :64]
     attn = jnp.dot(merged_ref[...], out_ref[...].reshape(width, width), preferred_element_type=F32)
     attn_ref[...] = attn
     middle = x_ref[...].astype(F32) + by_micro(gate_ref, rows) * attn
@@ -296,14 +311,19 @@
                 for h in range(heads):
                     pair = m * heads + h
                     lanes = slice((at * heads + h) * 64, (at * heads + h + 1) * 64)
-                    if pair < blocks:
-                        do_ref[at * blocks + pair, :rows] = do_sum[m * rows : (m + 1) * rows, lanes]
+                    half, top = rows // 2, m * rows
+                    if pair < blocks and stripe:
+                        do_ref[at * blocks + pair, :half, :64] = do_sum[top : top + half, lanes]
+                        do_ref[at * blocks + pair, :half, 64:] = do_sum[top + half : top + rows, lanes]
+                    elif pair < blocks:
+                        do_ref[at * blocks + pair] = do_sum[top : top + rows, lanes]
                     else:
                         for b in range(blocks):
-                            top = m * rows + b * stripe
-                            do_ref[at * blocks + b, rows:] = do_sum[top : top + stripe, lanes]
+                            do_ref[at * blocks + b, half:, :64] = do_sum[top : top + stripe, lanes]
+                            do_ref[at * blocks + b, half:, 64:] = jnp.zeros((stripe, 64), BF)
+                            top += stripe
             for b in range(micro * heads, blocks):
-                do_ref[at * blocks + b, :rows] = jnp.zeros((rows, 64), BF)
+                do_ref[at * blocks + b] = jnp.zeros((rows, 64), BF)
 
 
 def feed_weights_body(rows, place_ref, ex_ref, re_ref, bias_ref, gate_ref, *refs):
@@ -445,6 +465,185 @@
         ),
         name="attend_back",
     )(ranges, q, sq.reshape(steps, 1, rows), lse, o, do, k, v, sk)
+
+
+def spread(ref, at, rows):
+    return ref[pl.ds(pl.multiple_of(at, rows), rows), :]
+
+
+def keys_mask(low, high, at, count):
+    position = at + lax.broadcasted_iota(jnp.int32, (count, low.shape[1]), 0)
+    return (position >= low) & (position < high)
+
+
+QB, KB = 256, 512
+
+
+def attend_all_body(
+    blocks, groups, rows, stripe,
+    place_ref, range_ref, last_range_ref, low_ref, high_ref, last_low_ref, last_high_ref, cos_ref, sin_ref, *refs,
+):
+    ins = refs[:blocks]
+    message, q_ref, k_ref, v_ref, zq_ref, zk_ref, zv_ref, o_ref, zo_ref, lse_ref, zlse_ref = refs[blocks : blocks + 11]
+    kept, wide, scores = refs[blocks + 11 :]
+    span = blocks * rows
+    size = groups * span
+    me_u, me_b = place_ref[0], place_ref[1]
+    for g in range(groups):
+        for j in range(blocks):
+            kept[pl.ds(pl.multiple_of((me_b ^ j) * rows, rows), rows), :] = spread(ins[j], (me_u ^ g) * rows, rows)
+        at = slice(g * span, (g + 1) * span)
+        cos, sin = cos_ref[at], sin_ref[at]
+        tables = turn_tables(cos, sin, True)
+        x = turn(kept[:, :128].astype(F32), tables[0])
+        q_ref[at] = (x[:, :64] * 0.125).astype(BF)
+        k_ref[at] = x[:, 64:].astype(BF)
+        v_ref[at] = kept[:, 256:320]
+        x = turn(kept[:, 128:256].astype(F32), tables[1])
+        wide[at] = x[:, :64] * 0.125
+        zk_ref[at] = x[:, 64:].astype(BF)
+        zv_ref[at] = kept[:, 320:]
+    tail = slice(size, size + KB - QB)
+    for ref in (k_ref, v_ref, zk_ref, zv_ref):
+        ref[tail] = jnp.zeros((KB - QB, 64), BF)
+    devices = groups * blocks
+    for d in range(0, devices, 2):
+        zq_ref[d * stripe : (d + 2) * stripe] = jnp.concatenate(
+            [spread(wide, (d + e) * rows + me_b * stripe, stripe) for e in range(2)], 0
+        ).astype(BF)
+
+    def block(q, low, high, first, stop, keys, values):
+        count = q.shape[0]
+
+        def score(t, high_s):
+            at = pl.multiple_of((first + 2 * t) * QB, QB)
+            s = lax.dot_general(keys[pl.ds(at, KB), :], q, NT, preferred_element_type=F32)
+            s = jnp.where(keys_mask(low, high, at, KB), s, NEG)
+            scores[t, :, :count] = s
+            return jnp.maximum(high_s, jnp.max(s, 0, keepdims=True))
+
+        steps = (stop - first + 1) // 2
+        top = lax.fori_loop(0, steps, score, jnp.full((1, count), NEG, F32))
+
+        def weigh(t, carry):
+            total, acc = carry
+            at = pl.multiple_of((first + 2 * t) * QB, QB)
+            p = jnp.exp(scores[t, :, :count] - top)
+            return total + jnp.sum(p, 0, keepdims=True), acc + lax.dot_general(
+                values[pl.ds(at, KB), :], p.astype(BF), TN, preferred_element_type=F32
+            )
+
+        total, acc = lax.fori_loop(
+            0, steps, weigh, (jnp.zeros((1, count), F32), jnp.zeros((64, count), F32))
+        )
+        return (acc / total).T, top + jnp.log(total)
+
+    half = rows // 2
+
+    def run(i, _):
+        o, lse = block(
+            spread(q_ref, i * QB, QB), low_ref[i], high_ref[i], range_ref[2 * i], range_ref[2 * i + 1], k_ref, v_ref
+        )
+        o = o.astype(BF)
+        o_ref[pl.ds(pl.multiple_of(i * QB, QB), QB), :] = o
+        lse_ref[i] = lse
+        for d in range(QB // rows):
+            message[i * (QB // rows) + d, :half] = jnp.concatenate(
+                [o[d * rows : d * rows + half], o[d * rows + half : (d + 1) * rows]], 1
+            )
+        return 0
+
+    lax.fori_loop(0, size // QB, run, 0)
+    few = zlse_ref.shape[2]
+
+    def run_last(i, _):
+        o, lse = block(
+            spread(zq_ref, i * few, few), last_low_ref[i], last_high_ref[i],
+            last_range_ref[2 * i], last_range_ref[2 * i + 1], zk_ref, zv_ref,
+        )
+        zo_ref[pl.ds(pl.multiple_of(i * few, few), few), :] = o.astype(BF)
+        zlse_ref[i] = lse
+        o = jnp.concatenate([o, jnp.zeros_like(o)], 1)
+        for d in range(few // stripe):
+            message[i * (few // stripe) + d, half:] = o[d * stripe : (d + 1) * stripe].astype(BF)
+        return 0
+
+    lax.fori_loop(0, zlse_ref.shape[0], run_last, 0)
+
+
+def attend_all_back_body(
+    blocks, groups, rows, stripe,
+    place_ref, range_ref, last_range_ref, low_ref, high_ref, last_low_ref, last_high_ref, cos_ref, sin_ref,
+    do_ref, q_ref, k_ref, v_ref, zq_ref, zk_ref, zv_ref, o_ref, zo_ref, lse_ref, zlse_ref, *refs,
+):
+    outs = refs[:blocks]
+    kept, dq, dk, dv, zdq, zdk, zdv = refs[blocks:]
+    span = blocks * rows
+    size = groups * span
+    half = rows // 2
+    me_u, me_b = place_ref[0], place_ref[1]
+    for ref in (dk, dv, zdq, zdk, zdv):
+        ref[...] = jnp.zeros_like(ref)
+
+    def block(q, do, o, lse, low, high, first, stop, keys, values, dk_sum, dv_sum):
+        count = q.shape[0]
+        delta = jnp.sum((do.astype(F32) * o.astype(F32)).T, 0, keepdims=True)
+
+        def step(t, dq):
+            at = pl.multiple_of((first + 2 * t) * QB, QB)
+            here = pl.ds(at, KB)
+            k, v = keys[here, :], values[here, :]
+            s = lax.dot_general(k, q, NT, preferred_element_type=F32)
+            dp = lax.dot_general(v, do, NT, preferred_element_type=F32)
+            p = jnp.where(keys_mask(low, high, at, KB), jnp.exp(s - lse), 0.0)
+            ds = (p * (dp - delta)).astype(BF)
+            dv_sum[here, :] += jnp.dot(p.astype(BF), do, preferred_element_type=F32)
+            dk_sum[here, :] += jnp.dot(ds, q, preferred_element_type=F32)
+            return dq + lax.dot_general(k, ds, TN, preferred_element_type=F32)
+
+        return (
+            lax.fori_loop(0, (stop - first + 1) // 2, step, jnp.zeros((64, count), F32)) * 0.125
+        ).T
+
+    def run(i, _):
+        came = []
+        for d in range(QB // rows):
+            x = do_ref[i * (QB // rows) + d]
+            came += [x[:half, :64], x[:half, 64:]]
+        at = pl.ds(pl.multiple_of(i * QB, QB), QB)
+        dq[at, :] = block(
+            q_ref[at, :], jnp.concatenate(came, 0), o_ref[at, :], lse_ref[i], low_ref[i], high_ref[i],
+            range_ref[2 * i], range_ref[2 * i + 1], k_ref, v_ref, dk, dv,
+        )
+        return 0
+
+    lax.fori_loop(0, size // QB, run, 0)
+    few = zlse_ref.shape[2]
+
+    def run_last(i, _):
+        came = [
+            do_ref[i * (few // stripe) + d].astype(F32)[half:, :64] for d in range(few // stripe)
+        ]
+        at = pl.ds(pl.multiple_of(i * few, few), few)
+        x = block(
+            zq_ref[at, :], jnp.concatenate(came, 0).astype(BF), zo_ref[at, :], zlse_ref[i],
+            last_low_ref[i], last_high_ref[i], last_range_ref[2 * i], last_range_ref[2 * i + 1],
+            zk_ref, zv_ref, zdk, zdv,
+        )
+        for d in range(few // stripe):
+            to = (i * (few // stripe) + d) * rows + me_b * stripe
+            zdq[pl.ds(pl.multiple_of(to, stripe), stripe), :] = x[d * stripe : (d + 1) * stripe]
+        return 0
+
+    lax.fori_loop(0, zlse_ref.shape[0], run_last, 0)
+    for g in range(groups):
+        at = slice(g * span, (g + 1) * span)
+        tables = [(c, -s) for c, s in turn_tables(cos_ref[at], sin_ref[at], True)]
+        kept[:, :128] = turn(jnp.concatenate([dq[at], dk[at]], 1), tables[0]).astype(BF)
+        kept[:, 128:256] = turn(jnp.concatenate([zdq[at], zdk[at]], 1), tables[1]).astype(BF)
+        kept[:, 256:] = jnp.concatenate([dv[at], zdv[at]], 1).astype(BF)
+        for j in range(blocks):
+            outs[j][pl.ds(pl.multiple_of((me_u ^ g) * rows, rows), rows), :] = spread(kept, (me_b ^ j) * rows, rows)
 
 
 def on_device(
@@ -488,19 +687,57 @@
     n1, r1 = norm(values)
     n1_b = n1.astype(BF)
     n1_group = swap([n1_b] * groups, "ulysses")
-    gathered = lax.all_gather(
+    in_split = input_weight.reshape(gain_rows, 3, groups, heads, head_width)
+    in_split = jnp.concatenate(
+        [
+            in_split[:, :2].transpose(2, 0, 3, 1, 4).reshape(groups, 1, gain_rows, -1),
+            in_split[:, 2].transpose(1, 0, 2, 3).reshape(groups, 1, gain_rows, -1),
+        ],
+        3,
+    )
+    in_lanes = heads * 3 * head_width
+
+    condition = time_features(time_step, modulate_weight.shape[1] // 2)
+    mod_own = jnp.einsum(
+        "mc,fc->mf", condition, modulate_weight, preferred_element_type=F32
+    ) + modulate_bias.astype(F32)
+    small = jnp.concatenate(
+        [
+            mod_own.reshape(-1),
+            attend_gain.astype(F32),
+            feed_gain.astype(F32),
+            reduce_bias.astype(F32),
+            expand_bias.astype(F32),
+        ]
+    )
+    small_lanes = 64 * -(-small.shape[0] // (32 * gain_rows))
+    small = jnp.pad(small, (0, small_lanes * gain_rows // 2 - small.shape[0]))
+    small_high = small.astype(BF)
+    small_low = (small - lax.reduce_precision(small, 8, 7)).astype(BF)
+    small = jnp.concatenate([small_high, small_low]).reshape(1, 1, gain_rows, small_lanes)
+    came = exchange(
         jnp.concatenate(
+            [
+                jnp.broadcast_to(in_split, (groups, blocks) + in_split.shape[2:]),
+                jnp.broadcast_to(small, (groups, blocks) + small.shape[2:]),
+            ],
+            3,
+        ).reshape(devices, gain_rows, in_lanes + small_lanes)
+    )
+    small_all = came[:, :, in_lanes:].astype(F32).reshape(devices, 2, -1)
+    small_all = small_all[:, 0] + small_all[:, 1]
+    in_own = came.reshape(width, in_lanes + small_lanes)
+
+    weight_pack = jnp.concatenate(
             [
                 reduce_weight,
                 output_weight,
                 expand_weight.reshape(gain_rows, folds, width).transpose(1, 0, 2).reshape(-1, width),
             ],
             0,
-        ),
-        ALL,
-        axis=0,
-        tiled=False,
-    )
+        )
+    weight_pack, in_own = lax.optimization_barrier((weight_pack, in_own))
+    gathered = lax.all_gather(weight_pack, ALL, axis=0, tiled=False)
     unit = gain_rows
     while unit % 8:
         unit *= 2
@@ -516,36 +753,6 @@
         )
     wide = unit * folds
 
-    in_split = input_weight.reshape(gain_rows, 3, groups, heads, head_width)
-    in_split = jnp.concatenate(
-        [
-            in_split[:, :2].transpose(2, 0, 3, 1, 4).reshape(groups, 1, gain_rows, -1),
-            in_split[:, 2].transpose(1, 0, 2, 3).reshape(groups, 1, gain_rows, -1),
-        ],
-        3,
-    )
-    in_own = exchange(
-        jnp.broadcast_to(in_split, (groups, blocks) + in_split.shape[2:]).reshape(
-            (devices,) + in_split.shape[2:]
-        )
-    ).reshape(width, heads * 3 * head_width)
-
-    condition = time_features(time_step, modulate_weight.shape[1] // 2)
-    mod_own = jnp.einsum(
-        "mc,fc->mf", condition, modulate_weight, preferred_element_type=F32
-    ) + modulate_bias.astype(F32)
-    small = jnp.concatenate(
-        [
-            mod_own.reshape(-1),
-            attend_gain.astype(F32),
-            feed_gain.astype(F32),
-            reduce_bias.astype(F32),
-            expand_bias.astype(F32),
-        ]
-    )
-    small_size = -(-small.shape[0] // 1024) * 1024
-    small = jnp.pad(small, (0, small_size - small.shape[0])).reshape(1, -1, 128)
-    small_all = exchange(jnp.broadcast_to(small, (devices,) + small.shape[1:])).reshape(devices, -1)
     at = micro * mod_rows
     mods = small_all[:, :at].reshape(devices, micro, mod_rows).transpose(1, 0, 2).reshape(micro, -1)
     gain1 = small_all[:, at : at + gain_rows].reshape(-1)
@@ -576,9 +783,12 @@
     key_block = math.gcd(size, 256)
     first = jnp.arange(size // query_rows, dtype=jnp.int32) * query_rows
     ranges = key_ranges(first, first + query_rows - 1, pair_lengths, key_block)
-    segment_column = segment[:, None]
+    small_path = extra and size % KB == 0 and rows % 16 == 0 and stripe % 8 == 0 and size <= 4096
 
     count = groups * rows
+    striped = lambda x: lax.dynamic_slice_in_dim(
+        x.reshape((devices, rows) + x.shape[1:]), block_id * stripe, stripe, 1
+    ).reshape((devices * stripe,) + x.shape[1:])
     smem = pl.BlockSpec(memory_space=pltpu.SMEM)
     outgoing = pl.pallas_call(
         functools.partial(project_body, blocks, pairs, heads, extra),
@@ -598,49 +808,72 @@
     table_spec = pl.BlockSpec((span, 128), lambda i, p: (i ^ p[0], 0))
     by_rows = pl.BlockSpec((rows, lanes), lambda i, p: (i, 0))
     parts = 6 if extra else 3
-    turned = pl.pallas_call(
-        functools.partial(rotate_in_body, blocks, extra),
-        grid_spec=pltpu.PrefetchScalarGridSpec(
-            num_scalar_prefetch=1,
-            grid=(groups,),
-            in_specs=[table_spec, table_spec] + [by_rows] * blocks,
-            out_specs=[by_span] * parts,
-            scratch_shapes=[pltpu.VMEM((span, lanes), BF)],
-        ),
-        out_shape=[jax.ShapeDtypeStruct((size, 64), BF)] * parts,
-        name="rotate_in",
-    )(place, cos_table, sin_table, *incoming)
-    query, key, value = turned[:3]
-    attended, lse = attend(
-        ranges, query, segment, key, value, segment_column, query_rows, key_block
-    )
-    message = attended.reshape(devices, rows, head_width)
-    if extra:
-        striped = lambda x: lax.dynamic_slice_in_dim(
-            x.reshape((devices, rows) + x.shape[1:]), block_id * stripe, stripe, 1
-        ).reshape((devices * stripe,) + x.shape[1:])
-        last_key, last_value = turned[4:]
-        last_query = striped(turned[3])
-        last_query_segment = striped(last_segment)
-        last_rows = math.gcd(devices * stripe, 128)
+    if small_path:
+        last_rows = 128
         chunk = last_rows // stripe
         last_first = jnp.arange(devices // chunk, dtype=jnp.int32) * (chunk * rows) + block_id * stripe
         last_ranges = key_ranges(
-            last_first, last_first + (chunk - 1) * rows + stripe - 1, last_lengths, key_block
-        )
-        last_column = last_segment[:, None]
-        last_attended, last_lse = attend(
-            last_ranges, last_query, last_query_segment, last_key, last_value, last_column, last_rows, key_block
-        )
-        message = jnp.concatenate(
-            [message, last_attended.reshape(devices, stripe, head_width)], 1
-        )
+            last_first, last_first + (chunk - 1) * rows + stripe - 1, last_lengths, QB
+        )
+        bounds = []
+        for where, lens, pick, lump in (
+            (position, pair_lengths, lambda x: x, QB),
+            (last_position, last_lengths, striped, last_rows),
+        ):
+            low = index - where
+            ends = jnp.cumsum(lens)
+            high = jnp.min(jnp.where(ends[None, :] > index[:, None], ends[None, :], 1 << 30), 1)
+            bounds += [pick(low).reshape(-1, 1, lump), pick(high).reshape(-1, 1, lump)]
+        whole = lambda *shape: jax.ShapeDtypeStruct(shape, BF)
+        saved_shapes = [
+            whole(size, 64), whole(size + KB - QB, 64), whole(size + KB - QB, 64),
+            whole(devices * stripe, 64), whole(size + KB - QB, 64), whole(size + KB - QB, 64),
+            whole(size, 64), whole(devices * stripe, 64),
+            jax.ShapeDtypeStruct(bounds[0].shape, F32), jax.ShapeDtypeStruct(bounds[2].shape, F32),
+        ]
+        attend_args = (place, ranges, last_ranges, *bounds, cos_table, sin_table)
+        specs = [smem] * 3 + [whole_vmem()] * 6
+        message, *saved = pl.pallas_call(
+            functools.partial(attend_all_body, blocks, groups, rows, stripe),
+            in_specs=specs + [whole_vmem()] * blocks,
+            out_specs=[whole_vmem()] * 11,
+            out_shape=[whole(devices, rows // 2 + stripe, 128)] + saved_shapes,
+            scratch_shapes=[
+                pltpu.VMEM((span, lanes), BF),
+                pltpu.VMEM((size, 64), F32),
+                pltpu.VMEM((size // KB + 1, KB, QB), F32),
+            ],
+            cost_estimate=pl.CostEstimate(
+                flops=size * size * 64, transcendentals=size * size // 2, bytes_accessed=16 * size * 128
+            ),
+            name="attend_all",
+        )(*attend_args, *incoming)
+    else:
+        assert not extra
+        turned = pl.pallas_call(
+            functools.partial(rotate_in_body, blocks, extra),
+            grid_spec=pltpu.PrefetchScalarGridSpec(
+                num_scalar_prefetch=1,
+                grid=(groups,),
+                in_specs=[table_spec, table_spec] + [by_rows] * blocks,
+                out_specs=[by_span] * parts,
+                scratch_shapes=[pltpu.VMEM((span, lanes), BF)],
+            ),
+            out_shape=[jax.ShapeDtypeStruct((size, 64), BF)] * parts,
+            name="rotate_in",
+        )(place, cos_table, sin_table, *incoming)
+        query, key, value = turned[:3]
+        attended, lse = attend(
+            ranges, query, segment, key, value, segment[:, None], query_rows, key_block
+        )
+        message = attended.reshape(devices, rows, head_width)
     came = exchange(message)
 
     ex_spec = lambda f: pl.BlockSpec((units, unit, width), f)
     flat = pl.BlockSpec((own, width), lambda i: (0, 0))
     vec = lambda n: pl.BlockSpec((n, width), lambda i: (0, 0))
-    message_spec = pl.BlockSpec((devices, rows + stripe, head_width), lambda i: (0, 0, 0))
+    message_shape = message.shape
+    message_spec = pl.BlockSpec(message_shape, lambda i: (0, 0, 0))
     sizes = (groups, blocks, heads, micro, rows, stripe)
     own_f32 = jax.ShapeDtypeStruct((own, width), F32)
     own_bf = jax.ShapeDtypeStruct((own, width), BF)
@@ -672,7 +905,7 @@
         out_specs=[flat, flat, flat, message_spec, vec(5 * micro)],
         out_shape=[
             own_bf, own_f32, own_bf,
-            jax.ShapeDtypeStruct((devices, rows + stripe, head_width), BF),
+            jax.ShapeDtypeStruct(message_shape, BF),
             jax.ShapeDtypeStruct((5 * micro, width), F32),
         ],
         scratch_shapes=[
@@ -688,6 +921,9 @@
     d_gate2, d_shift2, p2, d_gate1, dm_sums = [
         sums[i * micro : (i + 1) * micro] for i in range(5)
     ]
+
+    output_part = lax.dot_general(merged, grad_attn, TN, preferred_element_type=F32).astype(BF)
+    output_part = output_part.reshape(groups, width // groups, width)
 
     flat_p = pl.BlockSpec((own, width), lambda i, p: (0, 0))
     square = pl.BlockSpec((width, width), lambda i, p: (0, 0))
@@ -724,7 +960,61 @@
         ],
         1,
     )
+    do_came, feed_part, output_part = lax.optimization_barrier((do_came, feed_part, output_part))
+    output_part = swap(
+        [
+            lax.dynamic_index_in_dim(output_part, group_id ^ k, 0, keepdims=False)
+            for k in range(groups)
+        ],
+        "ulysses",
+    )
+
     feed_sum = lax.psum_scatter(feed_part, "blk", scatter_dimension=0, tiled=True)[0]
+    output_part = sum(x.astype(F32) for x in output_part).astype(BF).reshape(blocks, gain_rows, width)
+    output_part = swap(
+        [
+            lax.dynamic_index_in_dim(output_part, block_id ^ k, 0, keepdims=False)
+            for k in range(blocks)
+        ],
+        "blk",
+    )
+    if small_path:
+        leaving = pl.pallas_call(
+            functools.partial(attend_all_back_body, blocks, groups, rows, stripe),
+            in_specs=specs + [whole_vmem()] * 11,
+            out_specs=[whole_vmem()] * blocks,
+            out_shape=[whole(count, lanes)] * blocks,
+            scratch_shapes=[pltpu.VMEM((span, lanes), BF), pltpu.VMEM((size, 64), F32)]
+            + [pltpu.VMEM((size + KB - QB, 64), F32)] * 2
+            + [pltpu.VMEM((size, 64), F32)]
+            + [pltpu.VMEM((size + KB - QB, 64), F32)] * 2,
+            cost_estimate=pl.CostEstimate(
+                flops=2 * size * size * 64, transcendentals=size * size // 2, bytes_accessed=16 * size * 128
+            ),
+            name="attend_all_back",
+        )(*attend_args, do_came, *saved)
+    else:
+        grads = attend_back(
+            ranges, query, segment, lse, attended, do_came.reshape(size, head_width), key, value,
+            segment[:, None], query_rows, key_block,
+        )
+        leaving = pl.pallas_call(
+            functools.partial(rotate_out_body, blocks, extra),
+            grid_spec=pltpu.PrefetchScalarGridSpec(
+                num_scalar_prefetch=1,
+                grid=(groups,),
+                in_specs=[table_spec, table_spec] + [by_span] * parts,
+                out_specs=[by_rows] * blocks,
+                scratch_shapes=[pltpu.VMEM((span, lanes), BF)],
+            ),
+            out_shape=[jax.ShapeDtypeStruct((count, lanes), BF)] * blocks,
+            name="rotate_out",
+        )(place, cos_table, sin_table, *grads)
+    leaving, output_part = lax.optimization_barrier((leaving, output_part))
+    output_grad = sum(x.astype(F32) for x in output_part)
+    back = swap(leaving, "blk")
+    back, feed_sum = lax.optimization_barrier((back, feed_sum))
+
     reduce_grad = feed_sum[:ff_rows].astype(F32)
     expand_rows = feed_sum[ff_rows:].reshape(groups, gain_rows, width)
     expand_came = jnp.stack(
@@ -743,63 +1033,6 @@
         ],
         1,
     ).astype(F32)
-
-    output_part = lax.dot_general(merged, grad_attn, TN, preferred_element_type=F32).astype(BF)
-    output_part = output_part.reshape(groups, width // groups, width)
-    output_part = sum(
-        x.astype(F32)
-        for x in swap(
-            [
-                lax.dynamic_index_in_dim(output_part, group_id ^ k, 0, keepdims=False)
-                for k in range(groups)
-            ],
-            "ulysses",
-        )
-    )
-    output_part = output_part.astype(BF).reshape(blocks, gain_rows, width)
-    output_grad = sum(
-        x.astype(F32)
-        for x in swap(
-            [
-                lax.dynamic_index_in_dim(output_part, block_id ^ k, 0, keepdims=False)
-                for k in range(blocks)
-            ],
-            "blk",
-        )
-    )
-
-    do_pair = do_came[:, :rows].reshape(size, head_width)
-    grads = list(
-        attend_back(
-            ranges, query, segment, lse, attended, do_pair, key, value, segment_column, query_rows, key_block
-        )
-    )
-    if extra:
-        dq_last, dk_last, dv_last = attend_back(
-            last_ranges, last_query, last_query_segment, last_lse, last_attended,
-            do_came[:, rows:].reshape(devices * stripe, head_width),
-            last_key, last_value, last_column, last_rows, key_block,
-        )
-        dq_last = lax.dynamic_update_slice_in_dim(
-            jnp.zeros((devices, rows, head_width), BF),
-            dq_last.reshape(devices, stripe, head_width),
-            block_id * stripe,
-            1,
-        ).reshape(size, head_width)
-        grads += [dq_last, dk_last, dv_last]
-    leaving = pl.pallas_call(
-        functools.partial(rotate_out_body, blocks, extra),
-        grid_spec=pltpu.PrefetchScalarGridSpec(
-            num_scalar_prefetch=1,
-            grid=(groups,),
-            in_specs=[table_spec, table_spec] + [by_span] * parts,
-            out_specs=[by_rows] * blocks,
-            scratch_shapes=[pltpu.VMEM((span, lanes), BF)],
-        ),
-        out_shape=[jax.ShapeDtypeStruct((count, lanes), BF)] * blocks,
-        name="rotate_out",
-    )(place, cos_table, sin_table, *grads)
-    back = swap(leaving, "blk")
 
     returned = pl.pallas_call(
         functools.partial(project_back_body, blocks, pairs, heads, extra),
@@ -846,7 +1079,6 @@
         ],
         1,
     ).astype(BF)
-    in_lanes = heads * 3 * head_width
     taken = small_parts.shape[1]
     small_rows = 8 * -(-taken // (8 * in_lanes))
     small_parts = jnp.pad(small_parts, ((0, 0), (0, small_rows * in_lanes - taken)))

time: 436 us -> 355 us (0.81); the launches traced: 428 us -> 352 us
  waiting for transfers between devices: 182 us -> 145 us
  Pallas kernels: 88.5 us -> 70.2 us
  local copies, waits for them, and re-layouts: 32.1 us -> 19.9 us
  starting transfers between devices: 82.5 us -> 76.4 us
    all_to_all x5 -> x4, waiting for transfers between devices: 66.9 us -> 35 us  [exchange(): return lax.all_to_all(x, ALL, split_axis=0, concat_axis=0, tiled=True)]
    pallas_call x6 -> x2, Pallas kernels: 55 us -> 37.3 us  [the longest x1 18.9 us: on_device(): pl.pallas_call(functools.partial(attend_all_back_body, blocks, groups, ro...]
    all_to_all x5 -> x4, starting transfers between devices: 38.9 us -> 32.2 us  [exchange(): return lax.all_to_all(x, ALL, split_axis=0, concat_axis=0, tiled=True)]
    ppermute x39, waiting for transfers between devices: 115 us -> 110 us  [swap(): lax.ppermute(x, axis, [(i, i ^ k) for i in range(size)])]
  transfers between devices with their start and end apart: 46 -> 45, of which waited for: 20 -> 19; matrix products, arithmetic and copies ran while one was open for 11% -> 7% of each run, Pallas kernels for 17% -> 18%
where the time goes in v3:
time: 355 us; the launch traced here: 352 us
  waiting for transfers between devices  145 us (41%)
  starting transfers between devices  76.4 us (22%)
  Pallas kernels  70.2 us (20%)
  other arithmetic  23.9 us (7%)
  local copies, waits for them, and re-layouts  19.9 us (6%)
  between operations  15 us (4%)
    ppermute x39, waiting for transfers between devices, swap(): lax.ppermute(x, axis, [(i, i ^ k) for i in range(size)])  110 us
    ppermute x39, starting transfers between devices, swap(): lax.ppermute(x, axis, [(i, i ^ k) for i in range(size)])  44.1 us
    all_to_all x4, waiting for transfers between devices, exchange(): return lax.all_to_all(x, ALL, split_axis=0, concat_axis=0, tiled=True)  35 us
    all_to_all x4, starting transfers between devices, exchange(): return lax.all_to_all(x, ALL, split_axis=0, concat_axis=0, tiled=True)  32.2 us
    pallas_call x1, Pallas kernels, on_device(): pl.pallas_call(functools.partial(attend_all_back_body, blocks, groups, ro...  18.9 us
    pallas_call x1, Pallas kernels, on_device(): pl.pallas_call(functools.partial(attend_all_body, blocks, groups, rows, s...  18.4 us
    pallas_call x1, Pallas kernels, on_device(): pl.pallas_call(functools.partial(feed_body, *sizes), grid=(folds,), in_sp...  11.5 us
    pallas_call x1, Pallas kernels, on_device(): pl.pallas_call(functools.partial(feed_weights_body, rows), grid_spec=pltp...  8.54 us
  transfers between devices with their start and end apart: 45, of which 19 were waited for; matrix products, arithmetic and copies ran while one was open for 7% of the time, Pallas kernels for 18%

profile of v3, /device:TPU:0, one launch (start us, length us, event | category | flops | bytes accessed | tf_op | source)
XLA Modules:
  0.0 352.4 jit_solution(1519829010800340398)
XLA Ops:
  8.9 2.8 concatenate.53
  14.9 7.3 %all-to-all-start = ((bf16[32,24,640]{2,1,0:T(8,128)(2,1)}), bf16[32,24,640]{2,1,0:T(8,128)(2,1)S(1)}, u32[]{:S(2)}, u32[]{:S(2)}) async-start(bf16[32,24,640]{2,1,0:T(8,128)(2,1)} %bitcast.6), calls=%async_computation | async-start | bytes 1966080 | tf_op jit(solution)/shard_map/all_to_all | solution.py:19
  23.1 25.3 %all-to-all-done = bf16[32,24,640]{2,1,0:T(8,128)(2,1)S(1)} async-done(((bf16[32,24,640]{2,1,0:T(8,128)(2,1)}), bf16[32,24,640]{2,1,0:T(8,128)(2,1)S(1)}, u32[]{:S(2)}, u32[]{:S(2)}) %all-to-all-start) | async-done | bytes 983072 | tf_op jit(solution)/shard_map/all_to_all | solution.py:19
  53.7 5.6 %sine_multiply_fusion = (f32[2048,128]{1,0:T(8,128)}, f32[2048,128]{1,0:T(8,128)}) fusion(f32[128]{0:T(128)S(1)} %compare_select_fusion, f32[128]{0:T(128)S(1)} %mul.174, f32[2048]{0:T(1024)S(1)} %subtract_convert_fusion, f32[2048]{0:T(1024)S(1)} %subtract_convert_fusion.1, pred[128]{0:T(512)(128)(4,1)S(1)} %iota_compare_fusion.5), kind=kLoop, calls=%fused_computation.5 | loop fusion | flops 786432 | bytes 2114688 | tf_op jit(solution)/shard_map/mul | solution.py:781
  61.0 5.8 %collective-permute-done.2.refs_3_ = bf16[3,64,768]{2,1,0:T(8,128)(2,1)S(1)} collective-permute-done((bf16[3,64,768]{2,1,0:T(8,128)(2,1)S(1)}, bf16[3,64,768]{2,1,0:T(8,128)(2,1)S(1)}, u32[]{:S(2)}, u32[]{:S(2)}) %collective-permute-start.2) | collective-permute-done | bytes 294944 | tf_op jit(solution)/shard_map/ppermute | solution.py:50
  67.5 4.4 %project.1 = (bf16[256,384]{1,0:T(8,128)(2,1)}, bf16[256,384]{1,0:T(8,128)(2,1)}, bf16[256,384]{1,0:T(8,128)(2,1)}, bf16[256,384]{1,0:T(8,128)(2,1)}, bf16[256,3...) custom-call(s32[2]{0:T(128)} %pad_add_fusion.2.place_ref, ...), custom_call_target="tpu_custom_call" | custom-call | flops 679477248 | bytes 1179648 | tf_op jit(solution)/shard_map/project/pallas_call | solution.py:793
  73.9 2.9 collective-permute-start.5
  76.8 2.9 collective-permute-start.7
  79.7 2.1 collective-permute-done.3.refs_1_
  81.8 9.1 %collective-permute-done.4.refs_2_ = bf16[256,384]{1,0:T(8,128)(2,1)S(1)} collective-permute-done((bf16[256,384]{1,0:T(8,128)(2,1)}, bf16[256,384]{1,0:T(8,128)(2,1)S(1)}, u32[]{:S(2)}, u32[]{:S(2)}) %collective-permute-start.4) | collective-permute-done | bytes 196640 | tf_op jit(solution)/shard_map/ppermute | solution.py:50
  92.9 8.9 %collective-permute-done.5.refs_3_ = bf16[256,384]{1,0:T(8,128)(2,1)S(1)} collective-permute-done((bf16[256,384]{1,0:T(8,128)(2,1)}, bf16[256,384]{1,0:T(8,128)(2,1)S(1)}, u32[]{:S(2)}, u32[]{:S(2)}) %collective-permute-start.5) | collective-permute-done | bytes 196640 | tf_op jit(solution)/shard_map/ppermute | solution.py:50
  101.8 17.5 %collective-permute-done.7.refs_5_ = bf16[256,384]{1,0:T(8,128)(2,1)S(1)} collective-permute-done((bf16[256,384]{1,0:T(8,128)(2,1)}, bf16[256,384]{1,0:T(8,128)(2,1)S(1)}, u32[]{:S(2)}, u32[]{:S(2)}) %collective-permute-start.7) | collective-permute-done | bytes 196640 | tf_op jit(solution)/shard_map/ppermute | solution.py:50
  120.1 18.4 %attend_all.1 = (bf16[32,40,128]{2,1,0:T(8,128)(2,1)}, bf16[2048,64]{1,0:T(8,128)(2,1)}, bf16[2304,64]{1,0:T(8,128)(2,1)}, bf16[2304,64]{1,0:T(8,128)(2,1)}, bf1...) custom-call(s32[2]{0:T(128)} %pad_add_fusion.2.place_ref, ...), custom_call_target="tpu_custom_call" | custom-call | flops 268435456 | bytes 4194304 | tf_op jit(solution)/shard_map/attend_all/pallas_call | solution.py:836
  138.5 15.1 %all-to-all-start.1 = ((bf16[32,40,128]{2,1,0:T(8,128)(2,1)}), bf16[32,40,128]{2,1,0:T(8,128)(2,1)S(1)}, u32[]{:S(2)}, u32[]{:S(2)}) async-start(bf16[32,40,128]{2,1,0:T(8,128)(2,1)} %get-tuple-element.98), calls=%async_computation.1 | async-start | bytes 655360 | tf_op jit(solution)/shard_map/all_to_all | solution.py:19
  153.7 1.7 collective-permute-start.14
  157.0 8.6 %all-to-all-done.1.came_ref = bf16[32,40,128]{2,1,0:T(8,128)(2,1)S(1)} async-done(((bf16[32,40,128]{2,1,0:T(8,128)(2,1)}), bf16[32,40,128]{2,1,0:T(8,128)(2,1)S(1)}, u32[]{:S(2)}, u32[]{:S(2)}) %all-to-all-start.1) | async-done | bytes 327712 | tf_op jit(solution)/shard_map/all_to_all | solution.py:19
  166.3 3.1 middle.1
  171.3 11.5 %feed.1 = (bf16[192,768]{1,0:T(8,128)(2,1)}, f32[192,768]{1,0:T(8,128)}, bf16[192,768]{1,0:T(8,128)(2,1)}, bf16[32,40,128]{2,1,0:T(8,128)(2,1)}, f32[15,768]{1,0:T(8,128)}) custom-call(bf16[32,216,768]{2,1,0:T(8,128)(2,1)} %bitcast.148, bf16[32,216,768]{2,1,0:T(8,128)(2,1)} %bitcast.149, bf16[32,216,768]{2,1,0:T(8,128)(2,1)} %bitcast.150, ...), custom_call_target="tpu_custom_call" | custom-call | flops 3623878656 | bytes 9437184 | tf_op jit(solution)/shard_map/feed/pallas_call | solution.py:893
  182.8 2.6 all-to-all-start.2
  185.4 1.5 convolution_convert_fusion
  187.9 8.5 %feed_weights.1 = (bf16[768,768]{1,0:T(8,128)(2,1)}, bf16[768,768]{1,0:T(8,128)(2,1)}, f32[1,768]{1,0:T(1,128)}) custom-call(s32[2]{0:T(128)} %pad_add_fusion.2.place_ref, bf16[32,216,768]{2,1,0:T(8,128)(2,1)} %bitcast.151, bf16[32,216,768]{2,1,0:T(8,128)(2,1)} %bitcast.152, f32[4,1,768]{2,1,0:T(1,128)} %reshape.581.ex_bias_ref.bias_ref, ...), custom_call_target="tpu_custom_call" | custom-call | flops 4529848320 | bytes 9437184 | tf_op jit(solution)/shard_map/feed_weights/pallas_call | solution.py:930
  196.4 1.5 copy.76
  198.1 1.6 pad_maximum_fusion
  200.3 1.4 collective-permute-start.18
  202.2 7.1 %collective-permute-done.18 = bf16[192,768]{1,0:T(8,128)(2,1)S(1)} collective-permute-done((bf16[192,768]{1,0:T(8,128)(2,1)S(1)}, bf16[192,768]{1,0:T(8,128)(2,1)S(1)}, u32[]{:S(2)}, u32[]{:S(2)}) %collective-permute-start.18) | collective-permute-done | bytes 294944 | tf_op jit(solution)/shard_map/ppermute | solution.py:50
  209.4 6.6 %collective-permute-done.17 = bf16[192,768]{1,0:T(8,128)(2,1)S(1)} collective-permute-done((bf16[192,768]{1,0:T(8,128)(2,1)S(1)}, bf16[192,768]{1,0:T(8,128)(2,1)S(1)}, u32[]{:S(2)}, u32[]{:S(2)}) %collective-permute-start.17) | collective-permute-done | bytes 294944 | tf_op jit(solution)/shard_map/ppermute | solution.py:50
  216.2 1.7 collective-permute-start.19
  217.9 1.5 collective-permute-start.20
  219.7 2.7 collective-permute-start.22
  222.4 1.3 collective-permute-start.23
  223.7 3.5 collective-permute-start.24
  227.4 18.9 %attend_all_back.1 = (bf16[256,384]{1,0:T(8,128)(2,1)}, bf16[256,384]{1,0:T(8,128)(2,1)}, bf16[256,384]{1,0:T(8,128)(2,1)}, bf16[256,384]{1,0:T(8,128)(2,1)}, bf...) custom-call(s32[2]{0:T(128)} %pad_add_fusion.2.place_ref, ...), custom_call_target="tpu_custom_call" | custom-call | flops 536870912 | bytes 4194304 | tf_op jit(solution)/shard_map/attend_all_back/pallas_call | solution.py:982
  246.4 1.7 collective-permute-start.26
  248.3 1.9 collective-permute-start.28
  251.2 3.0 collective-permute-start.30
  255.4 4.0 %collective-permute-start.31 = (bf16[256,384]{1,0:T(8,128)(2,1)}, bf16[256,384]{1,0:T(8,128)(2,1)S(1)}, u32[]{:S(2)}, u32[]{:S(2)}) collective-permute-start(bf16[256,384]{1,0:T(8,128)(2,1)} %get-tuple-element.135), channel_id=1, source_target_pairs={{0,6},{1,7},{2,4},{3,5},{4,2},{5,3},{6,0},{7,1},{8,14},{9,15},{10,... | collective-permute-start | bytes 589832 | tf_op jit(solution)/shard_map/ppermute | solution.py:50
  260.4 1.3 collective-permute-start.32
  262.3 16.6 %collective-permute-done.29.refs_8_ = bf16[256,384]{1,0:T(8,128)(2,1)S(1)} collective-permute-done((bf16[256,384]{1,0:T(8,128)(2,1)}, bf16[256,384]{1,0:T(8,128)(2,1)S(1)}, u32[]{:S(2)}, u32[]{:S(2)}) %collective-permute-start.29) | collective-permute-done | bytes 196640 | tf_op jit(solution)/shard_map/ppermute | solution.py:50
  278.9 11.0 %collective-permute-done.30.refs_9_ = bf16[256,384]{1,0:T(8,128)(2,1)S(1)} collective-permute-done((bf16[256,384]{1,0:T(8,128)(2,1)}, bf16[256,384]{1,0:T(8,128)(2,1)S(1)}, u32[]{:S(2)}, u32[]{:S(2)}) %collective-permute-start.30) | collective-permute-done | bytes 196640 | tf_op jit(solution)/shard_map/ppermute | solution.py:50
  290.7 5.3 %project_back.1 = (bf16[3,64,768]{2,1,0:T(8,128)(2,1)}, bf16[3,64,768]{2,1,0:T(8,128)(2,1)}, bf16[3,64,768]{2,1,0:T(8,128)(2,1)}, bf16[3,64,768]{2,1,0:T(8,128)(...) custom-call(s32[2]{0:T(128)} %pad_add_fusion.2.place_ref, f32[3,768]{1,0:T(4,128)} %get-tuple-element.209.c_ref, ...), custom_call_target="tpu_custom_call" | custom-call | flops 1358954496 | bytes 1179648 | tf_op jit(solution)/shard_map/project_back/pallas_call | solution.py:1037
  300.7 7.2 %all-to-all-start.3 = ((bf16[32,32,576]{2,1,0:T(8,128)(2,1)}), bf16[32,32,576]{2,1,0:T(8,128)(2,1)S(1)}, u32[]{:S(2)}, u32[]{:S(2)}) async-start(bf16[32,32,576]{2,1,0:T(8,128)(2,1)} %pad_maximum_fusion.1), calls=%async_computation.4 | async-start | bytes 2621440 | tf_op jit(solution)/shard_map/all_to_all | solution.py:19
  308.7 1.6 collective-permute-start.38
  311.3 1.8 collective-permute-start.35
  313.4 4.0 %collective-permute-done.38 = bf16[24,768]{1,0:T(8,128)(2,1)S(1)} collective-permute-done((bf16[24,768]{1,0:T(8,128)(2,1)S(1)}, bf16[24,768]{1,0:T(8,128)(2,1)S(1)}, u32[]{:S(2)}, u32[]{:S(2)}) %collective-permute-start.38) | collective-permute-done | bytes 36896 | tf_op jit(solution)/shard_map/ppermute | solution.py:50
  317.4 1.5 collective-permute-start.33
  318.9 3.2 collective-permute-done.37
  322.9 8.9 %collective-permute-done.35 = bf16[3,64,768]{2,1,0:T(8,128)(2,1)S(1)} collective-permute-done((bf16[3,64,768]{2,1,0:T(8,128)(2,1)S(1)}, bf16[3,64,768]{2,1,0:T(8,128)(2,1)S(1)}, u32[]{:S(2)}, u32[]{:S(2)}) %collective-permute-start.35) | collective-permute-done | bytes 294944 | tf_op jit(solution)/shard_map/ppermute | solution.py:50
  331.8 6.9 %collective-permute-done.34 = bf16[3,64,768]{2,1,0:T(8,128)(2,1)S(1)} collective-permute-done((bf16[3,64,768]{2,1,0:T(8,128)(2,1)S(1)}, bf16[3,64,768]{2,1,0:T(8,128)(2,1)S(1)}, u32[]{:S(2)}, u32[]{:S(2)}) %collective-permute-start.34) | collective-permute-done | bytes 294944 | tf_op jit(solution)/shard_map/ppermute | solution.py:50
  (284 shorter events, 44.2 us)
Async XLA Ops:
  14.9 33.5 %all-to-all-start = ((bf16[32,24,640]{2,1,0:T(8,128)(2,1)}), bf16[32,24,640]{2,1,0:T(8,128)(2,1)S(1)}, u32[]{:S(2)}, u32[]{:S(2)}) async-start(bf16[32,24,640]{2,1,0:T(8,128)(2,1)} %bitcast.6), calls=%async_computation | async-start | bytes 1966080 | tf_op jit(solution)/shard_map/all_to_all | solution.py:19
  22.2 143.3 %all-gather.3.cloned.1.call-start = ((), (), s32[]{:S(2)}) async-start(), calls=%async_computation.6 | async-start | bytes 10948608 | tf_op jit(solution)/shard_map/all_gather | solution.py:740
  49.0 12.0 %collective-permute-start = (bf16[3,64,768]{2,1,0:T(8,128)(2,1)S(1)}, bf16[3,64,768]{2,1,0:T(8,128)(2,1)S(1)}, u32[]{:S(2)}, u32[]{:S(2)}) collective-permute-start(bf16[3,64,768]{2,1,0:T(8,128)(2,1)S(1)} %fusion.5.refs_0_), channel_id=1, source_target_pairs={{0,8},{8,0},{16,24},{24,16},{1,9},{9,1},{17,25},{25,17},{2,10},{10... | collective-permute-start | bytes 884744 | tf_op jit(solution)/shard_map/ppermute | solution.py:50
  49.1 11.9 %collective-permute-start.1 = (bf16[3,64,768]{2,1,0:T(8,128)(2,1)S(1)}, bf16[3,64,768]{2,1,0:T(8,128)(2,1)S(1)}, u32[]{:S(2)}, u32[]{:S(2)}) collective-permute-start(bf16[3,64,768]{2,1,0:T(8,128)(2,1)S(1)} %fusion.5.refs_0_), channel_id=1, source_target_pairs={{0,16},{8,24},{16,0},{24,8},{1,17},{9,25},{17,1},{25,9},{2,18},{10... | collective-permute-start | bytes 884744 | tf_op jit(solution)/shard_map/ppermute | solution.py:50
  49.9 16.8 %collective-permute-start.2 = (bf16[3,64,768]{2,1,0:T(8,128)(2,1)S(1)}, bf16[3,64,768]{2,1,0:T(8,128)(2,1)S(1)}, u32[]{:S(2)}, u32[]{:S(2)}) collective-permute-start(bf16[3,64,768]{2,1,0:T(8,128)(2,1)S(1)} %fusion.5.refs_0_), channel_id=1, source_target_pairs={{0,24},{8,16},{16,8},{24,0},{1,25},{9,17},{17,9},{25,1},{2,26},{10... | collective-permute-start | bytes 884744 | tf_op jit(solution)/shard_map/ppermute | solution.py:50
  71.9 9.9 %collective-permute-start.3 = (bf16[256,384]{1,0:T(8,128)(2,1)}, bf16[256,384]{1,0:T(8,128)(2,1)S(1)}, u32[]{:S(2)}, u32[]{:S(2)}) collective-permute-start(bf16[256,384]{1,0:T(8,128)(2,1)} %get-tuple-element.91), channel_id=1, source_target_pairs={{0,1},{1,0},{2,3},{3,2},{4,5},{5,4},{6,7},{7,6},{8,9},{9,8},{10,11... | collective-permute-start | bytes 589832 | tf_op jit(solution)/shard_map/ppermute | solution.py:50
  72.4 18.5 %collective-permute-start.4 = (bf16[256,384]{1,0:T(8,128)(2,1)}, bf16[256,384]{1,0:T(8,128)(2,1)S(1)}, u32[]{:S(2)}, u32[]{:S(2)}) collective-permute-start(bf16[256,384]{1,0:T(8,128)(2,1)} %get-tuple-element.92), channel_id=1, source_target_pairs={{0,2},{1,3},{2,0},{3,1},{4,6},{5,7},{6,4},{7,5},{8,10},{9,11},{10,... | collective-permute-start | bytes 589832 | tf_op jit(solution)/shard_map/ppermute | solution.py:50
  73.9 27.9 %collective-permute-start.5 = (bf16[256,384]{1,0:T(8,128)(2,1)}, bf16[256,384]{1,0:T(8,128)(2,1)S(1)}, u32[]{:S(2)}, u32[]{:S(2)}) collective-permute-start(bf16[256,384]{1,0:T(8,128)(2,1)} %get-tuple-element.93), channel_id=1, source_target_pairs={{0,3},{1,2},{2,1},{3,0},{4,7},{5,6},{6,5},{7,4},{8,11},{9,10},{10,... | collective-permute-start | bytes 589832 | tf_op jit(solution)/shard_map/ppermute | solution.py:50
  76.8 25.0 %collective-permute-start.6 = (bf16[256,384]{1,0:T(8,128)(2,1)}, bf16[256,384]{1,0:T(8,128)(2,1)S(1)}, u32[]{:S(2)}, u32[]{:S(2)}) collective-permute-start(bf16[256,384]{1,0:T(8,128)(2,1)} %get-tuple-element.94), channel_id=1, source_target_pairs={{0,4},{1,5},{2,6},{3,7},{4,0},{5,1},{6,2},{7,3},{8,12},{9,13},{10,... | collective-permute-start | bytes 589832 | tf_op jit(solution)/shard_map/ppermute | solution.py:50
  76.8 42.5 %collective-permute-start.7 = (bf16[256,384]{1,0:T(8,128)(2,1)}, bf16[256,384]{1,0:T(8,128)(2,1)S(1)}, u32[]{:S(2)}, u32[]{:S(2)}) collective-permute-start(bf16[256,384]{1,0:T(8,128)(2,1)} %get-tuple-element.95), channel_id=1, source_target_pairs={{0,5},{1,4},{2,7},{3,6},{4,1},{5,0},{6,3},{7,2},{8,13},{9,12},{10,... | collective-permute-start | bytes 589832 | tf_op jit(solution)/shard_map/ppermute | solution.py:50
  81.8 37.5 %collective-permute-start.8 = (bf16[256,384]{1,0:T(8,128)(2,1)}, bf16[256,384]{1,0:T(8,128)(2,1)S(1)}, u32[]{:S(2)}, u32[]{:S(2)}) collective-permute-start(bf16[256,384]{1,0:T(8,128)(2,1)} %get-tuple-element.96), channel_id=1, source_target_pairs={{0,6},{1,7},{2,4},{3,5},{4,2},{5,3},{6,0},{7,1},{8,14},{9,15},{10,... | collective-permute-start | bytes 589832 | tf_op jit(solution)/shard_map/ppermute | solution.py:50
  90.9 28.4 %collective-permute-start.9 = (bf16[256,384]{1,0:T(8,128)(2,1)}, bf16[256,384]{1,0:T(8,128)(2,1)S(1)}, u32[]{:S(2)}, u32[]{:S(2)}) collective-permute-start(bf16[256,384]{1,0:T(8,128)(2,1)} %get-tuple-element.97), channel_id=1, source_target_pairs={{0,7},{1,6},{2,5},{3,4},{4,3},{5,2},{6,1},{7,0},{8,15},{9,14},{10,... | collective-permute-start | bytes 589832 | tf_op jit(solution)/shard_map/ppermute | solution.py:50
  138.5 27.1 %all-to-all-start.1 = ((bf16[32,40,128]{2,1,0:T(8,128)(2,1)}), bf16[32,40,128]{2,1,0:T(8,128)(2,1)S(1)}, u32[]{:S(2)}, u32[]{:S(2)}) async-start(bf16[32,40,128]{2,1,0:T(8,128)(2,1)} %get-tuple-element.98), calls=%async_computation.1 | async-start | bytes 655360 | tf_op jit(solution)/shard_map/all_to_all | solution.py:19
  153.6 16.6 %collective-permute-start.13 = (bf16[192,768]{1,0:T(8,128)(2,1)S(1)}, bf16[192,768]{1,0:T(8,128)(2,1)S(1)}, u32[]{:S(2)}, u32[]{:S(2)}) collective-permute-start(bf16[192,768]{1,0:T(8,128)(2,1)S(1)} %bitcast.165), channel_id=1, source_target_pairs={{0,8},{8,0},{16,24},{24,16},{1,9},{9,1},{17,25},{25,17},{2,10},{10... | collective-permute-start | bytes 884744 | tf_op jit(solution)/shard_map/ppermute | solution.py:50
  153.7 33.2 %collective-permute-start.14 = (bf16[192,768]{1,0:T(8,128)(2,1)S(1)}, bf16[192,768]{1,0:T(8,128)(2,1)S(1)}, u32[]{:S(2)}, u32[]{:S(2)}) collective-permute-start(bf16[192,768]{1,0:T(8,128)(2,1)S(1)} %bitcast.166), channel_id=1, source_target_pairs={{0,16},{8,24},{16,0},{24,8},{1,17},{9,25},{17,1},{25,9},{2,18},{10... | collective-permute-start | bytes 884744 | tf_op jit(solution)/shard_map/ppermute | solution.py:50
  155.4 31.5 %collective-permute-start.15 = (bf16[192,768]{1,0:T(8,128)(2,1)S(1)}, bf16[192,768]{1,0:T(8,128)(2,1)S(1)}, u32[]{:S(2)}, u32[]{:S(2)}) collective-permute-start(bf16[192,768]{1,0:T(8,128)(2,1)S(1)} %bitcast.167), channel_id=1, source_target_pairs={{0,24},{8,16},{16,8},{24,0},{1,25},{9,17},{17,9},{25,1},{2,26},{10... | collective-permute-start | bytes 884744 | tf_op jit(solution)/shard_map/ppermute | solution.py:50
  169.4 17.6 %collective-permute-start.10 = (bf16[192,768]{1,0:T(8,128)(2,1)}, bf16[192,768]{1,0:T(8,128)(2,1)S(1)}, u32[]{:S(2)}, u32[]{:S(2)}) collective-permute-start(bf16[192,768]{1,0:T(8,128)(2,1)} %get-tuple-element.99.second_ref.refs_0_), channel_id=1, source_target_pairs={{0,8},{8,0},{16,24},{24,16},{1,9},{9,1},{17,25},{25,17},{2,10},{10... | collective-permute-start | bytes 884744 | tf_op jit(solution)/shard_map/ppermute | solution.py:50
  169.4 17.6 %collective-permute-start.11 = (bf16[192,768]{1,0:T(8,128)(2,1)}, bf16[192,768]{1,0:T(8,128)(2,1)}, u32[]{:S(2)}, u32[]{:S(2)}) collective-permute-start(bf16[192,768]{1,0:T(8,128)(2,1)} %get-tuple-element.99.second_ref.refs_0_), channel_id=1, source_target_pairs={{0,16},{8,24},{16,0},{24,8},{1,17},{9,25},{17,1},{25,9},{2,18},{10... | collective-permute-start | bytes 884744 | tf_op jit(solution)/shard_map/ppermute | solution.py:50
  170.3 16.7 %collective-permute-start.12 = (bf16[192,768]{1,0:T(8,128)(2,1)}, bf16[192,768]{1,0:T(8,128)(2,1)}, u32[]{:S(2)}, u32[]{:S(2)}) collective-permute-start(bf16[192,768]{1,0:T(8,128)(2,1)} %get-tuple-element.99.second_ref.refs_0_), channel_id=1, source_target_pairs={{0,24},{8,16},{16,8},{24,0},{1,25},{9,17},{17,9},{25,1},{2,26},{10... | collective-permute-start | bytes 884744 | tf_op jit(solution)/shard_map/ppermute | solution.py:50
  182.8 16.9 %all-to-all-start.2 = ((bf16[32,40,128]{2,1,0:T(8,128)(2,1)}), bf16[32,40,128]{2,1,0:T(8,128)(2,1)S(1)}, u32[]{:S(2)}, u32[]{:S(2)}) async-start(bf16[32,40,128]{2,1,0:T(8,128)(2,1)} %get-tuple-element.104), calls=%async_computation.2 | async-start | bytes 655360 | tf_op jit(solution)/shard_map/all_to_all | solution.py:19
  185.4 104.6 %reduce-scatter.2.cloned.1.call-start = ((), (), s32[]{:S(2)}) async-start(), calls=%async_computation.5 | async-start | bytes 2654208 | tf_op jit(solution)/shard_map/reduce_scatter | solution.py:972
  200.3 9.0 %collective-permute-start.18 = (bf16[192,768]{1,0:T(8,128)(2,1)S(1)}, bf16[192,768]{1,0:T(8,128)(2,1)S(1)}, u32[]{:S(2)}, u32[]{:S(2)}) collective-permute-start(bf16[192,768]{1,0:T(8,128)(2,1)S(1)} %get-tuple-element.181), channel_id=1, source_target_pairs={{0,24},{8,16},{16,8},{24,0},{1,25},{9,17},{17,9},{25,1},{2,26},{10... | collective-permute-start | bytes 884744 | tf_op jit(solution)/shard_map/ppermute | solution.py:50
  201.8 14.2 %collective-permute-start.17 = (bf16[192,768]{1,0:T(8,128)(2,1)S(1)}, bf16[192,768]{1,0:T(8,128)(2,1)S(1)}, u32[]{:S(2)}, u32[]{:S(2)}) collective-permute-start(bf16[192,768]{1,0:T(8,128)(2,1)S(1)} %get-tuple-element.182), channel_id=1, source_target_pairs={{0,16},{8,24},{16,0},{24,8},{1,17},{9,25},{17,1},{25,9},{2,18},{10... | collective-permute-start | bytes 884744 | tf_op jit(solution)/shard_map/ppermute | solution.py:50
  202.1 13.9 %collective-permute-start.16 = (bf16[192,768]{1,0:T(8,128)(2,1)S(1)}, bf16[192,768]{1,0:T(8,128)(2,1)S(1)}, u32[]{:S(2)}, u32[]{:S(2)}) collective-permute-start(bf16[192,768]{1,0:T(8,128)(2,1)S(1)} %get-tuple-element.180), channel_id=1, source_target_pairs={{0,8},{8,0},{16,24},{24,16},{1,9},{9,1},{17,25},{25,17},{2,10},{10... | collective-permute-start | bytes 884744 | tf_op jit(solution)/shard_map/ppermute | solution.py:50
  216.2 7.6 %collective-permute-start.19 = (bf16[24,768]{1,0:T(8,128)(2,1)S(1)}, bf16[24,768]{1,0:T(8,128)(2,1)S(1)}, u32[]{:S(2)}, u32[]{:S(2)}) collective-permute-start(bf16[24,768]{1,0:T(8,128)(2,1)S(1)} %get-tuple-element.191), channel_id=1, source_target_pairs={{0,1},{1,0},{2,3},{3,2},{4,5},{5,4},{6,7},{7,6},{8,9},{9,8},{10,11... | collective-permute-start | bytes 110600 | tf_op jit(solution)/shard_map/ppermute | solution.py:50
  217.9 9.3 %collective-permute-start.20 = (bf16[24,768]{1,0:T(8,128)(2,1)S(1)}, bf16[24,768]{1,0:T(8,128)(2,1)S(1)}, u32[]{:S(2)}, u32[]{:S(2)}) collective-permute-start(bf16[24,768]{1,0:T(8,128)(2,1)S(1)} %get-tuple-element.190), channel_id=1, source_target_pairs={{0,2},{1,3},{2,0},{3,1},{4,6},{5,7},{6,4},{7,5},{8,10},{9,11},{10,... | collective-permute-start | bytes 110600 | tf_op jit(solution)/shard_map/ppermute | solution.py:50
  219.4 26.9 %collective-permute-start.21 = (bf16[24,768]{1,0:T(8,128)(2,1)S(1)}, bf16[24,768]{1,0:T(8,128)(2,1)S(1)}, u32[]{:S(2)}, u32[]{:S(2)}) collective-permute-start(bf16[24,768]{1,0:T(8,128)(2,1)S(1)} %get-tuple-element.189), channel_id=1, source_target_pairs={{0,3},{1,2},{2,1},{3,0},{4,7},{5,6},{6,5},{7,4},{8,11},{9,10},{10,... | collective-permute-start | bytes 110600 | tf_op jit(solution)/shard_map/ppermute | solution.py:50
  219.7 26.6 %collective-permute-start.22 = (bf16[24,768]{1,0:T(8,128)(2,1)S(1)}, bf16[24,768]{1,0:T(8,128)(2,1)S(1)}, u32[]{:S(2)}, u32[]{:S(2)}) collective-permute-start(bf16[24,768]{1,0:T(8,128)(2,1)S(1)} %get-tuple-element.188), channel_id=1, source_target_pairs={{0,4},{1,5},{2,6},{3,7},{4,0},{5,1},{6,2},{7,3},{8,12},{9,13},{10,... | collective-permute-start | bytes 110600 | tf_op jit(solution)/shard_map/ppermute | solution.py:50
  222.4 23.9 %collective-permute-start.23 = (bf16[24,768]{1,0:T(8,128)(2,1)S(1)}, bf16[24,768]{1,0:T(8,128)(2,1)S(1)}, u32[]{:S(2)}, u32[]{:S(2)}) collective-permute-start(bf16[24,768]{1,0:T(8,128)(2,1)S(1)} %get-tuple-element.187), channel_id=1, source_target_pairs={{0,5},{1,4},{2,7},{3,6},{4,1},{5,0},{6,3},{7,2},{8,13},{9,12},{10,... | collective-permute-start | bytes 110600 | tf_op jit(solution)/shard_map/ppermute | solution.py:50
  223.7 22.6 %collective-permute-start.24 = (bf16[24,768]{1,0:T(8,128)(2,1)S(1)}, bf16[24,768]{1,0:T(8,128)(2,1)S(1)}, u32[]{:S(2)}, u32[]{:S(2)}) collective-permute-start(bf16[24,768]{1,0:T(8,128)(2,1)S(1)} %get-tuple-element.186), channel_id=1, source_target_pairs={{0,6},{1,7},{2,4},{3,5},{4,2},{5,3},{6,0},{7,1},{8,14},{9,15},{10,... | collective-permute-start | bytes 110600 | tf_op jit(solution)/shard_map/ppermute | solution.py:50
  227.2 19.2 %collective-permute-start.25 = (bf16[24,768]{1,0:T(8,128)(2,1)S(1)}, bf16[24,768]{1,0:T(8,128)(2,1)S(1)}, u32[]{:S(2)}, u32[]{:S(2)}) collective-permute-start(bf16[24,768]{1,0:T(8,128)(2,1)S(1)} %get-tuple-element.185), channel_id=1, source_target_pairs={{0,7},{1,6},{2,5},{3,4},{4,3},{5,2},{6,1},{7,0},{8,15},{9,14},{10,... | collective-permute-start | bytes 110600 | tf_op jit(solution)/shard_map/ppermute | solution.py:50
  246.4 9.1 %collective-permute-start.26 = (bf16[256,384]{1,0:T(8,128)(2,1)}, bf16[256,384]{1,0:T(8,128)(2,1)S(1)}, u32[]{:S(2)}, u32[]{:S(2)}) collective-permute-start(bf16[256,384]{1,0:T(8,128)(2,1)} %get-tuple-element.130), channel_id=1, source_target_pairs={{0,1},{1,0},{2,3},{3,2},{4,5},{5,4},{6,7},{7,6},{8,9},{9,8},{10,11... | collective-permute-start | bytes 589832 | tf_op jit(solution)/shard_map/ppermute | solution.py:50
  248.0 12.4 %collective-permute-start.27 = (bf16[256,384]{1,0:T(8,128)(2,1)}, bf16[256,384]{1,0:T(8,128)(2,1)S(1)}, u32[]{:S(2)}, u32[]{:S(2)}) collective-permute-start(bf16[256,384]{1,0:T(8,128)(2,1)} %get-tuple-element.131), channel_id=1, source_target_pairs={{0,2},{1,3},{2,0},{3,1},{4,6},{5,7},{6,4},{7,5},{8,10},{9,11},{10,... | collective-permute-start | bytes 589832 | tf_op jit(solution)/shard_map/ppermute | solution.py:50
  248.3 13.9 %collective-permute-start.28 = (bf16[256,384]{1,0:T(8,128)(2,1)}, bf16[256,384]{1,0:T(8,128)(2,1)S(1)}, u32[]{:S(2)}, u32[]{:S(2)}) collective-permute-start(bf16[256,384]{1,0:T(8,128)(2,1)} %get-tuple-element.132), channel_id=1, source_target_pairs={{0,3},{1,2},{2,1},{3,0},{4,7},{5,6},{6,5},{7,4},{8,11},{9,10},{10,... | collective-permute-start | bytes 589832 | tf_op jit(solution)/shard_map/ppermute | solution.py:50
  250.2 28.7 %collective-permute-start.29 = (bf16[256,384]{1,0:T(8,128)(2,1)}, bf16[256,384]{1,0:T(8,128)(2,1)S(1)}, u32[]{:S(2)}, u32[]{:S(2)}) collective-permute-start(bf16[256,384]{1,0:T(8,128)(2,1)} %get-tuple-element.133), channel_id=1, source_target_pairs={{0,4},{1,5},{2,6},{3,7},{4,0},{5,1},{6,2},{7,3},{8,12},{9,13},{10,... | collective-permute-start | bytes 589832 | tf_op jit(solution)/shard_map/ppermute | solution.py:50
  251.2 38.7 %collective-permute-start.30 = (bf16[256,384]{1,0:T(8,128)(2,1)}, bf16[256,384]{1,0:T(8,128)(2,1)S(1)}, u32[]{:S(2)}, u32[]{:S(2)}) collective-permute-start(bf16[256,384]{1,0:T(8,128)(2,1)} %get-tuple-element.134), channel_id=1, source_target_pairs={{0,5},{1,4},{2,7},{3,6},{4,1},{5,0},{6,3},{7,2},{8,13},{9,12},{10,... | collective-permute-start | bytes 589832 | tf_op jit(solution)/shard_map/ppermute | solution.py:50
  255.4 34.5 %collective-permute-start.31 = (bf16[256,384]{1,0:T(8,128)(2,1)}, bf16[256,384]{1,0:T(8,128)(2,1)S(1)}, u32[]{:S(2)}, u32[]{:S(2)}) collective-permute-start(bf16[256,384]{1,0:T(8,128)(2,1)} %get-tuple-element.135), channel_id=1, source_target_pairs={{0,6},{1,7},{2,4},{3,5},{4,2},{5,3},{6,0},{7,1},{8,14},{9,15},{10,... | collective-permute-start | bytes 589832 | tf_op jit(solution)/shard_map/ppermute | solution.py:50
  260.4 29.5 %collective-permute-start.32 = (bf16[256,384]{1,0:T(8,128)(2,1)}, bf16[256,384]{1,0:T(8,128)(2,1)S(1)}, u32[]{:S(2)}, u32[]{:S(2)}) collective-permute-start(bf16[256,384]{1,0:T(8,128)(2,1)} %get-tuple-element.136), channel_id=1, source_target_pairs={{0,7},{1,6},{2,5},{3,4},{4,3},{5,2},{6,1},{7,0},{8,15},{9,14},{10,... | collective-permute-start | bytes 589832 | tf_op jit(solution)/shard_map/ppermute | solution.py:50
  300.6 38.0 %copy-start.2 = (bf16[3,64,768]{2,1,0:T(8,128)(2,1)S(1)}, bf16[3,64,768]{2,1,0:T(8,128)(2,1)}, u32[]{:S(2)}) copy-start(bf16[3,64,768]{2,1,0:T(8,128)(2,1)} %param.14) | copy-start | bytes 884740
  300.6 38.0 %copy-start.13 = (bf16[3,64,768]{2,1,0:T(8,128)(2,1)S(1)}, bf16[3,64,768]{2,1,0:T(8,128)(2,1)}, u32[]{:S(2)}) copy-start(bf16[3,64,768]{2,1,0:T(8,128)(2,1)} %get-tuple-element.146) | copy-start | bytes 884740
  300.6 38.0 %copy-start.22 = (f32[3,768]{1,0:T(4,128)S(1)}, f32[3,768]{1,0:T(4,128)}, u32[]{:S(2)}) copy-start(f32[3,768]{1,0:T(4,128)} %get-tuple-element.209.c_ref) | copy-start | bytes 27652
  300.7 40.4 %all-to-all-start.3 = ((bf16[32,32,576]{2,1,0:T(8,128)(2,1)}), bf16[32,32,576]{2,1,0:T(8,128)(2,1)S(1)}, u32[]{:S(2)}, u32[]{:S(2)}) async-start(bf16[32,32,576]{2,1,0:T(8,128)(2,1)} %pad_maximum_fusion.1), calls=%async_computation.4 | async-start | bytes 2621440 | tf_op jit(solution)/shard_map/all_to_all | solution.py:19
  308.7 8.7 %collective-permute-start.38 = (bf16[24,768]{1,0:T(8,128)(2,1)S(1)}, bf16[24,768]{1,0:T(8,128)(2,1)S(1)}, u32[]{:S(2)}, u32[]{:S(2)}) collective-permute-start(bf16[24,768]{1,0:T(8,128)(2,1)S(1)} %get-tuple-element.198), channel_id=1, source_target_pairs={{0,24},{8,16},{16,8},{24,0},{1,25},{9,17},{17,9},{25,1},{2,26},{10... | collective-permute-start | bytes 110600 | tf_op jit(solution)/shard_map/ppermute | solution.py:50
  310.2 11.9 %collective-permute-start.37 = (bf16[24,768]{1,0:T(8,128)(2,1)S(1)}, bf16[24,768]{1,0:T(8,128)(2,1)S(1)}, u32[]{:S(2)}, u32[]{:S(2)}) collective-permute-start(bf16[24,768]{1,0:T(8,128)(2,1)S(1)} %get-tuple-element.199), channel_id=1, source_target_pairs={{0,16},{8,24},{16,0},{24,8},{1,17},{9,25},{17,1},{25,9},{2,18},{10... | collective-permute-start | bytes 110600 | tf_op jit(solution)/shard_map/ppermute | solution.py:50
  310.6 11.5 %collective-permute-start.36 = (bf16[24,768]{1,0:T(8,128)(2,1)S(1)}, bf16[24,768]{1,0:T(8,128)(2,1)S(1)}, u32[]{:S(2)}, u32[]{:S(2)}) collective-permute-start(bf16[24,768]{1,0:T(8,128)(2,1)S(1)} %get-tuple-element.200), channel_id=1, source_target_pairs={{0,8},{8,0},{16,24},{24,16},{1,9},{9,1},{17,25},{25,17},{2,10},{10... | collective-permute-start | bytes 110600 | tf_op jit(solution)/shard_map/ppermute | solution.py:50
  311.3 20.5 %collective-permute-start.35 = (bf16[3,64,768]{2,1,0:T(8,128)(2,1)S(1)}, bf16[3,64,768]{2,1,0:T(8,128)(2,1)S(1)}, u32[]{:S(2)}, u32[]{:S(2)}) collective-permute-start(bf16[3,64,768]{2,1,0:T(8,128)(2,1)S(1)} %copy-done.31), channel_id=1, source_target_pairs={{0,24},{8,16},{16,8},{24,0},{1,25},{9,17},{17,9},{25,1},{2,26},{10... | collective-permute-start | bytes 884744 | tf_op jit(solution)/shard_map/ppermute | solution.py:50
  313.1 25.6 %collective-permute-start.34 = (bf16[3,64,768]{2,1,0:T(8,128)(2,1)S(1)}, bf16[3,64,768]{2,1,0:T(8,128)(2,1)S(1)}, u32[]{:S(2)}, u32[]{:S(2)}) collective-permute-start(bf16[3,64,768]{2,1,0:T(8,128)(2,1)S(1)} %copy-done.30), channel_id=1, source_target_pairs={{0,16},{8,24},{16,0},{24,8},{1,17},{9,25},{17,1},{25,9},{2,18},{10... | collective-permute-start | bytes 884744 | tf_op jit(solution)/shard_map/ppermute | solution.py:50
  317.4 21.3 %collective-permute-start.33 = (bf16[3,64,768]{2,1,0:T(8,128)(2,1)S(1)}, bf16[3,64,768]{2,1,0:T(8,128)(2,1)S(1)}, u32[]{:S(2)}, u32[]{:S(2)}) collective-permute-start(bf16[3,64,768]{2,1,0:T(8,128)(2,1)S(1)} %copy-done.29), channel_id=1, source_target_pairs={{0,8},{8,0},{16,24},{24,16},{1,9},{9,1},{17,25},{25,17},{2,10},{10... | collective-permute-start | bytes 884744 | tf_op jit(solution)/shard_map/ppermute | solution.py:50
  (43 other events, 534.7 us)
Sparse Core Ops, SparseCore 0:
  48.6 113.4 all-gather.2
  199.8 89.6 reduce-scatter.1

commit v4 on v3

--- a/solution.py
+++ b/solution.py
@@ -61,6 +61,16 @@
         x = jnp.where((index & bit) != 0, flipped, y).reshape(shape)
         bit *= 2
     return x
+
+
+def halve(x, axis, index, bit):
+    size = lax.axis_size(axis)
+    y = x.reshape((-1, 2) + x.shape[1:])
+    mine = (index // bit) % 2
+    sent = lax.dynamic_index_in_dim(y, 1 - mine, 1, keepdims=False)
+    kept = lax.dynamic_index_in_dim(y, mine, 1, keepdims=False)
+    came = lax.ppermute(sent, axis, [(i, i ^ bit) for i in range(size)])
+    return (kept.astype(F32) + came.astype(F32)).astype(BF)
 
 
 def project_body(blocks, pairs, heads, extra, place_ref, c_ref, shift_ref, w_ref, *refs):
@@ -736,7 +746,9 @@
             ],
             0,
         )
-    weight_pack, in_own = lax.optimization_barrier((weight_pack, in_own))
+    weight_pack, in_own, small_all, n1_group = lax.optimization_barrier(
+        (weight_pack, in_own, small_all, n1_group)
+    )
     gathered = lax.all_gather(weight_pack, ALL, axis=0, tiled=False)
     unit = gain_rows
     while unit % 8:
@@ -969,15 +981,8 @@
         "ulysses",
     )
 
-    feed_sum = lax.psum_scatter(feed_part, "blk", scatter_dimension=0, tiled=True)[0]
-    output_part = sum(x.astype(F32) for x in output_part).astype(BF).reshape(blocks, gain_rows, width)
-    output_part = swap(
-        [
-            lax.dynamic_index_in_dim(output_part, block_id ^ k, 0, keepdims=False)
-            for k in range(blocks)
-        ],
-        "blk",
-    )
+    feed_half = halve(feed_part, "blk", block_id, 1)
+
     if small_path:
         leaving = pl.pallas_call(
             functools.partial(attend_all_back_body, blocks, groups, rows, stripe),
@@ -1011,28 +1016,10 @@
             name="rotate_out",
         )(place, cos_table, sin_table, *grads)
     leaving, output_part = lax.optimization_barrier((leaving, output_part))
-    output_grad = sum(x.astype(F32) for x in output_part)
     back = swap(leaving, "blk")
-    back, feed_sum = lax.optimization_barrier((back, feed_sum))
-
-    reduce_grad = feed_sum[:ff_rows].astype(F32)
-    expand_rows = feed_sum[ff_rows:].reshape(groups, gain_rows, width)
-    expand_came = jnp.stack(
-        swap(
-            [
-                lax.dynamic_index_in_dim(expand_rows, group_id ^ k, 0, keepdims=False)
-                for k in range(groups)
-            ],
-            "ulysses",
-        )
-    )
-    expand_grad = jnp.concatenate(
-        [
-            lax.dynamic_index_in_dim(expand_came, group_id ^ k, 0, keepdims=False)
-            for k in range(groups)
-        ],
-        1,
-    ).astype(F32)
+    output_part = sum(x.astype(F32) for x in output_part).astype(BF).reshape(blocks, gain_rows, width)
+    output_part = halve(output_part, "blk", block_id, 1)
+    back, feed_half, output_part = lax.optimization_barrier((back, feed_half, output_part))
 
     returned = pl.pallas_call(
         functools.partial(project_back_body, blocks, pairs, heads, extra),
@@ -1082,19 +1069,51 @@
     taken = small_parts.shape[1]
     small_rows = 8 * -(-taken // (8 * in_lanes))
     small_parts = jnp.pad(small_parts, ((0, 0), (0, small_rows * in_lanes - taken)))
-    final = exchange(
-        jnp.concatenate(
+    input_part = jnp.concatenate(
+        [
+            input_part.reshape(groups, blocks, gain_rows, in_lanes),
+            small_parts.reshape(groups, blocks, small_rows, in_lanes),
+        ],
+        2,
+    ).transpose(1, 0, 2, 3)
+    input_sum = halve(input_part, "blk", block_id, 1)
+    weight_sum, bit = jnp.concatenate([feed_half, output_part], 1), 2
+    while bit < blocks:
+        weight_sum = halve(weight_sum, "blk", block_id, bit)
+        input_sum = halve(input_sum, "blk", block_id, bit)
+        bit *= 2
+    weight_sum, input_sum = weight_sum[0], input_sum[0]
+    final = jnp.stack(
+        swap(
             [
-                input_part.reshape(devices, gain_rows, in_lanes),
-                small_parts.reshape(devices, small_rows, in_lanes),
+                lax.dynamic_index_in_dim(input_sum, group_id ^ k, 0, keepdims=False)
+                for k in range(groups)
             ],
-            1,
+            "ulysses",
         )
     )
     small_sum = jnp.sum(final[:, gain_rows:].astype(F32), 0).reshape(-1)
-    input_sum = jnp.sum(
-        final[:, :gain_rows].astype(F32).reshape(groups, blocks, gain_rows, in_lanes), 1
-    )
+    input_sum = unscramble(final[:, :gain_rows], group_id, 0).astype(F32)
+    reduce_grad = weight_sum[:ff_rows].astype(F32)
+    output_grad = weight_sum[-gain_rows:].astype(F32)
+    expand_rows = weight_sum[ff_rows:-gain_rows].reshape(groups, gain_rows, width)
+    expand_came = jnp.stack(
+        swap(
+            [
+                lax.dynamic_index_in_dim(expand_rows, group_id ^ k, 0, keepdims=False)
+                for k in range(groups)
+            ],
+            "ulysses",
+        )
+    )
+    expand_grad = jnp.concatenate(
+        [
+            lax.dynamic_index_in_dim(expand_came, group_id ^ k, 0, keepdims=False)
+            for k in range(groups)
+        ],
+        1,
+    ).astype(F32)
+
     two = heads * 2 * head_width
     input_grad = jnp.concatenate(
         [

time: 355 us -> 340 us (0.958)
  waiting for transfers between devices: 145 us -> 119 us
  starting transfers between devices: 76.4 us -> 83.5 us
  other arithmetic: 23.9 us -> 28.4 us
    ppermute x39 -> x35, waiting for transfers between devices: 110 us -> 51.9 us  [swap(): lax.ppermute(x, axis, [(i, i ^ k) for i in range(size)])]
    ppermute x0 -> x7, waiting for transfers between devices: none -> 25.2 us  [halve(): came = lax.ppermute(sent, axis, [(i, i ^ bit) for i in range(size)])]
    ppermute x0 -> x7, starting transfers between devices: none -> 19.1 us  [halve(): came = lax.ppermute(sent, axis, [(i, i ^ bit) for i in range(size)])]
    ppermute x39 -> x35, starting transfers between devices: 44.1 us -> 35.9 us  [swap(): lax.ppermute(x, axis, [(i, i ^ k) for i in range(size)])]
    all_gather x1, waiting for transfers between devices: 0.01 us -> 4.2 us  [on_device(): gathered = lax.all_gather(weight_pack, ALL, axis=0, tiled=False)]
    all_to_all x4 -> x3, starting transfers between devices: 32.2 us -> 28.5 us  [exchange(): return lax.all_to_all(x, ALL, split_axis=0, concat_axis=0, tiled=True)]
    all_to_all x4 -> x3, waiting for transfers between devices: 35 us -> 37.5 us  [exchange(): return lax.all_to_all(x, ALL, split_axis=0, concat_axis=0, tiled=True)]
  transfers between devices with their start and end apart: 45 -> 46, of which waited for: 19 -> 16; matrix products, arithmetic and copies ran while one was open for 7% -> 10% of each run, Pallas kernels for 18% -> 19%
where the time goes in v4:
time: 340 us
  waiting for transfers between devices  119 us (35%)
  starting transfers between devices  83.5 us (25%)
  Pallas kernels  69.9 us (21%)
  other arithmetic  28.4 us (8%)
  local copies, waits for them, and re-layouts  22.1 us (6%)
  between operations  15.3 us (4%)
    ppermute x35, waiting for transfers between devices, swap(): lax.ppermute(x, axis, [(i, i ^ k) for i in range(size)])  51.9 us
    all_to_all x3, waiting for transfers between devices, exchange(): return lax.all_to_all(x, ALL, split_axis=0, concat_axis=0, tiled=True)  37.5 us
    ppermute x35, starting transfers between devices, swap(): lax.ppermute(x, axis, [(i, i ^ k) for i in range(size)])  35.9 us
    all_to_all x3, starting transfers between devices, exchange(): return lax.all_to_all(x, ALL, split_axis=0, concat_axis=0, tiled=True)  28.5 us
    ppermute x7, waiting for transfers between devices, halve(): came = lax.ppermute(sent, axis, [(i, i ^ bit) for i in range(size)])  25.2 us
    ppermute x7, starting transfers between devices, halve(): came = lax.ppermute(sent, axis, [(i, i ^ bit) for i in range(size)])  19.1 us
    pallas_call x1, Pallas kernels, on_device(): pl.pallas_call(functools.partial(attend_all_back_body, blocks, groups, ro...  18.9 us
    pallas_call x1, Pallas kernels, on_device(): pl.pallas_call(functools.partial(attend_all_body, blocks, groups, rows, s...  18.2 us
  transfers between devices with their start and end apart: 46, of which 16 were waited for; matrix products, arithmetic and copies ran while one was open for 10% of the time, Pallas kernels for 19%

profile of v4, /device:TPU:0, one launch (start us, length us, event | category | flops | bytes accessed | tf_op | source)
XLA Modules:
  0.0 339.6 jit_solution(6256586887839504249)
XLA Ops:
  9.5 2.8 concatenate.56
  15.5 7.3 %all-to-all-start = ((bf16[32,24,640]{2,1,0:T(8,128)(2,1)}), bf16[32,24,640]{2,1,0:T(8,128)(2,1)S(1)}, u32[]{:S(2)}, u32[]{:S(2)}) async-start(bf16[32,24,640]{2,1,0:T(8,128)(2,1)} %bitcast.6), calls=%async_computation | async-start | bytes 1966080 | tf_op jit(solution)/shard_map/all_to_all | solution.py:19
  23.7 1.7 collective-permute-start.1
  26.2 22.7 %all-to-all-done = bf16[32,24,640]{2,1,0:T(8,128)(2,1)S(1)} async-done(((bf16[32,24,640]{2,1,0:T(8,128)(2,1)}), bf16[32,24,640]{2,1,0:T(8,128)(2,1)S(1)}, u32[]{:S(2)}, u32[]{:S(2)}) %all-to-all-start) | async-done | bytes 983072 | tf_op jit(solution)/shard_map/all_to_all | solution.py:19
  52.3 5.7 %sine_multiply_fusion = (f32[2048,128]{1,0:T(8,128)}, f32[2048,128]{1,0:T(8,128)}) fusion(f32[128]{0:T(128)S(1)} %compare_select_fusion, f32[128]{0:T(128)S(1)} %mul.177, f32[2048]{0:T(1024)S(1)} %subtract_convert_fusion, f32[2048]{0:T(1024)S(1)} %subtract_convert_fusion.1, pred[128]{0:T(512)(128)(4,1)S(1)} %iota_compare_fusion.5), kind=kLoop, calls=%fused_computation.12 | loop fusion | flops 786432 | bytes 2114688 | tf_op jit(solution)/shard_map/mul | solution.py:793
  59.2 4.4 %project.1 = (bf16[256,384]{1,0:T(8,128)(2,1)}, bf16[256,384]{1,0:T(8,128)(2,1)}, bf16[256,384]{1,0:T(8,128)(2,1)}, bf16[256,384]{1,0:T(8,128)(2,1)}, bf16[256,3...) custom-call(s32[2]{0:T(128)} %pad_add_fusion.2.place_ref, ...), custom_call_target="tpu_custom_call" | custom-call | flops 679477248 | bytes 1179648 | tf_op jit(solution)/shard_map/project/pallas_call | solution.py:805
  68.6 1.5 collective-permute-start.6
  70.0 1.7 collective-permute-start.7
  71.7 3.1 collective-permute-start.8
  74.9 6.4 %collective-permute-done.4.refs_2_ = bf16[256,384]{1,0:T(8,128)(2,1)S(1)} collective-permute-done((bf16[256,384]{1,0:T(8,128)(2,1)}, bf16[256,384]{1,0:T(8,128)(2,1)S(1)}, u32[]{:S(2)}, u32[]{:S(2)}) %collective-permute-start.4) | collective-permute-done | bytes 196640 | tf_op jit(solution)/shard_map/ppermute | solution.py:50
  81.3 1.6 collective-permute-start.9
  84.4 1.8 collective-permute-done.5.refs_3_
  86.3 18.9 %collective-permute-done.7.refs_5_ = bf16[256,384]{1,0:T(8,128)(2,1)S(1)} collective-permute-done((bf16[256,384]{1,0:T(8,128)(2,1)}, bf16[256,384]{1,0:T(8,128)(2,1)S(1)}, u32[]{:S(2)}, u32[]{:S(2)}) %collective-permute-start.7) | collective-permute-done | bytes 196640 | tf_op jit(solution)/shard_map/ppermute | solution.py:50
  106.0 18.2 %attend_all.1 = (bf16[32,40,128]{2,1,0:T(8,128)(2,1)}, bf16[2048,64]{1,0:T(8,128)(2,1)}, bf16[2304,64]{1,0:T(8,128)(2,1)}, bf16[2304,64]{1,0:T(8,128)(2,1)}, bf1...) custom-call(s32[2]{0:T(128)} %pad_add_fusion.2.place_ref, ...), custom_call_target="tpu_custom_call" | custom-call | flops 268435456 | bytes 4194304 | tf_op jit(solution)/shard_map/attend_all/pallas_call | solution.py:848
  124.2 17.3 %all-to-all-start.1 = ((bf16[32,40,128]{2,1,0:T(8,128)(2,1)}), bf16[32,40,128]{2,1,0:T(8,128)(2,1)S(1)}, u32[]{:S(2)}, u32[]{:S(2)}) async-start(bf16[32,40,128]{2,1,0:T(8,128)(2,1)} %get-tuple-element.105), calls=%async_computation.1 | async-start | bytes 655360 | tf_op jit(solution)/shard_map/all_to_all | solution.py:19
  141.6 1.7 collective-permute-start.14
  144.9 14.7 %all-to-all-done.1.came_ref = bf16[32,40,128]{2,1,0:T(8,128)(2,1)S(1)} async-done(((bf16[32,40,128]{2,1,0:T(8,128)(2,1)}), bf16[32,40,128]{2,1,0:T(8,128)(2,1)S(1)}, u32[]{:S(2)}, u32[]{:S(2)}) %all-to-all-start.1) | async-done | bytes 327712 | tf_op jit(solution)/shard_map/all_to_all | solution.py:19
  159.6 4.2 %all-gather.3.cloned.1.call-done = bf16[6912,768]{1,0:T(8,128)(2,1)} async-done(((bf16[216,768]{1,0:T(8,128)(2,1)}), bf16[6912,768]{1,0:T(8,128)(2,1)}) %all-gather.3.cloned.1.call-update) | async-done | bytes 10616848 | tf_op jit(solution)/shard_map/all_gather | solution.py:752
  163.8 3.1 middle.1
  167.1 1.5 collective-permute-start.11
  168.7 11.5 %feed.1 = (bf16[192,768]{1,0:T(8,128)(2,1)}, f32[192,768]{1,0:T(8,128)}, bf16[192,768]{1,0:T(8,128)(2,1)}, bf16[32,40,128]{2,1,0:T(8,128)(2,1)}, f32[15,768]{1,0:T(8,128)}) custom-call(bf16[32,216,768]{2,1,0:T(8,128)(2,1)} %bitcast.187, bf16[32,216,768]{2,1,0:T(8,128)(2,1)} %bitcast.188, bf16[32,216,768]{2,1,0:T(8,128)(2,1)} %bitcast.189, ...), custom_call_target="tpu_custom_call" | custom-call | flops 3623878656 | bytes 9437184 | tf_op jit(solution)/shard_map/feed/pallas_call | solution.py:905
  180.2 3.9 %all-to-all-start.2 = ((bf16[32,40,128]{2,1,0:T(8,128)(2,1)}), bf16[32,40,128]{2,1,0:T(8,128)(2,1)}, u32[]{:S(2)}, u32[]{:S(2)}) async-start(bf16[32,40,128]{2,1,0:T(8,128)(2,1)} %get-tuple-element.111), calls=%async_computation.2 | async-start | bytes 655360 | tf_op jit(solution)/shard_map/all_to_all | solution.py:19
  184.1 1.5 convolution_convert_fusion
  186.7 8.5 %feed_weights.1 = (bf16[768,768]{1,0:T(8,128)(2,1)}, bf16[768,768]{1,0:T(8,128)(2,1)}, f32[1,768]{1,0:T(1,128)}) custom-call(s32[2]{0:T(128)} %pad_add_fusion.2.place_ref, bf16[32,216,768]{2,1,0:T(8,128)(2,1)} %bitcast.190, bf16[32,216,768]{2,1,0:T(8,128)(2,1)} %bitcast.191, f32[4,1,768]{2,1,0:T(1,128)} %reshape.627.ex_bias_ref.bias_ref, ...), custom_call_target="tpu_custom_call" | custom-call | flops 4529848320 | bytes 9437184 | tf_op jit(solution)/shard_map/feed_weights/pallas_call | solution.py:942
  195.2 1.5 copy.97
  198.1 1.7 collective-permute-start.26
  206.2 18.9 %attend_all_back.1 = (bf16[256,384]{1,0:T(8,128)(2,1)}, bf16[256,384]{1,0:T(8,128)(2,1)}, bf16[256,384]{1,0:T(8,128)(2,1)}, bf16[256,384]{1,0:T(8,128)(2,1)}, bf...) custom-call(s32[2]{0:T(128)} %pad_add_fusion.2.place_ref, ...), custom_call_target="tpu_custom_call" | custom-call | flops 536870912 | bytes 4194304 | tf_op jit(solution)/shard_map/attend_all_back/pallas_call | solution.py:987
  226.5 1.7 collective-permute-start.19
  228.2 1.5 collective-permute-start.20
  230.0 2.2 collective-permute-done.27
  232.2 2.0 collective-permute-start.22
  236.0 1.9 collective-permute-start.23
  238.0 4.3 %collective-permute-done.20.refs_6_ = bf16[256,384]{1,0:T(8,128)(2,1)S(1)} collective-permute-done((bf16[256,384]{1,0:T(8,128)(2,1)S(1)}, bf16[256,384]{1,0:T(8,128)(2,1)S(1)}, u32[]{:S(2)}, u32[]{:S(2)}) %collective-permute-start.20) | collective-permute-done | bytes 196640 | tf_op jit(solution)/shard_map/ppermute | solution.py:50
  242.3 1.5 collective-permute-start.24
  243.8 2.2 collective-permute-start.25
  246.0 1.5 fusion
  247.7 14.3 %collective-permute-done.23.refs_9_ = bf16[256,384]{1,0:T(8,128)(2,1)S(1)} collective-permute-done((bf16[256,384]{1,0:T(8,128)(2,1)S(1)}, bf16[256,384]{1,0:T(8,128)(2,1)S(1)}, u32[]{:S(2)}, u32[]{:S(2)}) %collective-permute-start.23) | collective-permute-done | bytes 196640 | tf_op jit(solution)/shard_map/ppermute | solution.py:50
  263.3 5.3 %project_back.1 = (bf16[3,64,768]{2,1,0:T(8,128)(2,1)}, bf16[3,64,768]{2,1,0:T(8,128)(2,1)}, bf16[3,64,768]{2,1,0:T(8,128)(2,1)}, bf16[3,64,768]{2,1,0:T(8,128)(...) custom-call(s32[2]{0:T(128)} %pad_add_fusion.2.place_ref, f32[3,768]{1,0:T(4,128)} %get-tuple-element.210.c_ref, ...), custom_call_target="tpu_custom_call" | custom-call | flops 1358954496 | bytes 1179648 | tf_op jit(solution)/shard_map/project_back/pallas_call | solution.py:1024
  268.8 1.7 collective-permute-start.29
  274.3 1.8 collective-permute-start.31
  276.3 5.6 %collective-permute-start.37 = (bf16[2,216,768]{2,1,0:T(8,128)(2,1)S(1)}, bf16[2,216,768]{2,1,0:T(8,128)(2,1)S(1)}, u32[]{:S(2)}, u32[]{:S(2)}) collective-permute-start(bf16[2,216,768]{2,1,0:T(8,128)(2,1)S(1)} %dynamic-slice_bitcast_fusion.1), channel_id=1, source_target_pairs={{0,2},{1,3},{2,0},{3,1},{4,6},{5,7},{6,4},{7,5},{8,10},{9,11},{10,... | collective-permute-start | bytes 1990664 | tf_op jit(solution)/shard_map/ppermute | solution.py:72
  282.0 2.6 collective-permute-done.29
  286.9 4.4 %collective-permute-done.31 = bf16[4,4,32,576]{3,2,1,0:T(8,128)(2,1)S(1)} collective-permute-done((bf16[4,4,32,576]{3,2,1,0:T(8,128)(2,1)S(1)}, bf16[4,4,32,576]{3,2,1,0:T(8,128)(2,1)S(1)}, u32[]{:S(2)}, u32[]{:S(2)}) %collective-permute-start.31) | collective-permute-done | bytes 589856 | tf_op jit(solution)/shard_map/ppermute | solution.py:72
  291.5 6.9 %collective-permute-start.32 = (bf16[2,4,32,576]{3,2,1,0:T(8,128)(2,1)S(1)}, bf16[2,4,32,576]{3,2,1,0:T(8,128)(2,1)S(1)}, u32[]{:S(2)}, u32[]{:S(2)}) collective-permute-start(bf16[2,4,32,576]{3,2,1,0:T(8,128)(2,1)S(1)} %dynamic-slice_bitcast_fusion.3), channel_id=1, source_target_pairs={{0,2},{1,3},{2,0},{3,1},{4,6},{5,7},{6,4},{7,5},{8,10},{9,11},{10,... | collective-permute-start | bytes 884744 | tf_op jit(solution)/shard_map/ppermute | solution.py:72
  298.7 2.5 collective-permute-start.38
  301.2 11.3 %collective-permute-done.32 = bf16[2,4,32,576]{3,2,1,0:T(8,128)(2,1)S(1)} collective-permute-done((bf16[2,4,32,576]{3,2,1,0:T(8,128)(2,1)S(1)}, bf16[2,4,32,576]{3,2,1,0:T(8,128)(2,1)S(1)}, u32[]{:S(2)}, u32[]{:S(2)}) %collective-permute-start.32) | collective-permute-done | bytes 294944 | tf_op jit(solution)/shard_map/ppermute | solution.py:72
  312.6 7.3 %collective-permute-done.38 = bf16[1,216,768]{2,1,0:T(8,128)(2,1)S(1)} collective-permute-done((bf16[1,216,768]{2,1,0:T(8,128)(2,1)S(1)}, bf16[1,216,768]{2,1,0:T(8,128)(2,1)S(1)}, u32[]{:S(2)}, u32[]{:S(2)}) %collective-permute-start.38) | collective-permute-done | bytes 331808 | tf_op jit(solution)/shard_map/ppermute | solution.py:72
  321.2 1.5 collective-permute-start.39
  (324 shorter events, 52.3 us)
Async XLA Ops:
  15.5 33.5 %all-to-all-start = ((bf16[32,24,640]{2,1,0:T(8,128)(2,1)}), bf16[32,24,640]{2,1,0:T(8,128)(2,1)S(1)}, u32[]{:S(2)}, u32[]{:S(2)}) async-start(bf16[32,24,640]{2,1,0:T(8,128)(2,1)} %bitcast.6), calls=%async_computation | async-start | bytes 1966080 | tf_op jit(solution)/shard_map/all_to_all | solution.py:19
  22.8 141.0 %all-gather.3.cloned.1.call-start = ((), (), s32[]{:S(2)}) async-start(), calls=%async_computation.3 | async-start | bytes 10948608 | tf_op jit(solution)/shard_map/all_gather | solution.py:752
  23.4 26.0 %collective-permute-start = (bf16[3,64,768]{2,1,0:T(8,128)(2,1)S(1)}, bf16[3,64,768]{2,1,0:T(8,128)(2,1)S(1)}, u32[]{:S(2)}, u32[]{:S(2)}) collective-permute-start(bf16[3,64,768]{2,1,0:T(8,128)(2,1)S(1)} %fusion.8.refs_0_), channel_id=1, source_target_pairs={{0,8},{8,0},{16,24},{24,16},{1,9},{9,1},{17,25},{25,17},{2,10},{10... | collective-permute-start | bytes 884744 | tf_op jit(solution)/shard_map/ppermute | solution.py:50
  23.7 25.7 %collective-permute-start.1 = (bf16[3,64,768]{2,1,0:T(8,128)(2,1)S(1)}, bf16[3,64,768]{2,1,0:T(8,128)(2,1)S(1)}, u32[]{:S(2)}, u32[]{:S(2)}) collective-permute-start(bf16[3,64,768]{2,1,0:T(8,128)(2,1)S(1)} %fusion.8.refs_0_), channel_id=1, source_target_pairs={{0,16},{8,24},{16,0},{24,8},{1,17},{9,25},{17,1},{25,9},{2,18},{10... | collective-permute-start | bytes 884744 | tf_op jit(solution)/shard_map/ppermute | solution.py:50
  25.4 24.0 %collective-permute-start.2 = (bf16[3,64,768]{2,1,0:T(8,128)(2,1)S(1)}, bf16[3,64,768]{2,1,0:T(8,128)(2,1)S(1)}, u32[]{:S(2)}, u32[]{:S(2)}) collective-permute-start(bf16[3,64,768]{2,1,0:T(8,128)(2,1)S(1)} %fusion.8.refs_0_), channel_id=1, source_target_pairs={{0,24},{8,16},{16,8},{24,0},{1,25},{9,17},{17,9},{25,1},{2,26},{10... | collective-permute-start | bytes 884744 | tf_op jit(solution)/shard_map/ppermute | solution.py:50
  63.6 8.1 %collective-permute-start.3 = (bf16[256,384]{1,0:T(8,128)(2,1)}, bf16[256,384]{1,0:T(8,128)(2,1)S(1)}, u32[]{:S(2)}, u32[]{:S(2)}) collective-permute-start(bf16[256,384]{1,0:T(8,128)(2,1)} %get-tuple-element.98), channel_id=1, source_target_pairs={{0,1},{1,0},{2,3},{3,2},{4,5},{5,4},{6,7},{7,6},{8,9},{9,8},{10,11... | collective-permute-start | bytes 589832 | tf_op jit(solution)/shard_map/ppermute | solution.py:50
  64.5 16.8 %collective-permute-start.4 = (bf16[256,384]{1,0:T(8,128)(2,1)}, bf16[256,384]{1,0:T(8,128)(2,1)S(1)}, u32[]{:S(2)}, u32[]{:S(2)}) collective-permute-start(bf16[256,384]{1,0:T(8,128)(2,1)} %get-tuple-element.99), channel_id=1, source_target_pairs={{0,2},{1,3},{2,0},{3,1},{4,6},{5,7},{6,4},{7,5},{8,10},{9,11},{10,... | collective-permute-start | bytes 589832 | tf_op jit(solution)/shard_map/ppermute | solution.py:50
  67.1 19.2 %collective-permute-start.5 = (bf16[256,384]{1,0:T(8,128)(2,1)}, bf16[256,384]{1,0:T(8,128)(2,1)S(1)}, u32[]{:S(2)}, u32[]{:S(2)}) collective-permute-start(bf16[256,384]{1,0:T(8,128)(2,1)} %get-tuple-element.100), channel_id=1, source_target_pairs={{0,3},{1,2},{2,1},{3,0},{4,7},{5,6},{6,5},{7,4},{8,11},{9,10},{10,... | collective-permute-start | bytes 589832 | tf_op jit(solution)/shard_map/ppermute | solution.py:50
  68.6 17.7 %collective-permute-start.6 = (bf16[256,384]{1,0:T(8,128)(2,1)}, bf16[256,384]{1,0:T(8,128)(2,1)S(1)}, u32[]{:S(2)}, u32[]{:S(2)}) collective-permute-start(bf16[256,384]{1,0:T(8,128)(2,1)} %get-tuple-element.101), channel_id=1, source_target_pairs={{0,4},{1,5},{2,6},{3,7},{4,0},{5,1},{6,2},{7,3},{8,12},{9,13},{10,... | collective-permute-start | bytes 589832 | tf_op jit(solution)/shard_map/ppermute | solution.py:50
  70.0 35.2 %collective-permute-start.7 = (bf16[256,384]{1,0:T(8,128)(2,1)}, bf16[256,384]{1,0:T(8,128)(2,1)S(1)}, u32[]{:S(2)}, u32[]{:S(2)}) collective-permute-start(bf16[256,384]{1,0:T(8,128)(2,1)} %get-tuple-element.102), channel_id=1, source_target_pairs={{0,5},{1,4},{2,7},{3,6},{4,1},{5,0},{6,3},{7,2},{8,13},{9,12},{10,... | collective-permute-start | bytes 589832 | tf_op jit(solution)/shard_map/ppermute | solution.py:50
  71.7 33.5 %copy-start.40 = (bf16[256,384]{1,0:T(8,128)(2,1)}, bf16[256,384]{1,0:T(8,128)(2,1)S(1)}, u32[]{:S(2)}) copy-start(bf16[256,384]{1,0:T(8,128)(2,1)S(1)} %collective-permute-done.3.refs_1_) | copy-start | bytes 589828
  71.7 33.5 %collective-permute-start.8 = (bf16[256,384]{1,0:T(8,128)(2,1)}, bf16[256,384]{1,0:T(8,128)(2,1)S(1)}, u32[]{:S(2)}, u32[]{:S(2)}) collective-permute-start(bf16[256,384]{1,0:T(8,128)(2,1)} %get-tuple-element.103), channel_id=1, source_target_pairs={{0,6},{1,7},{2,4},{3,5},{4,2},{5,3},{6,0},{7,1},{8,14},{9,15},{10,... | collective-permute-start | bytes 589832 | tf_op jit(solution)/shard_map/ppermute | solution.py:50
  81.3 23.9 %collective-permute-start.9 = (bf16[256,384]{1,0:T(8,128)(2,1)}, bf16[256,384]{1,0:T(8,128)(2,1)S(1)}, u32[]{:S(2)}, u32[]{:S(2)}) collective-permute-start(bf16[256,384]{1,0:T(8,128)(2,1)} %get-tuple-element.104), channel_id=1, source_target_pairs={{0,7},{1,6},{2,5},{3,4},{4,3},{5,2},{6,1},{7,0},{8,15},{9,14},{10,... | collective-permute-start | bytes 589832 | tf_op jit(solution)/shard_map/ppermute | solution.py:50
  106.0 35.4 %copy-start.8 = (bf16[3,64,768]{2,1,0:T(8,128)(2,1)S(1)}, bf16[3,64,768]{2,1,0:T(8,128)(2,1)}, u32[]{:S(2)}) copy-start(bf16[3,64,768]{2,1,0:T(8,128)(2,1)} %param.15) | copy-start | bytes 884740
  124.2 35.4 %all-to-all-start.1 = ((bf16[32,40,128]{2,1,0:T(8,128)(2,1)}), bf16[32,40,128]{2,1,0:T(8,128)(2,1)S(1)}, u32[]{:S(2)}, u32[]{:S(2)}) async-start(bf16[32,40,128]{2,1,0:T(8,128)(2,1)} %get-tuple-element.105), calls=%async_computation.1 | async-start | bytes 655360 | tf_op jit(solution)/shard_map/all_to_all | solution.py:19
  141.5 27.1 %collective-permute-start.13 = (bf16[192,768]{1,0:T(8,128)(2,1)S(1)}, bf16[192,768]{1,0:T(8,128)(2,1)S(1)}, u32[]{:S(2)}, u32[]{:S(2)}) collective-permute-start(bf16[192,768]{1,0:T(8,128)(2,1)S(1)} %bitcast.212), channel_id=1, source_target_pairs={{0,8},{8,0},{16,24},{24,16},{1,9},{9,1},{17,25},{25,17},{2,10},{10... | collective-permute-start | bytes 884744 | tf_op jit(solution)/shard_map/ppermute | solution.py:50
  141.6 44.0 %collective-permute-start.14 = (bf16[192,768]{1,0:T(8,128)(2,1)S(1)}, bf16[192,768]{1,0:T(8,128)(2,1)S(1)}, u32[]{:S(2)}, u32[]{:S(2)}) collective-permute-start(bf16[192,768]{1,0:T(8,128)(2,1)S(1)} %bitcast.213), channel_id=1, source_target_pairs={{0,16},{8,24},{16,0},{24,8},{1,17},{9,25},{17,1},{25,9},{2,18},{10... | collective-permute-start | bytes 884744 | tf_op jit(solution)/shard_map/ppermute | solution.py:50
  143.3 42.4 %collective-permute-start.15 = (bf16[192,768]{1,0:T(8,128)(2,1)S(1)}, bf16[192,768]{1,0:T(8,128)(2,1)S(1)}, u32[]{:S(2)}, u32[]{:S(2)}) collective-permute-start(bf16[192,768]{1,0:T(8,128)(2,1)S(1)} %bitcast.214), channel_id=1, source_target_pairs={{0,24},{8,16},{16,8},{24,0},{1,25},{9,17},{17,9},{25,1},{2,26},{10... | collective-permute-start | bytes 884744 | tf_op jit(solution)/shard_map/ppermute | solution.py:50
  166.9 18.8 %collective-permute-start.10 = (bf16[192,768]{1,0:T(8,128)(2,1)}, bf16[192,768]{1,0:T(8,128)(2,1)S(1)}, u32[]{:S(2)}, u32[]{:S(2)}) collective-permute-start(bf16[192,768]{1,0:T(8,128)(2,1)} %get-tuple-element.106.second_ref.refs_0_), channel_id=1, source_target_pairs={{0,8},{8,0},{16,24},{24,16},{1,9},{9,1},{17,25},{25,17},{2,10},{10... | collective-permute-start | bytes 884744 | tf_op jit(solution)/shard_map/ppermute | solution.py:50
  167.1 18.6 %collective-permute-start.11 = (bf16[192,768]{1,0:T(8,128)(2,1)}, bf16[192,768]{1,0:T(8,128)(2,1)S(1)}, u32[]{:S(2)}, u32[]{:S(2)}) collective-permute-start(bf16[192,768]{1,0:T(8,128)(2,1)} %get-tuple-element.106.second_ref.refs_0_), channel_id=1, source_target_pairs={{0,16},{8,24},{16,0},{24,8},{1,17},{9,25},{17,1},{25,9},{2,18},{10... | collective-permute-start | bytes 884744 | tf_op jit(solution)/shard_map/ppermute | solution.py:50
  168.6 17.1 %collective-permute-start.12 = (bf16[192,768]{1,0:T(8,128)(2,1)}, bf16[192,768]{1,0:T(8,128)(2,1)}, u32[]{:S(2)}, u32[]{:S(2)}) collective-permute-start(bf16[192,768]{1,0:T(8,128)(2,1)} %get-tuple-element.106.second_ref.refs_0_), channel_id=1, source_target_pairs={{0,24},{8,16},{16,8},{24,0},{1,25},{9,17},{17,9},{25,1},{2,26},{10... | collective-permute-start | bytes 884744 | tf_op jit(solution)/shard_map/ppermute | solution.py:50
  180.2 16.8 %all-to-all-start.2 = ((bf16[32,40,128]{2,1,0:T(8,128)(2,1)}), bf16[32,40,128]{2,1,0:T(8,128)(2,1)}, u32[]{:S(2)}, u32[]{:S(2)}) async-start(bf16[32,40,128]{2,1,0:T(8,128)(2,1)} %get-tuple-element.111), calls=%async_computation.2 | async-start | bytes 655360 | tf_op jit(solution)/shard_map/all_to_all | solution.py:19
  198.1 45.7 %collective-permute-start.26 = (bf16[4,192,768]{2,1,0:T(8,128)(2,1)}, bf16[4,192,768]{2,1,0:T(8,128)(2,1)}, u32[]{:S(2)}, u32[]{:S(2)}) collective-permute-start(bf16[4,192,768]{2,1,0:T(8,128)(2,1)} %dynamic-slice_bitcast_fusion), channel_id=1, source_target_pairs={{0,1},{1,0},{2,3},{3,2},{4,5},{5,4},{6,7},{7,6},{8,9},{9,8},{10,11... | collective-permute-start | bytes 3538952 | tf_op jit(solution)/shard_map/ppermute | solution.py:72
  200.9 24.3 %collective-permute-start.16 = (bf16[192,768]{1,0:T(8,128)(2,1)}, bf16[192,768]{1,0:T(8,128)(2,1)S(1)}, u32[]{:S(2)}, u32[]{:S(2)}) collective-permute-start(bf16[192,768]{1,0:T(8,128)(2,1)} %get-tuple-element.186), channel_id=1, source_target_pairs={{0,8},{8,0},{16,24},{24,16},{1,9},{9,1},{17,25},{25,17},{2,10},{10... | collective-permute-start | bytes 884744 | tf_op jit(solution)/shard_map/ppermute | solution.py:50
  200.9 24.3 %collective-permute-start.17 = (bf16[192,768]{1,0:T(8,128)(2,1)}, bf16[192,768]{1,0:T(8,128)(2,1)S(1)}, u32[]{:S(2)}, u32[]{:S(2)}) collective-permute-start(bf16[192,768]{1,0:T(8,128)(2,1)} %get-tuple-element.185), channel_id=1, source_target_pairs={{0,16},{8,24},{16,0},{24,8},{1,17},{9,25},{17,1},{25,9},{2,18},{10... | collective-permute-start | bytes 884744 | tf_op jit(solution)/shard_map/ppermute | solution.py:50
  202.3 22.9 %collective-permute-start.18 = (bf16[192,768]{1,0:T(8,128)(2,1)}, bf16[192,768]{1,0:T(8,128)(2,1)S(1)}, u32[]{:S(2)}, u32[]{:S(2)}) collective-permute-start(bf16[192,768]{1,0:T(8,128)(2,1)} %get-tuple-element.184), channel_id=1, source_target_pairs={{0,24},{8,16},{16,8},{24,0},{1,25},{9,17},{17,9},{25,1},{2,26},{10... | collective-permute-start | bytes 884744 | tf_op jit(solution)/shard_map/ppermute | solution.py:50
  225.4 6.7 %collective-permute-start.27 = (bf16[4,24,768]{2,1,0:T(8,128)(2,1)S(1)}, bf16[4,24,768]{2,1,0:T(8,128)(2,1)S(1)}, u32[]{:S(2)}, u32[]{:S(2)}) collective-permute-start(bf16[4,24,768]{2,1,0:T(8,128)(2,1)S(1)} %dynamic-slice_bitcast_fusion.8), channel_id=1, source_target_pairs={{0,1},{1,0},{2,3},{3,2},{4,5},{5,4},{6,7},{7,6},{8,9},{9,8},{10,11... | collective-permute-start | bytes 442376 | tf_op jit(solution)/shard_map/ppermute | solution.py:72
  226.5 9.5 %collective-permute-start.19 = (bf16[256,384]{1,0:T(8,128)(2,1)S(1)}, bf16[256,384]{1,0:T(8,128)(2,1)S(1)}, u32[]{:S(2)}, u32[]{:S(2)}) collective-permute-start(bf16[256,384]{1,0:T(8,128)(2,1)S(1)} %copy-done.46), channel_id=1, source_target_pairs={{0,1},{1,0},{2,3},{3,2},{4,5},{5,4},{6,7},{7,6},{8,9},{9,8},{10,11... | collective-permute-start | bytes 589832 | tf_op jit(solution)/shard_map/ppermute | solution.py:50
  228.2 14.1 %collective-permute-start.20 = (bf16[256,384]{1,0:T(8,128)(2,1)S(1)}, bf16[256,384]{1,0:T(8,128)(2,1)S(1)}, u32[]{:S(2)}, u32[]{:S(2)}) collective-permute-start(bf16[256,384]{1,0:T(8,128)(2,1)S(1)} %copy-done.43), channel_id=1, source_target_pairs={{0,2},{1,3},{2,0},{3,1},{4,6},{5,7},{6,4},{7,5},{8,10},{9,11},{10,... | collective-permute-start | bytes 589832 | tf_op jit(solution)/shard_map/ppermute | solution.py:50
  229.7 17.9 %collective-permute-start.21 = (bf16[256,384]{1,0:T(8,128)(2,1)S(1)}, bf16[256,384]{1,0:T(8,128)(2,1)S(1)}, u32[]{:S(2)}, u32[]{:S(2)}) collective-permute-start(bf16[256,384]{1,0:T(8,128)(2,1)S(1)} %copy-done.41), channel_id=1, source_target_pairs={{0,3},{1,2},{2,1},{3,0},{4,7},{5,6},{6,5},{7,4},{8,11},{9,10},{10,... | collective-permute-start | bytes 589832 | tf_op jit(solution)/shard_map/ppermute | solution.py:50
  232.2 15.5 %collective-permute-start.22 = (bf16[256,384]{1,0:T(8,128)(2,1)S(1)}, bf16[256,384]{1,0:T(8,128)(2,1)S(1)}, u32[]{:S(2)}, u32[]{:S(2)}) collective-permute-start(bf16[256,384]{1,0:T(8,128)(2,1)S(1)} %copy-done.39), channel_id=1, source_target_pairs={{0,4},{1,5},{2,6},{3,7},{4,0},{5,1},{6,2},{7,3},{8,12},{9,13},{10,... | collective-permute-start | bytes 589832 | tf_op jit(solution)/shard_map/ppermute | solution.py:50
  236.0 25.9 %collective-permute-start.23 = (bf16[256,384]{1,0:T(8,128)(2,1)S(1)}, bf16[256,384]{1,0:T(8,128)(2,1)S(1)}, u32[]{:S(2)}, u32[]{:S(2)}) collective-permute-start(bf16[256,384]{1,0:T(8,128)(2,1)S(1)} %copy-done.38), channel_id=1, source_target_pairs={{0,5},{1,4},{2,7},{3,6},{4,1},{5,0},{6,3},{7,2},{8,13},{9,12},{10,... | collective-permute-start | bytes 589832 | tf_op jit(solution)/shard_map/ppermute | solution.py:50
  242.3 19.6 %collective-permute-start.24 = (bf16[256,384]{1,0:T(8,128)(2,1)S(1)}, bf16[256,384]{1,0:T(8,128)(2,1)S(1)}, u32[]{:S(2)}, u32[]{:S(2)}) collective-permute-start(bf16[256,384]{1,0:T(8,128)(2,1)S(1)} %copy-done.37), channel_id=1, source_target_pairs={{0,6},{1,7},{2,4},{3,5},{4,2},{5,3},{6,0},{7,1},{8,14},{9,15},{10,... | collective-permute-start | bytes 589832 | tf_op jit(solution)/shard_map/ppermute | solution.py:50
  243.8 19.5 %collective-permute-start.25 = (bf16[256,384]{1,0:T(8,128)(2,1)S(1)}, bf16[256,384]{1,0:T(8,128)(2,1)}, u32[]{:S(2)}, u32[]{:S(2)}) collective-permute-start(bf16[256,384]{1,0:T(8,128)(2,1)S(1)} %copy-done.36), channel_id=1, source_target_pairs={{0,7},{1,6},{2,5},{3,4},{4,3},{5,2},{6,1},{7,0},{8,15},{9,14},{10,... | collective-permute-start | bytes 589832 | tf_op jit(solution)/shard_map/ppermute | solution.py:50
  268.7 13.3 %collective-permute-start.30 = (bf16[3,64,768]{2,1,0:T(8,128)(2,1)}, bf16[3,64,768]{2,1,0:T(8,128)(2,1)S(1)}, u32[]{:S(2)}, u32[]{:S(2)}) collective-permute-start(bf16[3,64,768]{2,1,0:T(8,128)(2,1)} %get-tuple-element.160), channel_id=1, source_target_pairs={{0,24},{8,16},{16,8},{24,0},{1,25},{9,17},{17,9},{25,1},{2,26},{10... | collective-permute-start | bytes 884744 | tf_op jit(solution)/shard_map/ppermute | solution.py:50
  268.8 15.8 %collective-permute-start.29 = (bf16[3,64,768]{2,1,0:T(8,128)(2,1)}, bf16[3,64,768]{2,1,0:T(8,128)(2,1)S(1)}, u32[]{:S(2)}, u32[]{:S(2)}) collective-permute-start(bf16[3,64,768]{2,1,0:T(8,128)(2,1)} %get-tuple-element.159), channel_id=1, source_target_pairs={{0,16},{8,24},{16,0},{24,8},{1,17},{9,25},{17,1},{25,9},{2,18},{10... | collective-permute-start | bytes 884744 | tf_op jit(solution)/shard_map/ppermute | solution.py:50
  270.4 14.2 %collective-permute-start.28 = (bf16[3,64,768]{2,1,0:T(8,128)(2,1)}, bf16[3,64,768]{2,1,0:T(8,128)(2,1)}, u32[]{:S(2)}, u32[]{:S(2)}) collective-permute-start(bf16[3,64,768]{2,1,0:T(8,128)(2,1)} %get-tuple-element.158), channel_id=1, source_target_pairs={{0,8},{8,0},{16,24},{24,16},{1,9},{9,1},{17,25},{25,17},{2,10},{10... | collective-permute-start | bytes 884744 | tf_op jit(solution)/shard_map/ppermute | solution.py:50
  274.3 17.0 %collective-permute-start.31 = (bf16[4,4,32,576]{3,2,1,0:T(8,128)(2,1)S(1)}, bf16[4,4,32,576]{3,2,1,0:T(8,128)(2,1)S(1)}, u32[]{:S(2)}, u32[]{:S(2)}) collective-permute-start(bf16[4,4,32,576]{3,2,1,0:T(8,128)(2,1)S(1)} %dynamic-slice_bitcast_fusion.2), channel_id=1, source_target_pairs={{0,1},{1,0},{2,3},{3,2},{4,5},{5,4},{6,7},{7,6},{8,9},{9,8},{10,11... | collective-permute-start | bytes 1769480 | tf_op jit(solution)/shard_map/ppermute | solution.py:72
  276.3 22.1 %collective-permute-start.37 = (bf16[2,216,768]{2,1,0:T(8,128)(2,1)S(1)}, bf16[2,216,768]{2,1,0:T(8,128)(2,1)S(1)}, u32[]{:S(2)}, u32[]{:S(2)}) collective-permute-start(bf16[2,216,768]{2,1,0:T(8,128)(2,1)S(1)} %dynamic-slice_bitcast_fusion.1), channel_id=1, source_target_pairs={{0,2},{1,3},{2,0},{3,1},{4,6},{5,7},{6,4},{7,5},{8,10},{9,11},{10,... | collective-permute-start | bytes 1990664 | tf_op jit(solution)/shard_map/ppermute | solution.py:72
  291.5 20.9 %collective-permute-start.32 = (bf16[2,4,32,576]{3,2,1,0:T(8,128)(2,1)S(1)}, bf16[2,4,32,576]{3,2,1,0:T(8,128)(2,1)S(1)}, u32[]{:S(2)}, u32[]{:S(2)}) collective-permute-start(bf16[2,4,32,576]{3,2,1,0:T(8,128)(2,1)S(1)} %dynamic-slice_bitcast_fusion.3), channel_id=1, source_target_pairs={{0,2},{1,3},{2,0},{3,1},{4,6},{5,7},{6,4},{7,5},{8,10},{9,11},{10,... | collective-permute-start | bytes 884744 | tf_op jit(solution)/shard_map/ppermute | solution.py:72
  298.7 21.3 %collective-permute-start.38 = (bf16[1,216,768]{2,1,0:T(8,128)(2,1)S(1)}, bf16[1,216,768]{2,1,0:T(8,128)(2,1)S(1)}, u32[]{:S(2)}, u32[]{:S(2)}) collective-permute-start(bf16[1,216,768]{2,1,0:T(8,128)(2,1)S(1)} %constant_dynamic-slice_fusion.1), channel_id=1, source_target_pairs={{0,4},{1,5},{2,6},{3,7},{4,0},{5,1},{6,2},{7,3},{8,12},{9,13},{10,... | collective-permute-start | bytes 995336 | tf_op jit(solution)/shard_map/ppermute | solution.py:72
  312.6 10.8 %collective-permute-start.33 = (bf16[1,4,32,576]{3,2,1,0:T(8,128)(2,1)S(1)}, bf16[1,4,32,576]{3,2,1,0:T(8,128)(2,1)S(1)}, u32[]{:S(2)}, u32[]{:S(2)}) collective-permute-start(bf16[1,4,32,576]{3,2,1,0:T(8,128)(2,1)S(1)} %constant_dynamic-slice_fusion.2), channel_id=1, source_target_pairs={{0,4},{1,5},{2,6},{3,7},{4,0},{5,1},{6,2},{7,3},{8,12},{9,13},{10,... | collective-permute-start | bytes 442376 | tf_op jit(solution)/shard_map/ppermute | solution.py:72
  320.8 4.4 %collective-permute-start.41 = (bf16[24,768]{1,0:T(8,128)(2,1)S(1)}, bf16[24,768]{1,0:T(8,128)(2,1)S(1)}, u32[]{:S(2)}, u32[]{:S(2)}) collective-permute-start(bf16[24,768]{1,0:T(8,128)(2,1)S(1)} %get-tuple-element.199), channel_id=1, source_target_pairs={{0,24},{8,16},{16,8},{24,0},{1,25},{9,17},{17,9},{25,1},{2,26},{10... | collective-permute-start | bytes 110600 | tf_op jit(solution)/shard_map/ppermute | solution.py:50
  320.9 4.5 %collective-permute-start.40 = (bf16[24,768]{1,0:T(8,128)(2,1)S(1)}, bf16[24,768]{1,0:T(8,128)(2,1)S(1)}, u32[]{:S(2)}, u32[]{:S(2)}) collective-permute-start(bf16[24,768]{1,0:T(8,128)(2,1)S(1)} %get-tuple-element.200), channel_id=1, source_target_pairs={{0,16},{8,24},{16,0},{24,8},{1,17},{9,25},{17,1},{25,9},{2,18},{10... | collective-permute-start | bytes 110600 | tf_op jit(solution)/shard_map/ppermute | solution.py:50
  321.2 4.2 %collective-permute-start.39 = (bf16[24,768]{1,0:T(8,128)(2,1)S(1)}, bf16[24,768]{1,0:T(8,128)(2,1)S(1)}, u32[]{:S(2)}, u32[]{:S(2)}) collective-permute-start(bf16[24,768]{1,0:T(8,128)(2,1)S(1)} %get-tuple-element.201), channel_id=1, source_target_pairs={{0,8},{8,0},{16,24},{24,16},{1,9},{9,1},{17,25},{25,17},{2,10},{10... | collective-permute-start | bytes 110600 | tf_op jit(solution)/shard_map/ppermute | solution.py:50
  323.5 3.7 %collective-permute-start.36 = (bf16[32,576]{1,0:T(8,128)(2,1)S(1)}, bf16[32,576]{1,0:T(8,128)(2,1)S(1)}, u32[]{:S(2)}, u32[]{:S(2)}) collective-permute-start(bf16[32,576]{1,0:T(8,128)(2,1)S(1)} %get-tuple-element.191), channel_id=1, source_target_pairs={{0,24},{8,16},{16,8},{24,0},{1,25},{9,17},{17,9},{25,1},{2,26},{10... | collective-permute-start | bytes 110600 | tf_op jit(solution)/shard_map/ppermute | solution.py:50
  323.9 4.4 %collective-permute-start.35 = (bf16[32,576]{1,0:T(8,128)(2,1)S(1)}, bf16[32,576]{1,0:T(8,128)(2,1)S(1)}, u32[]{:S(2)}, u32[]{:S(2)}) collective-permute-start(bf16[32,576]{1,0:T(8,128)(2,1)S(1)} %get-tuple-element.192), channel_id=1, source_target_pairs={{0,16},{8,24},{16,0},{24,8},{1,17},{9,25},{17,1},{25,9},{2,18},{10... | collective-permute-start | bytes 110600 | tf_op jit(solution)/shard_map/ppermute | solution.py:50
  325.2 3.1 collective-permute-start.34
  (54 other events, 482.7 us)
Sparse Core Ops, SparseCore 0:
  49.6 114.1 all-gather.2

commit v5 on v4

--- a/solution.py
+++ b/solution.py
@@ -489,131 +489,277 @@
 QB, KB = 256, 512
 
 
-def attend_all_body(
-    blocks, groups, rows, stripe,
-    place_ref, range_ref, last_range_ref, low_ref, high_ref, last_low_ref, last_high_ref, cos_ref, sin_ref, *refs,
+def project_small_body(blocks, heads, c_ref, shift_ref, w_ref, *refs):
+    groups = len(refs) - 3
+    tokens, out_ref, last_ref, wide = refs[:groups], *refs[groups:]
+    micro, rows, width = tokens[0].shape
+    count = groups * rows
+    half, stripe = count // 2, rows // blocks
+    end = 192 * heads
+    weights = [w_ref[:, c : min(c + 128, end)] for c in range(0, end, 128)]
+    for m in range(micro):
+        a = jnp.concatenate(
+            [(x[m].astype(F32) * c_ref[m][None] + shift_ref[m][None]).astype(BF) for x in tokens], 0
+        )
+        parts = [jnp.dot(a, w, preferred_element_type=F32) for w in weights]
+        v = jnp.concatenate(parts[heads:], 1)
+        for h in range(heads):
+            pair = m * heads + h
+            own_v = v[:, h * 64 : (h + 1) * 64]
+            if pair < blocks:
+                out_ref[pair, :count] = parts[h].astype(BF)
+                out_ref[pair, count : count + half] = jnp.concatenate([own_v[:half], own_v[half:]], 1).astype(BF)
+            else:
+                wide[...] = parts[h]
+                last_ref[...] = jnp.concatenate([parts[h][:, 64:], own_v], 1).astype(BF)
+    for to in range(blocks):
+        pieces = [
+            wide[k * rows + to * stripe : k * rows + (to + 1) * stripe, :64] for k in range(groups)
+        ]
+        out_ref[to, count + half :] = jnp.concatenate(
+            [jnp.concatenate(pieces[:2], 0), jnp.concatenate(pieces[2:], 0)], 1
+        ).astype(BF)
+
+
+def pick_piece(x, k):
+    y = jnp.where((k & 1) != 0, x[8:], x[:8])
+    return jnp.where(k >= 2, y[:, 64:], y[:, :64])
+
+
+def project_back_small_body(blocks, heads, c_ref, shift_ref, w_ref, *refs):
+    wide = refs[-1]
+    few = blocks // 2
+    groups = (len(refs) - few - 5) // 2
+    tokens, in_ref, lasts = refs[:groups], refs[groups], refs[groups + 1 : groups + 1 + few]
+    outs = refs[groups + 1 + few : 2 * groups + 1 + few]
+    grad_ref, sum_ref, dot_ref = refs[2 * groups + 1 + few : -1]
+    micro, rows, width = tokens[0].shape
+    count = groups * rows
+    half, stripe = count // 2, rows // blocks
+    for j in range(blocks):
+        x = in_ref[j, count + half :].astype(F32)
+        pieces = [x[:8, :64], x[8:, :64], x[:8, 64:], x[8:, 64:]]
+        for k in range(groups):
+            wide[k * rows + j * stripe : k * rows + (j + 1) * stripe] = pieces[k]
+    all_a, all_g = [], []
+    for m in range(micro):
+        n = jnp.concatenate([x[m] for x in tokens], 0).astype(F32)
+        a = (n * c_ref[m][None] + shift_ref[m][None]).astype(BF)
+        qk, v = [], []
+        for h in range(heads):
+            pair = m * heads + h
+            if pair < blocks:
+                qk.append(in_ref[pair, :count])
+                x = in_ref[pair, count : count + half]
+                v.append(jnp.concatenate([x[:, :64], x[:, 64:]], 0))
+            else:
+                x = sum(ref[...].astype(F32) for ref in lasts).astype(BF)
+                qk.append(jnp.concatenate([wide[...].astype(BF), x[:, :64]], 1))
+                v.append(x[:, 64:])
+        g = jnp.concatenate(qk + v, 1)
+        da = lax.dot_general(g, w_ref[:, : 192 * heads], NT, preferred_element_type=F32)
+        for k in range(groups):
+            outs[k][m] = da[k * rows : (k + 1) * rows].astype(BF)
+        sum_ref[m : m + 1] = jnp.sum(da, 0, keepdims=True)
+        dot_ref[m : m + 1] = jnp.sum(da * n, 0, keepdims=True)
+        all_a.append(a)
+        all_g.append(g)
+    grad_ref[...] = lax.dot_general(
+        jnp.concatenate(all_a, 0), jnp.concatenate(all_g, 0), TN, preferred_element_type=F32
+    ).astype(BF)
+
+
+def attend_block(scores, q, low, high, first, stop, keys, values):
+    count = q.shape[0]
+
+    def score(t, top):
+        at = pl.multiple_of((first + 2 * t) * QB, QB)
+        s = lax.dot_general(keys[pl.ds(at, KB), :], q, NT, preferred_element_type=F32)
+        s = jnp.where(keys_mask(low, high, at, KB), s, NEG)
+        scores[t, :, :count] = s
+        return jnp.maximum(top, jnp.max(s, 0, keepdims=True))
+
+    steps = (stop - first + 1) // 2
+    top = lax.fori_loop(0, steps, score, jnp.full((1, count), NEG, F32))
+
+    def weigh(t, carry):
+        total, acc = carry
+        at = pl.multiple_of((first + 2 * t) * QB, QB)
+        p = jnp.exp(scores[t, :, :count] - top)
+        return total + jnp.sum(p, 0, keepdims=True), acc + lax.dot_general(
+            values[pl.ds(at, KB), :], p.astype(BF), TN, preferred_element_type=F32
+        )
+
+    total, acc = lax.fori_loop(
+        0, steps, weigh, (jnp.zeros((1, count), F32), jnp.zeros((64, count), F32))
+    )
+    return (acc / total).T, top + jnp.log(total)
+
+
+def attend_own_body(
+    blocks, groups, rows, place_ref, range_ref, low_ref, high_ref, cos_ref, sin_ref, *refs
 ):
-    ins = refs[:blocks]
-    message, q_ref, k_ref, v_ref, zq_ref, zk_ref, zv_ref, o_ref, zo_ref, lse_ref, zlse_ref = refs[blocks : blocks + 11]
-    kept, wide, scores = refs[blocks + 11 :]
+    in_ref, message, q_ref, k_ref, v_ref, o_ref, lse_ref, kept, kept_v, scores = refs
     span = blocks * rows
     size = groups * span
+    count = groups * rows
+    half = rows // 2
     me_u, me_b = place_ref[0], place_ref[1]
     for g in range(groups):
+        k = me_u ^ g
         for j in range(blocks):
-            kept[pl.ds(pl.multiple_of((me_b ^ j) * rows, rows), rows), :] = spread(ins[j], (me_u ^ g) * rows, rows)
+            to = slice(j * rows, (j + 1) * rows)
+            kept[to, :] = in_ref[j, pl.ds(pl.multiple_of(k * rows, rows), rows), :]
+            pair = in_ref[j, pl.ds(pl.multiple_of(count + (k & 1) * rows, rows), rows), :].astype(F32)
+            kept_v[to, :] = jnp.where(k >= 2, pair[:, 64:], pair[:, :64]).astype(BF)
         at = slice(g * span, (g + 1) * span)
-        cos, sin = cos_ref[at], sin_ref[at]
-        tables = turn_tables(cos, sin, True)
-        x = turn(kept[:, :128].astype(F32), tables[0])
+        x = turn(kept[...].astype(F32), turn_tables(cos_ref[at], sin_ref[at], False)[0])
         q_ref[at] = (x[:, :64] * 0.125).astype(BF)
         k_ref[at] = x[:, 64:].astype(BF)
-        v_ref[at] = kept[:, 256:320]
-        x = turn(kept[:, 128:256].astype(F32), tables[1])
-        wide[at] = x[:, :64] * 0.125
-        zk_ref[at] = x[:, 64:].astype(BF)
-        zv_ref[at] = kept[:, 320:]
+        v_ref[at] = kept_v[...]
     tail = slice(size, size + KB - QB)
-    for ref in (k_ref, v_ref, zk_ref, zv_ref):
+    for ref in (k_ref, v_ref):
         ref[tail] = jnp.zeros((KB - QB, 64), BF)
-    devices = groups * blocks
-    for d in range(0, devices, 2):
-        zq_ref[d * stripe : (d + 2) * stripe] = jnp.concatenate(
-            [spread(wide, (d + e) * rows + me_b * stripe, stripe) for e in range(2)], 0
-        ).astype(BF)
-
-    def block(q, low, high, first, stop, keys, values):
-        count = q.shape[0]
-
-        def score(t, high_s):
-            at = pl.multiple_of((first + 2 * t) * QB, QB)
-            s = lax.dot_general(keys[pl.ds(at, KB), :], q, NT, preferred_element_type=F32)
-            s = jnp.where(keys_mask(low, high, at, KB), s, NEG)
-            scores[t, :, :count] = s
-            return jnp.maximum(high_s, jnp.max(s, 0, keepdims=True))
-
-        steps = (stop - first + 1) // 2
-        top = lax.fori_loop(0, steps, score, jnp.full((1, count), NEG, F32))
-
-        def weigh(t, carry):
-            total, acc = carry
-            at = pl.multiple_of((first + 2 * t) * QB, QB)
-            p = jnp.exp(scores[t, :, :count] - top)
-            return total + jnp.sum(p, 0, keepdims=True), acc + lax.dot_general(
-                values[pl.ds(at, KB), :], p.astype(BF), TN, preferred_element_type=F32
-            )
-
-        total, acc = lax.fori_loop(
-            0, steps, weigh, (jnp.zeros((1, count), F32), jnp.zeros((64, count), F32))
-        )
-        return (acc / total).T, top + jnp.log(total)
-
-    half = rows // 2
 
     def run(i, _):
-        o, lse = block(
-            spread(q_ref, i * QB, QB), low_ref[i], high_ref[i], range_ref[2 * i], range_ref[2 * i + 1], k_ref, v_ref
+        o, lse = attend_block(
+            scores, spread(q_ref, i * QB, QB), low_ref[i], high_ref[i],
+            range_ref[2 * i], range_ref[2 * i + 1], k_ref, v_ref,
         )
         o = o.astype(BF)
         o_ref[pl.ds(pl.multiple_of(i * QB, QB), QB), :] = o
         lse_ref[i] = lse
         for d in range(QB // rows):
-            message[i * (QB // rows) + d, :half] = jnp.concatenate(
+            message[i * (QB // rows) + d] = jnp.concatenate(
                 [o[d * rows : d * rows + half], o[d * rows + half : (d + 1) * rows]], 1
             )
         return 0
 
     lax.fori_loop(0, size // QB, run, 0)
-    few = zlse_ref.shape[2]
-
-    def run_last(i, _):
-        o, lse = block(
-            spread(zq_ref, i * few, few), last_low_ref[i], last_high_ref[i],
-            last_range_ref[2 * i], last_range_ref[2 * i + 1], zk_ref, zv_ref,
-        )
-        zo_ref[pl.ds(pl.multiple_of(i * few, few), few), :] = o.astype(BF)
-        zlse_ref[i] = lse
+
+
+def stripe_tables(place_ref, cos_ref, sin_ref, wide_cos, wide_sin, devices, rows, stripe):
+    for d in range(devices):
+        at = slice(d * stripe, (d + 1) * stripe)
+        wide_cos[at] = spread(cos_ref, d * rows + place_ref[1] * stripe, stripe)
+        wide_sin[at] = spread(sin_ref, d * rows + place_ref[1] * stripe, stripe)
+    return turn_tables(wide_cos[...], wide_sin[...], True)[1]
+
+
+def attend_last_body(
+    blocks, groups, rows, stripe, place_ref, range_ref, low_ref, high_ref, cos_ref, sin_ref, *refs
+):
+    in_ref, last_ins, own_ref = refs[0], refs[1:3], refs[3]
+    message, q_ref, k_ref, v_ref, o_ref, lse_ref, kept, wide, wide_cos, wide_sin, scores = refs[4:]
+    span = blocks * rows
+    size = groups * span
+    devices = groups * blocks
+    count = groups * rows
+    half = rows // 2
+    me_u, me_b = place_ref[0], place_ref[1]
+    for g in range(groups):
+        k = me_u ^ g
+        for j in range(blocks):
+            at = (g * blocks + j) * stripe
+            wide[at : at + stripe, :64] = pick_piece(in_ref[j, count + count // 2 :].astype(F32), k)
+            to = pl.ds(pl.multiple_of((me_b ^ j) * rows, rows), rows)
+            kept[to, :] = last_ins[j & 1][j >> 1, pl.ds(pl.multiple_of(k * rows, rows), rows), :]
+        at = slice(g * span, (g + 1) * span)
+        x = turn(kept[...].astype(F32), turn_tables(cos_ref[at], sin_ref[at], True)[1])
+        k_ref[at] = x[:, :64].astype(BF)
+        v_ref[at] = kept[:, 64:]
+    tail = slice(size, size + KB - QB)
+    for ref in (k_ref, v_ref):
+        ref[tail] = jnp.zeros((KB - QB, 64), BF)
+    wide[:, 64:] = jnp.zeros((devices * stripe, 64), F32)
+    x = turn(wide[...], stripe_tables(place_ref, cos_ref, sin_ref, wide_cos, wide_sin, devices, rows, stripe))
+    q_ref[...] = (x[:, :64] * 0.125).astype(BF)
+    message[:, :half] = own_ref[...]
+    few = lse_ref.shape[2]
+
+    def run(i, _):
+        o, lse = attend_block(
+            scores, spread(q_ref, i * few, few), low_ref[i], high_ref[i],
+            range_ref[2 * i], range_ref[2 * i + 1], k_ref, v_ref,
+        )
+        o_ref[pl.ds(pl.multiple_of(i * few, few), few), :] = o.astype(BF)
+        lse_ref[i] = lse
         o = jnp.concatenate([o, jnp.zeros_like(o)], 1)
         for d in range(few // stripe):
             message[i * (few // stripe) + d, half:] = o[d * stripe : (d + 1) * stripe].astype(BF)
         return 0
 
-    lax.fori_loop(0, zlse_ref.shape[0], run_last, 0)
-
-
-def attend_all_back_body(
-    blocks, groups, rows, stripe,
-    place_ref, range_ref, last_range_ref, low_ref, high_ref, last_low_ref, last_high_ref, cos_ref, sin_ref,
-    do_ref, q_ref, k_ref, v_ref, zq_ref, zk_ref, zv_ref, o_ref, zo_ref, lse_ref, zlse_ref, *refs,
+    lax.fori_loop(0, lse_ref.shape[0], run, 0)
+
+
+def attend_block_back(q, do, o, lse, low, high, first, stop, keys, values, dk_sum, dv_sum):
+    count = q.shape[0]
+    delta = jnp.sum((do.astype(F32) * o.astype(F32)).T, 0, keepdims=True)
+
+    def step(t, dq):
+        at = pl.multiple_of((first + 2 * t) * QB, QB)
+        here = pl.ds(at, KB)
+        k, v = keys[here, :], values[here, :]
+        s = lax.dot_general(k, q, NT, preferred_element_type=F32)
+        dp = lax.dot_general(v, do, NT, preferred_element_type=F32)
+        p = jnp.where(keys_mask(low, high, at, KB), jnp.exp(s - lse), 0.0)
+        ds = (p * (dp - delta)).astype(BF)
+        dv_sum[here, :] += jnp.dot(p.astype(BF), do, preferred_element_type=F32)
+        dk_sum[here, :] += jnp.dot(ds, q, preferred_element_type=F32)
+        return dq + lax.dot_general(k, ds, TN, preferred_element_type=F32)
+
+    return (
+        lax.fori_loop(0, (stop - first + 1) // 2, step, jnp.zeros((64, count), F32)) * 0.125
+    ).T
+
+
+def attend_last_back_body(
+    blocks, groups, rows, stripe, place_ref, range_ref, low_ref, high_ref, cos_ref, sin_ref,
+    do_ref, q_ref, k_ref, v_ref, o_ref, lse_ref, dq_ref, last_ref, kept, wide_cos, wide_sin, dk, dv,
 ):
-    outs = refs[:blocks]
-    kept, dq, dk, dv, zdq, zdk, zdv = refs[blocks:]
+    span = blocks * rows
+    devices = groups * blocks
+    half = rows // 2
+    for ref in (dk, dv):
+        ref[...] = jnp.zeros(ref.shape, F32)
+    few = lse_ref.shape[2]
+    dq_ref[:, 64:] = jnp.zeros((devices * stripe, 64), F32)
+
+    def run(i, _):
+        came = [
+            do_ref[i * (few // stripe) + d].astype(F32)[half:, :64] for d in range(few // stripe)
+        ]
+        at = pl.ds(pl.multiple_of(i * few, few), few)
+        dq_ref[at, :64] = attend_block_back(
+            q_ref[at, :], jnp.concatenate(came, 0).astype(BF), o_ref[at, :], lse_ref[i],
+            low_ref[i], high_ref[i], range_ref[2 * i], range_ref[2 * i + 1], k_ref, v_ref, dk, dv,
+        )
+        return 0
+
+    lax.fori_loop(0, lse_ref.shape[0], run, 0)
+    cos, sin = stripe_tables(place_ref, cos_ref, sin_ref, wide_cos, wide_sin, devices, rows, stripe)
+    dq_ref[...] = turn(dq_ref[...], (cos, -sin))
+    for g in range(groups):
+        at = slice(g * span, (g + 1) * span)
+        k = place_ref[0] ^ g
+        cos, sin = turn_tables(cos_ref[at], sin_ref[at], True)[1]
+        x = turn(jnp.concatenate([dk[at], jnp.zeros_like(dk[at])], 1), (cos, -sin))[:, :64]
+        kept[...] = jnp.concatenate([x, dv[at]], 1).astype(BF)
+        for b in range(blocks):
+            last_ref[b, pl.ds(pl.multiple_of(k * rows, rows), rows), :] = kept[b * rows : (b + 1) * rows]
+
+
+def attend_own_back_body(
+    blocks, groups, rows, stripe, place_ref, range_ref, low_ref, high_ref, cos_ref, sin_ref,
+    do_ref, q_ref, k_ref, v_ref, o_ref, lse_ref, last_dq_ref, out_ref, kept, kept_v, wide_v, dq, dk, dv,
+):
     span = blocks * rows
     size = groups * span
+    count = groups * rows
     half = rows // 2
     me_u, me_b = place_ref[0], place_ref[1]
-    for ref in (dk, dv, zdq, zdk, zdv):
-        ref[...] = jnp.zeros_like(ref)
-
-    def block(q, do, o, lse, low, high, first, stop, keys, values, dk_sum, dv_sum):
-        count = q.shape[0]
-        delta = jnp.sum((do.astype(F32) * o.astype(F32)).T, 0, keepdims=True)
-
-        def step(t, dq):
-            at = pl.multiple_of((first + 2 * t) * QB, QB)
-            here = pl.ds(at, KB)
-            k, v = keys[here, :], values[here, :]
-            s = lax.dot_general(k, q, NT, preferred_element_type=F32)
-            dp = lax.dot_general(v, do, NT, preferred_element_type=F32)
-            p = jnp.where(keys_mask(low, high, at, KB), jnp.exp(s - lse), 0.0)
-            ds = (p * (dp - delta)).astype(BF)
-            dv_sum[here, :] += jnp.dot(p.astype(BF), do, preferred_element_type=F32)
-            dk_sum[here, :] += jnp.dot(ds, q, preferred_element_type=F32)
-            return dq + lax.dot_general(k, ds, TN, preferred_element_type=F32)
-
-        return (
-            lax.fori_loop(0, (stop - first + 1) // 2, step, jnp.zeros((64, count), F32)) * 0.125
-        ).T
+    for ref in (dk, dv):
+        ref[...] = jnp.zeros(ref.shape, F32)
 
     def run(i, _):
         came = []
@@ -621,39 +767,32 @@
             x = do_ref[i * (QB // rows) + d]
             came += [x[:half, :64], x[:half, 64:]]
         at = pl.ds(pl.multiple_of(i * QB, QB), QB)
-        dq[at, :] = block(
+        dq[at, :] = attend_block_back(
             q_ref[at, :], jnp.concatenate(came, 0), o_ref[at, :], lse_ref[i], low_ref[i], high_ref[i],
             range_ref[2 * i], range_ref[2 * i + 1], k_ref, v_ref, dk, dv,
         )
         return 0
 
     lax.fori_loop(0, size // QB, run, 0)
-    few = zlse_ref.shape[2]
-
-    def run_last(i, _):
-        came = [
-            do_ref[i * (few // stripe) + d].astype(F32)[half:, :64] for d in range(few // stripe)
-        ]
-        at = pl.ds(pl.multiple_of(i * few, few), few)
-        x = block(
-            zq_ref[at, :], jnp.concatenate(came, 0).astype(BF), zo_ref[at, :], zlse_ref[i],
-            last_low_ref[i], last_high_ref[i], last_range_ref[2 * i], last_range_ref[2 * i + 1],
-            zk_ref, zv_ref, zdk, zdv,
-        )
-        for d in range(few // stripe):
-            to = (i * (few // stripe) + d) * rows + me_b * stripe
-            zdq[pl.ds(pl.multiple_of(to, stripe), stripe), :] = x[d * stripe : (d + 1) * stripe]
-        return 0
-
-    lax.fori_loop(0, zlse_ref.shape[0], run_last, 0)
     for g in range(groups):
         at = slice(g * span, (g + 1) * span)
-        tables = [(c, -s) for c, s in turn_tables(cos_ref[at], sin_ref[at], True)]
-        kept[:, :128] = turn(jnp.concatenate([dq[at], dk[at]], 1), tables[0]).astype(BF)
-        kept[:, 128:256] = turn(jnp.concatenate([zdq[at], zdk[at]], 1), tables[1]).astype(BF)
-        kept[:, 256:] = jnp.concatenate([dv[at], zdv[at]], 1).astype(BF)
-        for j in range(blocks):
-            outs[j][pl.ds(pl.multiple_of((me_u ^ g) * rows, rows), rows), :] = spread(kept, (me_b ^ j) * rows, rows)
+        k = me_u ^ g
+        cos, sin = turn_tables(cos_ref[at], sin_ref[at], False)[0]
+        kept[...] = turn(jnp.concatenate([dq[at], dk[at]], 1), (cos, -sin)).astype(BF)
+        kept_v[...] = dv[at].astype(BF)
+        for b in range(blocks):
+            out_ref[b, pl.ds(pl.multiple_of(k * rows, rows), rows), :] = kept[b * rows : (b + 1) * rows]
+        for b in range(blocks):
+            wide_v[g * blocks + b] = kept_v[b * rows : (b + 1) * rows]
+    for to in range(blocks):
+        v = [wide_v[(me_u ^ k) * blocks + to] for k in range(groups)]
+        out_ref[to, count : count + count // 2] = jnp.concatenate(
+            [jnp.concatenate(v[:2], 0), jnp.concatenate(v[2:], 0)], 1
+        )
+        z = [spread(last_dq_ref, ((me_u ^ k) * blocks + to) * stripe, stripe)[:, :64] for k in range(groups)]
+        out_ref[to, count + count // 2 :] = jnp.concatenate(
+            [jnp.concatenate(z[:2], 0), jnp.concatenate(z[2:], 0)], 1
+        ).astype(BF)
 
 
 def on_device(
@@ -693,10 +832,6 @@
     place = jnp.stack([group_id, block_id]).astype(jnp.int32)
     pair_micro = jnp.minimum(block_id // heads, micro - 1)
 
-    values = tokens.astype(F32)
-    n1, r1 = norm(values)
-    n1_b = n1.astype(BF)
-    n1_group = swap([n1_b] * groups, "ulysses")
     in_split = input_weight.reshape(gain_rows, 3, groups, heads, head_width)
     in_split = jnp.concatenate(
         [
@@ -711,31 +846,40 @@
     mod_own = jnp.einsum(
         "mc,fc->mf", condition, modulate_weight, preferred_element_type=F32
     ) + modulate_bias.astype(F32)
+    mod_lanes = 64 * -(-mod_rows // 64)
+    mod_own = jnp.pad(mod_own, ((0, 0), (0, mod_lanes - mod_rows))).reshape(-1, 64)
+    mod_high = lax.reduce_precision(mod_own, 8, 7)
+    mod_size = mod_own.shape[0]
+    vectors = jnp.pad(
+        jnp.stack([attend_gain, feed_gain, reduce_bias]), ((0, 0), (0, 64 - gain_rows))
+    )
+    ff_lanes = 64 * -(-ff_rows // 64)
     small = jnp.concatenate(
         [
-            mod_own.reshape(-1),
-            attend_gain.astype(F32),
-            feed_gain.astype(F32),
-            reduce_bias.astype(F32),
-            expand_bias.astype(F32),
-        ]
-    )
-    small_lanes = 64 * -(-small.shape[0] // (32 * gain_rows))
-    small = jnp.pad(small, (0, small_lanes * gain_rows // 2 - small.shape[0]))
-    small_high = small.astype(BF)
-    small_low = (small - lax.reduce_precision(small, 8, 7)).astype(BF)
-    small = jnp.concatenate([small_high, small_low]).reshape(1, 1, gain_rows, small_lanes)
-    came = exchange(
-        jnp.concatenate(
-            [
-                jnp.broadcast_to(in_split, (groups, blocks) + in_split.shape[2:]),
-                jnp.broadcast_to(small, (groups, blocks) + small.shape[2:]),
-            ],
-            3,
-        ).reshape(devices, gain_rows, in_lanes + small_lanes)
-    )
-    small_all = came[:, :, in_lanes:].astype(F32).reshape(devices, 2, -1)
-    small_all = small_all[:, 0] + small_all[:, 1]
+            mod_high.astype(BF),
+            (mod_own - mod_high).astype(BF),
+            vectors,
+            jnp.pad(expand_bias, (0, ff_lanes - ff_rows)).reshape(-1, 64),
+        ],
+        0,
+    )
+    small_lanes = 64 * -(-small.shape[0] // gain_rows)
+    small = jnp.pad(small, ((0, small_lanes * gain_rows // 64 - small.shape[0]), (0, 0)))
+    small = small.reshape(1, 1, gain_rows, small_lanes)
+    in_message = jnp.concatenate(
+        [
+            jnp.broadcast_to(in_split, (groups, blocks) + in_split.shape[2:]),
+            jnp.broadcast_to(small, (groups, blocks) + small.shape[2:]),
+        ],
+        3,
+    ).reshape(devices, gain_rows, in_lanes + small_lanes)
+    in_message, tokens, lengths = lax.optimization_barrier((in_message, tokens, lengths))
+    came = exchange(in_message)
+    values = tokens.astype(F32)
+    n1, r1 = norm(values)
+    n1_b = n1.astype(BF)
+    n1_group = swap([n1_b] * groups, "ulysses")
+    small_all = came[:, :, in_lanes:].reshape(devices, -1, 64)
     in_own = came.reshape(width, in_lanes + small_lanes)
 
     weight_pack = jnp.concatenate(
@@ -746,38 +890,6 @@
             ],
             0,
         )
-    weight_pack, in_own, small_all, n1_group = lax.optimization_barrier(
-        (weight_pack, in_own, small_all, n1_group)
-    )
-    gathered = lax.all_gather(weight_pack, ALL, axis=0, tiled=False)
-    unit = gain_rows
-    while unit % 8:
-        unit *= 2
-    units = width // unit
-    if unit != gain_rows:
-        gathered = jnp.concatenate(
-            [gathered[:, :ff_rows].reshape(units, -1, width)]
-            + [
-                gathered[:, at : at + gain_rows].reshape(units, unit, width)
-                for at in range(ff_rows, ff_rows + (folds + 1) * gain_rows, gain_rows)
-            ],
-            1,
-        )
-    wide = unit * folds
-
-    at = micro * mod_rows
-    mods = small_all[:, :at].reshape(devices, micro, mod_rows).transpose(1, 0, 2).reshape(micro, -1)
-    gain1 = small_all[:, at : at + gain_rows].reshape(-1)
-    at += gain_rows
-    gain2 = small_all[:, at : at + gain_rows].reshape(-1)
-    at += gain_rows
-    reduce_bias_f = small_all[:, at : at + gain_rows].reshape(1, -1)
-    at += gain_rows
-    expand_bias_f = small_all[:, at : at + ff_rows].reshape(folds, 1, width)
-    shift1, scale1, gate1, shift2, scale2, gate2 = jnp.split(mods, 6, 1)
-    c1 = gain1 * (1.0 + scale1)
-    c2 = gain2 * (1.0 + scale2)
-
     index = jnp.arange(size, dtype=jnp.int32)
     pair_lengths = lax.dynamic_index_in_dim(lengths, pair_micro, 0, keepdims=False)
     segment, position = doc_layout(index, pair_lengths)
@@ -795,33 +907,14 @@
     key_block = math.gcd(size, 256)
     first = jnp.arange(size // query_rows, dtype=jnp.int32) * query_rows
     ranges = key_ranges(first, first + query_rows - 1, pair_lengths, key_block)
-    small_path = extra and size % KB == 0 and rows % 16 == 0 and stripe % 8 == 0 and size <= 4096
-
-    count = groups * rows
+    small_path = extra and size % KB == 0 and rows == 64 and stripe == 8 and groups == 4 and size <= 4096
+
     striped = lambda x: lax.dynamic_slice_in_dim(
         x.reshape((devices, rows) + x.shape[1:]), block_id * stripe, stripe, 1
     ).reshape((devices * stripe,) + x.shape[1:])
-    smem = pl.BlockSpec(memory_space=pltpu.SMEM)
-    outgoing = pl.pallas_call(
-        functools.partial(project_body, blocks, pairs, heads, extra),
-        out_shape=[jax.ShapeDtypeStruct((count, lanes), BF)] * blocks,
-        in_specs=[smem] + [whole_vmem()] * (3 + groups),
-        out_specs=[whole_vmem()] * blocks,
-        scratch_shapes=[pltpu.VMEM((blocks, count, lanes), BF)],
-        cost_estimate=pl.CostEstimate(
-            flops=2 * micro * count * width * 3 * 64 * heads, transcendentals=0, bytes_accessed=8 * own * width
-        ),
-        name="project",
-    )(place, c1, shift1, in_own, *n1_group)
-    incoming = swap(outgoing, "blk")
-
-    span = blocks * rows
-    by_span = pl.BlockSpec((span, 64), lambda i, p: (i ^ p[0], 0))
-    table_spec = pl.BlockSpec((span, 128), lambda i, p: (i ^ p[0], 0))
-    by_rows = pl.BlockSpec((rows, lanes), lambda i, p: (i, 0))
-    parts = 6 if extra else 3
+    last_ranges = bounds = 0
     if small_path:
-        last_rows = 128
+        last_rows = min(256, devices * stripe)
         chunk = last_rows // stripe
         last_first = jnp.arange(devices // chunk, dtype=jnp.int32) * (chunk * rows) + block_id * stripe
         last_ranges = key_ranges(
@@ -836,30 +929,116 @@
             ends = jnp.cumsum(lens)
             high = jnp.min(jnp.where(ends[None, :] > index[:, None], ends[None, :], 1 << 30), 1)
             bounds += [pick(low).reshape(-1, 1, lump), pick(high).reshape(-1, 1, lump)]
+    in_own, small_all, n1_group, place, cos_table, sin_table, ranges, last_ranges, bounds = (
+        lax.optimization_barrier(
+            (in_own, small_all, n1_group, place, cos_table, sin_table, ranges, last_ranges, bounds)
+        )
+    )
+    weight_pack, in_own = lax.optimization_barrier((weight_pack, in_own))
+    gathered = lax.all_gather(weight_pack, ALL, axis=0, tiled=False)
+    unit = gain_rows
+    while unit % 8:
+        unit *= 2
+    units = width // unit
+    if unit != gain_rows:
+        gathered = jnp.concatenate(
+            [gathered[:, :ff_rows].reshape(units, -1, width)]
+            + [
+                gathered[:, at : at + gain_rows].reshape(units, unit, width)
+                for at in range(ff_rows, ff_rows + (folds + 1) * gain_rows, gain_rows)
+            ],
+            1,
+        )
+    wide = unit * folds
+
+    mods = small_all[:, :mod_size].astype(F32) + small_all[:, mod_size : 2 * mod_size].astype(F32)
+    mods = mods.reshape(devices, micro, mod_lanes)[:, :, :mod_rows].transpose(1, 0, 2).reshape(micro, -1)
+    at = 2 * mod_size
+    vectors = small_all[:, at : at + 3, :gain_rows].astype(F32).transpose(1, 0, 2).reshape(3, width)
+    gain1, gain2, reduce_bias_f = vectors[0], vectors[1], vectors[2:]
+    at += 3
+    expand_bias_f = small_all[:, at : at + ff_lanes // 64].reshape(devices, ff_lanes)[:, :ff_rows]
+    expand_bias_f = expand_bias_f.astype(F32).reshape(folds, 1, width)
+    shift1, scale1, gate1, shift2, scale2, gate2 = jnp.split(mods, 6, 1)
+    c1 = gain1 * (1.0 + scale1)
+    c2 = gain2 * (1.0 + scale2)
+
+    count = groups * rows
+    smem = pl.BlockSpec(memory_space=pltpu.SMEM)
+    message_rows = count + count // 2 + 16
+    if small_path:
+        outgoing, last_own = pl.pallas_call(
+            functools.partial(project_small_body, blocks, heads),
+            out_shape=[
+                jax.ShapeDtypeStruct((blocks, message_rows, 128), BF), jax.ShapeDtypeStruct((count, 128), BF),
+            ],
+            in_specs=[whole_vmem()] * (3 + groups),
+            out_specs=[whole_vmem()] * 2,
+            scratch_shapes=[pltpu.VMEM((count, 128), F32)],
+            cost_estimate=pl.CostEstimate(
+                flops=2 * micro * count * width * 3 * 64 * heads, transcendentals=0, bytes_accessed=8 * own * width
+            ),
+            name="project",
+        )(c1, shift1, in_own, *n1_group)
+        incoming = [lax.all_to_all(outgoing, "blk", split_axis=0, concat_axis=0, tiled=True)]
+        pass_on = lambda x, bit: lax.ppermute(x, "blk", [(i, i ^ bit) for i in range(blocks)])
+        last_four = jnp.stack([last_own] + [pass_on(last_own, bit) for bit in range(2, blocks, 2)])
+        last_keys = [last_four, pass_on(last_four, 1)]
+    else:
+        outgoing = pl.pallas_call(
+            functools.partial(project_body, blocks, pairs, heads, extra),
+            out_shape=[jax.ShapeDtypeStruct((count, lanes), BF)] * blocks,
+            in_specs=[smem] + [whole_vmem()] * (3 + groups),
+            out_specs=[whole_vmem()] * blocks,
+            scratch_shapes=[pltpu.VMEM((blocks, count, lanes), BF)],
+            name="project",
+        )(place, c1, shift1, in_own, *n1_group)
+        incoming = swap(outgoing, "blk")
+
+    span = blocks * rows
+    by_span = pl.BlockSpec((span, 64), lambda i, p: (i ^ p[0], 0))
+    table_spec = pl.BlockSpec((span, 128), lambda i, p: (i ^ p[0], 0))
+    by_rows = pl.BlockSpec((rows, lanes), lambda i, p: (i, 0))
+    parts = 6 if extra else 3
+    if small_path:
         whole = lambda *shape: jax.ShapeDtypeStruct(shape, BF)
-        saved_shapes = [
-            whole(size, 64), whole(size + KB - QB, 64), whole(size + KB - QB, 64),
-            whole(devices * stripe, 64), whole(size + KB - QB, 64), whole(size + KB - QB, 64),
-            whole(size, 64), whole(devices * stripe, 64),
-            jax.ShapeDtypeStruct(bounds[0].shape, F32), jax.ShapeDtypeStruct(bounds[2].shape, F32),
-        ]
-        attend_args = (place, ranges, last_ranges, *bounds, cos_table, sin_table)
-        specs = [smem] * 3 + [whole_vmem()] * 6
-        message, *saved = pl.pallas_call(
-            functools.partial(attend_all_body, blocks, groups, rows, stripe),
-            in_specs=specs + [whole_vmem()] * blocks,
-            out_specs=[whole_vmem()] * 11,
-            out_shape=[whole(devices, rows // 2 + stripe, 128)] + saved_shapes,
+        f32 = lambda *shape: jax.ShapeDtypeStruct(shape, F32)
+        padded = whole(size + KB - QB, 64)
+        own_args = (place, ranges, *bounds[:2], cos_table, sin_table)
+        last_args = (place, last_ranges, *bounds[2:], cos_table, sin_table)
+        specs = [smem] * 2 + [whole_vmem()] * 4
+        own_message, *own_saved = pl.pallas_call(
+            functools.partial(attend_own_body, blocks, groups, rows),
+            in_specs=specs + [whole_vmem()],
+            out_specs=[whole_vmem()] * 6,
+            out_shape=[
+                whole(devices, rows // 2, 128), whole(size, 64), padded, padded, whole(size, 64), f32(*bounds[0].shape),
+            ],
             scratch_shapes=[
-                pltpu.VMEM((span, lanes), BF),
-                pltpu.VMEM((size, 64), F32),
+                pltpu.VMEM((span, 128), BF), pltpu.VMEM((span, 64), BF),
                 pltpu.VMEM((size // KB + 1, KB, QB), F32),
             ],
             cost_estimate=pl.CostEstimate(
                 flops=size * size * 64, transcendentals=size * size // 2, bytes_accessed=16 * size * 128
             ),
-            name="attend_all",
-        )(*attend_args, *incoming)
+            name="attend_own",
+        )(*own_args, *incoming)
+        message, *last_saved = pl.pallas_call(
+            functools.partial(attend_last_body, blocks, groups, rows, stripe),
+            in_specs=specs + [whole_vmem()] * 4,
+            out_specs=[whole_vmem()] * 6,
+            out_shape=[
+                whole(devices, rows // 2 + stripe, 128), whole(devices * stripe, 64), padded, padded,
+                whole(devices * stripe, 64), f32(*bounds[2].shape),
+            ],
+            scratch_shapes=[pltpu.VMEM((span, 128), BF)]
+            + [pltpu.VMEM((devices * stripe, 128), F32)] * 3
+            + [pltpu.VMEM((size // KB + 1, KB, last_rows), F32)],
+            cost_estimate=pl.CostEstimate(
+                flops=size * size * 16, transcendentals=size * size // 8, bytes_accessed=16 * size * 64
+            ),
+            name="attend_last",
+        )(*last_args, *incoming, *last_keys, own_message)
     else:
         assert not extra
         turned = pl.pallas_call(
@@ -984,20 +1163,36 @@
     feed_half = halve(feed_part, "blk", block_id, 1)
 
     if small_path:
+        last_dq, last_leaving = pl.pallas_call(
+            functools.partial(attend_last_back_body, blocks, groups, rows, stripe),
+            in_specs=specs + [whole_vmem()] * 6,
+            out_specs=[whole_vmem()] * 2,
+            out_shape=[f32(devices * stripe, 128), whole(blocks, count, 128)],
+            scratch_shapes=[pltpu.VMEM((span, 128), BF)]
+            + [pltpu.VMEM((devices * stripe, 128), F32)] * 2
+            + [pltpu.VMEM((size + KB - QB, 64), F32)] * 2,
+            cost_estimate=pl.CostEstimate(
+                flops=size * size * 32, transcendentals=size * size // 8, bytes_accessed=16 * size * 64
+            ),
+            name="attend_last_back",
+        )(*last_args, do_came, *last_saved)
+        last_half = halve(last_leaving, "blk", block_id, 1)
+        do_came, last_dq = lax.optimization_barrier((do_came, last_dq))
         leaving = pl.pallas_call(
-            functools.partial(attend_all_back_body, blocks, groups, rows, stripe),
-            in_specs=specs + [whole_vmem()] * 11,
-            out_specs=[whole_vmem()] * blocks,
-            out_shape=[whole(count, lanes)] * blocks,
-            scratch_shapes=[pltpu.VMEM((span, lanes), BF), pltpu.VMEM((size, 64), F32)]
-            + [pltpu.VMEM((size + KB - QB, 64), F32)] * 2
-            + [pltpu.VMEM((size, 64), F32)]
+            functools.partial(attend_own_back_body, blocks, groups, rows, stripe),
+            in_specs=specs + [whole_vmem()] * 7,
+            out_specs=whole_vmem(),
+            out_shape=whole(blocks, message_rows, 128),
+            scratch_shapes=[
+                pltpu.VMEM((span, 128), BF), pltpu.VMEM((span, 64), BF),
+                pltpu.VMEM((devices, rows, 64), BF), pltpu.VMEM((size, 64), F32),
+            ]
             + [pltpu.VMEM((size + KB - QB, 64), F32)] * 2,
             cost_estimate=pl.CostEstimate(
                 flops=2 * size * size * 64, transcendentals=size * size // 2, bytes_accessed=16 * size * 128
             ),
-            name="attend_all_back",
-        )(*attend_args, do_came, *saved)
+            name="attend_own_back",
+        )(*own_args, do_came, *own_saved, last_dq)
     else:
         grads = attend_back(
             ranges, query, segment, lse, attended, do_came.reshape(size, head_width), key, value,
@@ -1015,28 +1210,49 @@
             out_shape=[jax.ShapeDtypeStruct((count, lanes), BF)] * blocks,
             name="rotate_out",
         )(place, cos_table, sin_table, *grads)
-    leaving, output_part = lax.optimization_barrier((leaving, output_part))
-    back = swap(leaving, "blk")
+    if small_path:
+        leaving, last_half, output_part = lax.optimization_barrier((leaving, last_half, output_part))
+        back = [lax.all_to_all(leaving, "blk", split_axis=0, concat_axis=0, tiled=True)]
+        back += [
+            pass_on(lax.dynamic_index_in_dim(last_half, (block_id // 2) ^ k, 0, keepdims=False), 2 * k)
+            if k
+            else lax.dynamic_index_in_dim(last_half, block_id // 2, 0, keepdims=False)
+            for k in range(blocks // 2)
+        ]
+    else:
+        leaving, output_part = lax.optimization_barrier((leaving, output_part))
+        back = swap(leaving, "blk")
     output_part = sum(x.astype(F32) for x in output_part).astype(BF).reshape(blocks, gain_rows, width)
     output_part = halve(output_part, "blk", block_id, 1)
-    back, feed_half, output_part = lax.optimization_barrier((back, feed_half, output_part))
-
+    weight_sum = halve(feed_half, "blk", block_id, 2)
+    back, weight_sum, output_part = lax.optimization_barrier((back, weight_sum, output_part))
+    output_part = halve(output_part, "blk", block_id, 2)
+    weight_sum, weight_bit = jnp.concatenate([weight_sum, output_part], 1), 4
+
+    if small_path:
+        back_body = functools.partial(project_back_small_body, blocks, heads)
+        back_scratch = [pltpu.VMEM((count, 64), F32)]
+        back_args, back_specs = (), []
+    else:
+        back_args, back_specs = (place,), [smem]
+        back_body = functools.partial(project_back_body, blocks, pairs, heads, extra)
+        back_scratch = [pltpu.VMEM((blocks, count, lanes), BF)]
     returned = pl.pallas_call(
-        functools.partial(project_back_body, blocks, pairs, heads, extra),
+        back_body,
         out_shape=[jax.ShapeDtypeStruct((micro, rows, width), BF)] * groups
         + [
             jax.ShapeDtypeStruct((width, heads * 3 * head_width), BF),
             jax.ShapeDtypeStruct((micro, width), F32),
             jax.ShapeDtypeStruct((micro, width), F32),
         ],
-        in_specs=[smem] + [whole_vmem()] * (3 + groups + blocks),
+        in_specs=back_specs + [whole_vmem()] * (3 + groups + len(back)),
         out_specs=[whole_vmem()] * (groups + 3),
-        scratch_shapes=[pltpu.VMEM((blocks, count, lanes), BF)],
+        scratch_shapes=back_scratch,
         cost_estimate=pl.CostEstimate(
             flops=4 * micro * count * width * 3 * 64 * heads, transcendentals=0, bytes_accessed=8 * own * width
         ),
         name="project_back",
-    )(place, c1, shift1, in_own, *n1_group, *back)
+    )(*back_args, c1, shift1, in_own, *n1_group, *back)
     input_part, d_shift1, p1 = returned[groups:]
     grad_first = sum(x.astype(F32) for x in swap(returned[:groups], "ulysses"))
     e = grad_first * c1[:, None]
@@ -1069,19 +1285,20 @@
     taken = small_parts.shape[1]
     small_rows = 8 * -(-taken // (8 * in_lanes))
     small_parts = jnp.pad(small_parts, ((0, 0), (0, small_rows * in_lanes - taken)))
-    input_part = jnp.concatenate(
-        [
-            input_part.reshape(groups, blocks, gain_rows, in_lanes),
-            small_parts.reshape(groups, blocks, small_rows, in_lanes),
-        ],
-        2,
-    ).transpose(1, 0, 2, 3)
-    input_sum = halve(input_part, "blk", block_id, 1)
-    weight_sum, bit = jnp.concatenate([feed_half, output_part], 1), 2
+    input_sum = halve(
+        input_part.reshape(groups, blocks, gain_rows, in_lanes).transpose(1, 0, 2, 3), "blk", block_id, 1
+    )
+    small_parts = halve(
+        small_parts.reshape(groups, blocks, small_rows, in_lanes).transpose(1, 0, 2, 3), "blk", block_id, 1
+    )
+    input_sum = jnp.concatenate([input_sum, small_parts], 2)
+    bit = 2
     while bit < blocks:
-        weight_sum = halve(weight_sum, "blk", block_id, bit)
         input_sum = halve(input_sum, "blk", block_id, bit)
         bit *= 2
+    while weight_bit < blocks:
+        weight_sum = halve(weight_sum, "blk", block_id, weight_bit)
+        weight_bit *= 2
     weight_sum, input_sum = weight_sum[0], input_sum[0]
     final = jnp.stack(
         swap(

time: 340 us -> 333 us (0.979)
  starting transfers between devices: 83.5 us -> 54.1 us
  waiting for transfers between devices: 119 us -> 131 us
  Pallas kernels: 69.9 us -> 78.1 us
    ppermute x35 -> x21, waiting for transfers between devices: 51.9 us -> 6.04 us  [swap(): lax.ppermute(x, axis, [(i, i ^ k) for i in range(size)])]
    ppermute x0 -> x7, waiting for transfers between devices: none -> 44.8 us  [on_device(): lax.ppermute(x, 'blk', [(i, i ^ bit) for i in range(blocks)])]
    ppermute x7 -> x10, waiting for transfers between devices: 25.2 us -> 53.9 us  [halve(): came = lax.ppermute(sent, axis, [(i, i ^ bit) for i in range(size)])]
    ppermute x35 -> x21, starting transfers between devices: 35.9 us -> 14.6 us  [swap(): lax.ppermute(x, axis, [(i, i ^ k) for i in range(size)])]
    all_to_all x3, starting transfers between devices: 28.5 us -> 12.2 us  [exchange(): return lax.all_to_all(x, ALL, split_axis=0, concat_axis=0, tiled=True)]
    all_to_all x3, waiting for transfers between devices: 37.5 us -> 24.5 us  [exchange(): return lax.all_to_all(x, ALL, split_axis=0, concat_axis=0, tiled=True)]
    ppermute x7 -> x10, starting transfers between devices: 19.1 us -> 8.02 us  [halve(): came = lax.ppermute(sent, axis, [(i, i ^ bit) for i in range(size)])]
    ppermute x0 -> x7, starting transfers between devices: none -> 9.9 us  [on_device(): lax.ppermute(x, 'blk', [(i, i ^ bit) for i in range(blocks)])]
  transfers between devices with their start and end apart: 46 -> 44, of which waited for: 16 -> 17; matrix products, arithmetic and copies ran while one was open for 10% -> 11% of each run, Pallas kernels for 19% -> 22%
where the time goes in v5:
time: 333 us; the launch traced here: 332 us
  waiting for transfers between devices  131 us (39%)
  Pallas kernels  78.1 us (23%)
  starting transfers between devices  54.1 us (16%)
  other arithmetic  28.4 us (9%)
  local copies, waits for them, and re-layouts  20.5 us (6%)
  between operations  18.5 us (6%)
    ppermute x10, waiting for transfers between devices, halve(): came = lax.ppermute(sent, axis, [(i, i ^ bit) for i in range(size)])  53.9 us
    ppermute x7, waiting for transfers between devices, on_device(): lax.ppermute(x, 'blk', [(i, i ^ bit) for i in range(blocks)])  44.8 us
    all_to_all x3, waiting for transfers between devices, exchange(): return lax.all_to_all(x, ALL, split_axis=0, concat_axis=0, tiled=True)  24.5 us
    pallas_call x1, Pallas kernels, on_device(): pl.pallas_call(functools.partial(attend_own_body, blocks, groups, rows),...  15.8 us
    pallas_call x1, Pallas kernels, on_device(): pl.pallas_call(functools.partial(attend_own_back_body, blocks, groups, ro...  14.8 us
    ppermute x21, starting transfers between devices, swap(): lax.ppermute(x, axis, [(i, i ^ k) for i in range(size)])  14.6 us
    all_to_all x3, starting transfers between devices, exchange(): return lax.all_to_all(x, ALL, split_axis=0, concat_axis=0, tiled=True)  12.2 us
    pallas_call x1, Pallas kernels, on_device(): pl.pallas_call(functools.partial(feed_body, *sizes), grid=(folds,), in_sp...  11.5 us
  transfers between devices with their start and end apart: 44, of which 17 were waited for; matrix products, arithmetic and copies ran while one was open for 11% of the time, Pallas kernels for 22%

profile of v5, /device:TPU:0, one launch (start us, length us, event | category | flops | bytes accessed | tf_op | source)
XLA Modules:
  0.0 331.9 jit_solution(5153581822012267825)
XLA Ops:
  7.2 1.1 reshape.563
  14.5 2.6 collective-permute-start.1
  17.1 6.1 %all-to-all-start = ((bf16[32,24,640]{2,1,0:T(8,128)(2,1)}), bf16[32,24,640]{2,1,0:T(8,128)(2,1)S(1)}, u32[]{:S(2)}, u32[]{:S(2)}) async-start(bf16[32,24,640]{2,1,0:T(8,128)(2,1)} %bitcast.9), calls=%async_computation | async-start | bytes 1966080 | tf_op jit(solution)/shard_map/all_to_all | solution.py:19
  31.3 5.7 %sine_multiply_fusion = (f32[2048,128]{1,0:T(8,128)}, f32[2048,128]{1,0:T(8,128)}) fusion(f32[128]{0:T(128)S(1)} %compare_select_fusion.2, f32[128]{0:T(128)S(1)} %mul.164, f32[2048]{0:T(1024)S(1)} %subtract_convert_fusion, f32[2048]{0:T(1024)S(1)} %subtract_convert_fusion.1, pred[128]{0:T(512)(128)(4,1)S(1)} %iota_compare_fusion.7), kind=kLoop, calls=%fused_computation.8 | loop fusion | flops 786432 | bytes 2114688 | tf_op jit(solution)/shard_map/mul | solution.py:905
  38.9 10.4 %all-to-all-done = bf16[32,24,640]{2,1,0:T(8,128)(2,1)S(1)} async-done(((bf16[32,24,640]{2,1,0:T(8,128)(2,1)}), bf16[32,24,640]{2,1,0:T(8,128)(2,1)S(1)}, u32[]{:S(2)}, u32[]{:S(2)}) %all-to-all-start) | async-done | bytes 983072 | tf_op jit(solution)/shard_map/all_to_all | solution.py:19
  51.0 4.2 %project.1 = (bf16[8,400,128]{2,1,0:T(8,128)(2,1)}, bf16[256,128]{1,0:T(8,128)(2,1)}) custom-call(f32[3,768]{1,0:T(4,128)} %get-tuple-element.204.c_ref, f32[3,768]{1,0:T(4,128)} %get-tuple-element.203.shift_ref, bf16[768,640]{1,0:T(8,128)(2,1)} %bitcast.235, bf16[3,64,768]{2,1,0:T(8,128)(2,1)} %copy-done.16, bf16[3,64,768]{2,1,0:T(8,128)(2,1)} %copy-done.36, ...), custom_call_target="tpu_custom_call" | custom-call | flops 679477248 | bytes 1179648 | tf_op jit(solution)/shard_map/project/pallas_call | solution.py:970
  55.2 3.7 %all-to-all-start.1 = ((bf16[8,400,128]{2,1,0:T(8,128)(2,1)}), bf16[8,400,128]{2,1,0:T(8,128)(2,1)S(1)}, u32[]{:S(2)}, u32[]{:S(2)}) async-start(bf16[8,400,128]{2,1,0:T(8,128)(2,1)} %get-tuple-element.102), calls=%async_computation.1 | async-start | bytes 1638400 | tf_op jit(solution)/shard_map/all_to_all | solution.py:983
  58.9 3.7 %collective-permute-start.5 = (bf16[256,128]{1,0:T(8,128)(2,1)S(1)}, bf16[256,128]{1,0:T(8,128)(2,1)S(1)}, u32[]{:S(2)}, u32[]{:S(2)}) collective-permute-start(bf16[256,128]{1,0:T(8,128)(2,1)S(1)} %copy-done.28), channel_id=1, source_target_pairs={{0,6},{1,7},{2,4},{3,5},{4,2},{5,3},{6,0},{7,1},{8,14},{9,15},{10,... | collective-permute-start | bytes 196616 | tf_op jit(solution)/shard_map/ppermute | solution.py:984
  63.4 20.1 %collective-permute-done.5 = bf16[256,128]{1,0:T(8,128)(2,1)S(1)} collective-permute-done((bf16[256,128]{1,0:T(8,128)(2,1)S(1)}, bf16[256,128]{1,0:T(8,128)(2,1)S(1)}, u32[]{:S(2)}, u32[]{:S(2)}) %collective-permute-start.5) | collective-permute-done | bytes 65568 | tf_op jit(solution)/shard_map/ppermute | solution.py:984
  83.4 20.8 %collective-permute-done.4 = bf16[256,128]{1,0:T(8,128)(2,1)S(1)} collective-permute-done((bf16[256,128]{1,0:T(8,128)(2,1)S(1)}, bf16[256,128]{1,0:T(8,128)(2,1)S(1)}, u32[]{:S(2)}, u32[]{:S(2)}) %collective-permute-start.4) | collective-permute-done | bytes 65568 | tf_op jit(solution)/shard_map/ppermute | solution.py:984
  106.2 15.8 %attend_own.1 = (bf16[32,32,128]{2,1,0:T(8,128)(2,1)}, bf16[2048,64]{1,0:T(8,128)(2,1)}, bf16[2304,64]{1,0:T(8,128)(2,1)}, bf16[2304,64]{1,0:T(8,128)(2,1)}, bf1...) custom-call(s32[2]{0:T(128)} %pad_add_fusion.1.place_ref, s32[16]{0:T(128)} %reshape.573.range_ref, s32[8,1,256]{2,1,0:T(1,128)} %bitcast.265, ...), custom_call_target="tpu_custom_call" | custom-call | flops 268435456 | bytes 4194304 | tf_op jit(solution)/shard_map/attend_own/pallas_call | solution.py:1010
  122.7 8.3 %attend_last.1 = (bf16[32,40,128]{2,1,0:T(8,128)(2,1)}, bf16[256,64]{1,0:T(8,128)(2,1)}, bf16[2304,64]{1,0:T(8,128)(2,1)}, bf16[2304,64]{1,0:T(8,128)(2,1)}, bf1...) custom-call(s32[2]{0:T(128)} %pad_add_fusion.1.place_ref, s32[2]{0:T(128)} %add_bitcast_fusion.range_ref, ...), custom_call_target="tpu_custom_call" | custom-call | flops 67108864 | bytes 2097152 | tf_op jit(solution)/shard_map/attend_last/pallas_call | solution.py:1026
  131.0 2.8 all-to-all-start.2
  133.9 1.6 collective-permute-start.11
  137.3 14.0 %all-to-all-done.2.came_ref = bf16[32,40,128]{2,1,0:T(8,128)(2,1)S(1)} async-done(((bf16[32,40,128]{2,1,0:T(8,128)(2,1)}), bf16[32,40,128]{2,1,0:T(8,128)(2,1)S(1)}, u32[]{:S(2)}, u32[]{:S(2)}) %all-to-all-start.2) | async-done | bytes 327712 | tf_op jit(solution)/shard_map/all_to_all | solution.py:19
  151.3 1.4 all-gather.3.cloned.1.call-done
  152.7 3.1 middle.1
  156.1 1.4 collective-permute-start.8
  157.7 11.5 %feed.1 = (bf16[192,768]{1,0:T(8,128)(2,1)}, f32[192,768]{1,0:T(8,128)}, bf16[192,768]{1,0:T(8,128)(2,1)}, bf16[32,40,128]{2,1,0:T(8,128)(2,1)}, f32[15,768]{1,0:T(8,128)}) custom-call(bf16[32,216,768]{2,1,0:T(8,128)(2,1)} %bitcast.218, bf16[32,216,768]{2,1,0:T(8,128)(2,1)} %bitcast.219, bf16[32,216,768]{2,1,0:T(8,128)(2,1)} %bitcast.220, ...), custom_call_target="tpu_custom_call" | custom-call | flops 3623878656 | bytes 9437184 | tf_op jit(solution)/shard_map/feed/pallas_call | solution.py:1084
  169.2 3.3 all-to-all-start.3
  172.5 1.5 convolution_convert_fusion
  175.0 8.5 %feed_weights.1 = (bf16[768,768]{1,0:T(8,128)(2,1)}, bf16[768,768]{1,0:T(8,128)(2,1)}, f32[1,768]{1,0:T(1,128)}) custom-call(s32[2]{0:T(128)} %pad_add_fusion.1.place_ref, bf16[32,216,768]{2,1,0:T(8,128)(2,1)} %bitcast.221, bf16[32,216,768]{2,1,0:T(8,128)(2,1)} %bitcast.222, f32[4,1,768]{2,1,0:T(1,128)} %reshape.613.ex_bias_ref.bias_ref, ...), custom_call_target="tpu_custom_call" | custom-call | flops 4529848320 | bytes 9437184 | tf_op jit(solution)/shard_map/feed_weights/pallas_call | solution.py:1121
  183.6 1.5 copy.116
  185.4 1.1 dynamic-slice_bitcast_fusion
  186.5 1.6 collective-permute-start.20
  188.1 7.0 %attend_last_back.1 = (f32[256,128]{1,0:T(8,128)}, bf16[8,256,128]{2,1,0:T(8,128)(2,1)}) custom-call(s32[2]{0:T(128)} %pad_add_fusion.1.place_ref, s32[2]{0:T(128)} %add_bitcast_fusion.range_ref, s32[1,1,256]{2,1,0:T(1,128)} %reshape_reshape.12.low_ref, s32[1,1,256]{2,1,0:T(1,128)} %reshape_reshape.13.high_ref, f32[2048,128]{1,0:T(8,128)} %get-tuple-element.95.cos_ref, ...), custom_call_target="tpu_custom_call" | custom-call | flops 134217728 | bytes 2097152 | tf_op jit(solution)/shard_map/attend_last_back/pallas_call | solution.py:1166
  195.0 1.7 dynamic-slice_bitcast_fusion.8
  198.3 1.6 collective-permute-start.15
  201.9 14.8 %attend_own_back.1 = bf16[8,400,128]{2,1,0:T(8,128)(2,1)} custom-call(s32[2]{0:T(128)} %pad_add_fusion.1.place_ref, s32[16]{0:T(128)} %reshape.573.range_ref, s32[8,1,256]{2,1,0:T(1,128)} %bitcast.266, s32[8,1,256]{2,1,0:T(1,128)} %bitcast.275, f32[2048,128]{1,0:T(8,128)} %get-tuple-element.95.cos_ref, f32[2048,128]{1,0:T(8,128)} %get-tuple-element.96.sin_ref, ...), custom_call_target="tpu_custom_call" | custom-call | flops 536870912 | bytes 4194304 | tf_op jit(solution)/shard_map/attend_own_back/pallas_call | solution.py:1181
  216.7 3.9 %collective-permute-done.13 = bf16[4,256,128]{2,1,0:T(8,128)(2,1)} collective-permute-done((bf16[4,256,128]{2,1,0:T(8,128)(2,1)}, bf16[4,256,128]{2,1,0:T(8,128)(2,1)}, u32[]{:S(2)}, u32[]{:S(2)}) %collective-permute-start.13) | collective-permute-done | bytes 262176 | tf_op jit(solution)/shard_map/ppermute | solution.py:72
  221.7 5.6 %all-to-all-start.4 = ((bf16[8,400,128]{2,1,0:T(8,128)(2,1)}), bf16[8,400,128]{2,1,0:T(8,128)(2,1)}, u32[]{:S(2)}, u32[]{:S(2)}) async-start(bf16[8,400,128]{2,1,0:T(8,128)(2,1)} %attend_own_back.1), calls=%async_computation.4 | async-start | bytes 1638400 | tf_op jit(solution)/shard_map/all_to_all | solution.py:1215
  227.3 1.3 add_convert_fusion.1
  228.6 1.6 fusion
  230.2 2.1 collective-permute-start.21
  232.3 1.5 collective-permute-start.22
  235.1 2.4 collective-permute-start.18
  237.5 1.5 collective-permute-start.19
  238.9 1.4 collective-permute-done.22
  240.4 16.7 %collective-permute-done.21 = bf16[2,192,768]{2,1,0:T(8,128)(2,1)S(1)} collective-permute-done((bf16[2,192,768]{2,1,0:T(8,128)(2,1)S(1)}, bf16[2,192,768]{2,1,0:T(8,128)(2,1)S(1)}, u32[]{:S(2)}, u32[]{:S(2)}) %collective-permute-start.21) | collective-permute-done | bytes 589856 | tf_op jit(solution)/shard_map/ppermute | solution.py:72
  257.8 3.4 %collective-permute-done.19.refs_8_ = bf16[256,128]{1,0:T(8,128)(2,1)S(1)} collective-permute-done((bf16[256,128]{1,0:T(8,128)(2,1)S(1)}, bf16[256,128]{1,0:T(8,128)(2,1)S(1)}, u32[]{:S(2)}, u32[]{:S(2)}) %collective-permute-start.19) | collective-permute-done | bytes 65568 | tf_op jit(solution)/shard_map/ppermute | solution.py:984
  261.8 4.9 %project_back.1 = (bf16[3,64,768]{2,1,0:T(8,128)(2,1)}, bf16[3,64,768]{2,1,0:T(8,128)(2,1)}, bf16[3,64,768]{2,1,0:T(8,128)(2,1)}, bf16[3,64,768]{2,1,0:T(8,128)(...) custom-call(f32[3,768]{1,0:T(4,128)} %get-tuple-element.204.c_ref, ...), custom_call_target="tpu_custom_call" | custom-call | flops 1358954496 | bytes 1179648 | tf_op jit(solution)/shard_map/project_back/pallas_call | solution.py:1240
  266.8 1.6 collective-permute-start.24
  272.0 1.4 collective-permute-start.27
  273.7 4.2 %collective-permute-done.33 = bf16[2,24,768]{2,1,0:T(8,128)(2,1)S(1)} collective-permute-done((bf16[2,24,768]{2,1,0:T(8,128)(2,1)S(1)}, bf16[2,24,768]{2,1,0:T(8,128)(2,1)S(1)}, u32[]{:S(2)}, u32[]{:S(2)}) %collective-permute-start.33) | collective-permute-done | bytes 73760 | tf_op jit(solution)/shard_map/ppermute | solution.py:72
  278.8 3.8 %collective-permute-done.24 = bf16[3,64,768]{2,1,0:T(8,128)(2,1)S(1)} collective-permute-done((bf16[3,64,768]{2,1,0:T(8,128)(2,1)}, bf16[3,64,768]{2,1,0:T(8,128)(2,1)S(1)}, u32[]{:S(2)}, u32[]{:S(2)}) %collective-permute-start.24) | collective-permute-done | bytes 294944 | tf_op jit(solution)/shard_map/ppermute | solution.py:50
  284.0 11.1 %collective-permute-done.34 = bf16[1,216,768]{2,1,0:T(8,128)(2,1)S(1)} collective-permute-done((bf16[1,216,768]{2,1,0:T(8,128)(2,1)S(1)}, bf16[1,216,768]{2,1,0:T(8,128)(2,1)S(1)}, u32[]{:S(2)}, u32[]{:S(2)}) %collective-permute-start.34) | collective-permute-done | bytes 331808 | tf_op jit(solution)/shard_map/ppermute | solution.py:72
  298.8 7.0 %collective-permute-done.28 = bf16[2,4,32,576]{3,2,1,0:T(8,128)(2,1)S(1)} collective-permute-done((bf16[2,4,32,576]{3,2,1,0:T(8,128)(2,1)S(1)}, bf16[2,4,32,576]{3,2,1,0:T(8,128)(2,1)S(1)}, u32[]{:S(2)}, u32[]{:S(2)}) %collective-permute-start.28) | collective-permute-done | bytes 294944 | tf_op jit(solution)/shard_map/ppermute | solution.py:72
  306.1 9.6 %collective-permute-done.29 = bf16[1,4,32,576]{3,2,1,0:T(8,128)(2,1)S(1)} collective-permute-done((bf16[1,4,32,576]{3,2,1,0:T(8,128)(2,1)S(1)}, bf16[1,4,32,576]{3,2,1,0:T(8,128)(2,1)S(1)}, u32[]{:S(2)}, u32[]{:S(2)}) %collective-permute-start.29) | collective-permute-done | bytes 147488 | tf_op jit(solution)/shard_map/ppermute | solution.py:72
  (298 shorter events, 47.7 us)
Async XLA Ops:
  13.9 15.9 %copy-start.16 = (bf16[3,64,768]{2,1,0:T(8,128)(2,1)}, bf16[3,64,768]{2,1,0:T(8,128)(2,1)S(1)}, u32[]{:S(2)}) copy-start(bf16[3,64,768]{2,1,0:T(8,128)(2,1)S(1)} %fusion.8.refs_0_) | copy-start | bytes 884740
  13.9 35.6 %collective-permute-start = (bf16[3,64,768]{2,1,0:T(8,128)(2,1)S(1)}, bf16[3,64,768]{2,1,0:T(8,128)(2,1)S(1)}, u32[]{:S(2)}, u32[]{:S(2)}) collective-permute-start(bf16[3,64,768]{2,1,0:T(8,128)(2,1)S(1)} %fusion.8.refs_0_), channel_id=1, source_target_pairs={{0,8},{8,0},{16,24},{24,16},{1,9},{9,1},{17,25},{25,17},{2,10},{10... | collective-permute-start | bytes 884744 | tf_op jit(solution)/shard_map/ppermute | solution.py:50
  14.5 35.1 %collective-permute-start.1 = (bf16[3,64,768]{2,1,0:T(8,128)(2,1)S(1)}, bf16[3,64,768]{2,1,0:T(8,128)(2,1)S(1)}, u32[]{:S(2)}, u32[]{:S(2)}) collective-permute-start(bf16[3,64,768]{2,1,0:T(8,128)(2,1)S(1)} %fusion.8.refs_0_), channel_id=1, source_target_pairs={{0,16},{8,24},{16,0},{24,8},{1,17},{9,25},{17,1},{25,9},{2,18},{10... | collective-permute-start | bytes 884744 | tf_op jit(solution)/shard_map/ppermute | solution.py:50
  17.0 32.5 %collective-permute-start.2 = (bf16[3,64,768]{2,1,0:T(8,128)(2,1)S(1)}, bf16[3,64,768]{2,1,0:T(8,128)(2,1)S(1)}, u32[]{:S(2)}, u32[]{:S(2)}) collective-permute-start(bf16[3,64,768]{2,1,0:T(8,128)(2,1)S(1)} %fusion.8.refs_0_), channel_id=1, source_target_pairs={{0,24},{8,16},{16,8},{24,0},{1,25},{9,17},{17,9},{25,1},{2,26},{10... | collective-permute-start | bytes 884744 | tf_op jit(solution)/shard_map/ppermute | solution.py:50
  17.1 32.2 %all-to-all-start = ((bf16[32,24,640]{2,1,0:T(8,128)(2,1)}), bf16[32,24,640]{2,1,0:T(8,128)(2,1)S(1)}, u32[]{:S(2)}, u32[]{:S(2)}) async-start(bf16[32,24,640]{2,1,0:T(8,128)(2,1)} %bitcast.9), calls=%async_computation | async-start | bytes 1966080 | tf_op jit(solution)/shard_map/all_to_all | solution.py:19
  23.2 129.5 %all-gather.3.cloned.1.call-start = ((), (), s32[]{:S(2)}) async-start(), calls=%async_computation.5 | async-start | bytes 10948608 | tf_op jit(solution)/shard_map/all_gather | solution.py:938
  55.2 50.1 %all-to-all-start.1 = ((bf16[8,400,128]{2,1,0:T(8,128)(2,1)}), bf16[8,400,128]{2,1,0:T(8,128)(2,1)S(1)}, u32[]{:S(2)}, u32[]{:S(2)}) async-start(bf16[8,400,128]{2,1,0:T(8,128)(2,1)} %get-tuple-element.102), calls=%async_computation.1 | async-start | bytes 1638400 | tf_op jit(solution)/shard_map/all_to_all | solution.py:983
  58.9 24.5 %collective-permute-start.5 = (bf16[256,128]{1,0:T(8,128)(2,1)S(1)}, bf16[256,128]{1,0:T(8,128)(2,1)S(1)}, u32[]{:S(2)}, u32[]{:S(2)}) collective-permute-start(bf16[256,128]{1,0:T(8,128)(2,1)S(1)} %copy-done.28), channel_id=1, source_target_pairs={{0,6},{1,7},{2,4},{3,5},{4,2},{5,3},{6,0},{7,1},{8,14},{9,15},{10,... | collective-permute-start | bytes 196616 | tf_op jit(solution)/shard_map/ppermute | solution.py:984
  62.7 41.6 %collective-permute-start.4 = (bf16[256,128]{1,0:T(8,128)(2,1)S(1)}, bf16[256,128]{1,0:T(8,128)(2,1)S(1)}, u32[]{:S(2)}, u32[]{:S(2)}) collective-permute-start(bf16[256,128]{1,0:T(8,128)(2,1)S(1)} %copy-done.28), channel_id=1, source_target_pairs={{0,4},{1,5},{2,6},{3,7},{4,0},{5,1},{6,2},{7,3},{8,12},{9,13},{10,... | collective-permute-start | bytes 196616 | tf_op jit(solution)/shard_map/ppermute | solution.py:984
  62.7 41.6 %collective-permute-start.3 = (bf16[256,128]{1,0:T(8,128)(2,1)S(1)}, bf16[256,128]{1,0:T(8,128)(2,1)S(1)}, u32[]{:S(2)}, u32[]{:S(2)}) collective-permute-start(bf16[256,128]{1,0:T(8,128)(2,1)S(1)} %copy-done.28), channel_id=1, source_target_pairs={{0,2},{1,3},{2,0},{3,1},{4,6},{5,7},{6,4},{7,5},{8,10},{9,11},{10,... | collective-permute-start | bytes 196616 | tf_op jit(solution)/shard_map/ppermute | solution.py:984
  104.3 17.8 %copy-start.10 = (bf16[4,256,128]{2,1,0:T(8,128)(2,1)}, bf16[4,256,128]{2,1,0:T(8,128)(2,1)S(1)}, u32[]{:S(2)}) copy-start(bf16[4,256,128]{2,1,0:T(8,128)(2,1)S(1)} %pad_maximum_fusion.4.refs_1_) | copy-start | bytes 786436
  104.3 17.8 %collective-permute-start.6 = (bf16[4,256,128]{2,1,0:T(8,128)(2,1)S(1)}, bf16[4,256,128]{2,1,0:T(8,128)(2,1)S(1)}, u32[]{:S(2)}, u32[]{:S(2)}) collective-permute-start(bf16[4,256,128]{2,1,0:T(8,128)(2,1)S(1)} %pad_maximum_fusion.4.refs_1_), channel_id=1, source_target_pairs={{0,1},{1,0},{2,3},{3,2},{4,5},{5,4},{6,7},{7,6},{8,9},{9,8},{10,11... | collective-permute-start | bytes 786440 | tf_op jit(solution)/shard_map/ppermute | solution.py:984
  131.0 20.3 %all-to-all-start.2 = ((bf16[32,40,128]{2,1,0:T(8,128)(2,1)}), bf16[32,40,128]{2,1,0:T(8,128)(2,1)S(1)}, u32[]{:S(2)}, u32[]{:S(2)}) async-start(bf16[32,40,128]{2,1,0:T(8,128)(2,1)} %get-tuple-element.108), calls=%async_computation.2 | async-start | bytes 655360 | tf_op jit(solution)/shard_map/all_to_all | solution.py:19
  133.8 23.6 %collective-permute-start.10 = (bf16[192,768]{1,0:T(8,128)(2,1)S(1)}, bf16[192,768]{1,0:T(8,128)(2,1)S(1)}, u32[]{:S(2)}, u32[]{:S(2)}) collective-permute-start(bf16[192,768]{1,0:T(8,128)(2,1)S(1)} %bitcast.244), channel_id=1, source_target_pairs={{0,8},{8,0},{16,24},{24,16},{1,9},{9,1},{17,25},{25,17},{2,10},{10... | collective-permute-start | bytes 884744 | tf_op jit(solution)/shard_map/ppermute | solution.py:50
  133.9 40.1 %collective-permute-start.11 = (bf16[192,768]{1,0:T(8,128)(2,1)S(1)}, bf16[192,768]{1,0:T(8,128)(2,1)S(1)}, u32[]{:S(2)}, u32[]{:S(2)}) collective-permute-start(bf16[192,768]{1,0:T(8,128)(2,1)S(1)} %bitcast.245), channel_id=1, source_target_pairs={{0,16},{8,24},{16,0},{24,8},{1,17},{9,25},{17,1},{25,9},{2,18},{10... | collective-permute-start | bytes 884744 | tf_op jit(solution)/shard_map/ppermute | solution.py:50
  135.5 38.5 %collective-permute-start.12 = (bf16[192,768]{1,0:T(8,128)(2,1)S(1)}, bf16[192,768]{1,0:T(8,128)(2,1)S(1)}, u32[]{:S(2)}, u32[]{:S(2)}) collective-permute-start(bf16[192,768]{1,0:T(8,128)(2,1)S(1)} %bitcast.246), channel_id=1, source_target_pairs={{0,24},{8,16},{16,8},{24,0},{1,25},{9,17},{17,9},{25,1},{2,26},{10... | collective-permute-start | bytes 884744 | tf_op jit(solution)/shard_map/ppermute | solution.py:50
  155.8 18.2 %collective-permute-start.7 = (bf16[192,768]{1,0:T(8,128)(2,1)}, bf16[192,768]{1,0:T(8,128)(2,1)S(1)}, u32[]{:S(2)}, u32[]{:S(2)}) collective-permute-start(bf16[192,768]{1,0:T(8,128)(2,1)} %get-tuple-element.109.second_ref.refs_0_), channel_id=1, source_target_pairs={{0,8},{8,0},{16,24},{24,16},{1,9},{9,1},{17,25},{25,17},{2,10},{10... | collective-permute-start | bytes 884744 | tf_op jit(solution)/shard_map/ppermute | solution.py:50
  156.1 18.0 %collective-permute-start.8 = (bf16[192,768]{1,0:T(8,128)(2,1)}, bf16[192,768]{1,0:T(8,128)(2,1)S(1)}, u32[]{:S(2)}, u32[]{:S(2)}) collective-permute-start(bf16[192,768]{1,0:T(8,128)(2,1)} %get-tuple-element.109.second_ref.refs_0_), channel_id=1, source_target_pairs={{0,16},{8,24},{16,0},{24,8},{1,17},{9,25},{17,1},{25,9},{2,18},{10... | collective-permute-start | bytes 884744 | tf_op jit(solution)/shard_map/ppermute | solution.py:50
  157.5 16.6 %collective-permute-start.9 = (bf16[192,768]{1,0:T(8,128)(2,1)}, bf16[192,768]{1,0:T(8,128)(2,1)}, u32[]{:S(2)}, u32[]{:S(2)}) collective-permute-start(bf16[192,768]{1,0:T(8,128)(2,1)} %get-tuple-element.109.second_ref.refs_0_), channel_id=1, source_target_pairs={{0,24},{8,16},{16,8},{24,0},{1,25},{9,17},{17,9},{25,1},{2,26},{10... | collective-permute-start | bytes 884744 | tf_op jit(solution)/shard_map/ppermute | solution.py:50
  157.7 14.8 %copy-start.15 = (bf16[192,768]{1,0:T(8,128)(2,1)S(1)}, bf16[192,768]{1,0:T(8,128)(2,1)}, u32[]{:S(2)}) copy-start(bf16[192,768]{1,0:T(8,128)(2,1)} %get-tuple-element.117) | copy-start | bytes 884740
  169.2 16.2 %all-to-all-start.3 = ((bf16[32,40,128]{2,1,0:T(8,128)(2,1)}), bf16[32,40,128]{2,1,0:T(8,128)(2,1)}, u32[]{:S(2)}, u32[]{:S(2)}) async-start(bf16[32,40,128]{2,1,0:T(8,128)(2,1)} %get-tuple-element.114), calls=%async_computation.3 | async-start | bytes 655360 | tf_op jit(solution)/shard_map/all_to_all | solution.py:19
  186.5 42.1 %collective-permute-start.20 = (bf16[4,192,768]{2,1,0:T(8,128)(2,1)}, bf16[4,192,768]{2,1,0:T(8,128)(2,1)}, u32[]{:S(2)}, u32[]{:S(2)}) collective-permute-start(bf16[4,192,768]{2,1,0:T(8,128)(2,1)} %dynamic-slice_bitcast_fusion), channel_id=1, source_target_pairs={{0,1},{1,0},{2,3},{3,2},{4,5},{5,4},{6,7},{7,6},{8,9},{9,8},{10,11... | collective-permute-start | bytes 3538952 | tf_op jit(solution)/shard_map/ppermute | solution.py:72
  196.7 23.9 %collective-permute-start.13 = (bf16[4,256,128]{2,1,0:T(8,128)(2,1)}, bf16[4,256,128]{2,1,0:T(8,128)(2,1)}, u32[]{:S(2)}, u32[]{:S(2)}) collective-permute-start(bf16[4,256,128]{2,1,0:T(8,128)(2,1)} %dynamic-slice_bitcast_fusion.8), channel_id=1, source_target_pairs={{0,1},{1,0},{2,3},{3,2},{4,5},{5,4},{6,7},{7,6},{8,9},{9,8},{10,11... | collective-permute-start | bytes 786440 | tf_op jit(solution)/shard_map/ppermute | solution.py:72
  198.3 23.3 %collective-permute-start.14 = (bf16[192,768]{1,0:T(8,128)(2,1)}, bf16[192,768]{1,0:T(8,128)(2,1)}, u32[]{:S(2)}, u32[]{:S(2)}) collective-permute-start(bf16[192,768]{1,0:T(8,128)(2,1)} %get-tuple-element.179), channel_id=1, source_target_pairs={{0,8},{8,0},{16,24},{24,16},{1,9},{9,1},{17,25},{25,17},{2,10},{10... | collective-permute-start | bytes 884744 | tf_op jit(solution)/shard_map/ppermute | solution.py:50
  198.3 23.4 %collective-permute-start.15 = (bf16[192,768]{1,0:T(8,128)(2,1)}, bf16[192,768]{1,0:T(8,128)(2,1)}, u32[]{:S(2)}, u32[]{:S(2)}) collective-permute-start(bf16[192,768]{1,0:T(8,128)(2,1)} %get-tuple-element.178), channel_id=1, source_target_pairs={{0,16},{8,24},{16,0},{24,8},{1,17},{9,25},{17,1},{25,9},{2,18},{10... | collective-permute-start | bytes 884744 | tf_op jit(solution)/shard_map/ppermute | solution.py:50
  199.9 21.8 %collective-permute-start.16 = (bf16[192,768]{1,0:T(8,128)(2,1)}, bf16[192,768]{1,0:T(8,128)(2,1)}, u32[]{:S(2)}, u32[]{:S(2)}) collective-permute-start(bf16[192,768]{1,0:T(8,128)(2,1)} %get-tuple-element.177), channel_id=1, source_target_pairs={{0,24},{8,16},{16,8},{24,0},{1,25},{9,17},{17,9},{25,1},{2,26},{10... | collective-permute-start | bytes 884744 | tf_op jit(solution)/shard_map/ppermute | solution.py:50
  201.9 18.7 %copy-start.13 = (bf16[8,256,128]{2,1,0:T(8,128)(2,1)S(1)}, bf16[8,256,128]{2,1,0:T(8,128)(2,1)}, u32[]{:S(2)}) copy-start(bf16[8,256,128]{2,1,0:T(8,128)(2,1)} %get-tuple-element.133) | copy-start | bytes 1572868
  221.7 39.5 %all-to-all-start.4 = ((bf16[8,400,128]{2,1,0:T(8,128)(2,1)}), bf16[8,400,128]{2,1,0:T(8,128)(2,1)}, u32[]{:S(2)}, u32[]{:S(2)}) async-start(bf16[8,400,128]{2,1,0:T(8,128)(2,1)} %attend_own_back.1), calls=%async_computation.4 | async-start | bytes 1638400 | tf_op jit(solution)/shard_map/all_to_all | solution.py:1215
  230.2 26.8 %collective-permute-start.21 = (bf16[2,192,768]{2,1,0:T(8,128)(2,1)S(1)}, bf16[2,192,768]{2,1,0:T(8,128)(2,1)S(1)}, u32[]{:S(2)}, u32[]{:S(2)}) collective-permute-start(bf16[2,192,768]{2,1,0:T(8,128)(2,1)S(1)} %dynamic-slice_bitcast_fusion.1), channel_id=1, source_target_pairs={{0,2},{1,3},{2,0},{3,1},{4,6},{5,7},{6,4},{7,5},{8,10},{9,11},{10,... | collective-permute-start | bytes 1769480 | tf_op jit(solution)/shard_map/ppermute | solution.py:72
  232.3 8.0 %collective-permute-start.22 = (bf16[4,24,768]{2,1,0:T(8,128)(2,1)S(1)}, bf16[4,24,768]{2,1,0:T(8,128)(2,1)S(1)}, u32[]{:S(2)}, u32[]{:S(2)}) collective-permute-start(bf16[4,24,768]{2,1,0:T(8,128)(2,1)S(1)} %dynamic-slice_bitcast_fusion.10), channel_id=1, source_target_pairs={{0,1},{1,0},{2,3},{3,2},{4,5},{5,4},{6,7},{7,6},{8,9},{9,8},{10,11... | collective-permute-start | bytes 442376 | tf_op jit(solution)/shard_map/ppermute | solution.py:72
  234.6 23.2 %collective-permute-start.17 = (bf16[256,128]{1,0:T(8,128)(2,1)S(1)}, bf16[256,128]{1,0:T(8,128)(2,1)S(1)}, u32[]{:S(2)}, u32[]{:S(2)}) collective-permute-start(bf16[256,128]{1,0:T(8,128)(2,1)S(1)} %get-tuple-element.185), channel_id=1, source_target_pairs={{0,2},{1,3},{2,0},{3,1},{4,6},{5,7},{6,4},{7,5},{8,10},{9,11},{10,... | collective-permute-start | bytes 196616 | tf_op jit(solution)/shard_map/ppermute | solution.py:984
  235.1 22.6 %collective-permute-start.18 = (bf16[256,128]{1,0:T(8,128)(2,1)S(1)}, bf16[256,128]{1,0:T(8,128)(2,1)S(1)}, u32[]{:S(2)}, u32[]{:S(2)}) collective-permute-start(bf16[256,128]{1,0:T(8,128)(2,1)S(1)} %get-tuple-element.184), channel_id=1, source_target_pairs={{0,4},{1,5},{2,6},{3,7},{4,0},{5,1},{6,2},{7,3},{8,12},{9,13},{10,... | collective-permute-start | bytes 196616 | tf_op jit(solution)/shard_map/ppermute | solution.py:984
  237.5 23.7 %collective-permute-start.19 = (bf16[256,128]{1,0:T(8,128)(2,1)S(1)}, bf16[256,128]{1,0:T(8,128)(2,1)S(1)}, u32[]{:S(2)}, u32[]{:S(2)}) collective-permute-start(bf16[256,128]{1,0:T(8,128)(2,1)S(1)} %get-tuple-element.183), channel_id=1, source_target_pairs={{0,6},{1,7},{2,4},{3,5},{4,2},{5,3},{6,0},{7,1},{8,14},{9,15},{10,... | collective-permute-start | bytes 196616 | tf_op jit(solution)/shard_map/ppermute | solution.py:984
  266.7 12.1 %collective-permute-start.25 = (bf16[3,64,768]{2,1,0:T(8,128)(2,1)}, bf16[3,64,768]{2,1,0:T(8,128)(2,1)S(1)}, u32[]{:S(2)}, u32[]{:S(2)}) collective-permute-start(bf16[3,64,768]{2,1,0:T(8,128)(2,1)} %get-tuple-element.150), channel_id=1, source_target_pairs={{0,24},{8,16},{16,8},{24,0},{1,25},{9,17},{17,9},{25,1},{2,26},{10... | collective-permute-start | bytes 884744 | tf_op jit(solution)/shard_map/ppermute | solution.py:50
  266.8 15.8 %collective-permute-start.24 = (bf16[3,64,768]{2,1,0:T(8,128)(2,1)}, bf16[3,64,768]{2,1,0:T(8,128)(2,1)S(1)}, u32[]{:S(2)}, u32[]{:S(2)}) collective-permute-start(bf16[3,64,768]{2,1,0:T(8,128)(2,1)} %get-tuple-element.149), channel_id=1, source_target_pairs={{0,16},{8,24},{16,0},{24,8},{1,17},{9,25},{17,1},{25,9},{2,18},{10... | collective-permute-start | bytes 884744 | tf_op jit(solution)/shard_map/ppermute | solution.py:50
  268.3 14.3 %collective-permute-start.23 = (bf16[3,64,768]{2,1,0:T(8,128)(2,1)}, bf16[3,64,768]{2,1,0:T(8,128)(2,1)S(1)}, u32[]{:S(2)}, u32[]{:S(2)}) collective-permute-start(bf16[3,64,768]{2,1,0:T(8,128)(2,1)} %get-tuple-element.148), channel_id=1, source_target_pairs={{0,8},{8,0},{16,24},{24,16},{1,9},{9,1},{17,25},{25,17},{2,10},{10... | collective-permute-start | bytes 884744 | tf_op jit(solution)/shard_map/ppermute | solution.py:50
  272.0 6.7 %collective-permute-start.27 = (bf16[4,4,8,576]{3,2,1,0:T(8,128)(2,1)S(1)}, bf16[4,4,8,576]{3,2,1,0:T(8,128)(2,1)S(1)}, u32[]{:S(2)}, u32[]{:S(2)}) collective-permute-start(bf16[4,4,8,576]{3,2,1,0:T(8,128)(2,1)S(1)} %dynamic-slice_bitcast_fusion.9), channel_id=1, source_target_pairs={{0,1},{1,0},{2,3},{3,2},{4,5},{5,4},{6,7},{7,6},{8,9},{9,8},{10,11... | collective-permute-start | bytes 442376 | tf_op jit(solution)/shard_map/ppermute | solution.py:72
  273.5 4.4 %collective-permute-start.33 = (bf16[2,24,768]{2,1,0:T(8,128)(2,1)S(1)}, bf16[2,24,768]{2,1,0:T(8,128)(2,1)S(1)}, u32[]{:S(2)}, u32[]{:S(2)}) collective-permute-start(bf16[2,24,768]{2,1,0:T(8,128)(2,1)S(1)} %dynamic-slice_bitcast_fusion.11), channel_id=1, source_target_pairs={{0,2},{1,3},{2,0},{3,1},{4,6},{5,7},{6,4},{7,5},{8,10},{9,11},{10,... | collective-permute-start | bytes 221192 | tf_op jit(solution)/shard_map/ppermute | solution.py:72
  277.9 17.9 %collective-permute-start.26 = (bf16[4,4,24,576]{3,2,1,0:T(8,128)(2,1)S(1)}, bf16[4,4,24,576]{3,2,1,0:T(8,128)(2,1)S(1)}, u32[]{:S(2)}, u32[]{:S(2)}) collective-permute-start(bf16[4,4,24,576]{3,2,1,0:T(8,128)(2,1)S(1)} %dynamic-slice_bitcast_fusion.2), channel_id=1, source_target_pairs={{0,1},{1,0},{2,3},{3,2},{4,5},{5,4},{6,7},{7,6},{8,9},{9,8},{10,11... | collective-permute-start | bytes 1327112 | tf_op jit(solution)/shard_map/ppermute | solution.py:72
  278.7 16.4 %collective-permute-start.34 = (bf16[1,216,768]{2,1,0:T(8,128)(2,1)S(1)}, bf16[1,216,768]{2,1,0:T(8,128)(2,1)S(1)}, u32[]{:S(2)}, u32[]{:S(2)}) collective-permute-start(bf16[1,216,768]{2,1,0:T(8,128)(2,1)S(1)} %fusion.17), channel_id=1, source_target_pairs={{0,4},{1,5},{2,6},{3,7},{4,0},{5,1},{6,2},{7,3},{8,12},{9,13},{10,... | collective-permute-start | bytes 995336 | tf_op jit(solution)/shard_map/ppermute | solution.py:72
  296.1 9.7 %collective-permute-start.28 = (bf16[2,4,32,576]{3,2,1,0:T(8,128)(2,1)S(1)}, bf16[2,4,32,576]{3,2,1,0:T(8,128)(2,1)S(1)}, u32[]{:S(2)}, u32[]{:S(2)}) collective-permute-start(bf16[2,4,32,576]{3,2,1,0:T(8,128)(2,1)S(1)} %dynamic-slice_bitcast_fusion.3), channel_id=1, source_target_pairs={{0,2},{1,3},{2,0},{3,1},{4,6},{5,7},{6,4},{7,5},{8,10},{9,11},{10,... | collective-permute-start | bytes 884744 | tf_op jit(solution)/shard_map/ppermute | solution.py:72
  296.3 9.8 %collective-permute-start.37 = (bf16[24,768]{1,0:T(8,128)(2,1)S(1)}, bf16[24,768]{1,0:T(8,128)(2,1)S(1)}, u32[]{:S(2)}, u32[]{:S(2)}) collective-permute-start(bf16[24,768]{1,0:T(8,128)(2,1)S(1)} %get-tuple-element.196), channel_id=1, source_target_pairs={{0,24},{8,16},{16,8},{24,0},{1,25},{9,17},{17,9},{25,1},{2,26},{10... | collective-permute-start | bytes 110600 | tf_op jit(solution)/shard_map/ppermute | solution.py:50
  297.1 8.9 %collective-permute-start.36 = (bf16[24,768]{1,0:T(8,128)(2,1)S(1)}, bf16[24,768]{1,0:T(8,128)(2,1)S(1)}, u32[]{:S(2)}, u32[]{:S(2)}) collective-permute-start(bf16[24,768]{1,0:T(8,128)(2,1)S(1)} %get-tuple-element.197), channel_id=1, source_target_pairs={{0,16},{8,24},{16,0},{24,8},{1,17},{9,25},{17,1},{25,9},{2,18},{10... | collective-permute-start | bytes 110600 | tf_op jit(solution)/shard_map/ppermute | solution.py:50
  298.0 8.1 %collective-permute-start.35 = (bf16[24,768]{1,0:T(8,128)(2,1)S(1)}, bf16[24,768]{1,0:T(8,128)(2,1)S(1)}, u32[]{:S(2)}, u32[]{:S(2)}) collective-permute-start(bf16[24,768]{1,0:T(8,128)(2,1)S(1)} %get-tuple-element.198), channel_id=1, source_target_pairs={{0,8},{8,0},{16,24},{24,16},{1,9},{9,1},{17,25},{25,17},{2,10},{10... | collective-permute-start | bytes 110600 | tf_op jit(solution)/shard_map/ppermute | solution.py:50
  306.0 9.8 %collective-permute-start.29 = (bf16[1,4,32,576]{3,2,1,0:T(8,128)(2,1)S(1)}, bf16[1,4,32,576]{3,2,1,0:T(8,128)(2,1)S(1)}, u32[]{:S(2)}, u32[]{:S(2)}) collective-permute-start(bf16[1,4,32,576]{3,2,1,0:T(8,128)(2,1)S(1)} %constant_dynamic-slice_fusion.1), channel_id=1, source_target_pairs={{0,4},{1,5},{2,6},{3,7},{4,0},{5,1},{6,2},{7,3},{8,12},{9,13},{10,... | collective-permute-start | bytes 442376 | tf_op jit(solution)/shard_map/ppermute | solution.py:72
  315.8 3.8 %collective-permute-start.32 = (bf16[32,576]{1,0:T(8,128)(2,1)S(1)}, bf16[32,576]{1,0:T(8,128)(2,1)S(1)}, u32[]{:S(2)}, u32[]{:S(2)}) collective-permute-start(bf16[32,576]{1,0:T(8,128)(2,1)S(1)} %get-tuple-element.188), channel_id=1, source_target_pairs={{0,24},{8,16},{16,8},{24,0},{1,25},{9,17},{17,9},{25,1},{2,26},{10... | collective-permute-start | bytes 110600 | tf_op jit(solution)/shard_map/ppermute | solution.py:50
  316.6 4.0 %collective-permute-start.31 = (bf16[32,576]{1,0:T(8,128)(2,1)S(1)}, bf16[32,576]{1,0:T(8,128)(2,1)S(1)}, u32[]{:S(2)}, u32[]{:S(2)}) collective-permute-start(bf16[32,576]{1,0:T(8,128)(2,1)S(1)} %get-tuple-element.189), channel_id=1, source_target_pairs={{0,16},{8,24},{16,0},{24,8},{1,17},{9,25},{17,1},{25,9},{2,18},{10... | collective-permute-start | bytes 110600 | tf_op jit(solution)/shard_map/ppermute | solution.py:50
  317.5 3.2 collective-permute-start.30
  (38 other events, 189.3 us)
Sparse Core Ops, SparseCore 0:
  49.7 102.9 all-gather.2

commit v6 on v5

--- a/solution.py
+++ b/solution.py
@@ -336,9 +336,9 @@
                 do_ref[at * blocks + b] = jnp.zeros((rows, 64), BF)
 
 
-def feed_weights_body(rows, place_ref, ex_ref, re_ref, bias_ref, gate_ref, *refs):
-    groups = (len(refs) - 3) // 2
-    reduce_ref, expand_ref, sum_ref = refs[2 * groups :]
+def feed_weights_body(rows, blocks, place_ref, ex_ref, re_ref, bias_ref, gate_ref, *refs):
+    groups = (len(refs) - 2) // 2
+    out_ref, sum_ref = refs[2 * groups :]
     width = refs[0].shape[-1]
     second = jnp.concatenate([x[...] for x in refs[:groups]], 0)
     gate = by_micro(gate_ref, rows)
@@ -352,8 +352,15 @@
     du = lax.dot_general(dm, reduce, NT, preferred_element_type=F32) * slope
     du = du.astype(BF)
     sum_ref[...] = jnp.sum(du.astype(F32), 0, keepdims=True)
-    reduce_ref[...] = lax.dot_general(g.astype(BF), dm, TN, preferred_element_type=F32).astype(BF)
-    expand_ref[...] = lax.dot_general(second, du, TN, preferred_element_type=F32).astype(BF)
+    per, each = width // blocks, width // (groups * blocks)
+    x = lax.dot_general(g.astype(BF), dm, TN, preferred_element_type=F32)
+    for b in range(blocks):
+        out_ref[b, :per] = x[b * per : (b + 1) * per].astype(BF)
+    x = lax.dot_general(second, du, TN, preferred_element_type=F32)
+    for k in range(groups):
+        for b in range(blocks):
+            at = (k * blocks + b) * each
+            out_ref[b, per + k * each : per + (k + 1) * each] = x[at : at + each].astype(BF)
 
 
 def attend_body(block, range_ref, q_ref, sq_ref, k_ref, v_ref, sk_ref, o_ref, lse_ref):
@@ -715,7 +722,7 @@
 
 def attend_last_back_body(
     blocks, groups, rows, stripe, place_ref, range_ref, low_ref, high_ref, cos_ref, sin_ref,
-    do_ref, q_ref, k_ref, v_ref, o_ref, lse_ref, dq_ref, last_ref, kept, wide_cos, wide_sin, dk, dv,
+    do_ref, q_ref, k_ref, v_ref, o_ref, lse_ref, dq_ref, keep_ref, send_ref, kept, wide_cos, wide_sin, dk, dv,
 ):
     span = blocks * rows
     devices = groups * blocks
@@ -745,8 +752,11 @@
         cos, sin = turn_tables(cos_ref[at], sin_ref[at], True)[1]
         x = turn(jnp.concatenate([dk[at], jnp.zeros_like(dk[at])], 1), (cos, -sin))[:, :64]
         kept[...] = jnp.concatenate([x, dv[at]], 1).astype(BF)
-        for b in range(blocks):
-            last_ref[b, pl.ds(pl.multiple_of(k * rows, rows), rows), :] = kept[b * rows : (b + 1) * rows]
+        to = pl.ds(pl.multiple_of(k * rows, rows), rows)
+        for z in range(blocks // 2):
+            mine = 2 * z + (place_ref[1] & 1)
+            keep_ref[z, to, :] = spread(kept, mine * rows, rows)
+            send_ref[z, to, :] = spread(kept, (mine ^ 1) * rows, rows)
 
 
 def attend_own_back_body(
@@ -1113,13 +1123,9 @@
         sums[i * micro : (i + 1) * micro] for i in range(5)
     ]
 
-    output_part = lax.dot_general(merged, grad_attn, TN, preferred_element_type=F32).astype(BF)
-    output_part = output_part.reshape(groups, width // groups, width)
-
     flat_p = pl.BlockSpec((own, width), lambda i, p: (0, 0))
-    square = pl.BlockSpec((width, width), lambda i, p: (0, 0))
-    reduce_part, expand_part, bias_part = pl.pallas_call(
-        functools.partial(feed_weights_body, rows),
+    feed_part, bias_part = pl.pallas_call(
+        functools.partial(feed_weights_body, rows, blocks),
         grid_spec=pltpu.PrefetchScalarGridSpec(
             num_scalar_prefetch=1,
             grid=(1,),
@@ -1130,11 +1136,13 @@
                 pl.BlockSpec((micro, width), lambda i, p: (0, 0)),
             ]
             + [flat_p] * (2 * groups),
-            out_specs=[square, square, pl.BlockSpec((1, width), lambda i, p: (0, 0))],
+            out_specs=[
+                pl.BlockSpec((blocks, ff_rows + groups * gain_rows, width), lambda i, p: (0, 0, 0)),
+                pl.BlockSpec((1, width), lambda i, p: (0, 0)),
+            ],
         ),
         out_shape=[
-            jax.ShapeDtypeStruct((width, width), BF),
-            jax.ShapeDtypeStruct((width, width), BF),
+            jax.ShapeDtypeStruct((blocks, ff_rows + groups * gain_rows, width), BF),
             jax.ShapeDtypeStruct((1, width), F32),
         ],
         cost_estimate=pl.CostEstimate(
@@ -1142,32 +1150,15 @@
         ),
         name="feed_weights",
     )(place, gathered, gathered, expand_bias_f, gate2, *second_group, *dy_group)
-    feed_part = jnp.concatenate(
-        [
-            reduce_part.reshape(blocks, ff_rows, width),
-            expand_part.reshape(groups, blocks, gain_rows, width)
-            .transpose(1, 0, 2, 3)
-            .reshape(blocks, groups * gain_rows, width),
-        ],
-        1,
-    )
-    do_came, feed_part, output_part = lax.optimization_barrier((do_came, feed_part, output_part))
-    output_part = swap(
-        [
-            lax.dynamic_index_in_dim(output_part, group_id ^ k, 0, keepdims=False)
-            for k in range(groups)
-        ],
-        "ulysses",
-    )
-
-    feed_half = halve(feed_part, "blk", block_id, 1)
+    do_came, feed_part = lax.optimization_barrier((do_came, feed_part))
+    feed_sum = lax.psum_scatter(feed_part, "blk", scatter_dimension=0, tiled=True)[0]
 
     if small_path:
-        last_dq, last_leaving = pl.pallas_call(
+        last_dq, last_kept, last_sent = pl.pallas_call(
             functools.partial(attend_last_back_body, blocks, groups, rows, stripe),
             in_specs=specs + [whole_vmem()] * 6,
-            out_specs=[whole_vmem()] * 2,
-            out_shape=[f32(devices * stripe, 128), whole(blocks, count, 128)],
+            out_specs=[whole_vmem()] * 3,
+            out_shape=[f32(devices * stripe, 128)] + [whole(blocks // 2, count, 128)] * 2,
             scratch_shapes=[pltpu.VMEM((span, 128), BF)]
             + [pltpu.VMEM((devices * stripe, 128), F32)] * 2
             + [pltpu.VMEM((size + KB - QB, 64), F32)] * 2,
@@ -1176,7 +1167,7 @@
             ),
             name="attend_last_back",
         )(*last_args, do_came, *last_saved)
-        last_half = halve(last_leaving, "blk", block_id, 1)
+        last_half = (last_kept.astype(F32) + pass_on(last_sent, 1).astype(F32)).astype(BF)
         do_came, last_dq = lax.optimization_barrier((do_came, last_dq))
         leaving = pl.pallas_call(
             functools.partial(attend_own_back_body, blocks, groups, rows, stripe),
@@ -1211,7 +1202,7 @@
             name="rotate_out",
         )(place, cos_table, sin_table, *grads)
     if small_path:
-        leaving, last_half, output_part = lax.optimization_barrier((leaving, last_half, output_part))
+        leaving, last_half = lax.optimization_barrier((leaving, last_half))
         back = [lax.all_to_all(leaving, "blk", split_axis=0, concat_axis=0, tiled=True)]
         back += [
             pass_on(lax.dynamic_index_in_dim(last_half, (block_id // 2) ^ k, 0, keepdims=False), 2 * k)
@@ -1220,14 +1211,20 @@
             for k in range(blocks // 2)
         ]
     else:
-        leaving, output_part = lax.optimization_barrier((leaving, output_part))
         back = swap(leaving, "blk")
+    leaving, merged, grad_attn = lax.optimization_barrier((leaving, merged, grad_attn))
+    output_part = lax.dot_general(merged, grad_attn, TN, preferred_element_type=F32).astype(BF)
+    output_part = output_part.reshape(groups, width // groups, width)
+
+    output_part = swap(
+        [
+            lax.dynamic_index_in_dim(output_part, group_id ^ k, 0, keepdims=False)
+            for k in range(groups)
+        ],
+        "ulysses",
+    )
+
     output_part = sum(x.astype(F32) for x in output_part).astype(BF).reshape(blocks, gain_rows, width)
-    output_part = halve(output_part, "blk", block_id, 1)
-    weight_sum = halve(feed_half, "blk", block_id, 2)
-    back, weight_sum, output_part = lax.optimization_barrier((back, weight_sum, output_part))
-    output_part = halve(output_part, "blk", block_id, 2)
-    weight_sum, weight_bit = jnp.concatenate([weight_sum, output_part], 1), 4
 
     if small_path:
         back_body = functools.partial(project_back_small_body, blocks, heads)
@@ -1288,18 +1285,32 @@
     input_sum = halve(
         input_part.reshape(groups, blocks, gain_rows, in_lanes).transpose(1, 0, 2, 3), "blk", block_id, 1
     )
-    small_parts = halve(
-        small_parts.reshape(groups, blocks, small_rows, in_lanes).transpose(1, 0, 2, 3), "blk", block_id, 1
-    )
-    input_sum = jnp.concatenate([input_sum, small_parts], 2)
+    out_lanes = output_part.shape[1] * output_part.shape[2] // in_lanes
+    rest = jnp.concatenate(
+        [
+            small_parts.reshape(groups, blocks, small_rows, in_lanes)
+            .transpose(1, 0, 2, 3)
+            .reshape(blocks, groups * small_rows, in_lanes),
+            output_part.reshape(blocks, out_lanes, in_lanes),
+        ],
+        1,
+    )
+    rest = halve(rest, "blk", block_id, 1)
+    input_sum, rest, feed_sum = lax.optimization_barrier((input_sum, rest, feed_sum))
+    input_sum = jnp.concatenate(
+        [input_sum.reshape(blocks // 2, groups * gain_rows, in_lanes), rest], 1
+    )
     bit = 2
     while bit < blocks:
         input_sum = halve(input_sum, "blk", block_id, bit)
         bit *= 2
-    while weight_bit < blocks:
-        weight_sum = halve(weight_sum, "blk", block_id, weight_bit)
-        weight_bit *= 2
-    weight_sum, input_sum = weight_sum[0], input_sum[0]
+    input_sum = input_sum[0]
+    at = groups * gain_rows
+    small_sum = input_sum[at : at + groups * small_rows]
+    output_grad = input_sum[at + groups * small_rows :].reshape(gain_rows, width).astype(F32)
+    input_sum = jnp.concatenate(
+        [input_sum[:at].reshape(groups, gain_rows, in_lanes), small_sum.reshape(groups, small_rows, in_lanes)], 1
+    )
     final = jnp.stack(
         swap(
             [
@@ -1311,9 +1322,8 @@
     )
     small_sum = jnp.sum(final[:, gain_rows:].astype(F32), 0).reshape(-1)
     input_sum = unscramble(final[:, :gain_rows], group_id, 0).astype(F32)
-    reduce_grad = weight_sum[:ff_rows].astype(F32)
-    output_grad = weight_sum[-gain_rows:].astype(F32)
-    expand_rows = weight_sum[ff_rows:-gain_rows].reshape(groups, gain_rows, width)
+    reduce_grad = feed_sum[:ff_rows].astype(F32)
+    expand_rows = feed_sum[ff_rows:].reshape(groups, gain_rows, width)
     expand_came = jnp.stack(
         swap(
             [

time: 333 us -> 321 us (0.964)
  other arithmetic: 28.4 us -> 22.7 us
    ppermute x10 -> x4, waiting for transfers between devices: 53.9 us -> 27.9 us  [halve(): came = lax.ppermute(sent, axis, [(i, i ^ bit) for i in range(size)])]
    ppermute x21, waiting for transfers between devices: 6.04 us -> 18.1 us  [swap(): lax.ppermute(x, axis, [(i, i ^ k) for i in range(size)])]
    ppermute x7 -> x8, waiting for transfers between devices: 44.8 us -> 53.6 us  [on_device(): lax.ppermute(x, 'blk', [(i, i ^ bit) for i in range(blocks)])]
    ppermute x10 -> x4, starting transfers between devices: 8.02 us -> 6.21 us  [halve(): came = lax.ppermute(sent, axis, [(i, i ^ bit) for i in range(size)])]
    ppermute x7 -> x8, starting transfers between devices: 9.9 us -> 10.1 us  [on_device(): lax.ppermute(x, 'blk', [(i, i ^ bit) for i in range(blocks)])]
  transfers between devices with their start and end apart: 44 -> 40, of which waited for: 17 -> 18; matrix products, arithmetic and copies ran while one was open for 11% -> 8% of each run, Pallas kernels for 22% -> 22%
where the time goes in v6:
time: 321 us; the launch traced here: 319 us
  waiting for transfers between devices  128 us (40%)
  Pallas kernels  78.7 us (25%)
  starting transfers between devices  52.7 us (16%)
  other arithmetic  22.7 us (7%)
  between operations  18.6 us (6%)
  local copies, waits for them, and re-layouts  18 us (6%)
    ppermute x8, waiting for transfers between devices, on_device(): lax.ppermute(x, 'blk', [(i, i ^ bit) for i in range(blocks)])  53.6 us
    ppermute x4, waiting for transfers between devices, halve(): came = lax.ppermute(sent, axis, [(i, i ^ bit) for i in range(size)])  27.9 us
    all_to_all x3, waiting for transfers between devices, exchange(): return lax.all_to_all(x, ALL, split_axis=0, concat_axis=0, tiled=True)  27 us
    ppermute x21, waiting for transfers between devices, swap(): lax.ppermute(x, axis, [(i, i ^ k) for i in range(size)])  18.1 us
    pallas_call x1, Pallas kernels, on_device(): pl.pallas_call(functools.partial(attend_own_body, blocks, groups, rows),...  15.8 us
    pallas_call x1, Pallas kernels, on_device(): pl.pallas_call(functools.partial(attend_own_back_body, blocks, groups, ro...  14.8 us
    ppermute x21, starting transfers between devices, swap(): lax.ppermute(x, axis, [(i, i ^ k) for i in range(size)])  14.7 us
    all_to_all x3, starting transfers between devices, exchange(): return lax.all_to_all(x, ALL, split_axis=0, concat_axis=0, tiled=True)  14.3 us
  transfers between devices with their start and end apart: 40, of which 18 were waited for; matrix products, arithmetic and copies ran while one was open for 8% of the time, Pallas kernels for 22%

profile of v6, /device:TPU:0, one launch (start us, length us, event | category | flops | bytes accessed | tf_op | source)
XLA Modules:
  0.0 319.4 jit_solution(8968582544226498151)
XLA Ops:
  7.2 1.1 reshape.532
  11.7 1.1 pad_maximum_fusion
  13.9 2.6 collective-permute-start.1
  16.5 6.1 %all-to-all-start = ((bf16[32,24,640]{2,1,0:T(8,128)(2,1)}), bf16[32,24,640]{2,1,0:T(8,128)(2,1)S(1)}, u32[]{:S(2)}, u32[]{:S(2)}) async-start(bf16[32,24,640]{2,1,0:T(8,128)(2,1)} %bitcast.9), calls=%async_computation | async-start | bytes 1966080 | tf_op jit(solution)/shard_map/all_to_all | solution.py:19
  30.8 5.7 %sine_multiply_fusion = (f32[2048,128]{1,0:T(8,128)}, f32[2048,128]{1,0:T(8,128)}) fusion(f32[128]{0:T(128)S(1)} %compare_select_fusion.2, f32[128]{0:T(128)S(1)} %mul.164, f32[2048]{0:T(1024)S(1)} %subtract_convert_fusion, f32[2048]{0:T(1024)S(1)} %subtract_convert_fusion.1, pred[128]{0:T(512)(128)(4,1)S(1)} %iota_compare_fusion.7), kind=kLoop, calls=%fused_computation.2 | loop fusion | flops 786432 | bytes 2114688 | tf_op jit(solution)/shard_map/mul | solution.py:915
  38.5 10.3 %all-to-all-done = bf16[32,24,640]{2,1,0:T(8,128)(2,1)S(1)} async-done(((bf16[32,24,640]{2,1,0:T(8,128)(2,1)}), bf16[32,24,640]{2,1,0:T(8,128)(2,1)S(1)}, u32[]{:S(2)}, u32[]{:S(2)}) %all-to-all-start) | async-done | bytes 983072 | tf_op jit(solution)/shard_map/all_to_all | solution.py:19
  50.4 4.2 %project.1 = (bf16[8,400,128]{2,1,0:T(8,128)(2,1)}, bf16[256,128]{1,0:T(8,128)(2,1)}) custom-call(f32[3,768]{1,0:T(4,128)} %get-tuple-element.191.c_ref, f32[3,768]{1,0:T(4,128)} %get-tuple-element.190.shift_ref, bf16[768,640]{1,0:T(8,128)(2,1)} %bitcast.187, bf16[3,64,768]{2,1,0:T(8,128)(2,1)} %copy-done.14, bf16[3,64,768]{2,1,0:T(8,128)(2,1)} %copy-done.36, ...), custom_call_target="tpu_custom_call" | custom-call | flops 679477248 | bytes 1179648 | tf_op jit(solution)/shard_map/project/pallas_call | solution.py:980
  54.6 3.5 %all-to-all-start.1 = ((bf16[8,400,128]{2,1,0:T(8,128)(2,1)}), bf16[8,400,128]{2,1,0:T(8,128)(2,1)S(1)}, u32[]{:S(2)}, u32[]{:S(2)}) async-start(bf16[8,400,128]{2,1,0:T(8,128)(2,1)} %get-tuple-element.95), calls=%async_computation.1 | async-start | bytes 1638400 | tf_op jit(solution)/shard_map/all_to_all | solution.py:993
  58.2 1.9 collective-permute-start.3
  60.1 2.4 collective-permute-start.4
  62.6 16.1 %collective-permute-done.3 = bf16[256,128]{1,0:T(8,128)(2,1)S(1)} collective-permute-done((bf16[256,128]{1,0:T(8,128)(2,1)}, bf16[256,128]{1,0:T(8,128)(2,1)S(1)}, u32[]{:S(2)}, u32[]{:S(2)}) %collective-permute-start.3) | collective-permute-done | bytes 65568 | tf_op jit(solution)/shard_map/ppermute | solution.py:994
  78.7 21.0 %collective-permute-done.4 = bf16[256,128]{1,0:T(8,128)(2,1)S(1)} collective-permute-done((bf16[256,128]{1,0:T(8,128)(2,1)}, bf16[256,128]{1,0:T(8,128)(2,1)S(1)}, u32[]{:S(2)}, u32[]{:S(2)}) %collective-permute-start.4) | collective-permute-done | bytes 65568 | tf_op jit(solution)/shard_map/ppermute | solution.py:994
  101.9 15.8 %attend_own.1 = (bf16[32,32,128]{2,1,0:T(8,128)(2,1)}, bf16[2048,64]{1,0:T(8,128)(2,1)}, bf16[2304,64]{1,0:T(8,128)(2,1)}, bf16[2304,64]{1,0:T(8,128)(2,1)}, bf1...) custom-call(s32[2]{0:T(128)} %pad_add_fusion.1.place_ref, s32[16]{0:T(128)} %reshape.542.range_ref, s32[8,1,256]{2,1,0:T(1,128)} %bitcast.211, ...), custom_call_target="tpu_custom_call" | custom-call | flops 268435456 | bytes 4194304 | tf_op jit(solution)/shard_map/attend_own/pallas_call | solution.py:1020
  118.4 8.3 %attend_last.1 = (bf16[32,40,128]{2,1,0:T(8,128)(2,1)}, bf16[256,64]{1,0:T(8,128)(2,1)}, bf16[2304,64]{1,0:T(8,128)(2,1)}, bf16[2304,64]{1,0:T(8,128)(2,1)}, bf1...) custom-call(s32[2]{0:T(128)} %pad_add_fusion.1.place_ref, s32[2]{0:T(128)} %add_bitcast_fusion.range_ref, ...), custom_call_target="tpu_custom_call" | custom-call | flops 67108864 | bytes 2097152 | tf_op jit(solution)/shard_map/attend_last/pallas_call | solution.py:1036
  126.7 5.5 %all-to-all-start.2 = ((bf16[32,40,128]{2,1,0:T(8,128)(2,1)}), bf16[32,40,128]{2,1,0:T(8,128)(2,1)S(1)}, u32[]{:S(2)}, u32[]{:S(2)}) async-start(bf16[32,40,128]{2,1,0:T(8,128)(2,1)} %get-tuple-element.101), calls=%async_computation.2 | async-start | bytes 655360 | tf_op jit(solution)/shard_map/all_to_all | solution.py:19
  132.4 1.7 collective-permute-start.11
  135.7 15.3 %all-to-all-done.2.came_ref = bf16[32,40,128]{2,1,0:T(8,128)(2,1)S(1)} async-done(((bf16[32,40,128]{2,1,0:T(8,128)(2,1)}), bf16[32,40,128]{2,1,0:T(8,128)(2,1)S(1)}, u32[]{:S(2)}, u32[]{:S(2)}) %all-to-all-start.2) | async-done | bytes 327712 | tf_op jit(solution)/shard_map/all_to_all | solution.py:19
  151.0 1.6 all-gather.3.cloned.1.call-done
  152.6 3.1 middle.1
  155.9 1.5 collective-permute-start.8
  157.5 11.5 %feed.1 = (bf16[192,768]{1,0:T(8,128)(2,1)}, f32[192,768]{1,0:T(8,128)}, bf16[192,768]{1,0:T(8,128)(2,1)}, bf16[32,40,128]{2,1,0:T(8,128)(2,1)}, f32[15,768]{1,0:T(8,128)}) custom-call(bf16[32,216,768]{2,1,0:T(8,128)(2,1)} %bitcast.171, bf16[32,216,768]{2,1,0:T(8,128)(2,1)} %bitcast.172, bf16[32,216,768]{2,1,0:T(8,128)(2,1)} %bitcast.173, ...), custom_call_target="tpu_custom_call" | custom-call | flops 3623878656 | bytes 9437184 | tf_op jit(solution)/shard_map/feed/pallas_call | solution.py:1094
  169.0 2.8 all-to-all-start.3
  173.6 9.0 %feed_weights.1 = (bf16[8,192,768]{2,1,0:T(8,128)(2,1)}, f32[1,768]{1,0:T(1,128)}) custom-call(s32[2]{0:T(128)} %pad_add_fusion.1.place_ref, bf16[32,216,768]{2,1,0:T(8,128)(2,1)} %bitcast.174, bf16[32,216,768]{2,1,0:T(8,128)(2,1)} %bitcast.175, f32[4,1,768]{2,1,0:T(1,128)} %reshape.575.ex_bias_ref.bias_ref, f32[3,768]{1,0:T(4,128)} %get-tuple-element.186.gate2_ref.gate_ref, ...), custom_call_target="tpu_custom_call" | custom-call | flops 4529848320 | bytes 9437184 | tf_op jit(solution)/shard_map/feed_weights/pallas_call | solution.py:1127
  182.5 1.4 all-to-all-done.3.do_ref
  184.6 7.1 %attend_last_back.1 = (f32[256,128]{1,0:T(8,128)}, bf16[4,256,128]{2,1,0:T(8,128)(2,1)}, bf16[4,256,128]{2,1,0:T(8,128)(2,1)}) custom-call(s32[2]{0:T(128)} %pad_add_fusion.1.place_ref, s32[2]{0:T(128)} %add_bitcast_fusion.range_ref, s32[1,1,256]{2,1,0:T(1,128)} %reshape_reshape.10.low_ref, s32[1,1,256]{2,1,0:T(1,128)} %reshape_reshape.11.high_ref, ...), custom_call_target="tpu_custom_call" | custom-call | flops 134217728 | bytes 2097152 | tf_op jit(solution)/shard_map/attend_last_back/pallas_call | solution.py:1157
  192.6 14.8 %attend_own_back.1 = bf16[8,400,128]{2,1,0:T(8,128)(2,1)} custom-call(s32[2]{0:T(128)} %pad_add_fusion.1.place_ref, s32[16]{0:T(128)} %reshape.542.range_ref, s32[8,1,256]{2,1,0:T(1,128)} %bitcast.212, s32[8,1,256]{2,1,0:T(1,128)} %bitcast.221, f32[2048,128]{1,0:T(8,128)} %get-tuple-element.88.cos_ref, f32[2048,128]{1,0:T(8,128)} %get-tuple-element.89.sin_ref, ...), custom_call_target="tpu_custom_call" | custom-call | flops 536870912 | bytes 4194304 | tf_op jit(solution)/shard_map/attend_own_back/pallas_call | solution.py:1172
  207.6 3.7 %all-to-all-start.4 = ((bf16[8,400,128]{2,1,0:T(8,128)(2,1)}), bf16[8,400,128]{2,1,0:T(8,128)(2,1)S(1)}, u32[]{:S(2)}, u32[]{:S(2)}) async-start(bf16[8,400,128]{2,1,0:T(8,128)(2,1)} %attend_own_back.1), calls=%async_computation.4 | async-start | bytes 1638400 | tf_op jit(solution)/shard_map/all_to_all | solution.py:1206
  212.4 1.0 collective-permute-start.22
  215.0 1.8 collective-permute-start.14
  216.8 2.4 collective-permute-start.15
  219.4 2.9 collective-permute-done.22
  222.3 5.4 %collective-permute-done.23 = bf16[192,768]{1,0:T(8,128)(2,1)S(1)} collective-permute-done((bf16[192,768]{1,0:T(8,128)(2,1)S(1)}, bf16[192,768]{1,0:T(8,128)(2,1)S(1)}, u32[]{:S(2)}, u32[]{:S(2)}) %collective-permute-start.23) | collective-permute-done | bytes 294944 | tf_op jit(solution)/shard_map/ppermute | solution.py:50
  228.4 7.4 %collective-permute-done.14.refs_6_ = bf16[256,128]{1,0:T(8,128)(2,1)S(1)} collective-permute-done((bf16[256,128]{1,0:T(8,128)(2,1)S(1)}, bf16[256,128]{1,0:T(8,128)(2,1)S(1)}, u32[]{:S(2)}, u32[]{:S(2)}) %collective-permute-start.14) | collective-permute-done | bytes 65568 | tf_op jit(solution)/shard_map/ppermute | solution.py:994
  235.8 9.2 %collective-permute-done.15.refs_7_ = bf16[256,128]{1,0:T(8,128)(2,1)S(1)} collective-permute-done((bf16[256,128]{1,0:T(8,128)(2,1)S(1)}, bf16[256,128]{1,0:T(8,128)(2,1)S(1)}, u32[]{:S(2)}, u32[]{:S(2)}) %collective-permute-start.15) | collective-permute-done | bytes 65568 | tf_op jit(solution)/shard_map/ppermute | solution.py:994
  245.9 4.9 %project_back.1 = (bf16[3,64,768]{2,1,0:T(8,128)(2,1)}, bf16[3,64,768]{2,1,0:T(8,128)(2,1)}, bf16[3,64,768]{2,1,0:T(8,128)(2,1)}, bf16[3,64,768]{2,1,0:T(8,128)(...) custom-call(f32[3,768]{1,0:T(4,128)} %get-tuple-element.191.c_ref, ...), custom_call_target="tpu_custom_call" | custom-call | flops 1358954496 | bytes 1179648 | tf_op jit(solution)/shard_map/project_back/pallas_call | solution.py:1237
  250.8 1.5 collective-permute-start.18
  256.1 1.4 collective-permute-start.24
  258.4 2.5 collective-permute-done.18
  260.9 5.4 %collective-permute-done.19 = bf16[3,64,768]{2,1,0:T(8,128)(2,1)S(1)} collective-permute-done((bf16[3,64,768]{2,1,0:T(8,128)(2,1)}, bf16[3,64,768]{2,1,0:T(8,128)(2,1)S(1)}, u32[]{:S(2)}, u32[]{:S(2)}) %collective-permute-start.19) | collective-permute-done | bytes 294944 | tf_op jit(solution)/shard_map/ppermute | solution.py:50
  266.8 2.4 collective-permute-done.24
  269.3 10.3 %collective-permute-done.20 = bf16[4,4,24,576]{3,2,1,0:T(8,128)(2,1)S(1)} collective-permute-done((bf16[4,4,24,576]{3,2,1,0:T(8,128)(2,1)S(1)}, bf16[4,4,24,576]{3,2,1,0:T(8,128)(2,1)S(1)}, u32[]{:S(2)}, u32[]{:S(2)}) %collective-permute-start.20) | collective-permute-done | bytes 442400 | tf_op jit(solution)/shard_map/ppermute | solution.py:72
  279.8 1.6 collective-permute-start.25
  283.2 1.5 collective-permute-start.31
  285.1 6.2 %collective-permute-done.25 = bf16[2,160,576]{2,1,0:T(8,128)(2,1)S(1)} collective-permute-done((bf16[2,160,576]{2,1,0:T(8,128)(2,1)S(1)}, bf16[2,160,576]{2,1,0:T(8,128)(2,1)S(1)}, u32[]{:S(2)}, u32[]{:S(2)}) %collective-permute-start.25) | collective-permute-done | bytes 368672 | tf_op jit(solution)/shard_map/ppermute | solution.py:72
  291.4 2.5 collective-permute-start.26
  293.9 9.0 %collective-permute-done.26 = bf16[1,160,576]{2,1,0:T(8,128)(2,1)S(1)} collective-permute-done((bf16[1,160,576]{2,1,0:T(8,128)(2,1)S(1)}, bf16[1,160,576]{2,1,0:T(8,128)(2,1)S(1)}, u32[]{:S(2)}, u32[]{:S(2)}) %collective-permute-start.26) | collective-permute-done | bytes 184352 | tf_op jit(solution)/shard_map/ppermute | solution.py:72
  303.1 1.6 collective-permute-start.28
  307.2 1.0 collective-permute-done.29
  (280 shorter events, 40.0 us)
Async XLA Ops:
  12.8 18.0 %copy-start.26 = (bf16[24,3072]{1,0:T(8,128)(2,1)S(1)}, bf16[24,3072]{1,0:T(8,128)(2,1)}, u32[]{:S(2)}) copy-start(bf16[24,3072]{1,0:T(8,128)(2,1)} %param.24) | copy-start | bytes 442372
  13.3 23.2 %copy-start.14 = (bf16[3,64,768]{2,1,0:T(8,128)(2,1)}, bf16[3,64,768]{2,1,0:T(8,128)(2,1)S(1)}, u32[]{:S(2)}) copy-start(bf16[3,64,768]{2,1,0:T(8,128)(2,1)S(1)} %fusion.7.refs_0_) | copy-start | bytes 884740
  13.4 35.6 %collective-permute-start = (bf16[3,64,768]{2,1,0:T(8,128)(2,1)S(1)}, bf16[3,64,768]{2,1,0:T(8,128)(2,1)S(1)}, u32[]{:S(2)}, u32[]{:S(2)}) collective-permute-start(bf16[3,64,768]{2,1,0:T(8,128)(2,1)S(1)} %fusion.7.refs_0_), channel_id=1, source_target_pairs={{0,8},{8,0},{16,24},{24,16},{1,9},{9,1},{17,25},{25,17},{2,10},{10... | collective-permute-start | bytes 884744 | tf_op jit(solution)/shard_map/ppermute | solution.py:50
  13.9 35.1 %collective-permute-start.1 = (bf16[3,64,768]{2,1,0:T(8,128)(2,1)S(1)}, bf16[3,64,768]{2,1,0:T(8,128)(2,1)S(1)}, u32[]{:S(2)}, u32[]{:S(2)}) collective-permute-start(bf16[3,64,768]{2,1,0:T(8,128)(2,1)S(1)} %fusion.7.refs_0_), channel_id=1, source_target_pairs={{0,16},{8,24},{16,0},{24,8},{1,17},{9,25},{17,1},{25,9},{2,18},{10... | collective-permute-start | bytes 884744 | tf_op jit(solution)/shard_map/ppermute | solution.py:50
  16.5 32.5 %collective-permute-start.2 = (bf16[3,64,768]{2,1,0:T(8,128)(2,1)S(1)}, bf16[3,64,768]{2,1,0:T(8,128)(2,1)S(1)}, u32[]{:S(2)}, u32[]{:S(2)}) collective-permute-start(bf16[3,64,768]{2,1,0:T(8,128)(2,1)S(1)} %fusion.7.refs_0_), channel_id=1, source_target_pairs={{0,24},{8,16},{16,8},{24,0},{1,25},{9,17},{17,9},{25,1},{2,26},{10... | collective-permute-start | bytes 884744 | tf_op jit(solution)/shard_map/ppermute | solution.py:50
  16.5 32.2 %all-to-all-start = ((bf16[32,24,640]{2,1,0:T(8,128)(2,1)}), bf16[32,24,640]{2,1,0:T(8,128)(2,1)S(1)}, u32[]{:S(2)}, u32[]{:S(2)}) async-start(bf16[32,24,640]{2,1,0:T(8,128)(2,1)} %bitcast.9), calls=%async_computation | async-start | bytes 1966080 | tf_op jit(solution)/shard_map/all_to_all | solution.py:19
  22.6 15.1 %copy-start.27 = (bf16[96,768]{1,0:T(8,128)(2,1)S(1)}, bf16[96,768]{1,0:T(8,128)(2,1)}, u32[]{:S(2)}) copy-start(bf16[96,768]{1,0:T(8,128)(2,1)} %param.26) | copy-start | bytes 442372
  22.6 15.1 %copy-start.30 = (bf16[24,768]{1,0:T(8,128)(2,1)S(1)}, bf16[24,768]{1,0:T(8,128)(2,1)}, u32[]{:S(2)}) copy-start(bf16[24,768]{1,0:T(8,128)(2,1)} %param.22) | copy-start | bytes 110596
  22.6 130.0 %all-gather.3.cloned.1.call-start = ((), (), s32[]{:S(2)}) async-start(), calls=%async_computation.7 | async-start | bytes 10948608 | tf_op jit(solution)/shard_map/all_gather | solution.py:948
  29.1 19.9 %copy-start.28 = (s32[2048]{0:T(1024)}, s32[2048]{0:T(1024)S(1)}, u32[]{:S(2)}) copy-start(s32[2048]{0:T(1024)S(1)} %get-tuple-element.206) | copy-start | bytes 24580
  54.6 46.3 %all-to-all-start.1 = ((bf16[8,400,128]{2,1,0:T(8,128)(2,1)}), bf16[8,400,128]{2,1,0:T(8,128)(2,1)S(1)}, u32[]{:S(2)}, u32[]{:S(2)}) async-start(bf16[8,400,128]{2,1,0:T(8,128)(2,1)} %get-tuple-element.95), calls=%async_computation.1 | async-start | bytes 1638400 | tf_op jit(solution)/shard_map/all_to_all | solution.py:993
  58.2 20.5 %collective-permute-start.3 = (bf16[256,128]{1,0:T(8,128)(2,1)}, bf16[256,128]{1,0:T(8,128)(2,1)S(1)}, u32[]{:S(2)}, u32[]{:S(2)}) collective-permute-start(bf16[256,128]{1,0:T(8,128)(2,1)} %get-tuple-element.96), channel_id=1, source_target_pairs={{0,2},{1,3},{2,0},{3,1},{4,6},{5,7},{6,4},{7,5},{8,10},{9,11},{10,... | collective-permute-start | bytes 196616 | tf_op jit(solution)/shard_map/ppermute | solution.py:994
  60.1 39.6 %collective-permute-start.4 = (bf16[256,128]{1,0:T(8,128)(2,1)}, bf16[256,128]{1,0:T(8,128)(2,1)S(1)}, u32[]{:S(2)}, u32[]{:S(2)}) collective-permute-start(bf16[256,128]{1,0:T(8,128)(2,1)} %get-tuple-element.96), channel_id=1, source_target_pairs={{0,4},{1,5},{2,6},{3,7},{4,0},{5,1},{6,2},{7,3},{8,12},{9,13},{10,... | collective-permute-start | bytes 196616 | tf_op jit(solution)/shard_map/ppermute | solution.py:994
  62.5 37.2 %collective-permute-start.5 = (bf16[256,128]{1,0:T(8,128)(2,1)}, bf16[256,128]{1,0:T(8,128)(2,1)S(1)}, u32[]{:S(2)}, u32[]{:S(2)}) collective-permute-start(bf16[256,128]{1,0:T(8,128)(2,1)} %get-tuple-element.96), channel_id=1, source_target_pairs={{0,6},{1,7},{2,4},{3,5},{4,2},{5,3},{6,0},{7,1},{8,14},{9,15},{10,... | collective-permute-start | bytes 196616 | tf_op jit(solution)/shard_map/ppermute | solution.py:994
  100.6 17.1 %copy-start.8 = (bf16[4,256,128]{2,1,0:T(8,128)(2,1)}, bf16[4,256,128]{2,1,0:T(8,128)(2,1)S(1)}, u32[]{:S(2)}) copy-start(bf16[4,256,128]{2,1,0:T(8,128)(2,1)S(1)} %pad_maximum_fusion.2.refs_1_) | copy-start | bytes 786436
  100.6 17.1 %collective-permute-start.6 = (bf16[4,256,128]{2,1,0:T(8,128)(2,1)S(1)}, bf16[4,256,128]{2,1,0:T(8,128)(2,1)S(1)}, u32[]{:S(2)}, u32[]{:S(2)}) collective-permute-start(bf16[4,256,128]{2,1,0:T(8,128)(2,1)S(1)} %pad_maximum_fusion.2.refs_1_), channel_id=1, source_target_pairs={{0,1},{1,0},{2,3},{3,2},{4,5},{5,4},{6,7},{7,6},{8,9},{9,8},{10,11... | collective-permute-start | bytes 786440 | tf_op jit(solution)/shard_map/ppermute | solution.py:994
  126.7 24.3 %all-to-all-start.2 = ((bf16[32,40,128]{2,1,0:T(8,128)(2,1)}), bf16[32,40,128]{2,1,0:T(8,128)(2,1)S(1)}, u32[]{:S(2)}, u32[]{:S(2)}) async-start(bf16[32,40,128]{2,1,0:T(8,128)(2,1)} %get-tuple-element.101), calls=%async_computation.2 | async-start | bytes 655360 | tf_op jit(solution)/shard_map/all_to_all | solution.py:19
  132.2 25.2 %collective-permute-start.10 = (bf16[192,768]{1,0:T(8,128)(2,1)S(1)}, bf16[192,768]{1,0:T(8,128)(2,1)S(1)}, u32[]{:S(2)}, u32[]{:S(2)}) collective-permute-start(bf16[192,768]{1,0:T(8,128)(2,1)S(1)} %bitcast.193), channel_id=1, source_target_pairs={{0,8},{8,0},{16,24},{24,16},{1,9},{9,1},{17,25},{25,17},{2,10},{10... | collective-permute-start | bytes 884744 | tf_op jit(solution)/shard_map/ppermute | solution.py:50
  132.4 39.4 %collective-permute-start.11 = (bf16[192,768]{1,0:T(8,128)(2,1)S(1)}, bf16[192,768]{1,0:T(8,128)(2,1)S(1)}, u32[]{:S(2)}, u32[]{:S(2)}) collective-permute-start(bf16[192,768]{1,0:T(8,128)(2,1)S(1)} %bitcast.194), channel_id=1, source_target_pairs={{0,16},{8,24},{16,0},{24,8},{1,17},{9,25},{17,1},{25,9},{2,18},{10... | collective-permute-start | bytes 884744 | tf_op jit(solution)/shard_map/ppermute | solution.py:50
  134.1 37.8 %collective-permute-start.12 = (bf16[192,768]{1,0:T(8,128)(2,1)S(1)}, bf16[192,768]{1,0:T(8,128)(2,1)S(1)}, u32[]{:S(2)}, u32[]{:S(2)}) collective-permute-start(bf16[192,768]{1,0:T(8,128)(2,1)S(1)} %bitcast.195), channel_id=1, source_target_pairs={{0,24},{8,16},{16,8},{24,0},{1,25},{9,17},{17,9},{25,1},{2,26},{10... | collective-permute-start | bytes 884744 | tf_op jit(solution)/shard_map/ppermute | solution.py:50
  155.7 16.2 %collective-permute-start.7 = (bf16[192,768]{1,0:T(8,128)(2,1)}, bf16[192,768]{1,0:T(8,128)(2,1)S(1)}, u32[]{:S(2)}, u32[]{:S(2)}) collective-permute-start(bf16[192,768]{1,0:T(8,128)(2,1)} %get-tuple-element.102.second_ref.refs_0_), channel_id=1, source_target_pairs={{0,8},{8,0},{16,24},{24,16},{1,9},{9,1},{17,25},{25,17},{2,10},{10... | collective-permute-start | bytes 884744 | tf_op jit(solution)/shard_map/ppermute | solution.py:50
  155.9 16.0 %collective-permute-start.8 = (bf16[192,768]{1,0:T(8,128)(2,1)}, bf16[192,768]{1,0:T(8,128)(2,1)S(1)}, u32[]{:S(2)}, u32[]{:S(2)}) collective-permute-start(bf16[192,768]{1,0:T(8,128)(2,1)} %get-tuple-element.102.second_ref.refs_0_), channel_id=1, source_target_pairs={{0,16},{8,24},{16,0},{24,8},{1,17},{9,25},{17,1},{25,9},{2,18},{10... | collective-permute-start | bytes 884744 | tf_op jit(solution)/shard_map/ppermute | solution.py:50
  157.4 14.5 %collective-permute-start.9 = (bf16[192,768]{1,0:T(8,128)(2,1)}, bf16[192,768]{1,0:T(8,128)(2,1)S(1)}, u32[]{:S(2)}, u32[]{:S(2)}) collective-permute-start(bf16[192,768]{1,0:T(8,128)(2,1)} %get-tuple-element.102.second_ref.refs_0_), channel_id=1, source_target_pairs={{0,24},{8,16},{16,8},{24,0},{1,25},{9,17},{17,9},{25,1},{2,26},{10... | collective-permute-start | bytes 884744 | tf_op jit(solution)/shard_map/ppermute | solution.py:50
  169.0 14.9 %all-to-all-start.3 = ((bf16[32,40,128]{2,1,0:T(8,128)(2,1)}), bf16[32,40,128]{2,1,0:T(8,128)(2,1)S(1)}, u32[]{:S(2)}, u32[]{:S(2)}) async-start(bf16[32,40,128]{2,1,0:T(8,128)(2,1)} %get-tuple-element.107), calls=%async_computation.3 | async-start | bytes 655360 | tf_op jit(solution)/shard_map/all_to_all | solution.py:19
  171.8 108.0 %reduce-scatter.2.cloned.1.call-start = ((), (), s32[]{:S(2)}) async-start(), calls=%async_computation.6 | async-start | bytes 2654208 | tf_op jit(solution)/shard_map/reduce_scatter | solution.py:1154
  191.7 15.8 %collective-permute-start.13 = (bf16[4,256,128]{2,1,0:T(8,128)(2,1)}, bf16[4,256,128]{2,1,0:T(8,128)(2,1)S(1)}, u32[]{:S(2)}, u32[]{:S(2)}) collective-permute-start(bf16[4,256,128]{2,1,0:T(8,128)(2,1)} %get-tuple-element.124), channel_id=1, source_target_pairs={{0,1},{1,0},{2,3},{3,2},{4,5},{5,4},{6,7},{7,6},{8,9},{9,8},{10,11... | collective-permute-start | bytes 786440 | tf_op jit(solution)/shard_map/ppermute | solution.py:994
  192.6 14.9 %copy-start.23 = (bf16[4,256,128]{2,1,0:T(8,128)(2,1)S(1)}, bf16[4,256,128]{2,1,0:T(8,128)(2,1)}, u32[]{:S(2)}) copy-start(bf16[4,256,128]{2,1,0:T(8,128)(2,1)} %get-tuple-element.123) | copy-start | bytes 786436
  207.6 37.3 %all-to-all-start.4 = ((bf16[8,400,128]{2,1,0:T(8,128)(2,1)}), bf16[8,400,128]{2,1,0:T(8,128)(2,1)S(1)}, u32[]{:S(2)}, u32[]{:S(2)}) async-start(bf16[8,400,128]{2,1,0:T(8,128)(2,1)} %attend_own_back.1), calls=%async_computation.4 | async-start | bytes 1638400 | tf_op jit(solution)/shard_map/all_to_all | solution.py:1206
  212.3 6.9 %collective-permute-start.21 = (bf16[192,768]{1,0:T(8,128)(2,1)S(1)}, bf16[192,768]{1,0:T(8,128)(2,1)S(1)}, u32[]{:S(2)}, u32[]{:S(2)}) collective-permute-start(bf16[192,768]{1,0:T(8,128)(2,1)S(1)} %get-tuple-element.163), channel_id=1, source_target_pairs={{0,8},{8,0},{16,24},{24,16},{1,9},{9,1},{17,25},{25,17},{2,10},{10... | collective-permute-start | bytes 884744 | tf_op jit(solution)/shard_map/ppermute | solution.py:50
  212.4 9.9 %collective-permute-start.22 = (bf16[192,768]{1,0:T(8,128)(2,1)S(1)}, bf16[192,768]{1,0:T(8,128)(2,1)S(1)}, u32[]{:S(2)}, u32[]{:S(2)}) collective-permute-start(bf16[192,768]{1,0:T(8,128)(2,1)S(1)} %get-tuple-element.165), channel_id=1, source_target_pairs={{0,16},{8,24},{16,0},{24,8},{1,17},{9,25},{17,1},{25,9},{2,18},{10... | collective-permute-start | bytes 884744 | tf_op jit(solution)/shard_map/ppermute | solution.py:50
  213.4 14.3 %collective-permute-start.23 = (bf16[192,768]{1,0:T(8,128)(2,1)S(1)}, bf16[192,768]{1,0:T(8,128)(2,1)S(1)}, u32[]{:S(2)}, u32[]{:S(2)}) collective-permute-start(bf16[192,768]{1,0:T(8,128)(2,1)S(1)} %get-tuple-element.164), channel_id=1, source_target_pairs={{0,24},{8,16},{16,8},{24,0},{1,25},{9,17},{17,9},{25,1},{2,26},{10... | collective-permute-start | bytes 884744 | tf_op jit(solution)/shard_map/ppermute | solution.py:50
  215.0 20.8 %collective-permute-start.14 = (bf16[256,128]{1,0:T(8,128)(2,1)S(1)}, bf16[256,128]{1,0:T(8,128)(2,1)S(1)}, u32[]{:S(2)}, u32[]{:S(2)}) collective-permute-start(bf16[256,128]{1,0:T(8,128)(2,1)S(1)} %get-tuple-element.170), channel_id=1, source_target_pairs={{0,2},{1,3},{2,0},{3,1},{4,6},{5,7},{6,4},{7,5},{8,10},{9,11},{10,... | collective-permute-start | bytes 196616 | tf_op jit(solution)/shard_map/ppermute | solution.py:994
  216.8 28.1 %collective-permute-start.15 = (bf16[256,128]{1,0:T(8,128)(2,1)S(1)}, bf16[256,128]{1,0:T(8,128)(2,1)S(1)}, u32[]{:S(2)}, u32[]{:S(2)}) collective-permute-start(bf16[256,128]{1,0:T(8,128)(2,1)S(1)} %get-tuple-element.169), channel_id=1, source_target_pairs={{0,4},{1,5},{2,6},{3,7},{4,0},{5,1},{6,2},{7,3},{8,12},{9,13},{10,... | collective-permute-start | bytes 196616 | tf_op jit(solution)/shard_map/ppermute | solution.py:994
  219.2 25.7 %collective-permute-start.16 = (bf16[256,128]{1,0:T(8,128)(2,1)S(1)}, bf16[256,128]{1,0:T(8,128)(2,1)S(1)}, u32[]{:S(2)}, u32[]{:S(2)}) collective-permute-start(bf16[256,128]{1,0:T(8,128)(2,1)S(1)} %get-tuple-element.168), channel_id=1, source_target_pairs={{0,6},{1,7},{2,4},{3,5},{4,2},{5,3},{6,0},{7,1},{8,14},{9,15},{10,... | collective-permute-start | bytes 196616 | tf_op jit(solution)/shard_map/ppermute | solution.py:994
  250.8 7.6 %collective-permute-start.17 = (bf16[3,64,768]{2,1,0:T(8,128)(2,1)}, bf16[3,64,768]{2,1,0:T(8,128)(2,1)S(1)}, u32[]{:S(2)}, u32[]{:S(2)}) collective-permute-start(bf16[3,64,768]{2,1,0:T(8,128)(2,1)} %get-tuple-element.128), channel_id=1, source_target_pairs={{0,8},{8,0},{16,24},{24,16},{1,9},{9,1},{17,25},{25,17},{2,10},{10... | collective-permute-start | bytes 884744 | tf_op jit(solution)/shard_map/ppermute | solution.py:50
  250.8 10.1 %collective-permute-start.18 = (bf16[3,64,768]{2,1,0:T(8,128)(2,1)}, bf16[3,64,768]{2,1,0:T(8,128)(2,1)S(1)}, u32[]{:S(2)}, u32[]{:S(2)}) collective-permute-start(bf16[3,64,768]{2,1,0:T(8,128)(2,1)} %get-tuple-element.129), channel_id=1, source_target_pairs={{0,16},{8,24},{16,0},{24,8},{1,17},{9,25},{17,1},{25,9},{2,18},{10... | collective-permute-start | bytes 884744 | tf_op jit(solution)/shard_map/ppermute | solution.py:50
  252.4 14.0 %collective-permute-start.19 = (bf16[3,64,768]{2,1,0:T(8,128)(2,1)}, bf16[3,64,768]{2,1,0:T(8,128)(2,1)S(1)}, u32[]{:S(2)}, u32[]{:S(2)}) collective-permute-start(bf16[3,64,768]{2,1,0:T(8,128)(2,1)} %get-tuple-element.130), channel_id=1, source_target_pairs={{0,24},{8,16},{16,8},{24,0},{1,25},{9,17},{17,9},{25,1},{2,26},{10... | collective-permute-start | bytes 884744 | tf_op jit(solution)/shard_map/ppermute | solution.py:50
  256.1 13.1 %collective-permute-start.24 = (bf16[4,64,576]{2,1,0:T(8,128)(2,1)S(1)}, bf16[4,64,576]{2,1,0:T(8,128)(2,1)S(1)}, u32[]{:S(2)}, u32[]{:S(2)}) collective-permute-start(bf16[4,64,576]{2,1,0:T(8,128)(2,1)S(1)} %fusion.23), channel_id=1, source_target_pairs={{0,1},{1,0},{2,3},{3,2},{4,5},{5,4},{6,7},{7,6},{8,9},{9,8},{10,11... | collective-permute-start | bytes 884744 | tf_op jit(solution)/shard_map/ppermute | solution.py:72
  257.6 21.9 %collective-permute-start.20 = (bf16[4,4,24,576]{3,2,1,0:T(8,128)(2,1)S(1)}, bf16[4,4,24,576]{3,2,1,0:T(8,128)(2,1)S(1)}, u32[]{:S(2)}, u32[]{:S(2)}) collective-permute-start(bf16[4,4,24,576]{3,2,1,0:T(8,128)(2,1)S(1)} %dynamic-slice_bitcast_fusion), channel_id=1, source_target_pairs={{0,1},{1,0},{2,3},{3,2},{4,5},{5,4},{6,7},{7,6},{8,9},{9,8},{10,11... | collective-permute-start | bytes 1327112 | tf_op jit(solution)/shard_map/ppermute | solution.py:72
  266.7 14.7 %copy-start.11 = (f32[192,768]{1,0:T(8,128)S(1)}, f32[192,768]{1,0:T(8,128)}, u32[]{:S(2)}) copy-start(f32[192,768]{1,0:T(8,128)} %get-tuple-element.106) | copy-start | bytes 1769476
  279.8 11.4 %collective-permute-start.25 = (bf16[2,160,576]{2,1,0:T(8,128)(2,1)S(1)}, bf16[2,160,576]{2,1,0:T(8,128)(2,1)S(1)}, u32[]{:S(2)}, u32[]{:S(2)}) collective-permute-start(bf16[2,160,576]{2,1,0:T(8,128)(2,1)S(1)} %fusion.19), channel_id=1, source_target_pairs={{0,2},{1,3},{2,0},{3,1},{4,6},{5,7},{6,4},{7,5},{8,10},{9,11},{10,... | collective-permute-start | bytes 1105928 | tf_op jit(solution)/shard_map/ppermute | solution.py:72
  283.1 10.8 %collective-permute-start.30 = (bf16[24,768]{1,0:T(8,128)(2,1)S(1)}, bf16[24,768]{1,0:T(8,128)(2,1)S(1)}, u32[]{:S(2)}, u32[]{:S(2)}) collective-permute-start(bf16[24,768]{1,0:T(8,128)(2,1)S(1)} %get-tuple-element.185), channel_id=1, source_target_pairs={{0,8},{8,0},{16,24},{24,16},{1,9},{9,1},{17,25},{25,17},{2,10},{10... | collective-permute-start | bytes 110600 | tf_op jit(solution)/shard_map/ppermute | solution.py:50
  283.2 10.7 %collective-permute-start.31 = (bf16[24,768]{1,0:T(8,128)(2,1)S(1)}, bf16[24,768]{1,0:T(8,128)(2,1)S(1)}, u32[]{:S(2)}, u32[]{:S(2)}) collective-permute-start(bf16[24,768]{1,0:T(8,128)(2,1)S(1)} %get-tuple-element.184), channel_id=1, source_target_pairs={{0,16},{8,24},{16,0},{24,8},{1,17},{9,25},{17,1},{25,9},{2,18},{10... | collective-permute-start | bytes 110600 | tf_op jit(solution)/shard_map/ppermute | solution.py:50
  284.7 9.2 %collective-permute-start.32 = (bf16[24,768]{1,0:T(8,128)(2,1)S(1)}, bf16[24,768]{1,0:T(8,128)(2,1)S(1)}, u32[]{:S(2)}, u32[]{:S(2)}) collective-permute-start(bf16[24,768]{1,0:T(8,128)(2,1)S(1)} %get-tuple-element.183), channel_id=1, source_target_pairs={{0,24},{8,16},{16,8},{24,0},{1,25},{9,17},{17,9},{25,1},{2,26},{10... | collective-permute-start | bytes 110600 | tf_op jit(solution)/shard_map/ppermute | solution.py:50
  291.4 11.5 %collective-permute-start.26 = (bf16[1,160,576]{2,1,0:T(8,128)(2,1)S(1)}, bf16[1,160,576]{2,1,0:T(8,128)(2,1)S(1)}, u32[]{:S(2)}, u32[]{:S(2)}) collective-permute-start(bf16[1,160,576]{2,1,0:T(8,128)(2,1)S(1)} %constant_dynamic-slice_fusion.1), channel_id=1, source_target_pairs={{0,4},{1,5},{2,6},{3,7},{4,0},{5,1},{6,2},{7,3},{8,12},{9,13},{10,... | collective-permute-start | bytes 552968 | tf_op jit(solution)/shard_map/ppermute | solution.py:72
  303.0 3.4 %collective-permute-start.27 = (bf16[32,576]{1,0:T(8,128)(2,1)S(1)}, bf16[32,576]{1,0:T(8,128)(2,1)S(1)}, u32[]{:S(2)}, u32[]{:S(2)}) collective-permute-start(bf16[32,576]{1,0:T(8,128)(2,1)S(1)} %get-tuple-element.175), channel_id=1, source_target_pairs={{0,8},{8,0},{16,24},{24,16},{1,9},{9,1},{17,25},{25,17},{2,10},{10... | collective-permute-start | bytes 110600 | tf_op jit(solution)/shard_map/ppermute | solution.py:50
  303.1 4.1 %collective-permute-start.28 = (bf16[32,576]{1,0:T(8,128)(2,1)S(1)}, bf16[32,576]{1,0:T(8,128)(2,1)S(1)}, u32[]{:S(2)}, u32[]{:S(2)}) collective-permute-start(bf16[32,576]{1,0:T(8,128)(2,1)S(1)} %get-tuple-element.176), channel_id=1, source_target_pairs={{0,16},{8,24},{16,0},{24,8},{1,17},{9,25},{17,1},{25,9},{2,18},{10... | collective-permute-start | bytes 110600 | tf_op jit(solution)/shard_map/ppermute | solution.py:50
  304.7 3.5 %collective-permute-start.29 = (bf16[32,576]{1,0:T(8,128)(2,1)S(1)}, bf16[32,576]{1,0:T(8,128)(2,1)S(1)}, u32[]{:S(2)}, u32[]{:S(2)}) collective-permute-start(bf16[32,576]{1,0:T(8,128)(2,1)S(1)} %get-tuple-element.177), channel_id=1, source_target_pairs={{0,24},{8,16},{16,8},{24,0},{1,25},{9,17},{17,9},{25,1},{2,26},{10... | collective-permute-start | bytes 110600 | tf_op jit(solution)/shard_map/ppermute | solution.py:50
  (34 other events, 134.9 us)
Sparse Core Ops, SparseCore 0:
  49.1 103.4 all-gather.2
  192.8 81.8 reduce-scatter.1

commit v7 on v6

--- a/solution.py
+++ b/solution.py
@@ -493,7 +493,7 @@
     return (position >= low) & (position < high)
 
 
-QB, KB = 256, 512
+QB, KB, STEP = 512, 512, 256
 
 
 def project_small_body(blocks, heads, c_ref, shift_ref, w_ref, *refs):
@@ -533,13 +533,13 @@
     return jnp.where(k >= 2, y[:, 64:], y[:, :64])
 
 
-def project_back_small_body(blocks, heads, c_ref, shift_ref, w_ref, *refs):
-    wide = refs[-1]
+def project_back_small_body(blocks, heads, place_ref, c_ref, shift_ref, w_ref, *refs):
+    wide, scattered = refs[-2:]
     few = blocks // 2
-    groups = (len(refs) - few - 5) // 2
+    groups = (len(refs) - few - 7) // 2
     tokens, in_ref, lasts = refs[:groups], refs[groups], refs[groups + 1 : groups + 1 + few]
     outs = refs[groups + 1 + few : 2 * groups + 1 + few]
-    grad_ref, sum_ref, dot_ref = refs[2 * groups + 1 + few : -1]
+    keep_ref, send_ref, sum_ref, dot_ref = refs[2 * groups + 1 + few : -2]
     micro, rows, width = tokens[0].shape
     count = groups * rows
     half, stripe = count // 2, rows // blocks
@@ -571,16 +571,23 @@
         dot_ref[m : m + 1] = jnp.sum(da * n, 0, keepdims=True)
         all_a.append(a)
         all_g.append(g)
-    grad_ref[...] = lax.dot_general(
+    x = lax.dot_general(
         jnp.concatenate(all_a, 0), jnp.concatenate(all_g, 0), TN, preferred_element_type=F32
-    ).astype(BF)
+    )
+    scattered[...] = x.reshape(scattered.shape)
+    mine = place_ref[1] & 1
+    for z in range(few):
+        for k in range(groups):
+            at = k * blocks + 2 * z
+            keep_ref[z, k] = scattered[at + mine].astype(BF)
+            send_ref[z, k] = scattered[at + 1 - mine].astype(BF)
 
 
 def attend_block(scores, q, low, high, first, stop, keys, values):
     count = q.shape[0]
 
     def score(t, top):
-        at = pl.multiple_of((first + 2 * t) * QB, QB)
+        at = pl.multiple_of((first + 2 * t) * STEP, STEP)
         s = lax.dot_general(keys[pl.ds(at, KB), :], q, NT, preferred_element_type=F32)
         s = jnp.where(keys_mask(low, high, at, KB), s, NEG)
         scores[t, :, :count] = s
@@ -591,7 +598,7 @@
 
     def weigh(t, carry):
         total, acc = carry
-        at = pl.multiple_of((first + 2 * t) * QB, QB)
+        at = pl.multiple_of((first + 2 * t) * STEP, STEP)
         p = jnp.exp(scores[t, :, :count] - top)
         return total + jnp.sum(p, 0, keepdims=True), acc + lax.dot_general(
             values[pl.ds(at, KB), :], p.astype(BF), TN, preferred_element_type=F32
@@ -624,9 +631,9 @@
         q_ref[at] = (x[:, :64] * 0.125).astype(BF)
         k_ref[at] = x[:, 64:].astype(BF)
         v_ref[at] = kept_v[...]
-    tail = slice(size, size + KB - QB)
+    tail = slice(size, size + KB - STEP)
     for ref in (k_ref, v_ref):
-        ref[tail] = jnp.zeros((KB - QB, 64), BF)
+        ref[tail] = jnp.zeros((KB - STEP, 64), BF)
 
     def run(i, _):
         o, lse = attend_block(
@@ -675,9 +682,9 @@
         x = turn(kept[...].astype(F32), turn_tables(cos_ref[at], sin_ref[at], True)[1])
         k_ref[at] = x[:, :64].astype(BF)
         v_ref[at] = kept[:, 64:]
-    tail = slice(size, size + KB - QB)
+    tail = slice(size, size + KB - STEP)
     for ref in (k_ref, v_ref):
-        ref[tail] = jnp.zeros((KB - QB, 64), BF)
+        ref[tail] = jnp.zeros((KB - STEP, 64), BF)
     wide[:, 64:] = jnp.zeros((devices * stripe, 64), F32)
     x = turn(wide[...], stripe_tables(place_ref, cos_ref, sin_ref, wide_cos, wide_sin, devices, rows, stripe))
     q_ref[...] = (x[:, :64] * 0.125).astype(BF)
@@ -704,7 +711,7 @@
     delta = jnp.sum((do.astype(F32) * o.astype(F32)).T, 0, keepdims=True)
 
     def step(t, dq):
-        at = pl.multiple_of((first + 2 * t) * QB, QB)
+        at = pl.multiple_of((first + 2 * t) * STEP, STEP)
         here = pl.ds(at, KB)
         k, v = keys[here, :], values[here, :]
         s = lax.dot_general(k, q, NT, preferred_element_type=F32)
@@ -913,7 +920,7 @@
     ) * jnp.tile(freqs, 4)[None, :]
     cos_table = jnp.cos(angles)
     sin_table = jnp.where((lane % 64 < 32)[None, :], -1.0, 1.0) * jnp.sin(angles)
-    query_rows = math.gcd(size, 256)
+    query_rows = math.gcd(size, QB)
     key_block = math.gcd(size, 256)
     first = jnp.arange(size // query_rows, dtype=jnp.int32) * query_rows
     ranges = key_ranges(first, first + query_rows - 1, pair_lengths, key_block)
@@ -928,7 +935,7 @@
         chunk = last_rows // stripe
         last_first = jnp.arange(devices // chunk, dtype=jnp.int32) * (chunk * rows) + block_id * stripe
         last_ranges = key_ranges(
-            last_first, last_first + (chunk - 1) * rows + stripe - 1, last_lengths, QB
+            last_first, last_first + (chunk - 1) * rows + stripe - 1, last_lengths, STEP
         )
         bounds = []
         for where, lens, pick, lump in (
@@ -1013,7 +1020,7 @@
     if small_path:
         whole = lambda *shape: jax.ShapeDtypeStruct(shape, BF)
         f32 = lambda *shape: jax.ShapeDtypeStruct(shape, F32)
-        padded = whole(size + KB - QB, 64)
+        padded = whole(size + KB - STEP, 64)
         own_args = (place, ranges, *bounds[:2], cos_table, sin_table)
         last_args = (place, last_ranges, *bounds[2:], cos_table, sin_table)
         specs = [smem] * 2 + [whole_vmem()] * 4
@@ -1161,7 +1168,7 @@
             out_shape=[f32(devices * stripe, 128)] + [whole(blocks // 2, count, 128)] * 2,
             scratch_shapes=[pltpu.VMEM((span, 128), BF)]
             + [pltpu.VMEM((devices * stripe, 128), F32)] * 2
-            + [pltpu.VMEM((size + KB - QB, 64), F32)] * 2,
+            + [pltpu.VMEM((size + KB - STEP, 64), F32)] * 2,
             cost_estimate=pl.CostEstimate(
                 flops=size * size * 32, transcendentals=size * size // 8, bytes_accessed=16 * size * 64
             ),
@@ -1178,7 +1185,7 @@
                 pltpu.VMEM((span, 128), BF), pltpu.VMEM((span, 64), BF),
                 pltpu.VMEM((devices, rows, 64), BF), pltpu.VMEM((size, 64), F32),
             ]
-            + [pltpu.VMEM((size + KB - QB, 64), F32)] * 2,
+            + [pltpu.VMEM((size + KB - STEP, 64), F32)] * 2,
             cost_estimate=pl.CostEstimate(
                 flops=2 * size * size * 64, transcendentals=size * size // 2, bytes_accessed=16 * size * 128
             ),
@@ -1228,41 +1235,30 @@
 
     if small_path:
         back_body = functools.partial(project_back_small_body, blocks, heads)
-        back_scratch = [pltpu.VMEM((count, 64), F32)]
-        back_args, back_specs = (), []
+        back_scratch = [
+            pltpu.VMEM((count, 64), F32), pltpu.VMEM((devices, gain_rows, heads * 3 * head_width), F32),
+        ]
+        back_args, back_specs = (place,), [smem]
+        back_grads = [jax.ShapeDtypeStruct((blocks // 2, groups, gain_rows, heads * 3 * head_width), BF)] * 2
     else:
         back_args, back_specs = (place,), [smem]
         back_body = functools.partial(project_back_body, blocks, pairs, heads, extra)
         back_scratch = [pltpu.VMEM((blocks, count, lanes), BF)]
+        back_grads = [jax.ShapeDtypeStruct((width, heads * 3 * head_width), BF)]
     returned = pl.pallas_call(
         back_body,
         out_shape=[jax.ShapeDtypeStruct((micro, rows, width), BF)] * groups
-        + [
-            jax.ShapeDtypeStruct((width, heads * 3 * head_width), BF),
-            jax.ShapeDtypeStruct((micro, width), F32),
-            jax.ShapeDtypeStruct((micro, width), F32),
-        ],
+        + back_grads
+        + [jax.ShapeDtypeStruct((micro, width), F32)] * 2,
         in_specs=back_specs + [whole_vmem()] * (3 + groups + len(back)),
-        out_specs=[whole_vmem()] * (groups + 3),
+        out_specs=[whole_vmem()] * (groups + 2 + len(back_grads)),
         scratch_shapes=back_scratch,
         cost_estimate=pl.CostEstimate(
             flops=4 * micro * count * width * 3 * 64 * heads, transcendentals=0, bytes_accessed=8 * own * width
         ),
         name="project_back",
     )(*back_args, c1, shift1, in_own, *n1_group, *back)
-    input_part, d_shift1, p1 = returned[groups:]
-    grad_first = sum(x.astype(F32) for x in swap(returned[:groups], "ulysses"))
-    e = grad_first * c1[:, None]
-    tokens_grad = (
-        grad_middle.reshape(micro, rows, width)
-        + r1
-        * (
-            e
-            - jnp.mean(e, -1, keepdims=True)
-            - n1 * jnp.mean(e * n1, -1, keepdims=True)
-        )
-    ).astype(BF)
-
+    *input_part, d_shift1, p1 = returned[groups:]
     grad_mods = jnp.concatenate(
         [d_shift1, p1 * gain1, d_gate1, d_shift2, p2 * gain2, d_gate2], 1
     )
@@ -1282,9 +1278,21 @@
     taken = small_parts.shape[1]
     small_rows = 8 * -(-taken // (8 * in_lanes))
     small_parts = jnp.pad(small_parts, ((0, 0), (0, small_rows * in_lanes - taken)))
-    input_sum = halve(
-        input_part.reshape(groups, blocks, gain_rows, in_lanes).transpose(1, 0, 2, 3), "blk", block_id, 1
-    )
+    if small_path:
+        kept, sent = input_part
+    else:
+        halves = (
+            input_part[0]
+            .reshape(groups, blocks, gain_rows, in_lanes)
+            .transpose(1, 0, 2, 3)
+            .reshape(blocks // 2, 2, groups, gain_rows, in_lanes)
+        )
+        sent = lax.dynamic_index_in_dim(halves, 1 - block_id % 2, 1, keepdims=False)
+        kept = lax.dynamic_index_in_dim(halves, block_id % 2, 1, keepdims=False)
+    sent, token_parts = lax.optimization_barrier((sent, returned[:groups]))
+    came = lax.ppermute(sent, "blk", [(i, i ^ 1) for i in range(blocks)])
+    input_sum = (kept.astype(F32) + came.astype(F32)).astype(BF)
+    token_parts = swap(token_parts, "ulysses")
     out_lanes = output_part.shape[1] * output_part.shape[2] // in_lanes
     rest = jnp.concatenate(
         [
@@ -1296,13 +1304,27 @@
         1,
     )
     rest = halve(rest, "blk", block_id, 1)
-    input_sum, rest, feed_sum = lax.optimization_barrier((input_sum, rest, feed_sum))
+    input_sum, rest, feed_sum, token_parts = lax.optimization_barrier((input_sum, rest, feed_sum, token_parts))
+    grad_first = sum(x.astype(F32) for x in token_parts)
+    e = grad_first * c1[:, None]
+    tokens_grad = (
+        grad_middle.reshape(micro, rows, width)
+        + r1
+        * (
+            e
+            - jnp.mean(e, -1, keepdims=True)
+            - n1 * jnp.mean(e * n1, -1, keepdims=True)
+        )
+    ).astype(BF)
+
     input_sum = jnp.concatenate(
         [input_sum.reshape(blocks // 2, groups * gain_rows, in_lanes), rest], 1
     )
     bit = 2
     while bit < blocks:
         input_sum = halve(input_sum, "blk", block_id, bit)
+        if bit == 2:
+            input_sum, feed_sum = lax.optimization_barrier((input_sum, feed_sum))
         bit *= 2
     input_sum = input_sum[0]
     at = groups * gain_rows

time: 321 us -> 314 us (0.978)
  Pallas kernels: 78.7 us -> 73.2 us
  waiting for transfers between devices: 128 us -> 124 us
  starting transfers between devices: 52.7 us -> 56.4 us
    ppermute x0 -> x1, waiting for transfers between devices: none -> 9.98 us  [on_device(): came = lax.ppermute(sent, 'blk', [(i, i ^ 1) for i in range(blocks)])]
    ppermute x21, waiting for transfers between devices: 18.1 us -> 10.5 us  [swap(): lax.ppermute(x, axis, [(i, i ^ k) for i in range(size)])]
    ppermute x8, waiting for transfers between devices: 53.6 us -> 48.6 us  [on_device(): lax.ppermute(x, 'blk', [(i, i ^ bit) for i in range(blocks)])]
    ppermute x4 -> x3, waiting for transfers between devices: 27.9 us -> 23.8 us  [halve(): came = lax.ppermute(sent, axis, [(i, i ^ bit) for i in range(size)])]
    pallas_call x1, Pallas kernels: 15.8 us -> 12.4 us  [on_device(): pl.pallas_call(functools.partial(attend_own_body, blocks, groups, rows),...]
  transfers between devices with their start and end apart: 40 -> 40, of which waited for: 18 -> 17; matrix products, arithmetic and copies ran while one was open for 8% -> 8% of each run, Pallas kernels for 22% -> 23%
where the time goes in v7:
time: 314 us
  waiting for transfers between devices  124 us (39%)
  Pallas kernels  73.2 us (23%)
  starting transfers between devices  56.4 us (18%)
  other arithmetic  23.7 us (8%)
  between operations  18.4 us (6%)
  local copies, waits for them, and re-layouts  17.9 us (6%)
    ppermute x8, waiting for transfers between devices, on_device(): lax.ppermute(x, 'blk', [(i, i ^ bit) for i in range(blocks)])  48.6 us
    all_to_all x3, waiting for transfers between devices, exchange(): return lax.all_to_all(x, ALL, split_axis=0, concat_axis=0, tiled=True)  28.6 us
    ppermute x3, waiting for transfers between devices, halve(): came = lax.ppermute(sent, axis, [(i, i ^ bit) for i in range(size)])  23.8 us
    all_to_all x3, starting transfers between devices, exchange(): return lax.all_to_all(x, ALL, split_axis=0, concat_axis=0, tiled=True)  15.8 us
    ppermute x21, starting transfers between devices, swap(): lax.ppermute(x, axis, [(i, i ^ k) for i in range(size)])  14.6 us
    pallas_call x1, Pallas kernels, on_device(): pl.pallas_call(functools.partial(attend_own_back_body, blocks, groups, ro...  12.4 us
    pallas_call x1, Pallas kernels, on_device(): pl.pallas_call(functools.partial(attend_own_body, blocks, groups, rows),...  12.4 us
    pallas_call x1, Pallas kernels, on_device(): pl.pallas_call(functools.partial(feed_body, *sizes), grid=(folds,), in_sp...  11.4 us
  transfers between devices with their start and end apart: 40, of which 17 were waited for; matrix products, arithmetic and copies ran while one was open for 8% of the time, Pallas kernels for 23%

profile of v7, /device:TPU:0, one launch (start us, length us, event | category | flops | bytes accessed | tf_op | source)
XLA Modules:
  0.0 313.8 jit_solution(12415867219266128770)
XLA Ops:
  7.2 1.1 reshape.524
  11.7 1.1 pad_maximum_fusion
  13.9 2.6 collective-permute-start.1
  16.6 6.1 %all-to-all-start = ((bf16[32,24,640]{2,1,0:T(8,128)(2,1)}), bf16[32,24,640]{2,1,0:T(8,128)(2,1)S(1)}, u32[]{:S(2)}, u32[]{:S(2)}) async-start(bf16[32,24,640]{2,1,0:T(8,128)(2,1)} %bitcast.9), calls=%async_computation | async-start | bytes 1966080 | tf_op jit(solution)/shard_map/all_to_all | solution.py:19
  30.9 5.7 %sine_multiply_fusion = (f32[2048,128]{1,0:T(8,128)}, f32[2048,128]{1,0:T(8,128)}) fusion(f32[128]{0:T(128)S(1)} %compare_select_fusion.2, f32[128]{0:T(128)S(1)} %mul.164, f32[2048]{0:T(1024)S(1)} %subtract_convert_fusion, f32[2048]{0:T(1024)S(1)} %subtract_convert_fusion.1, pred[128]{0:T(512)(128)(4,1)S(1)} %iota_compare_fusion.7), kind=kLoop, calls=%fused_computation.2 | loop fusion | flops 786432 | bytes 2114688 | tf_op jit(solution)/shard_map/mul | solution.py:922
  38.5 10.3 %all-to-all-done = bf16[32,24,640]{2,1,0:T(8,128)(2,1)S(1)} async-done(((bf16[32,24,640]{2,1,0:T(8,128)(2,1)}), bf16[32,24,640]{2,1,0:T(8,128)(2,1)S(1)}, u32[]{:S(2)}, u32[]{:S(2)}) %all-to-all-start) | async-done | bytes 983072 | tf_op jit(solution)/shard_map/all_to_all | solution.py:19
  50.4 4.2 %project.1 = (bf16[8,400,128]{2,1,0:T(8,128)(2,1)}, bf16[256,128]{1,0:T(8,128)(2,1)}) custom-call(f32[3,768]{1,0:T(4,128)} %get-tuple-element.215.c_ref, f32[3,768]{1,0:T(4,128)} %get-tuple-element.214.shift_ref, bf16[768,640]{1,0:T(8,128)(2,1)} %bitcast.177, bf16[3,64,768]{2,1,0:T(8,128)(2,1)} %copy-done.14, bf16[3,64,768]{2,1,0:T(8,128)(2,1)} %copy-done.36, ...), custom_call_target="tpu_custom_call" | custom-call | flops 679477248 | bytes 1179648 | tf_op jit(solution)/shard_map/project/pallas_call | solution.py:987
  54.7 3.5 %all-to-all-start.1 = ((bf16[8,400,128]{2,1,0:T(8,128)(2,1)}), bf16[8,400,128]{2,1,0:T(8,128)(2,1)S(1)}, u32[]{:S(2)}, u32[]{:S(2)}) async-start(bf16[8,400,128]{2,1,0:T(8,128)(2,1)} %get-tuple-element.107), calls=%async_computation.1 | async-start | bytes 1638400 | tf_op jit(solution)/shard_map/all_to_all | solution.py:1000
  58.2 1.9 collective-permute-start.3
  60.1 2.4 collective-permute-start.4
  62.7 16.1 %collective-permute-done.3 = bf16[256,128]{1,0:T(8,128)(2,1)S(1)} collective-permute-done((bf16[256,128]{1,0:T(8,128)(2,1)}, bf16[256,128]{1,0:T(8,128)(2,1)S(1)}, u32[]{:S(2)}, u32[]{:S(2)}) %collective-permute-start.3) | collective-permute-done | bytes 65568 | tf_op jit(solution)/shard_map/ppermute | solution.py:1001
  78.8 21.0 %collective-permute-done.4 = bf16[256,128]{1,0:T(8,128)(2,1)S(1)} collective-permute-done((bf16[256,128]{1,0:T(8,128)(2,1)}, bf16[256,128]{1,0:T(8,128)(2,1)S(1)}, u32[]{:S(2)}, u32[]{:S(2)}) %collective-permute-start.4) | collective-permute-done | bytes 65568 | tf_op jit(solution)/shard_map/ppermute | solution.py:1001
  101.9 12.4 %attend_own.1 = (bf16[32,32,128]{2,1,0:T(8,128)(2,1)}, bf16[2048,64]{1,0:T(8,128)(2,1)}, bf16[2304,64]{1,0:T(8,128)(2,1)}, bf16[2304,64]{1,0:T(8,128)(2,1)}, bf1...) custom-call(s32[2]{0:T(128)} %pad_add_fusion.1.place_ref, s32[8]{0:T(128)} %reshape.534.range_ref, s32[4,1,512]{2,1,0:T(1,128)} %bitcast.199, ...), custom_call_target="tpu_custom_call" | custom-call | flops 268435456 | bytes 4194304 | tf_op jit(solution)/shard_map/attend_own/pallas_call | solution.py:1027
  115.0 8.4 %attend_last.1 = (bf16[32,40,128]{2,1,0:T(8,128)(2,1)}, bf16[256,64]{1,0:T(8,128)(2,1)}, bf16[2304,64]{1,0:T(8,128)(2,1)}, bf16[2304,64]{1,0:T(8,128)(2,1)}, bf1...) custom-call(s32[2]{0:T(128)} %pad_add_fusion.1.place_ref, s32[2]{0:T(128)} %add_bitcast_fusion.range_ref, ...), custom_call_target="tpu_custom_call" | custom-call | flops 67108864 | bytes 2097152 | tf_op jit(solution)/shard_map/attend_last/pallas_call | solution.py:1043
  123.4 6.0 %all-to-all-start.2 = ((bf16[32,40,128]{2,1,0:T(8,128)(2,1)}), bf16[32,40,128]{2,1,0:T(8,128)(2,1)S(1)}, u32[]{:S(2)}, u32[]{:S(2)}) async-start(bf16[32,40,128]{2,1,0:T(8,128)(2,1)} %get-tuple-element.113), calls=%async_computation.2 | async-start | bytes 655360 | tf_op jit(solution)/shard_map/all_to_all | solution.py:19
  129.6 1.7 collective-permute-start.11
  132.9 16.9 %all-to-all-done.2.came_ref = bf16[32,40,128]{2,1,0:T(8,128)(2,1)S(1)} async-done(((bf16[32,40,128]{2,1,0:T(8,128)(2,1)}), bf16[32,40,128]{2,1,0:T(8,128)(2,1)S(1)}, u32[]{:S(2)}, u32[]{:S(2)}) %all-to-all-start.2) | async-done | bytes 327712 | tf_op jit(solution)/shard_map/all_to_all | solution.py:19
  149.8 1.9 all-gather.3.cloned.1.call-done
  151.8 3.1 middle.1
  155.1 1.5 collective-permute-start.8
  156.7 11.4 %feed.1 = (bf16[192,768]{1,0:T(8,128)(2,1)}, f32[192,768]{1,0:T(8,128)}, bf16[192,768]{1,0:T(8,128)(2,1)}, bf16[32,40,128]{2,1,0:T(8,128)(2,1)}, f32[15,768]{1,0:T(8,128)}) custom-call(bf16[32,216,768]{2,1,0:T(8,128)(2,1)} %bitcast.163, bf16[32,216,768]{2,1,0:T(8,128)(2,1)} %bitcast.164, bf16[32,216,768]{2,1,0:T(8,128)(2,1)} %bitcast.165, ...), custom_call_target="tpu_custom_call" | custom-call | flops 3623878656 | bytes 9437184 | tf_op jit(solution)/shard_map/feed/pallas_call | solution.py:1101
  168.1 3.7 %all-to-all-start.3 = ((bf16[32,40,128]{2,1,0:T(8,128)(2,1)}), bf16[32,40,128]{2,1,0:T(8,128)(2,1)S(1)}, u32[]{:S(2)}, u32[]{:S(2)}) async-start(bf16[32,40,128]{2,1,0:T(8,128)(2,1)} %get-tuple-element.119), calls=%async_computation.3 | async-start | bytes 655360 | tf_op jit(solution)/shard_map/all_to_all | solution.py:19
  173.6 9.0 %feed_weights.1 = (bf16[8,192,768]{2,1,0:T(8,128)(2,1)}, f32[1,768]{1,0:T(1,128)}) custom-call(s32[2]{0:T(128)} %pad_add_fusion.1.place_ref, bf16[32,216,768]{2,1,0:T(8,128)(2,1)} %bitcast.166, bf16[32,216,768]{2,1,0:T(8,128)(2,1)} %bitcast.167, f32[4,1,768]{2,1,0:T(1,128)} %reshape.565.ex_bias_ref.bias_ref, f32[3,768]{1,0:T(4,128)} %get-tuple-element.210.gate2_ref.gate_ref, ...), custom_call_target="tpu_custom_call" | custom-call | flops 4529848320 | bytes 9437184 | tf_op jit(solution)/shard_map/feed_weights/pallas_call | solution.py:1134
  182.6 1.4 all-to-all-done.3.do_ref
  184.7 7.1 %attend_last_back.1 = (f32[256,128]{1,0:T(8,128)}, bf16[4,256,128]{2,1,0:T(8,128)(2,1)}, bf16[4,256,128]{2,1,0:T(8,128)(2,1)}) custom-call(s32[2]{0:T(128)} %pad_add_fusion.1.place_ref, s32[2]{0:T(128)} %add_bitcast_fusion.range_ref, s32[1,1,256]{2,1,0:T(1,128)} %reshape_reshape.10.low_ref, s32[1,1,256]{2,1,0:T(1,128)} %reshape_reshape.11.high_ref, ...), custom_call_target="tpu_custom_call" | custom-call | flops 134217728 | bytes 2097152 | tf_op jit(solution)/shard_map/attend_last_back/pallas_call | solution.py:1164
  192.7 12.4 %attend_own_back.1 = bf16[8,400,128]{2,1,0:T(8,128)(2,1)} custom-call(s32[2]{0:T(128)} %pad_add_fusion.1.place_ref, s32[8]{0:T(128)} %reshape.534.range_ref, s32[4,1,512]{2,1,0:T(1,128)} %bitcast.200, s32[4,1,512]{2,1,0:T(1,128)} %bitcast.209, f32[2048,128]{1,0:T(8,128)} %get-tuple-element.100.cos_ref, f32[2048,128]{1,0:T(8,128)} %get-tuple-element.101.sin_ref, ...), custom_call_target="tpu_custom_call" | custom-call | flops 536870912 | bytes 4194304 | tf_op jit(solution)/shard_map/attend_own_back/pallas_call | solution.py:1179
  205.2 6.0 %all-to-all-start.4 = ((bf16[8,400,128]{2,1,0:T(8,128)(2,1)}), bf16[8,400,128]{2,1,0:T(8,128)(2,1)S(1)}, u32[]{:S(2)}, u32[]{:S(2)}) async-start(bf16[8,400,128]{2,1,0:T(8,128)(2,1)} %attend_own_back.1), calls=%async_computation.4 | async-start | bytes 1638400 | tf_op jit(solution)/shard_map/all_to_all | solution.py:1213
  212.2 1.6 collective-permute-start.19
  214.8 2.0 collective-permute-start.14
  216.8 2.4 collective-permute-start.15
  219.2 2.9 collective-permute-done.19
  222.0 5.4 %collective-permute-done.20 = bf16[192,768]{1,0:T(8,128)(2,1)S(1)} collective-permute-done((bf16[192,768]{1,0:T(8,128)(2,1)S(1)}, bf16[192,768]{1,0:T(8,128)(2,1)S(1)}, u32[]{:S(2)}, u32[]{:S(2)}) %collective-permute-start.20) | collective-permute-done | bytes 294944 | tf_op jit(solution)/shard_map/ppermute | solution.py:50
  228.1 2.5 collective-permute-done.14.refs_6_
  230.6 9.0 %collective-permute-done.15.refs_7_ = bf16[256,128]{1,0:T(8,128)(2,1)S(1)} collective-permute-done((bf16[256,128]{1,0:T(8,128)(2,1)S(1)}, bf16[256,128]{1,0:T(8,128)(2,1)S(1)}, u32[]{:S(2)}, u32[]{:S(2)}) %collective-permute-start.15) | collective-permute-done | bytes 65568 | tf_op jit(solution)/shard_map/ppermute | solution.py:1001
  240.6 5.3 %project_back.1 = (bf16[3,64,768]{2,1,0:T(8,128)(2,1)}, bf16[3,64,768]{2,1,0:T(8,128)(2,1)}, bf16[3,64,768]{2,1,0:T(8,128)(2,1)}, bf16[3,64,768]{2,1,0:T(8,128)(...) custom-call(s32[2]{0:T(128)} %pad_add_fusion.1.place_ref, ...), custom_call_target="tpu_custom_call" | custom-call | flops 1358954496 | bytes 1179648 | tf_op jit(solution)/shard_map/project_back/pallas_call | solution.py:1248
  249.8 1.5 collective-permute-start.17
  251.3 1.6 collective-permute-start.23
  253.2 7.1 %collective-permute-done.21 = bf16[4,64,576]{2,1,0:T(8,128)(2,1)S(1)} collective-permute-done((bf16[4,64,576]{2,1,0:T(8,128)(2,1)S(1)}, bf16[4,64,576]{2,1,0:T(8,128)(2,1)S(1)}, u32[]{:S(2)}, u32[]{:S(2)}) %collective-permute-start.21) | collective-permute-done | bytes 294944 | tf_op jit(solution)/shard_map/ppermute | solution.py:72
  260.4 10.0 %collective-permute-done.17 = bf16[4,4,24,576]{3,2,1,0:T(8,128)(2,1)S(1)} collective-permute-done((bf16[4,4,24,576]{3,2,1,0:T(8,128)(2,1)}, bf16[4,4,24,576]{3,2,1,0:T(8,128)(2,1)S(1)}, u32[]{:S(2)}, u32[]{:S(2)}) %collective-permute-start.17) | collective-permute-done | bytes 442400 | tf_op jit(solution)/shard_map/ppermute | solution.py:1293
  270.7 1.6 collective-permute-start.25
  272.2 1.4 fusion.54
  273.7 1.0 fusion.12
  274.7 7.1 %collective-permute-done.25 = bf16[2,160,576]{2,1,0:T(8,128)(2,1)S(1)} collective-permute-done((bf16[2,160,576]{2,1,0:T(8,128)(2,1)S(1)}, bf16[2,160,576]{2,1,0:T(8,128)(2,1)S(1)}, u32[]{:S(2)}, u32[]{:S(2)}) %collective-permute-start.25) | collective-permute-done | bytes 368672 | tf_op jit(solution)/shard_map/ppermute | solution.py:72
  282.7 1.5 collective-permute-start.31
  284.6 2.6 collective-permute-start.26
  287.7 9.6 %collective-permute-done.26 = bf16[1,160,576]{2,1,0:T(8,128)(2,1)S(1)} collective-permute-done((bf16[1,160,576]{2,1,0:T(8,128)(2,1)S(1)}, bf16[1,160,576]{2,1,0:T(8,128)(2,1)S(1)}, u32[]{:S(2)}, u32[]{:S(2)}) %collective-permute-start.26) | collective-permute-done | bytes 184352 | tf_op jit(solution)/shard_map/ppermute | solution.py:72
  297.5 1.5 collective-permute-start.28
  301.6 0.9 collective-permute-done.29
  (278 shorter events, 38.1 us)
Async XLA Ops:
  13.3 23.2 %copy-start.14 = (bf16[3,64,768]{2,1,0:T(8,128)(2,1)}, bf16[3,64,768]{2,1,0:T(8,128)(2,1)S(1)}, u32[]{:S(2)}) copy-start(bf16[3,64,768]{2,1,0:T(8,128)(2,1)S(1)} %fusion.6.refs_0_) | copy-start | bytes 884740
  13.4 24.4 %copy-start.27 = (bf16[96,768]{1,0:T(8,128)(2,1)S(1)}, bf16[96,768]{1,0:T(8,128)(2,1)}, u32[]{:S(2)}) copy-start(bf16[96,768]{1,0:T(8,128)(2,1)} %param.26) | copy-start | bytes 442372
  13.4 24.4 %copy-start.30 = (bf16[24,768]{1,0:T(8,128)(2,1)S(1)}, bf16[24,768]{1,0:T(8,128)(2,1)}, u32[]{:S(2)}) copy-start(bf16[24,768]{1,0:T(8,128)(2,1)} %param.22) | copy-start | bytes 110596
  13.4 35.6 %collective-permute-start = (bf16[3,64,768]{2,1,0:T(8,128)(2,1)S(1)}, bf16[3,64,768]{2,1,0:T(8,128)(2,1)S(1)}, u32[]{:S(2)}, u32[]{:S(2)}) collective-permute-start(bf16[3,64,768]{2,1,0:T(8,128)(2,1)S(1)} %fusion.6.refs_0_), channel_id=1, source_target_pairs={{0,8},{8,0},{16,24},{24,16},{1,9},{9,1},{17,25},{25,17},{2,10},{10... | collective-permute-start | bytes 884744 | tf_op jit(solution)/shard_map/ppermute | solution.py:50
  13.9 35.1 %collective-permute-start.1 = (bf16[3,64,768]{2,1,0:T(8,128)(2,1)S(1)}, bf16[3,64,768]{2,1,0:T(8,128)(2,1)S(1)}, u32[]{:S(2)}, u32[]{:S(2)}) collective-permute-start(bf16[3,64,768]{2,1,0:T(8,128)(2,1)S(1)} %fusion.6.refs_0_), channel_id=1, source_target_pairs={{0,16},{8,24},{16,0},{24,8},{1,17},{9,25},{17,1},{25,9},{2,18},{10... | collective-permute-start | bytes 884744 | tf_op jit(solution)/shard_map/ppermute | solution.py:50
  16.5 32.5 %collective-permute-start.2 = (bf16[3,64,768]{2,1,0:T(8,128)(2,1)S(1)}, bf16[3,64,768]{2,1,0:T(8,128)(2,1)S(1)}, u32[]{:S(2)}, u32[]{:S(2)}) collective-permute-start(bf16[3,64,768]{2,1,0:T(8,128)(2,1)S(1)} %fusion.6.refs_0_), channel_id=1, source_target_pairs={{0,24},{8,16},{16,8},{24,0},{1,25},{9,17},{17,9},{25,1},{2,26},{10... | collective-permute-start | bytes 884744 | tf_op jit(solution)/shard_map/ppermute | solution.py:50
  16.6 32.2 %all-to-all-start = ((bf16[32,24,640]{2,1,0:T(8,128)(2,1)}), bf16[32,24,640]{2,1,0:T(8,128)(2,1)S(1)}, u32[]{:S(2)}, u32[]{:S(2)}) async-start(bf16[32,24,640]{2,1,0:T(8,128)(2,1)} %bitcast.9), calls=%async_computation | async-start | bytes 1966080 | tf_op jit(solution)/shard_map/all_to_all | solution.py:19
  22.6 129.1 %all-gather.3.cloned.1.call-start = ((), (), s32[]{:S(2)}) async-start(), calls=%async_computation.7 | async-start | bytes 10948608 | tf_op jit(solution)/shard_map/all_gather | solution.py:955
  29.1 19.9 %copy-start.28 = (s32[2048]{0:T(1024)}, s32[2048]{0:T(1024)S(1)}, u32[]{:S(2)}) copy-start(s32[2048]{0:T(1024)S(1)} %get-tuple-element.230) | copy-start | bytes 24580
  54.7 46.3 %all-to-all-start.1 = ((bf16[8,400,128]{2,1,0:T(8,128)(2,1)}), bf16[8,400,128]{2,1,0:T(8,128)(2,1)S(1)}, u32[]{:S(2)}, u32[]{:S(2)}) async-start(bf16[8,400,128]{2,1,0:T(8,128)(2,1)} %get-tuple-element.107), calls=%async_computation.1 | async-start | bytes 1638400 | tf_op jit(solution)/shard_map/all_to_all | solution.py:1000
  58.2 20.5 %collective-permute-start.3 = (bf16[256,128]{1,0:T(8,128)(2,1)}, bf16[256,128]{1,0:T(8,128)(2,1)S(1)}, u32[]{:S(2)}, u32[]{:S(2)}) collective-permute-start(bf16[256,128]{1,0:T(8,128)(2,1)} %get-tuple-element.108), channel_id=1, source_target_pairs={{0,2},{1,3},{2,0},{3,1},{4,6},{5,7},{6,4},{7,5},{8,10},{9,11},{10,... | collective-permute-start | bytes 196616 | tf_op jit(solution)/shard_map/ppermute | solution.py:1001
  60.1 39.6 %collective-permute-start.4 = (bf16[256,128]{1,0:T(8,128)(2,1)}, bf16[256,128]{1,0:T(8,128)(2,1)S(1)}, u32[]{:S(2)}, u32[]{:S(2)}) collective-permute-start(bf16[256,128]{1,0:T(8,128)(2,1)} %get-tuple-element.108), channel_id=1, source_target_pairs={{0,4},{1,5},{2,6},{3,7},{4,0},{5,1},{6,2},{7,3},{8,12},{9,13},{10,... | collective-permute-start | bytes 196616 | tf_op jit(solution)/shard_map/ppermute | solution.py:1001
  62.5 37.2 %collective-permute-start.5 = (bf16[256,128]{1,0:T(8,128)(2,1)}, bf16[256,128]{1,0:T(8,128)(2,1)S(1)}, u32[]{:S(2)}, u32[]{:S(2)}) collective-permute-start(bf16[256,128]{1,0:T(8,128)(2,1)} %get-tuple-element.108), channel_id=1, source_target_pairs={{0,6},{1,7},{2,4},{3,5},{4,2},{5,3},{6,0},{7,1},{8,14},{9,15},{10,... | collective-permute-start | bytes 196616 | tf_op jit(solution)/shard_map/ppermute | solution.py:1001
  100.6 13.7 %collective-permute-start.6 = (bf16[4,256,128]{2,1,0:T(8,128)(2,1)S(1)}, bf16[4,256,128]{2,1,0:T(8,128)(2,1)S(1)}, u32[]{:S(2)}, u32[]{:S(2)}) collective-permute-start(bf16[4,256,128]{2,1,0:T(8,128)(2,1)S(1)} %pad_maximum_fusion.2.refs_1_), channel_id=1, source_target_pairs={{0,1},{1,0},{2,3},{3,2},{4,5},{5,4},{6,7},{7,6},{8,9},{9,8},{10,11... | collective-permute-start | bytes 786440 | tf_op jit(solution)/shard_map/ppermute | solution.py:1001
  123.4 26.4 %all-to-all-start.2 = ((bf16[32,40,128]{2,1,0:T(8,128)(2,1)}), bf16[32,40,128]{2,1,0:T(8,128)(2,1)S(1)}, u32[]{:S(2)}, u32[]{:S(2)}) async-start(bf16[32,40,128]{2,1,0:T(8,128)(2,1)} %get-tuple-element.113), calls=%async_computation.2 | async-start | bytes 655360 | tf_op jit(solution)/shard_map/all_to_all | solution.py:19
  129.4 27.1 %collective-permute-start.10 = (bf16[192,768]{1,0:T(8,128)(2,1)S(1)}, bf16[192,768]{1,0:T(8,128)(2,1)S(1)}, u32[]{:S(2)}, u32[]{:S(2)}) collective-permute-start(bf16[192,768]{1,0:T(8,128)(2,1)S(1)} %bitcast.182), channel_id=1, source_target_pairs={{0,8},{8,0},{16,24},{24,16},{1,9},{9,1},{17,25},{25,17},{2,10},{10... | collective-permute-start | bytes 884744 | tf_op jit(solution)/shard_map/ppermute | solution.py:50
  129.6 42.3 %collective-permute-start.11 = (bf16[192,768]{1,0:T(8,128)(2,1)S(1)}, bf16[192,768]{1,0:T(8,128)(2,1)S(1)}, u32[]{:S(2)}, u32[]{:S(2)}) collective-permute-start(bf16[192,768]{1,0:T(8,128)(2,1)S(1)} %bitcast.183), channel_id=1, source_target_pairs={{0,16},{8,24},{16,0},{24,8},{1,17},{9,25},{17,1},{25,9},{2,18},{10... | collective-permute-start | bytes 884744 | tf_op jit(solution)/shard_map/ppermute | solution.py:50
  131.3 40.6 %collective-permute-start.12 = (bf16[192,768]{1,0:T(8,128)(2,1)S(1)}, bf16[192,768]{1,0:T(8,128)(2,1)S(1)}, u32[]{:S(2)}, u32[]{:S(2)}) collective-permute-start(bf16[192,768]{1,0:T(8,128)(2,1)S(1)} %bitcast.184), channel_id=1, source_target_pairs={{0,24},{8,16},{16,8},{24,0},{1,25},{9,17},{17,9},{25,1},{2,26},{10... | collective-permute-start | bytes 884744 | tf_op jit(solution)/shard_map/ppermute | solution.py:50
  154.8 17.1 %collective-permute-start.7 = (bf16[192,768]{1,0:T(8,128)(2,1)}, bf16[192,768]{1,0:T(8,128)(2,1)S(1)}, u32[]{:S(2)}, u32[]{:S(2)}) collective-permute-start(bf16[192,768]{1,0:T(8,128)(2,1)} %get-tuple-element.114.second_ref.refs_0_), channel_id=1, source_target_pairs={{0,8},{8,0},{16,24},{24,16},{1,9},{9,1},{17,25},{25,17},{2,10},{10... | collective-permute-start | bytes 884744 | tf_op jit(solution)/shard_map/ppermute | solution.py:50
  155.1 16.8 %collective-permute-start.8 = (bf16[192,768]{1,0:T(8,128)(2,1)}, bf16[192,768]{1,0:T(8,128)(2,1)S(1)}, u32[]{:S(2)}, u32[]{:S(2)}) collective-permute-start(bf16[192,768]{1,0:T(8,128)(2,1)} %get-tuple-element.114.second_ref.refs_0_), channel_id=1, source_target_pairs={{0,16},{8,24},{16,0},{24,8},{1,17},{9,25},{17,1},{25,9},{2,18},{10... | collective-permute-start | bytes 884744 | tf_op jit(solution)/shard_map/ppermute | solution.py:50
  156.6 15.4 %collective-permute-start.9 = (bf16[192,768]{1,0:T(8,128)(2,1)}, bf16[192,768]{1,0:T(8,128)(2,1)S(1)}, u32[]{:S(2)}, u32[]{:S(2)}) collective-permute-start(bf16[192,768]{1,0:T(8,128)(2,1)} %get-tuple-element.114.second_ref.refs_0_), channel_id=1, source_target_pairs={{0,24},{8,16},{16,8},{24,0},{1,25},{9,17},{17,9},{25,1},{2,26},{10... | collective-permute-start | bytes 884744 | tf_op jit(solution)/shard_map/ppermute | solution.py:50
  168.1 15.8 %all-to-all-start.3 = ((bf16[32,40,128]{2,1,0:T(8,128)(2,1)}), bf16[32,40,128]{2,1,0:T(8,128)(2,1)S(1)}, u32[]{:S(2)}, u32[]{:S(2)}) async-start(bf16[32,40,128]{2,1,0:T(8,128)(2,1)} %get-tuple-element.119), calls=%async_computation.3 | async-start | bytes 655360 | tf_op jit(solution)/shard_map/all_to_all | solution.py:19
  171.8 98.8 %reduce-scatter.2.cloned.1.call-start = ((), (), s32[]{:S(2)}) async-start(), calls=%async_computation.6 | async-start | bytes 2654208 | tf_op jit(solution)/shard_map/reduce_scatter | solution.py:1161
  191.7 13.4 %collective-permute-start.13 = (bf16[4,256,128]{2,1,0:T(8,128)(2,1)}, bf16[4,256,128]{2,1,0:T(8,128)(2,1)S(1)}, u32[]{:S(2)}, u32[]{:S(2)}) collective-permute-start(bf16[4,256,128]{2,1,0:T(8,128)(2,1)} %get-tuple-element.136), channel_id=1, source_target_pairs={{0,1},{1,0},{2,3},{3,2},{4,5},{5,4},{6,7},{7,6},{8,9},{9,8},{10,11... | collective-permute-start | bytes 786440 | tf_op jit(solution)/shard_map/ppermute | solution.py:1001
  205.2 34.4 %all-to-all-start.4 = ((bf16[8,400,128]{2,1,0:T(8,128)(2,1)}), bf16[8,400,128]{2,1,0:T(8,128)(2,1)S(1)}, u32[]{:S(2)}, u32[]{:S(2)}) async-start(bf16[8,400,128]{2,1,0:T(8,128)(2,1)} %attend_own_back.1), calls=%async_computation.4 | async-start | bytes 1638400 | tf_op jit(solution)/shard_map/all_to_all | solution.py:1213
  212.1 7.1 %collective-permute-start.18 = (bf16[192,768]{1,0:T(8,128)(2,1)S(1)}, bf16[192,768]{1,0:T(8,128)(2,1)S(1)}, u32[]{:S(2)}, u32[]{:S(2)}) collective-permute-start(bf16[192,768]{1,0:T(8,128)(2,1)S(1)} %get-tuple-element.187), channel_id=1, source_target_pairs={{0,8},{8,0},{16,24},{24,16},{1,9},{9,1},{17,25},{25,17},{2,10},{10... | collective-permute-start | bytes 884744 | tf_op jit(solution)/shard_map/ppermute | solution.py:50
  212.2 9.9 %collective-permute-start.19 = (bf16[192,768]{1,0:T(8,128)(2,1)S(1)}, bf16[192,768]{1,0:T(8,128)(2,1)S(1)}, u32[]{:S(2)}, u32[]{:S(2)}) collective-permute-start(bf16[192,768]{1,0:T(8,128)(2,1)S(1)} %get-tuple-element.189), channel_id=1, source_target_pairs={{0,16},{8,24},{16,0},{24,8},{1,17},{9,25},{17,1},{25,9},{2,18},{10... | collective-permute-start | bytes 884744 | tf_op jit(solution)/shard_map/ppermute | solution.py:50
  213.7 13.7 %collective-permute-start.20 = (bf16[192,768]{1,0:T(8,128)(2,1)S(1)}, bf16[192,768]{1,0:T(8,128)(2,1)S(1)}, u32[]{:S(2)}, u32[]{:S(2)}) collective-permute-start(bf16[192,768]{1,0:T(8,128)(2,1)S(1)} %get-tuple-element.188), channel_id=1, source_target_pairs={{0,24},{8,16},{16,8},{24,0},{1,25},{9,17},{17,9},{25,1},{2,26},{10... | collective-permute-start | bytes 884744 | tf_op jit(solution)/shard_map/ppermute | solution.py:50
  214.8 15.9 %collective-permute-start.14 = (bf16[256,128]{1,0:T(8,128)(2,1)S(1)}, bf16[256,128]{1,0:T(8,128)(2,1)S(1)}, u32[]{:S(2)}, u32[]{:S(2)}) collective-permute-start(bf16[256,128]{1,0:T(8,128)(2,1)S(1)} %get-tuple-element.194), channel_id=1, source_target_pairs={{0,2},{1,3},{2,0},{3,1},{4,6},{5,7},{6,4},{7,5},{8,10},{9,11},{10,... | collective-permute-start | bytes 196616 | tf_op jit(solution)/shard_map/ppermute | solution.py:1001
  216.8 22.9 %collective-permute-start.15 = (bf16[256,128]{1,0:T(8,128)(2,1)S(1)}, bf16[256,128]{1,0:T(8,128)(2,1)S(1)}, u32[]{:S(2)}, u32[]{:S(2)}) collective-permute-start(bf16[256,128]{1,0:T(8,128)(2,1)S(1)} %get-tuple-element.193), channel_id=1, source_target_pairs={{0,4},{1,5},{2,6},{3,7},{4,0},{5,1},{6,2},{7,3},{8,12},{9,13},{10,... | collective-permute-start | bytes 196616 | tf_op jit(solution)/shard_map/ppermute | solution.py:1001
  219.1 20.5 %collective-permute-start.16 = (bf16[256,128]{1,0:T(8,128)(2,1)S(1)}, bf16[256,128]{1,0:T(8,128)(2,1)S(1)}, u32[]{:S(2)}, u32[]{:S(2)}) collective-permute-start(bf16[256,128]{1,0:T(8,128)(2,1)S(1)} %get-tuple-element.192), channel_id=1, source_target_pairs={{0,6},{1,7},{2,4},{3,5},{4,2},{5,3},{6,0},{7,1},{8,14},{9,15},{10,... | collective-permute-start | bytes 196616 | tf_op jit(solution)/shard_map/ppermute | solution.py:1001
  248.8 21.6 %copy-start.11 = (bf16[4,4,24,576]{3,2,1,0:T(8,128)(2,1)S(1)}, bf16[4,4,24,576]{3,2,1,0:T(8,128)(2,1)}, u32[]{:S(2)}) copy-start(bf16[4,4,24,576]{3,2,1,0:T(8,128)(2,1)} %get-tuple-element.139) | copy-start | bytes 1327108
  249.2 11.1 %collective-permute-start.21 = (bf16[4,64,576]{2,1,0:T(8,128)(2,1)S(1)}, bf16[4,64,576]{2,1,0:T(8,128)(2,1)S(1)}, u32[]{:S(2)}, u32[]{:S(2)}) collective-permute-start(bf16[4,64,576]{2,1,0:T(8,128)(2,1)S(1)} %fusion.22), channel_id=1, source_target_pairs={{0,1},{1,0},{2,3},{3,2},{4,5},{5,4},{6,7},{7,6},{8,9},{9,8},{10,11... | collective-permute-start | bytes 884744 | tf_op jit(solution)/shard_map/ppermute | solution.py:72
  249.8 20.6 %collective-permute-start.17 = (bf16[4,4,24,576]{3,2,1,0:T(8,128)(2,1)}, bf16[4,4,24,576]{3,2,1,0:T(8,128)(2,1)S(1)}, u32[]{:S(2)}, u32[]{:S(2)}) collective-permute-start(bf16[4,4,24,576]{3,2,1,0:T(8,128)(2,1)} %get-tuple-element.145), channel_id=1, source_target_pairs={{0,1},{1,0},{2,3},{3,2},{4,5},{5,4},{6,7},{7,6},{8,9},{9,8},{10,11... | collective-permute-start | bytes 1327112 | tf_op jit(solution)/shard_map/ppermute | solution.py:1293
  251.3 20.9 %copy-start.2 = (bf16[3,64,768]{2,1,0:T(8,128)(2,1)S(1)}, bf16[3,64,768]{2,1,0:T(8,128)(2,1)}, u32[]{:S(2)}) copy-start(bf16[3,64,768]{2,1,0:T(8,128)(2,1)} %param.14) | copy-start | bytes 884740
  251.3 20.9 %copy-start.16 = (bf16[3,64,768]{2,1,0:T(8,128)(2,1)S(1)}, bf16[3,64,768]{2,1,0:T(8,128)(2,1)}, u32[]{:S(2)}) copy-start(bf16[3,64,768]{2,1,0:T(8,128)(2,1)} %get-tuple-element.159) | copy-start | bytes 884740
  251.3 20.9 %copy-start.29 = (f32[3,768]{1,0:T(4,128)S(1)}, f32[3,768]{1,0:T(4,128)}, u32[]{:S(2)}) copy-start(f32[3,768]{1,0:T(4,128)} %get-tuple-element.215.c_ref) | copy-start | bytes 27652
  251.3 19.2 %collective-permute-start.22 = (bf16[3,64,768]{2,1,0:T(8,128)(2,1)}, bf16[3,64,768]{2,1,0:T(8,128)(2,1)S(1)}, u32[]{:S(2)}, u32[]{:S(2)}) collective-permute-start(bf16[3,64,768]{2,1,0:T(8,128)(2,1)} %get-tuple-element.156), channel_id=1, source_target_pairs={{0,8},{8,0},{16,24},{24,16},{1,9},{9,1},{17,25},{25,17},{2,10},{10... | collective-permute-start | bytes 884744 | tf_op jit(solution)/shard_map/ppermute | solution.py:50
  251.3 19.2 %collective-permute-start.23 = (bf16[3,64,768]{2,1,0:T(8,128)(2,1)}, bf16[3,64,768]{2,1,0:T(8,128)(2,1)}, u32[]{:S(2)}, u32[]{:S(2)}) collective-permute-start(bf16[3,64,768]{2,1,0:T(8,128)(2,1)} %get-tuple-element.157), channel_id=1, source_target_pairs={{0,16},{8,24},{16,0},{24,8},{1,17},{9,25},{17,1},{25,9},{2,18},{10... | collective-permute-start | bytes 884744 | tf_op jit(solution)/shard_map/ppermute | solution.py:50
  252.9 17.7 %collective-permute-start.24 = (bf16[3,64,768]{2,1,0:T(8,128)(2,1)}, bf16[3,64,768]{2,1,0:T(8,128)(2,1)}, u32[]{:S(2)}, u32[]{:S(2)}) collective-permute-start(bf16[3,64,768]{2,1,0:T(8,128)(2,1)} %get-tuple-element.158), channel_id=1, source_target_pairs={{0,24},{8,16},{16,8},{24,0},{1,25},{9,17},{17,9},{25,1},{2,26},{10... | collective-permute-start | bytes 884744 | tf_op jit(solution)/shard_map/ppermute | solution.py:50
  270.7 11.1 %collective-permute-start.25 = (bf16[2,160,576]{2,1,0:T(8,128)(2,1)S(1)}, bf16[2,160,576]{2,1,0:T(8,128)(2,1)S(1)}, u32[]{:S(2)}, u32[]{:S(2)}) collective-permute-start(bf16[2,160,576]{2,1,0:T(8,128)(2,1)S(1)} %fusion.18), channel_id=1, source_target_pairs={{0,2},{1,3},{2,0},{3,1},{4,6},{5,7},{6,4},{7,5},{8,10},{9,11},{10,... | collective-permute-start | bytes 1105928 | tf_op jit(solution)/shard_map/ppermute | solution.py:72
  282.6 4.6 %collective-permute-start.30 = (bf16[24,768]{1,0:T(8,128)(2,1)S(1)}, bf16[24,768]{1,0:T(8,128)(2,1)S(1)}, u32[]{:S(2)}, u32[]{:S(2)}) collective-permute-start(bf16[24,768]{1,0:T(8,128)(2,1)S(1)} %get-tuple-element.209), channel_id=1, source_target_pairs={{0,8},{8,0},{16,24},{24,16},{1,9},{9,1},{17,25},{25,17},{2,10},{10... | collective-permute-start | bytes 110600 | tf_op jit(solution)/shard_map/ppermute | solution.py:50
  282.7 4.5 %collective-permute-start.31 = (bf16[24,768]{1,0:T(8,128)(2,1)S(1)}, bf16[24,768]{1,0:T(8,128)(2,1)S(1)}, u32[]{:S(2)}, u32[]{:S(2)}) collective-permute-start(bf16[24,768]{1,0:T(8,128)(2,1)S(1)} %get-tuple-element.208), channel_id=1, source_target_pairs={{0,16},{8,24},{16,0},{24,8},{1,17},{9,25},{17,1},{25,9},{2,18},{10... | collective-permute-start | bytes 110600 | tf_op jit(solution)/shard_map/ppermute | solution.py:50
  284.2 3.4 %collective-permute-start.32 = (bf16[24,768]{1,0:T(8,128)(2,1)S(1)}, bf16[24,768]{1,0:T(8,128)(2,1)S(1)}, u32[]{:S(2)}, u32[]{:S(2)}) collective-permute-start(bf16[24,768]{1,0:T(8,128)(2,1)S(1)} %get-tuple-element.207), channel_id=1, source_target_pairs={{0,24},{8,16},{16,8},{24,0},{1,25},{9,17},{17,9},{25,1},{2,26},{10... | collective-permute-start | bytes 110600 | tf_op jit(solution)/shard_map/ppermute | solution.py:50
  284.6 12.7 %collective-permute-start.26 = (bf16[1,160,576]{2,1,0:T(8,128)(2,1)S(1)}, bf16[1,160,576]{2,1,0:T(8,128)(2,1)S(1)}, u32[]{:S(2)}, u32[]{:S(2)}) collective-permute-start(bf16[1,160,576]{2,1,0:T(8,128)(2,1)S(1)} %constant_dynamic-slice_fusion.1), channel_id=1, source_target_pairs={{0,4},{1,5},{2,6},{3,7},{4,0},{5,1},{6,2},{7,3},{8,12},{9,13},{10,... | collective-permute-start | bytes 552968 | tf_op jit(solution)/shard_map/ppermute | solution.py:72
  297.4 3.4 %collective-permute-start.27 = (bf16[32,576]{1,0:T(8,128)(2,1)S(1)}, bf16[32,576]{1,0:T(8,128)(2,1)S(1)}, u32[]{:S(2)}, u32[]{:S(2)}) collective-permute-start(bf16[32,576]{1,0:T(8,128)(2,1)S(1)} %get-tuple-element.199), channel_id=1, source_target_pairs={{0,8},{8,0},{16,24},{24,16},{1,9},{9,1},{17,25},{25,17},{2,10},{10... | collective-permute-start | bytes 110600 | tf_op jit(solution)/shard_map/ppermute | solution.py:50
  297.5 4.1 %collective-permute-start.28 = (bf16[32,576]{1,0:T(8,128)(2,1)S(1)}, bf16[32,576]{1,0:T(8,128)(2,1)S(1)}, u32[]{:S(2)}, u32[]{:S(2)}) collective-permute-start(bf16[32,576]{1,0:T(8,128)(2,1)S(1)} %get-tuple-element.200), channel_id=1, source_target_pairs={{0,16},{8,24},{16,0},{24,8},{1,17},{9,25},{17,1},{25,9},{2,18},{10... | collective-permute-start | bytes 110600 | tf_op jit(solution)/shard_map/ppermute | solution.py:50
  299.0 3.5 %collective-permute-start.29 = (bf16[32,576]{1,0:T(8,128)(2,1)S(1)}, bf16[32,576]{1,0:T(8,128)(2,1)S(1)}, u32[]{:S(2)}, u32[]{:S(2)}) collective-permute-start(bf16[32,576]{1,0:T(8,128)(2,1)S(1)} %get-tuple-element.201), channel_id=1, source_target_pairs={{0,24},{8,16},{16,8},{24,0},{1,25},{9,17},{17,9},{25,1},{2,26},{10... | collective-permute-start | bytes 110600 | tf_op jit(solution)/shard_map/ppermute | solution.py:50
  (34 other events, 159.4 us)
Sparse Core Ops, SparseCore 0:
  49.1 102.5 all-gather.2
  184.1 81.1 reduce-scatter.1

commit v8 on v7

--- a/solution.py
+++ b/solution.py
@@ -9,10 +9,15 @@
 from jax.sharding import PartitionSpec as P
 
 HEADS = 12
-ALL = ("ulysses", "blk")
+BLK = ("far", "near")
+ALL = ("ulysses", "far", "near")
 BF = jnp.bfloat16
 F32 = jnp.float32
 NEG = -1e30
+
+
+def axis_count(axis):
+    return math.prod(lax.axis_size(name) for name in ((axis,) if isinstance(axis, str) else axis))
 
 
 def exchange(x):
@@ -45,7 +50,7 @@
 
 
 def swap(blocks, axis):
-    size = lax.axis_size(axis)
+    size = axis_count(axis)
     return [
         x if k == 0 else lax.ppermute(x, axis, [(i, i ^ k) for i in range(size)])
         for k, x in enumerate(blocks)
@@ -64,7 +69,7 @@
 
 
 def halve(x, axis, index, bit):
-    size = lax.axis_size(axis)
+    size = axis_count(axis)
     y = x.reshape((-1, 2) + x.shape[1:])
     mine = (index // bit) % 2
     sent = lax.dynamic_index_in_dim(y, 1 - mine, 1, keepdims=False)
@@ -828,8 +833,8 @@
     reduce_weight,
     reduce_bias,
 ):
-    groups, blocks = lax.axis_size("ulysses"), lax.axis_size("blk")
-    group_id, block_id = lax.axis_index("ulysses"), lax.axis_index("blk")
+    groups, blocks = axis_count("ulysses"), axis_count(BLK)
+    group_id, block_id = lax.axis_index("ulysses"), lax.axis_index(BLK)
     devices = groups * blocks
     micro, rows, width = tokens.shape
     own = micro * rows
@@ -997,8 +1002,8 @@
             ),
             name="project",
         )(c1, shift1, in_own, *n1_group)
-        incoming = [lax.all_to_all(outgoing, "blk", split_axis=0, concat_axis=0, tiled=True)]
-        pass_on = lambda x, bit: lax.ppermute(x, "blk", [(i, i ^ bit) for i in range(blocks)])
+        incoming = [lax.all_to_all(outgoing, BLK, split_axis=0, concat_axis=0, tiled=True)]
+        pass_on = lambda x, bit: lax.ppermute(x, BLK, [(i, i ^ bit) for i in range(blocks)])
         last_four = jnp.stack([last_own] + [pass_on(last_own, bit) for bit in range(2, blocks, 2)])
         last_keys = [last_four, pass_on(last_four, 1)]
     else:
@@ -1010,7 +1015,7 @@
             scratch_shapes=[pltpu.VMEM((blocks, count, lanes), BF)],
             name="project",
         )(place, c1, shift1, in_own, *n1_group)
-        incoming = swap(outgoing, "blk")
+        incoming = swap(outgoing, BLK)
 
     span = blocks * rows
     by_span = pl.BlockSpec((span, 64), lambda i, p: (i ^ p[0], 0))
@@ -1158,7 +1163,8 @@
         name="feed_weights",
     )(place, gathered, gathered, expand_bias_f, gate2, *second_group, *dy_group)
     do_came, feed_part = lax.optimization_barrier((do_came, feed_part))
-    feed_sum = lax.psum_scatter(feed_part, "blk", scatter_dimension=0, tiled=True)[0]
+    feed_half = halve(feed_part, BLK, block_id, 1)
+    feed_sum = lax.psum_scatter(feed_half, "far", scatter_dimension=0, tiled=True)[0]
 
     if small_path:
         last_dq, last_kept, last_sent = pl.pallas_call(
@@ -1210,7 +1216,7 @@
         )(place, cos_table, sin_table, *grads)
     if small_path:
         leaving, last_half = lax.optimization_barrier((leaving, last_half))
-        back = [lax.all_to_all(leaving, "blk", split_axis=0, concat_axis=0, tiled=True)]
+        back = [lax.all_to_all(leaving, BLK, split_axis=0, concat_axis=0, tiled=True)]
         back += [
             pass_on(lax.dynamic_index_in_dim(last_half, (block_id // 2) ^ k, 0, keepdims=False), 2 * k)
             if k
@@ -1218,7 +1224,7 @@
             for k in range(blocks // 2)
         ]
     else:
-        back = swap(leaving, "blk")
+        back = swap(leaving, BLK)
     leaving, merged, grad_attn = lax.optimization_barrier((leaving, merged, grad_attn))
     output_part = lax.dot_general(merged, grad_attn, TN, preferred_element_type=F32).astype(BF)
     output_part = output_part.reshape(groups, width // groups, width)
@@ -1290,7 +1296,7 @@
         sent = lax.dynamic_index_in_dim(halves, 1 - block_id % 2, 1, keepdims=False)
         kept = lax.dynamic_index_in_dim(halves, block_id % 2, 1, keepdims=False)
     sent, token_parts = lax.optimization_barrier((sent, returned[:groups]))
-    came = lax.ppermute(sent, "blk", [(i, i ^ 1) for i in range(blocks)])
+    came = lax.ppermute(sent, BLK, [(i, i ^ 1) for i in range(blocks)])
     input_sum = (kept.astype(F32) + came.astype(F32)).astype(BF)
     token_parts = swap(token_parts, "ulysses")
     out_lanes = output_part.shape[1] * output_part.shape[2] // in_lanes
@@ -1303,7 +1309,7 @@
         ],
         1,
     )
-    rest = halve(rest, "blk", block_id, 1)
+    rest = halve(rest, BLK, block_id, 1)
     input_sum, rest, feed_sum, token_parts = lax.optimization_barrier((input_sum, rest, feed_sum, token_parts))
     grad_first = sum(x.astype(F32) for x in token_parts)
     e = grad_first * c1[:, None]
@@ -1322,7 +1328,7 @@
     )
     bit = 2
     while bit < blocks:
-        input_sum = halve(input_sum, "blk", block_id, bit)
+        input_sum = halve(input_sum, BLK, block_id, bit)
         if bit == 2:
             input_sum, feed_sum = lax.optimization_barrier((input_sum, feed_sum))
         bit *= 2
@@ -1400,13 +1406,15 @@
 
 
 def solution(mesh):
-    both = P(("ulysses", "blk"))
-    tall = P(("ulysses", "blk"), None)
-    seq = P(None, ("ulysses", "blk"), None)
+    groups, blocks = mesh.devices.shape
+    split = jax.sharding.Mesh(mesh.devices.reshape(groups, blocks // 2, 2), ALL)
+    both = P(ALL)
+    tall = P(ALL, None)
+    seq = P(None, ALL, None)
     in_specs = (
         seq, seq, P(), P(), tall, both, both, tall, tall, both, tall, both, tall, both,
     )
     out_specs = (seq, seq, tall, both, both, tall, tall, both, tall, both, tall, both)
     return jax.shard_map(
-        on_device, mesh=mesh, in_specs=in_specs, out_specs=out_specs, check_vma=False
-    )
+        on_device, mesh=split, in_specs=in_specs, out_specs=out_specs, check_vma=False
+    )

time: 314 us -> 313 us (level)
  waiting for transfers between devices: 124 us -> 113 us
  other arithmetic: 23.7 us -> 27.3 us
    ppermute x9, waiting for transfers between devices: 58.6 us -> 50.2 us  [the longest x8 43 us: on_device(): lax.ppermute(x, BLK, [(i, i ^ bit) for i in range(blocks)])]
    ppermute x3 -> x4, waiting for transfers between devices: 23.8 us -> 24 us  [halve(): came = lax.ppermute(sent, axis, [(i, i ^ bit) for i in range(size)])]
  transfers between devices with their start and end apart: 40 -> 41, of which waited for: 17 -> 17; matrix products, arithmetic and copies ran while one was open for 8% -> 10% of each run, Pallas kernels for 23% -> 22%
where the time goes in v8:
time: 313 us; the launch traced here: 312 us
  waiting for transfers between devices  113 us (36%)
  Pallas kernels  74.9 us (24%)
  starting transfers between devices  58.5 us (19%)
  other arithmetic  27.3 us (9%)
  local copies, waits for them, and re-layouts  19.4 us (6%)
  between operations  18.5 us (6%)
    ppermute x8, waiting for transfers between devices, on_device(): lax.ppermute(x, BLK, [(i, i ^ bit) for i in range(blocks)])  43 us
    all_to_all x3, waiting for transfers between devices, exchange(): return lax.all_to_all(x, ALL, split_axis=0, concat_axis=0, tiled=True)  28.8 us
    ppermute x4, waiting for transfers between devices, halve(): came = lax.ppermute(sent, axis, [(i, i ^ bit) for i in range(size)])  24 us
    all_to_all x3, starting transfers between devices, exchange(): return lax.all_to_all(x, ALL, split_axis=0, concat_axis=0, tiled=True)  15.1 us
    ppermute x21, starting transfers between devices, swap(): lax.ppermute(x, axis, [(i, i ^ k) for i in range(size)])  14.6 us
    ppermute x8, starting transfers between devices, on_device(): lax.ppermute(x, BLK, [(i, i ^ bit) for i in range(blocks)])  13.8 us
    pallas_call x1, Pallas kernels, on_device(): pl.pallas_call(functools.partial(attend_own_back_body, blocks, groups, ro...  13.3 us
    pallas_call x1, Pallas kernels, on_device(): pl.pallas_call(functools.partial(attend_own_body, blocks, groups, rows),...  13.1 us
  transfers between devices with their start and end apart: 41, of which 17 were waited for; matrix products, arithmetic and copies ran while one was open for 10% of the time, Pallas kernels for 22%

profile of v8, /device:TPU:0, one launch (start us, length us, event | category | flops | bytes accessed | tf_op | source)
XLA Modules:
  0.0 312.1 jit_solution(12286339371140171765)
XLA Ops:
  7.2 1.1 reshape.529
  11.7 1.1 pad_maximum_fusion
  13.9 2.6 collective-permute-start.1
  16.5 6.1 %all-to-all-start = ((bf16[32,24,640]{2,1,0:T(8,128)(2,1)}), bf16[32,24,640]{2,1,0:T(8,128)(2,1)S(1)}, u32[]{:S(2)}, u32[]{:S(2)}) async-start(bf16[32,24,640]{2,1,0:T(8,128)(2,1)} %bitcast.9), calls=%async_computation | async-start | bytes 1966080 | tf_op jit(solution)/shard_map/all_to_all | solution.py:24
  30.9 5.7 %sine_multiply_fusion = (f32[2048,128]{1,0:T(8,128)}, f32[2048,128]{1,0:T(8,128)}) fusion(f32[128]{0:T(128)S(1)} %compare_select_fusion.2, f32[128]{0:T(128)S(1)} %mul.168, f32[2048]{0:T(1024)S(1)} %subtract_convert_fusion, f32[2048]{0:T(1024)S(1)} %subtract_convert_fusion.1, pred[128]{0:T(512)(128)(4,1)S(1)} %iota_compare_fusion.7), kind=kLoop, calls=%fused_computation.5 | loop fusion | flops 786432 | bytes 2114688 | tf_op jit(solution)/shard_map/mul | solution.py:927
  38.5 10.3 %all-to-all-done = bf16[32,24,640]{2,1,0:T(8,128)(2,1)S(1)} async-done(((bf16[32,24,640]{2,1,0:T(8,128)(2,1)}), bf16[32,24,640]{2,1,0:T(8,128)(2,1)S(1)}, u32[]{:S(2)}, u32[]{:S(2)}) %all-to-all-start) | async-done | bytes 983072 | tf_op jit(solution)/shard_map/all_to_all | solution.py:24
  50.4 4.2 %project.1 = (bf16[8,400,128]{2,1,0:T(8,128)(2,1)}, bf16[256,128]{1,0:T(8,128)(2,1)}) custom-call(f32[3,768]{1,0:T(4,128)} %get-tuple-element.215.c_ref, f32[3,768]{1,0:T(4,128)} %get-tuple-element.214.shift_ref, bf16[768,640]{1,0:T(8,128)(2,1)} %bitcast.187, bf16[3,64,768]{2,1,0:T(8,128)(2,1)} %copy-done.14, bf16[3,64,768]{2,1,0:T(8,128)(2,1)} %copy-done.36, ...), custom_call_target="tpu_custom_call" | custom-call | flops 679477248 | bytes 1179648 | tf_op jit(solution)/shard_map/project/pallas_call | solution.py:992
  54.6 3.5 %all-to-all-start.1 = ((bf16[8,400,128]{2,1,0:T(8,128)(2,1)}), bf16[8,400,128]{2,1,0:T(8,128)(2,1)S(1)}, u32[]{:S(2)}, u32[]{:S(2)}) async-start(bf16[8,400,128]{2,1,0:T(8,128)(2,1)} %get-tuple-element.107), calls=%async_computation.1 | async-start | bytes 1638400 | tf_op jit(solution)/shard_map/all_to_all | solution.py:1005
  58.2 1.9 collective-permute-start.3
  60.1 2.4 collective-permute-start.4
  62.6 16.1 %collective-permute-done.3 = bf16[256,128]{1,0:T(8,128)(2,1)S(1)} collective-permute-done((bf16[256,128]{1,0:T(8,128)(2,1)}, bf16[256,128]{1,0:T(8,128)(2,1)S(1)}, u32[]{:S(2)}, u32[]{:S(2)}) %collective-permute-start.3) | collective-permute-done | bytes 65568 | tf_op jit(solution)/shard_map/ppermute | solution.py:1006
  78.7 21.0 %collective-permute-done.4 = bf16[256,128]{1,0:T(8,128)(2,1)S(1)} collective-permute-done((bf16[256,128]{1,0:T(8,128)(2,1)}, bf16[256,128]{1,0:T(8,128)(2,1)S(1)}, u32[]{:S(2)}, u32[]{:S(2)}) %collective-permute-start.4) | collective-permute-done | bytes 65568 | tf_op jit(solution)/shard_map/ppermute | solution.py:1006
  101.9 13.1 %attend_own.1 = (bf16[32,32,128]{2,1,0:T(8,128)(2,1)}, bf16[2048,64]{1,0:T(8,128)(2,1)}, bf16[2304,64]{1,0:T(8,128)(2,1)}, bf16[2304,64]{1,0:T(8,128)(2,1)}, bf1...) custom-call(s32[2]{0:T(128)} %pad_add_fusion.1.place_ref, s32[8]{0:T(128)} %reshape.539.range_ref, s32[4,1,512]{2,1,0:T(1,128)} %bitcast.209, ...), custom_call_target="tpu_custom_call" | custom-call | flops 268435456 | bytes 4194304 | tf_op jit(solution)/shard_map/attend_own/pallas_call | solution.py:1032
  115.7 8.3 %attend_last.1 = (bf16[32,40,128]{2,1,0:T(8,128)(2,1)}, bf16[256,64]{1,0:T(8,128)(2,1)}, bf16[2304,64]{1,0:T(8,128)(2,1)}, bf16[2304,64]{1,0:T(8,128)(2,1)}, bf1...) custom-call(s32[2]{0:T(128)} %pad_add_fusion.1.place_ref, s32[2]{0:T(128)} %add_bitcast_fusion.range_ref, ...), custom_call_target="tpu_custom_call" | custom-call | flops 67108864 | bytes 2097152 | tf_op jit(solution)/shard_map/attend_last/pallas_call | solution.py:1048
  124.0 6.1 %all-to-all-start.2 = ((bf16[32,40,128]{2,1,0:T(8,128)(2,1)}), bf16[32,40,128]{2,1,0:T(8,128)(2,1)S(1)}, u32[]{:S(2)}, u32[]{:S(2)}) async-start(bf16[32,40,128]{2,1,0:T(8,128)(2,1)} %get-tuple-element.113), calls=%async_computation.2 | async-start | bytes 655360 | tf_op jit(solution)/shard_map/all_to_all | solution.py:24
  130.2 1.7 collective-permute-start.11
  133.5 17.1 %all-to-all-done.2.came_ref = bf16[32,40,128]{2,1,0:T(8,128)(2,1)S(1)} async-done(((bf16[32,40,128]{2,1,0:T(8,128)(2,1)}), bf16[32,40,128]{2,1,0:T(8,128)(2,1)S(1)}, u32[]{:S(2)}, u32[]{:S(2)}) %all-to-all-start.2) | async-done | bytes 327712 | tf_op jit(solution)/shard_map/all_to_all | solution.py:24
  150.6 1.8 all-gather.3.cloned.1.call-done
  152.4 3.1 middle.1
  155.7 1.5 collective-permute-start.8
  157.3 11.4 %feed.1 = (bf16[192,768]{1,0:T(8,128)(2,1)}, f32[192,768]{1,0:T(8,128)}, bf16[192,768]{1,0:T(8,128)(2,1)}, bf16[32,40,128]{2,1,0:T(8,128)(2,1)}, f32[15,768]{1,0:T(8,128)}) custom-call(bf16[32,216,768]{2,1,0:T(8,128)(2,1)} %bitcast.171, bf16[32,216,768]{2,1,0:T(8,128)(2,1)} %bitcast.172, bf16[32,216,768]{2,1,0:T(8,128)(2,1)} %bitcast.173, ...), custom_call_target="tpu_custom_call" | custom-call | flops 3623878656 | bytes 9437184 | tf_op jit(solution)/shard_map/feed/pallas_call | solution.py:1106
  168.8 3.0 all-to-all-start.3
  173.5 9.0 %feed_weights.1 = (bf16[8,192,768]{2,1,0:T(8,128)(2,1)}, f32[1,768]{1,0:T(1,128)}) custom-call(s32[2]{0:T(128)} %pad_add_fusion.1.place_ref, bf16[32,216,768]{2,1,0:T(8,128)(2,1)} %bitcast.174, bf16[32,216,768]{2,1,0:T(8,128)(2,1)} %bitcast.175, f32[4,1,768]{2,1,0:T(1,128)} %reshape.571.ex_bias_ref.bias_ref, f32[3,768]{1,0:T(4,128)} %get-tuple-element.210.gate2_ref.gate_ref, ...), custom_call_target="tpu_custom_call" | custom-call | flops 4529848320 | bytes 9437184 | tf_op jit(solution)/shard_map/feed_weights/pallas_call | solution.py:1139
  182.5 1.4 all-to-all-done.3.do_ref
  184.6 7.0 %attend_last_back.1 = (f32[256,128]{1,0:T(8,128)}, bf16[4,256,128]{2,1,0:T(8,128)(2,1)}, bf16[4,256,128]{2,1,0:T(8,128)(2,1)}) custom-call(s32[2]{0:T(128)} %pad_add_fusion.1.place_ref, s32[2]{0:T(128)} %add_bitcast_fusion.range_ref, s32[1,1,256]{2,1,0:T(1,128)} %reshape_reshape.10.low_ref, s32[1,1,256]{2,1,0:T(1,128)} %reshape_reshape.11.high_ref, ...), custom_call_target="tpu_custom_call" | custom-call | flops 134217728 | bytes 2097152 | tf_op jit(solution)/shard_map/attend_last_back/pallas_call | solution.py:1170
  192.6 1.1 dynamic-slice_bitcast_fusion
  194.8 13.3 %attend_own_back.1 = bf16[8,400,128]{2,1,0:T(8,128)(2,1)} custom-call(s32[2]{0:T(128)} %pad_add_fusion.1.place_ref, s32[8]{0:T(128)} %reshape.539.range_ref, s32[4,1,512]{2,1,0:T(1,128)} %bitcast.210, s32[4,1,512]{2,1,0:T(1,128)} %bitcast.219, f32[2048,128]{1,0:T(8,128)} %get-tuple-element.100.cos_ref, f32[2048,128]{1,0:T(8,128)} %get-tuple-element.101.sin_ref, ...), custom_call_target="tpu_custom_call" | custom-call | flops 536870912 | bytes 4194304 | tf_op jit(solution)/shard_map/attend_own_back/pallas_call | solution.py:1185
  209.9 5.4 %all-to-all-start.4 = ((bf16[8,400,128]{2,1,0:T(8,128)(2,1)}), bf16[8,400,128]{2,1,0:T(8,128)(2,1)}, u32[]{:S(2)}, u32[]{:S(2)}) async-start(bf16[8,400,128]{2,1,0:T(8,128)(2,1)} %attend_own_back.1), calls=%async_computation.4 | async-start | bytes 1638400 | tf_op jit(solution)/shard_map/all_to_all | solution.py:1219
  216.4 1.6 collective-permute-start.19
  219.0 1.9 collective-permute-start.14
  220.9 2.4 collective-permute-start.15
  223.3 3.0 collective-permute-done.19
  226.3 3.7 %collective-permute-start.16 = (bf16[256,128]{1,0:T(8,128)(2,1)S(1)}, bf16[256,128]{1,0:T(8,128)(2,1)}, u32[]{:S(2)}, u32[]{:S(2)}) collective-permute-start(bf16[256,128]{1,0:T(8,128)(2,1)S(1)} %get-tuple-element.192), channel_id=1, source_target_pairs={{0,6},{1,7},{2,4},{3,5},{4,2},{5,3},{6,0},{7,1},{8,14},{9,15},{10,... | collective-permute-start | bytes 196616 | tf_op jit(solution)/shard_map/ppermute | solution.py:1006
  230.0 1.7 collective-permute-done.20
  232.3 2.6 fusion
  235.0 5.9 %collective-permute-done.15.refs_7_ = bf16[256,128]{1,0:T(8,128)(2,1)S(1)} collective-permute-done((bf16[256,128]{1,0:T(8,128)(2,1)S(1)}, bf16[256,128]{1,0:T(8,128)(2,1)S(1)}, u32[]{:S(2)}, u32[]{:S(2)}) %collective-permute-start.15) | collective-permute-done | bytes 65568 | tf_op jit(solution)/shard_map/ppermute | solution.py:1006
  241.6 5.5 %project_back.1 = (bf16[3,64,768]{2,1,0:T(8,128)(2,1)}, bf16[3,64,768]{2,1,0:T(8,128)(2,1)}, bf16[3,64,768]{2,1,0:T(8,128)(2,1)}, bf16[3,64,768]{2,1,0:T(8,128)(...) custom-call(s32[2]{0:T(128)} %pad_add_fusion.1.place_ref, ...), custom_call_target="tpu_custom_call" | custom-call | flops 1358954496 | bytes 1179648 | tf_op jit(solution)/shard_map/project_back/pallas_call | solution.py:1254
  250.4 1.3 collective-permute-start.21
  252.5 1.5 collective-permute-start.24
  254.4 6.8 %collective-permute-done.21 = bf16[4,64,576]{2,1,0:T(8,128)(2,1)S(1)} collective-permute-done((bf16[4,64,576]{2,1,0:T(8,128)(2,1)S(1)}, bf16[4,64,576]{2,1,0:T(8,128)(2,1)S(1)}, u32[]{:S(2)}, u32[]{:S(2)}) %collective-permute-start.21) | collective-permute-done | bytes 294944 | tf_op jit(solution)/shard_map/ppermute | solution.py:77
  261.2 7.2 %collective-permute-done.17 = bf16[4,4,24,576]{3,2,1,0:T(8,128)(2,1)S(1)} collective-permute-done((bf16[4,4,24,576]{3,2,1,0:T(8,128)(2,1)}, bf16[4,4,24,576]{3,2,1,0:T(8,128)(2,1)S(1)}, u32[]{:S(2)}, u32[]{:S(2)}) %collective-permute-start.17) | collective-permute-done | bytes 442400 | tf_op jit(solution)/shard_map/ppermute | solution.py:1299
  268.6 1.2 collective-permute-start.26
  269.8 1.4 fusion.55
  272.2 7.8 %collective-permute-done.26 = bf16[2,160,576]{2,1,0:T(8,128)(2,1)S(1)} collective-permute-done((bf16[2,160,576]{2,1,0:T(8,128)(2,1)S(1)}, bf16[2,160,576]{2,1,0:T(8,128)(2,1)S(1)}, u32[]{:S(2)}, u32[]{:S(2)}) %collective-permute-start.26) | collective-permute-done | bytes 368672 | tf_op jit(solution)/shard_map/ppermute | solution.py:77
  281.0 1.6 collective-permute-start.32
  282.8 1.7 collective-permute-start.27
  286.0 9.5 %collective-permute-done.27 = bf16[1,160,576]{2,1,0:T(8,128)(2,1)S(1)} collective-permute-done((bf16[1,160,576]{2,1,0:T(8,128)(2,1)S(1)}, bf16[1,160,576]{2,1,0:T(8,128)(2,1)S(1)}, u32[]{:S(2)}, u32[]{:S(2)}) %collective-permute-start.27) | collective-permute-done | bytes 184352 | tf_op jit(solution)/shard_map/ppermute | solution.py:77
  295.7 1.6 collective-permute-start.29
  (280 shorter events, 43.7 us)
Async XLA Ops:
  12.8 18.0 %copy-start.26 = (bf16[24,3072]{1,0:T(8,128)(2,1)S(1)}, bf16[24,3072]{1,0:T(8,128)(2,1)}, u32[]{:S(2)}) copy-start(bf16[24,3072]{1,0:T(8,128)(2,1)} %param.24) | copy-start | bytes 442372
  13.3 23.2 %copy-start.14 = (bf16[3,64,768]{2,1,0:T(8,128)(2,1)}, bf16[3,64,768]{2,1,0:T(8,128)(2,1)S(1)}, u32[]{:S(2)}) copy-start(bf16[3,64,768]{2,1,0:T(8,128)(2,1)S(1)} %fusion.7.refs_0_) | copy-start | bytes 884740
  13.4 35.6 %collective-permute-start = (bf16[3,64,768]{2,1,0:T(8,128)(2,1)S(1)}, bf16[3,64,768]{2,1,0:T(8,128)(2,1)S(1)}, u32[]{:S(2)}, u32[]{:S(2)}) collective-permute-start(bf16[3,64,768]{2,1,0:T(8,128)(2,1)S(1)} %fusion.7.refs_0_), channel_id=1, source_target_pairs={{0,8},{8,0},{16,24},{24,16},{1,9},{9,1},{17,25},{25,17},{2,10},{10... | collective-permute-start | bytes 884744 | tf_op jit(solution)/shard_map/ppermute | solution.py:55
  13.9 35.1 %collective-permute-start.1 = (bf16[3,64,768]{2,1,0:T(8,128)(2,1)S(1)}, bf16[3,64,768]{2,1,0:T(8,128)(2,1)S(1)}, u32[]{:S(2)}, u32[]{:S(2)}) collective-permute-start(bf16[3,64,768]{2,1,0:T(8,128)(2,1)S(1)} %fusion.7.refs_0_), channel_id=1, source_target_pairs={{0,16},{8,24},{16,0},{24,8},{1,17},{9,25},{17,1},{25,9},{2,18},{10... | collective-permute-start | bytes 884744 | tf_op jit(solution)/shard_map/ppermute | solution.py:55
  16.5 32.5 %collective-permute-start.2 = (bf16[3,64,768]{2,1,0:T(8,128)(2,1)S(1)}, bf16[3,64,768]{2,1,0:T(8,128)(2,1)S(1)}, u32[]{:S(2)}, u32[]{:S(2)}) collective-permute-start(bf16[3,64,768]{2,1,0:T(8,128)(2,1)S(1)} %fusion.7.refs_0_), channel_id=1, source_target_pairs={{0,24},{8,16},{16,8},{24,0},{1,25},{9,17},{17,9},{25,1},{2,26},{10... | collective-permute-start | bytes 884744 | tf_op jit(solution)/shard_map/ppermute | solution.py:55
  16.5 32.2 %all-to-all-start = ((bf16[32,24,640]{2,1,0:T(8,128)(2,1)}), bf16[32,24,640]{2,1,0:T(8,128)(2,1)S(1)}, u32[]{:S(2)}, u32[]{:S(2)}) async-start(bf16[32,24,640]{2,1,0:T(8,128)(2,1)} %bitcast.9), calls=%async_computation | async-start | bytes 1966080 | tf_op jit(solution)/shard_map/all_to_all | solution.py:24
  22.6 129.8 %all-gather.3.cloned.1.call-start = ((), (), s32[]{:S(2)}) async-start(), calls=%async_computation.7 | async-start | bytes 10948608 | tf_op jit(solution)/shard_map/all_gather | solution.py:960
  29.1 19.9 %copy-start.28 = (s32[2048]{0:T(1024)}, s32[2048]{0:T(1024)S(1)}, u32[]{:S(2)}) copy-start(s32[2048]{0:T(1024)S(1)} %get-tuple-element.230) | copy-start | bytes 24580
  54.6 46.3 %all-to-all-start.1 = ((bf16[8,400,128]{2,1,0:T(8,128)(2,1)}), bf16[8,400,128]{2,1,0:T(8,128)(2,1)S(1)}, u32[]{:S(2)}, u32[]{:S(2)}) async-start(bf16[8,400,128]{2,1,0:T(8,128)(2,1)} %get-tuple-element.107), calls=%async_computation.1 | async-start | bytes 1638400 | tf_op jit(solution)/shard_map/all_to_all | solution.py:1005
  58.2 20.5 %collective-permute-start.3 = (bf16[256,128]{1,0:T(8,128)(2,1)}, bf16[256,128]{1,0:T(8,128)(2,1)S(1)}, u32[]{:S(2)}, u32[]{:S(2)}) collective-permute-start(bf16[256,128]{1,0:T(8,128)(2,1)} %get-tuple-element.108), channel_id=1, source_target_pairs={{0,2},{1,3},{2,0},{3,1},{4,6},{5,7},{6,4},{7,5},{8,10},{9,11},{10,... | collective-permute-start | bytes 196616 | tf_op jit(solution)/shard_map/ppermute | solution.py:1006
  60.1 39.6 %collective-permute-start.4 = (bf16[256,128]{1,0:T(8,128)(2,1)}, bf16[256,128]{1,0:T(8,128)(2,1)S(1)}, u32[]{:S(2)}, u32[]{:S(2)}) collective-permute-start(bf16[256,128]{1,0:T(8,128)(2,1)} %get-tuple-element.108), channel_id=1, source_target_pairs={{0,4},{1,5},{2,6},{3,7},{4,0},{5,1},{6,2},{7,3},{8,12},{9,13},{10,... | collective-permute-start | bytes 196616 | tf_op jit(solution)/shard_map/ppermute | solution.py:1006
  62.5 37.2 %collective-permute-start.5 = (bf16[256,128]{1,0:T(8,128)(2,1)}, bf16[256,128]{1,0:T(8,128)(2,1)S(1)}, u32[]{:S(2)}, u32[]{:S(2)}) collective-permute-start(bf16[256,128]{1,0:T(8,128)(2,1)} %get-tuple-element.108), channel_id=1, source_target_pairs={{0,6},{1,7},{2,4},{3,5},{4,2},{5,3},{6,0},{7,1},{8,14},{9,15},{10,... | collective-permute-start | bytes 196616 | tf_op jit(solution)/shard_map/ppermute | solution.py:1006
  100.6 14.3 %collective-permute-start.6 = (bf16[4,256,128]{2,1,0:T(8,128)(2,1)S(1)}, bf16[4,256,128]{2,1,0:T(8,128)(2,1)S(1)}, u32[]{:S(2)}, u32[]{:S(2)}) collective-permute-start(bf16[4,256,128]{2,1,0:T(8,128)(2,1)S(1)} %pad_maximum_fusion.2.refs_1_), channel_id=1, source_target_pairs={{0,1},{1,0},{2,3},{3,2},{4,5},{5,4},{6,7},{7,6},{8,9},{9,8},{10,11... | collective-permute-start | bytes 786440 | tf_op jit(solution)/shard_map/ppermute | solution.py:1006
  124.0 26.6 %all-to-all-start.2 = ((bf16[32,40,128]{2,1,0:T(8,128)(2,1)}), bf16[32,40,128]{2,1,0:T(8,128)(2,1)S(1)}, u32[]{:S(2)}, u32[]{:S(2)}) async-start(bf16[32,40,128]{2,1,0:T(8,128)(2,1)} %get-tuple-element.113), calls=%async_computation.2 | async-start | bytes 655360 | tf_op jit(solution)/shard_map/all_to_all | solution.py:24
  130.1 27.1 %collective-permute-start.10 = (bf16[192,768]{1,0:T(8,128)(2,1)S(1)}, bf16[192,768]{1,0:T(8,128)(2,1)S(1)}, u32[]{:S(2)}, u32[]{:S(2)}) collective-permute-start(bf16[192,768]{1,0:T(8,128)(2,1)S(1)} %bitcast.192), channel_id=1, source_target_pairs={{0,8},{8,0},{16,24},{24,16},{1,9},{9,1},{17,25},{25,17},{2,10},{10... | collective-permute-start | bytes 884744 | tf_op jit(solution)/shard_map/ppermute | solution.py:55
  130.2 41.5 %collective-permute-start.11 = (bf16[192,768]{1,0:T(8,128)(2,1)S(1)}, bf16[192,768]{1,0:T(8,128)(2,1)S(1)}, u32[]{:S(2)}, u32[]{:S(2)}) collective-permute-start(bf16[192,768]{1,0:T(8,128)(2,1)S(1)} %bitcast.193), channel_id=1, source_target_pairs={{0,16},{8,24},{16,0},{24,8},{1,17},{9,25},{17,1},{25,9},{2,18},{10... | collective-permute-start | bytes 884744 | tf_op jit(solution)/shard_map/ppermute | solution.py:55
  131.9 39.9 %collective-permute-start.12 = (bf16[192,768]{1,0:T(8,128)(2,1)S(1)}, bf16[192,768]{1,0:T(8,128)(2,1)S(1)}, u32[]{:S(2)}, u32[]{:S(2)}) collective-permute-start(bf16[192,768]{1,0:T(8,128)(2,1)S(1)} %bitcast.194), channel_id=1, source_target_pairs={{0,24},{8,16},{16,8},{24,0},{1,25},{9,17},{17,9},{25,1},{2,26},{10... | collective-permute-start | bytes 884744 | tf_op jit(solution)/shard_map/ppermute | solution.py:55
  155.5 16.3 %collective-permute-start.7 = (bf16[192,768]{1,0:T(8,128)(2,1)}, bf16[192,768]{1,0:T(8,128)(2,1)S(1)}, u32[]{:S(2)}, u32[]{:S(2)}) collective-permute-start(bf16[192,768]{1,0:T(8,128)(2,1)} %get-tuple-element.114.second_ref.refs_0_), channel_id=1, source_target_pairs={{0,8},{8,0},{16,24},{24,16},{1,9},{9,1},{17,25},{25,17},{2,10},{10... | collective-permute-start | bytes 884744 | tf_op jit(solution)/shard_map/ppermute | solution.py:55
  155.7 16.1 %collective-permute-start.8 = (bf16[192,768]{1,0:T(8,128)(2,1)}, bf16[192,768]{1,0:T(8,128)(2,1)S(1)}, u32[]{:S(2)}, u32[]{:S(2)}) collective-permute-start(bf16[192,768]{1,0:T(8,128)(2,1)} %get-tuple-element.114.second_ref.refs_0_), channel_id=1, source_target_pairs={{0,16},{8,24},{16,0},{24,8},{1,17},{9,25},{17,1},{25,9},{2,18},{10... | collective-permute-start | bytes 884744 | tf_op jit(solution)/shard_map/ppermute | solution.py:55
  157.2 14.6 %collective-permute-start.9 = (bf16[192,768]{1,0:T(8,128)(2,1)}, bf16[192,768]{1,0:T(8,128)(2,1)S(1)}, u32[]{:S(2)}, u32[]{:S(2)}) collective-permute-start(bf16[192,768]{1,0:T(8,128)(2,1)} %get-tuple-element.114.second_ref.refs_0_), channel_id=1, source_target_pairs={{0,24},{8,16},{16,8},{24,0},{1,25},{9,17},{17,9},{25,1},{2,26},{10... | collective-permute-start | bytes 884744 | tf_op jit(solution)/shard_map/ppermute | solution.py:55
  168.8 15.1 %all-to-all-start.3 = ((bf16[32,40,128]{2,1,0:T(8,128)(2,1)}), bf16[32,40,128]{2,1,0:T(8,128)(2,1)S(1)}, u32[]{:S(2)}, u32[]{:S(2)}) async-start(bf16[32,40,128]{2,1,0:T(8,128)(2,1)} %get-tuple-element.119), calls=%async_computation.3 | async-start | bytes 655360 | tf_op jit(solution)/shard_map/all_to_all | solution.py:24
  191.6 16.5 %collective-permute-start.13 = (bf16[4,256,128]{2,1,0:T(8,128)(2,1)}, bf16[4,256,128]{2,1,0:T(8,128)(2,1)S(1)}, u32[]{:S(2)}, u32[]{:S(2)}) collective-permute-start(bf16[4,256,128]{2,1,0:T(8,128)(2,1)} %get-tuple-element.136), channel_id=1, source_target_pairs={{0,1},{1,0},{2,3},{3,2},{4,5},{5,4},{6,7},{7,6},{8,9},{9,8},{10,11... | collective-permute-start | bytes 786440 | tf_op jit(solution)/shard_map/ppermute | solution.py:1006
  193.7 38.6 %collective-permute-start.22 = (bf16[4,192,768]{2,1,0:T(8,128)(2,1)}, bf16[4,192,768]{2,1,0:T(8,128)(2,1)}, u32[]{:S(2)}, u32[]{:S(2)}) collective-permute-start(bf16[4,192,768]{2,1,0:T(8,128)(2,1)} %dynamic-slice_bitcast_fusion), channel_id=1, source_target_pairs={{0,1},{1,0},{2,3},{3,2},{4,5},{5,4},{6,7},{7,6},{8,9},{9,8},{10,11... | collective-permute-start | bytes 3538952 | tf_op jit(solution)/shard_map/ppermute | solution.py:77
  209.9 31.0 %all-to-all-start.4 = ((bf16[8,400,128]{2,1,0:T(8,128)(2,1)}), bf16[8,400,128]{2,1,0:T(8,128)(2,1)}, u32[]{:S(2)}, u32[]{:S(2)}) async-start(bf16[8,400,128]{2,1,0:T(8,128)(2,1)} %attend_own_back.1), calls=%async_computation.4 | async-start | bytes 1638400 | tf_op jit(solution)/shard_map/all_to_all | solution.py:1219
  215.3 53.3 %reduce-scatter.2.cloned.1.call-start = ((), (), s32[]{:S(2)}) async-start(), calls=%async_computation.6 | async-start | bytes 1474560 | tf_op jit(solution)/shard_map/reduce_scatter | solution.py:1167
  216.3 4.6 %collective-permute-start.18 = (bf16[192,768]{1,0:T(8,128)(2,1)S(1)}, bf16[192,768]{1,0:T(8,128)(2,1)S(1)}, u32[]{:S(2)}, u32[]{:S(2)}) collective-permute-start(bf16[192,768]{1,0:T(8,128)(2,1)S(1)} %get-tuple-element.187), channel_id=1, source_target_pairs={{0,8},{8,0},{16,24},{24,16},{1,9},{9,1},{17,25},{25,17},{2,10},{10... | collective-permute-start | bytes 884744 | tf_op jit(solution)/shard_map/ppermute | solution.py:55
  216.4 9.9 %collective-permute-start.19 = (bf16[192,768]{1,0:T(8,128)(2,1)S(1)}, bf16[192,768]{1,0:T(8,128)(2,1)S(1)}, u32[]{:S(2)}, u32[]{:S(2)}) collective-permute-start(bf16[192,768]{1,0:T(8,128)(2,1)S(1)} %get-tuple-element.189), channel_id=1, source_target_pairs={{0,16},{8,24},{16,0},{24,8},{1,17},{9,25},{17,1},{25,9},{2,18},{10... | collective-permute-start | bytes 884744 | tf_op jit(solution)/shard_map/ppermute | solution.py:55
  217.9 13.7 %collective-permute-start.20 = (bf16[192,768]{1,0:T(8,128)(2,1)S(1)}, bf16[192,768]{1,0:T(8,128)(2,1)S(1)}, u32[]{:S(2)}, u32[]{:S(2)}) collective-permute-start(bf16[192,768]{1,0:T(8,128)(2,1)S(1)} %get-tuple-element.188), channel_id=1, source_target_pairs={{0,24},{8,16},{16,8},{24,0},{1,25},{9,17},{17,9},{25,1},{2,26},{10... | collective-permute-start | bytes 884744 | tf_op jit(solution)/shard_map/ppermute | solution.py:55
  219.0 16.0 %collective-permute-start.14 = (bf16[256,128]{1,0:T(8,128)(2,1)S(1)}, bf16[256,128]{1,0:T(8,128)(2,1)S(1)}, u32[]{:S(2)}, u32[]{:S(2)}) collective-permute-start(bf16[256,128]{1,0:T(8,128)(2,1)S(1)} %get-tuple-element.194), channel_id=1, source_target_pairs={{0,2},{1,3},{2,0},{3,1},{4,6},{5,7},{6,4},{7,5},{8,10},{9,11},{10,... | collective-permute-start | bytes 196616 | tf_op jit(solution)/shard_map/ppermute | solution.py:1006
  220.9 20.1 %collective-permute-start.15 = (bf16[256,128]{1,0:T(8,128)(2,1)S(1)}, bf16[256,128]{1,0:T(8,128)(2,1)S(1)}, u32[]{:S(2)}, u32[]{:S(2)}) collective-permute-start(bf16[256,128]{1,0:T(8,128)(2,1)S(1)} %get-tuple-element.193), channel_id=1, source_target_pairs={{0,4},{1,5},{2,6},{3,7},{4,0},{5,1},{6,2},{7,3},{8,12},{9,13},{10,... | collective-permute-start | bytes 196616 | tf_op jit(solution)/shard_map/ppermute | solution.py:1006
  226.3 14.7 %collective-permute-start.16 = (bf16[256,128]{1,0:T(8,128)(2,1)S(1)}, bf16[256,128]{1,0:T(8,128)(2,1)}, u32[]{:S(2)}, u32[]{:S(2)}) collective-permute-start(bf16[256,128]{1,0:T(8,128)(2,1)S(1)} %get-tuple-element.192), channel_id=1, source_target_pairs={{0,6},{1,7},{2,4},{3,5},{4,2},{5,3},{6,0},{7,1},{8,14},{9,15},{10,... | collective-permute-start | bytes 196616 | tf_op jit(solution)/shard_map/ppermute | solution.py:1006
  250.0 18.4 %copy-start.11 = (bf16[4,4,24,576]{3,2,1,0:T(8,128)(2,1)S(1)}, bf16[4,4,24,576]{3,2,1,0:T(8,128)(2,1)}, u32[]{:S(2)}) copy-start(bf16[4,4,24,576]{3,2,1,0:T(8,128)(2,1)} %get-tuple-element.139) | copy-start | bytes 1327108
  250.4 10.7 %collective-permute-start.21 = (bf16[4,64,576]{2,1,0:T(8,128)(2,1)S(1)}, bf16[4,64,576]{2,1,0:T(8,128)(2,1)S(1)}, u32[]{:S(2)}, u32[]{:S(2)}) collective-permute-start(bf16[4,64,576]{2,1,0:T(8,128)(2,1)S(1)} %fusion.23), channel_id=1, source_target_pairs={{0,1},{1,0},{2,3},{3,2},{4,5},{5,4},{6,7},{7,6},{8,9},{9,8},{10,11... | collective-permute-start | bytes 884744 | tf_op jit(solution)/shard_map/ppermute | solution.py:77
  251.6 16.7 %collective-permute-start.17 = (bf16[4,4,24,576]{3,2,1,0:T(8,128)(2,1)}, bf16[4,4,24,576]{3,2,1,0:T(8,128)(2,1)S(1)}, u32[]{:S(2)}, u32[]{:S(2)}) collective-permute-start(bf16[4,4,24,576]{3,2,1,0:T(8,128)(2,1)} %get-tuple-element.145), channel_id=1, source_target_pairs={{0,1},{1,0},{2,3},{3,2},{4,5},{5,4},{6,7},{7,6},{8,9},{9,8},{10,11... | collective-permute-start | bytes 1327112 | tf_op jit(solution)/shard_map/ppermute | solution.py:1299
  252.5 17.3 %copy-start.2 = (bf16[3,64,768]{2,1,0:T(8,128)(2,1)S(1)}, bf16[3,64,768]{2,1,0:T(8,128)(2,1)}, u32[]{:S(2)}) copy-start(bf16[3,64,768]{2,1,0:T(8,128)(2,1)} %param.14) | copy-start | bytes 884740
  252.5 17.3 %copy-start.16 = (bf16[3,64,768]{2,1,0:T(8,128)(2,1)S(1)}, bf16[3,64,768]{2,1,0:T(8,128)(2,1)}, u32[]{:S(2)}) copy-start(bf16[3,64,768]{2,1,0:T(8,128)(2,1)} %get-tuple-element.159) | copy-start | bytes 884740
  252.5 17.3 %copy-start.29 = (f32[3,768]{1,0:T(4,128)S(1)}, f32[3,768]{1,0:T(4,128)}, u32[]{:S(2)}) copy-start(f32[3,768]{1,0:T(4,128)} %get-tuple-element.215.c_ref) | copy-start | bytes 27652
  252.5 16.0 %collective-permute-start.23 = (bf16[3,64,768]{2,1,0:T(8,128)(2,1)}, bf16[3,64,768]{2,1,0:T(8,128)(2,1)S(1)}, u32[]{:S(2)}, u32[]{:S(2)}) collective-permute-start(bf16[3,64,768]{2,1,0:T(8,128)(2,1)} %get-tuple-element.156), channel_id=1, source_target_pairs={{0,8},{8,0},{16,24},{24,16},{1,9},{9,1},{17,25},{25,17},{2,10},{10... | collective-permute-start | bytes 884744 | tf_op jit(solution)/shard_map/ppermute | solution.py:55
  252.5 16.0 %collective-permute-start.24 = (bf16[3,64,768]{2,1,0:T(8,128)(2,1)}, bf16[3,64,768]{2,1,0:T(8,128)(2,1)}, u32[]{:S(2)}, u32[]{:S(2)}) collective-permute-start(bf16[3,64,768]{2,1,0:T(8,128)(2,1)} %get-tuple-element.157), channel_id=1, source_target_pairs={{0,16},{8,24},{16,0},{24,8},{1,17},{9,25},{17,1},{25,9},{2,18},{10... | collective-permute-start | bytes 884744 | tf_op jit(solution)/shard_map/ppermute | solution.py:55
  254.0 14.5 %collective-permute-start.25 = (bf16[3,64,768]{2,1,0:T(8,128)(2,1)}, bf16[3,64,768]{2,1,0:T(8,128)(2,1)}, u32[]{:S(2)}, u32[]{:S(2)}) collective-permute-start(bf16[3,64,768]{2,1,0:T(8,128)(2,1)} %get-tuple-element.158), channel_id=1, source_target_pairs={{0,24},{8,16},{16,8},{24,0},{1,25},{9,17},{17,9},{25,1},{2,26},{10... | collective-permute-start | bytes 884744 | tf_op jit(solution)/shard_map/ppermute | solution.py:55
  268.6 11.3 %collective-permute-start.26 = (bf16[2,160,576]{2,1,0:T(8,128)(2,1)S(1)}, bf16[2,160,576]{2,1,0:T(8,128)(2,1)S(1)}, u32[]{:S(2)}, u32[]{:S(2)}) collective-permute-start(bf16[2,160,576]{2,1,0:T(8,128)(2,1)S(1)} %fusion.19), channel_id=1, source_target_pairs={{0,2},{1,3},{2,0},{3,1},{4,6},{5,7},{6,4},{7,5},{8,10},{9,11},{10,... | collective-permute-start | bytes 1105928 | tf_op jit(solution)/shard_map/ppermute | solution.py:77
  280.9 3.6 %collective-permute-start.31 = (bf16[24,768]{1,0:T(8,128)(2,1)S(1)}, bf16[24,768]{1,0:T(8,128)(2,1)S(1)}, u32[]{:S(2)}, u32[]{:S(2)}) collective-permute-start(bf16[24,768]{1,0:T(8,128)(2,1)S(1)} %get-tuple-element.209), channel_id=1, source_target_pairs={{0,8},{8,0},{16,24},{24,16},{1,9},{9,1},{17,25},{25,17},{2,10},{10... | collective-permute-start | bytes 110600 | tf_op jit(solution)/shard_map/ppermute | solution.py:55
  281.0 4.0 %collective-permute-start.32 = (bf16[24,768]{1,0:T(8,128)(2,1)S(1)}, bf16[24,768]{1,0:T(8,128)(2,1)S(1)}, u32[]{:S(2)}, u32[]{:S(2)}) collective-permute-start(bf16[24,768]{1,0:T(8,128)(2,1)S(1)} %get-tuple-element.208), channel_id=1, source_target_pairs={{0,16},{8,24},{16,0},{24,8},{1,17},{9,25},{17,1},{25,9},{2,18},{10... | collective-permute-start | bytes 110600 | tf_op jit(solution)/shard_map/ppermute | solution.py:55
  282.5 3.4 %collective-permute-start.33 = (bf16[24,768]{1,0:T(8,128)(2,1)S(1)}, bf16[24,768]{1,0:T(8,128)(2,1)S(1)}, u32[]{:S(2)}, u32[]{:S(2)}) collective-permute-start(bf16[24,768]{1,0:T(8,128)(2,1)S(1)} %get-tuple-element.207), channel_id=1, source_target_pairs={{0,24},{8,16},{16,8},{24,0},{1,25},{9,17},{17,9},{25,1},{2,26},{10... | collective-permute-start | bytes 110600 | tf_op jit(solution)/shard_map/ppermute | solution.py:55
  282.8 12.7 %collective-permute-start.27 = (bf16[1,160,576]{2,1,0:T(8,128)(2,1)S(1)}, bf16[1,160,576]{2,1,0:T(8,128)(2,1)S(1)}, u32[]{:S(2)}, u32[]{:S(2)}) collective-permute-start(bf16[1,160,576]{2,1,0:T(8,128)(2,1)S(1)} %constant_dynamic-slice_fusion.1), channel_id=1, source_target_pairs={{0,4},{1,5},{2,6},{3,7},{4,0},{5,1},{6,2},{7,3},{8,12},{9,13},{10,... | collective-permute-start | bytes 552968 | tf_op jit(solution)/shard_map/ppermute | solution.py:77
  295.7 3.4 %collective-permute-start.28 = (bf16[32,576]{1,0:T(8,128)(2,1)S(1)}, bf16[32,576]{1,0:T(8,128)(2,1)S(1)}, u32[]{:S(2)}, u32[]{:S(2)}) collective-permute-start(bf16[32,576]{1,0:T(8,128)(2,1)S(1)} %get-tuple-element.199), channel_id=1, source_target_pairs={{0,8},{8,0},{16,24},{24,16},{1,9},{9,1},{17,25},{25,17},{2,10},{10... | collective-permute-start | bytes 110600 | tf_op jit(solution)/shard_map/ppermute | solution.py:55
  295.7 4.1 %collective-permute-start.29 = (bf16[32,576]{1,0:T(8,128)(2,1)S(1)}, bf16[32,576]{1,0:T(8,128)(2,1)S(1)}, u32[]{:S(2)}, u32[]{:S(2)}) collective-permute-start(bf16[32,576]{1,0:T(8,128)(2,1)S(1)} %get-tuple-element.200), channel_id=1, source_target_pairs={{0,16},{8,24},{16,0},{24,8},{1,17},{9,25},{17,1},{25,9},{2,18},{10... | collective-permute-start | bytes 110600 | tf_op jit(solution)/shard_map/ppermute | solution.py:55
  297.3 3.5 %collective-permute-start.30 = (bf16[32,576]{1,0:T(8,128)(2,1)S(1)}, bf16[32,576]{1,0:T(8,128)(2,1)S(1)}, u32[]{:S(2)}, u32[]{:S(2)}) collective-permute-start(bf16[32,576]{1,0:T(8,128)(2,1)S(1)} %get-tuple-element.201), channel_id=1, source_target_pairs={{0,24},{8,16},{16,8},{24,0},{1,25},{9,17},{17,9},{25,1},{2,26},{10... | collective-permute-start | bytes 110600 | tf_op jit(solution)/shard_map/ppermute | solution.py:55
  (34 other events, 171.1 us)
Sparse Core Ops, SparseCore 0:
  49.1 103.2 all-gather.2
  235.1 30.8 reduce-scatter.1

commit v9 on v8

--- a/solution.py
+++ b/solution.py
@@ -342,8 +342,8 @@
 
 
 def feed_weights_body(rows, blocks, place_ref, ex_ref, re_ref, bias_ref, gate_ref, *refs):
-    groups = (len(refs) - 2) // 2
-    out_ref, sum_ref = refs[2 * groups :]
+    groups = (len(refs) - 4) // 2
+    keep_ref, send_ref, sum_ref, out_ref = refs[2 * groups :]
     width = refs[0].shape[-1]
     second = jnp.concatenate([x[...] for x in refs[:groups]], 0)
     gate = by_micro(gate_ref, rows)
@@ -366,6 +366,10 @@
         for b in range(blocks):
             at = (k * blocks + b) * each
             out_ref[b, per + k * each : per + (k + 1) * each] = x[at : at + each].astype(BF)
+    mine = place_ref[1] & 1
+    for z in range(blocks // 2):
+        keep_ref[z] = out_ref[2 * z + mine]
+        send_ref[z] = out_ref[2 * z + 1 - mine]
 
 
 def attend_body(block, range_ref, q_ref, sq_ref, k_ref, v_ref, sk_ref, o_ref, lse_ref):
@@ -1136,7 +1140,7 @@
     ]
 
     flat_p = pl.BlockSpec((own, width), lambda i, p: (0, 0))
-    feed_part, bias_part = pl.pallas_call(
+    feed_kept, feed_sent, bias_part = pl.pallas_call(
         functools.partial(feed_weights_body, rows, blocks),
         grid_spec=pltpu.PrefetchScalarGridSpec(
             num_scalar_prefetch=1,
@@ -1149,12 +1153,15 @@
             ]
             + [flat_p] * (2 * groups),
             out_specs=[
-                pl.BlockSpec((blocks, ff_rows + groups * gain_rows, width), lambda i, p: (0, 0, 0)),
+                pl.BlockSpec((blocks // 2, ff_rows + groups * gain_rows, width), lambda i, p: (0, 0, 0)),
+                pl.BlockSpec((blocks // 2, ff_rows + groups * gain_rows, width), lambda i, p: (0, 0, 0)),
                 pl.BlockSpec((1, width), lambda i, p: (0, 0)),
             ],
+            scratch_shapes=[pltpu.VMEM((blocks, ff_rows + groups * gain_rows, width), BF)],
         ),
         out_shape=[
-            jax.ShapeDtypeStruct((blocks, ff_rows + groups * gain_rows, width), BF),
+            jax.ShapeDtypeStruct((blocks // 2, ff_rows + groups * gain_rows, width), BF),
+            jax.ShapeDtypeStruct((blocks // 2, ff_rows + groups * gain_rows, width), BF),
             jax.ShapeDtypeStruct((1, width), F32),
         ],
         cost_estimate=pl.CostEstimate(
@@ -1162,8 +1169,9 @@
         ),
         name="feed_weights",
     )(place, gathered, gathered, expand_bias_f, gate2, *second_group, *dy_group)
-    do_came, feed_part = lax.optimization_barrier((do_came, feed_part))
-    feed_half = halve(feed_part, BLK, block_id, 1)
+    do_came, feed_kept, feed_sent = lax.optimization_barrier((do_came, feed_kept, feed_sent))
+    feed_came = lax.ppermute(feed_sent, BLK, [(i, i ^ 1) for i in range(blocks)])
+    feed_half = (feed_kept.astype(F32) + feed_came.astype(F32)).astype(BF)
     feed_sum = lax.psum_scatter(feed_half, "far", scatter_dimension=0, tiled=True)[0]
 
     if small_path:

time: 313 us -> 310 us (level)
  other arithmetic: 27.3 us -> 23.1 us
    ppermute x0 -> x1, waiting for transfers between devices: none -> 3.15 us  [on_device(): lax.ppermute(feed_sent, BLK, [(i, i ^ 1) for i in range(blocks)])]
    ppermute x4 -> x3, waiting for transfers between devices: 24 us -> 24.5 us  [halve(): came = lax.ppermute(sent, axis, [(i, i ^ bit) for i in range(size)])]
  transfers between devices with their start and end apart: 41 -> 41, of which waited for: 17 -> 17; matrix products, arithmetic and copies ran while one was open for 10% -> 8% of each run, Pallas kernels for 22% -> 22%
where the time goes in v9:
time: 310 us; the launch traced here: 308 us
  waiting for transfers between devices  113 us (36%)
  Pallas kernels  75.4 us (24%)
  starting transfers between devices  60.3 us (19%)
  other arithmetic  23.1 us (7%)
  between operations  18.5 us (6%)
  local copies, waits for them, and re-layouts  17.4 us (6%)
    ppermute x8, waiting for transfers between devices, on_device(): lax.ppermute(x, BLK, [(i, i ^ bit) for i in range(blocks)])  40.8 us
    all_to_all x3, waiting for transfers between devices, exchange(): return lax.all_to_all(x, ALL, split_axis=0, concat_axis=0, tiled=True)  26.2 us
    ppermute x3, waiting for transfers between devices, halve(): came = lax.ppermute(sent, axis, [(i, i ^ bit) for i in range(size)])  24.5 us
    ppermute x8, starting transfers between devices, on_device(): lax.ppermute(x, BLK, [(i, i ^ bit) for i in range(blocks)])  15.3 us
    ppermute x21, starting transfers between devices, swap(): lax.ppermute(x, axis, [(i, i ^ k) for i in range(size)])  14.6 us
    all_to_all x3, starting transfers between devices, exchange(): return lax.all_to_all(x, ALL, split_axis=0, concat_axis=0, tiled=True)  14.3 us
    pallas_call x1, Pallas kernels, on_device(): pl.pallas_call(functools.partial(attend_own_back_body, blocks, groups, ro...  13.3 us
    pallas_call x1, Pallas kernels, on_device(): pl.pallas_call(functools.partial(attend_own_body, blocks, groups, rows),...  13.1 us
  transfers between devices with their start and end apart: 41, of which 17 were waited for; matrix products, arithmetic and copies ran while one was open for 8% of the time, Pallas kernels for 22%

profile of v9, /device:TPU:0, one launch (start us, length us, event | category | flops | bytes accessed | tf_op | source)
XLA Modules:
  0.0 308.3 jit_solution(2735886518649302236)
XLA Ops:
  7.2 1.1 reshape.524
  11.7 1.1 pad_maximum_fusion
  13.9 2.6 collective-permute-start.1
  16.5 6.1 %all-to-all-start = ((bf16[32,24,640]{2,1,0:T(8,128)(2,1)}), bf16[32,24,640]{2,1,0:T(8,128)(2,1)S(1)}, u32[]{:S(2)}, u32[]{:S(2)}) async-start(bf16[32,24,640]{2,1,0:T(8,128)(2,1)} %bitcast.9), calls=%async_computation | async-start | bytes 1966080 | tf_op jit(solution)/shard_map/all_to_all | solution.py:24
  30.8 5.7 %sine_multiply_fusion = (f32[2048,128]{1,0:T(8,128)}, f32[2048,128]{1,0:T(8,128)}) fusion(f32[128]{0:T(128)S(1)} %compare_select_fusion.2, f32[128]{0:T(128)S(1)} %mul.168, f32[2048]{0:T(1024)S(1)} %subtract_convert_fusion, f32[2048]{0:T(1024)S(1)} %subtract_convert_fusion.1, pred[128]{0:T(512)(128)(4,1)S(1)} %iota_compare_fusion.7), kind=kLoop, calls=%fused_computation.3 | loop fusion | flops 786432 | bytes 2114688 | tf_op jit(solution)/shard_map/mul | solution.py:931
  38.5 10.3 %all-to-all-done = bf16[32,24,640]{2,1,0:T(8,128)(2,1)S(1)} async-done(((bf16[32,24,640]{2,1,0:T(8,128)(2,1)}), bf16[32,24,640]{2,1,0:T(8,128)(2,1)S(1)}, u32[]{:S(2)}, u32[]{:S(2)}) %all-to-all-start) | async-done | bytes 983072 | tf_op jit(solution)/shard_map/all_to_all | solution.py:24
  50.8 4.2 %project.1 = (bf16[8,400,128]{2,1,0:T(8,128)(2,1)}, bf16[256,128]{1,0:T(8,128)(2,1)}) custom-call(f32[3,768]{1,0:T(4,128)} %get-tuple-element.219.c_ref, f32[3,768]{1,0:T(4,128)} %get-tuple-element.218.shift_ref, bf16[768,640]{1,0:T(8,128)(2,1)} %bitcast.177, bf16[3,64,768]{2,1,0:T(8,128)(2,1)} %copy-done.14, bf16[3,64,768]{2,1,0:T(8,128)(2,1)} %copy-done.37, ...), custom_call_target="tpu_custom_call" | custom-call | flops 679477248 | bytes 1179648 | tf_op jit(solution)/shard_map/project/pallas_call | solution.py:996
  55.0 3.7 %all-to-all-start.1 = ((bf16[8,400,128]{2,1,0:T(8,128)(2,1)}), bf16[8,400,128]{2,1,0:T(8,128)(2,1)S(1)}, u32[]{:S(2)}, u32[]{:S(2)}) async-start(bf16[8,400,128]{2,1,0:T(8,128)(2,1)} %get-tuple-element.109), calls=%async_computation.1 | async-start | bytes 1638400 | tf_op jit(solution)/shard_map/all_to_all | solution.py:1009
  58.7 1.9 collective-permute-start.3
  60.6 2.4 collective-permute-start.4
  63.2 15.9 %collective-permute-done.3 = bf16[256,128]{1,0:T(8,128)(2,1)S(1)} collective-permute-done((bf16[256,128]{1,0:T(8,128)(2,1)S(1)}, bf16[256,128]{1,0:T(8,128)(2,1)S(1)}, u32[]{:S(2)}, u32[]{:S(2)}) %collective-permute-start.3) | collective-permute-done | bytes 65568 | tf_op jit(solution)/shard_map/ppermute | solution.py:1010
  79.1 20.7 %collective-permute-done.4 = bf16[256,128]{1,0:T(8,128)(2,1)S(1)} collective-permute-done((bf16[256,128]{1,0:T(8,128)(2,1)S(1)}, bf16[256,128]{1,0:T(8,128)(2,1)S(1)}, u32[]{:S(2)}, u32[]{:S(2)}) %collective-permute-start.4) | collective-permute-done | bytes 65568 | tf_op jit(solution)/shard_map/ppermute | solution.py:1010
  99.8 1.8 collective-permute-start.6
  102.5 13.1 %attend_own.1 = (bf16[32,32,128]{2,1,0:T(8,128)(2,1)}, bf16[2048,64]{1,0:T(8,128)(2,1)}, bf16[2304,64]{1,0:T(8,128)(2,1)}, bf16[2304,64]{1,0:T(8,128)(2,1)}, bf1...) custom-call(s32[2]{0:T(128)} %pad_add_fusion.1.place_ref, s32[8]{0:T(128)} %reshape.534.range_ref, s32[4,1,512]{2,1,0:T(1,128)} %bitcast.199, ...), custom_call_target="tpu_custom_call" | custom-call | flops 268435456 | bytes 4194304 | tf_op jit(solution)/shard_map/attend_own/pallas_call | solution.py:1036
  116.3 8.4 %attend_last.1 = (bf16[32,40,128]{2,1,0:T(8,128)(2,1)}, bf16[256,64]{1,0:T(8,128)(2,1)}, bf16[2304,64]{1,0:T(8,128)(2,1)}, bf16[2304,64]{1,0:T(8,128)(2,1)}, bf1...) custom-call(s32[2]{0:T(128)} %pad_add_fusion.1.place_ref, s32[2]{0:T(128)} %add_bitcast_fusion.range_ref, ...), custom_call_target="tpu_custom_call" | custom-call | flops 67108864 | bytes 2097152 | tf_op jit(solution)/shard_map/attend_last/pallas_call | solution.py:1052
  124.7 4.5 %all-to-all-start.2 = ((bf16[32,40,128]{2,1,0:T(8,128)(2,1)}), bf16[32,40,128]{2,1,0:T(8,128)(2,1)S(1)}, u32[]{:S(2)}, u32[]{:S(2)}) async-start(bf16[32,40,128]{2,1,0:T(8,128)(2,1)} %get-tuple-element.115), calls=%async_computation.2 | async-start | bytes 655360 | tf_op jit(solution)/shard_map/all_to_all | solution.py:24
  129.3 1.7 collective-permute-start.11
  132.6 15.1 %all-to-all-done.2.came_ref = bf16[32,40,128]{2,1,0:T(8,128)(2,1)S(1)} async-done(((bf16[32,40,128]{2,1,0:T(8,128)(2,1)}), bf16[32,40,128]{2,1,0:T(8,128)(2,1)S(1)}, u32[]{:S(2)}, u32[]{:S(2)}) %all-to-all-start.2) | async-done | bytes 327712 | tf_op jit(solution)/shard_map/all_to_all | solution.py:24
  147.7 3.7 %all-gather.3.cloned.1.call-done = bf16[6912,768]{1,0:T(8,128)(2,1)} async-done(((bf16[216,768]{1,0:T(8,128)(2,1)}), bf16[6912,768]{1,0:T(8,128)(2,1)}) %all-gather.3.cloned.1.call-update) | async-done | bytes 10616848 | tf_op jit(solution)/shard_map/all_gather | solution.py:964
  151.5 3.1 middle.1
  154.8 1.5 collective-permute-start.8
  156.4 11.4 %feed.1 = (bf16[192,768]{1,0:T(8,128)(2,1)}, f32[192,768]{1,0:T(8,128)}, bf16[192,768]{1,0:T(8,128)(2,1)}, bf16[32,40,128]{2,1,0:T(8,128)(2,1)}, f32[15,768]{1,0:T(8,128)}) custom-call(bf16[32,216,768]{2,1,0:T(8,128)(2,1)} %bitcast.163, bf16[32,216,768]{2,1,0:T(8,128)(2,1)} %bitcast.164, bf16[32,216,768]{2,1,0:T(8,128)(2,1)} %bitcast.165, ...), custom_call_target="tpu_custom_call" | custom-call | flops 3623878656 | bytes 9437184 | tf_op jit(solution)/shard_map/feed/pallas_call | solution.py:1110
  167.9 3.8 %all-to-all-start.3 = ((bf16[32,40,128]{2,1,0:T(8,128)(2,1)}), bf16[32,40,128]{2,1,0:T(8,128)(2,1)S(1)}, u32[]{:S(2)}, u32[]{:S(2)}) async-start(bf16[32,40,128]{2,1,0:T(8,128)(2,1)} %get-tuple-element.121), calls=%async_computation.3 | async-start | bytes 655360 | tf_op jit(solution)/shard_map/all_to_all | solution.py:24
  173.4 9.6 %feed_weights.1 = (bf16[4,192,768]{2,1,0:T(8,128)(2,1)}, bf16[4,192,768]{2,1,0:T(8,128)(2,1)}, f32[1,768]{1,0:T(1,128)}) custom-call(s32[2]{0:T(128)} %pad_add_fusion.1.place_ref, bf16[32,216,768]{2,1,0:T(8,128)(2,1)} %bitcast.166, bf16[32,216,768]{2,1,0:T(8,128)(2,1)} %bitcast.167, f32[4,1,768]{2,1,0:T(1,128)} %reshape.565.ex_bias_ref.bias_ref, ...), custom_call_target="tpu_custom_call" | custom-call | flops 4529848320 | bytes 9437184 | tf_op jit(solution)/shard_map/feed_weights/pallas_call | solution.py:1143
  184.5 7.0 %attend_last_back.1 = (f32[256,128]{1,0:T(8,128)}, bf16[4,256,128]{2,1,0:T(8,128)(2,1)}, bf16[4,256,128]{2,1,0:T(8,128)(2,1)}) custom-call(s32[2]{0:T(128)} %pad_add_fusion.1.place_ref, s32[2]{0:T(128)} %add_bitcast_fusion.range_ref, s32[1,1,256]{2,1,0:T(1,128)} %reshape_reshape.10.low_ref, s32[1,1,256]{2,1,0:T(1,128)} %reshape_reshape.11.high_ref, ...), custom_call_target="tpu_custom_call" | custom-call | flops 134217728 | bytes 2097152 | tf_op jit(solution)/shard_map/attend_last_back/pallas_call | solution.py:1178
  192.5 1.0 collective-permute-start.22
  193.5 13.3 %attend_own_back.1 = bf16[8,400,128]{2,1,0:T(8,128)(2,1)} custom-call(s32[2]{0:T(128)} %pad_add_fusion.1.place_ref, s32[8]{0:T(128)} %reshape.534.range_ref, s32[4,1,512]{2,1,0:T(1,128)} %bitcast.200, s32[4,1,512]{2,1,0:T(1,128)} %bitcast.209, f32[2048,128]{1,0:T(8,128)} %get-tuple-element.102.cos_ref, f32[2048,128]{1,0:T(8,128)} %get-tuple-element.103.sin_ref, ...), custom_call_target="tpu_custom_call" | custom-call | flops 536870912 | bytes 4194304 | tf_op jit(solution)/shard_map/attend_own_back/pallas_call | solution.py:1193
  207.0 5.2 %all-to-all-start.4 = ((bf16[8,400,128]{2,1,0:T(8,128)(2,1)}), bf16[8,400,128]{2,1,0:T(8,128)(2,1)}, u32[]{:S(2)}, u32[]{:S(2)}) async-start(bf16[8,400,128]{2,1,0:T(8,128)(2,1)} %attend_own_back.1), calls=%async_computation.4 | async-start | bytes 1638400 | tf_op jit(solution)/shard_map/all_to_all | solution.py:1227
  213.3 1.6 collective-permute-start.19
  215.9 1.9 collective-permute-start.14
  217.8 2.4 collective-permute-start.15
  220.1 3.0 collective-permute-done.19
  223.1 3.7 %collective-permute-start.16 = (bf16[256,128]{1,0:T(8,128)(2,1)S(1)}, bf16[256,128]{1,0:T(8,128)(2,1)}, u32[]{:S(2)}, u32[]{:S(2)}) collective-permute-start(bf16[256,128]{1,0:T(8,128)(2,1)S(1)} %get-tuple-element.196), channel_id=1, source_target_pairs={{0,6},{1,7},{2,4},{3,5},{4,2},{5,3},{6,0},{7,1},{8,14},{9,15},{10,... | collective-permute-start | bytes 196616 | tf_op jit(solution)/shard_map/ppermute | solution.py:1010
  226.9 1.7 collective-permute-done.20
  229.2 3.1 %collective-permute-done.22 = bf16[4,192,768]{2,1,0:T(8,128)(2,1)S(1)} collective-permute-done((bf16[4,192,768]{2,1,0:T(8,128)(2,1)}, bf16[4,192,768]{2,1,0:T(8,128)(2,1)S(1)}, u32[]{:S(2)}, u32[]{:S(2)}) %collective-permute-start.22) | collective-permute-done | bytes 1179680 | tf_op jit(solution)/shard_map/ppermute | solution.py:1173
  232.4 1.3 add_convert_fusion
  233.8 4.2 %collective-permute-done.15.refs_7_ = bf16[256,128]{1,0:T(8,128)(2,1)} collective-permute-done((bf16[256,128]{1,0:T(8,128)(2,1)S(1)}, bf16[256,128]{1,0:T(8,128)(2,1)}, u32[]{:S(2)}, u32[]{:S(2)}) %collective-permute-start.15) | collective-permute-done | bytes 65568 | tf_op jit(solution)/shard_map/ppermute | solution.py:1010
  237.9 5.3 %project_back.1 = (bf16[3,64,768]{2,1,0:T(8,128)(2,1)}, bf16[3,64,768]{2,1,0:T(8,128)(2,1)}, bf16[3,64,768]{2,1,0:T(8,128)(2,1)}, bf16[3,64,768]{2,1,0:T(8,128)(...) custom-call(s32[2]{0:T(128)} %pad_add_fusion.1.place_ref, ...), custom_call_target="tpu_custom_call" | custom-call | flops 1358954496 | bytes 1179648 | tf_op jit(solution)/shard_map/project_back/pallas_call | solution.py:1262
  246.6 1.3 collective-permute-start.21
  248.7 1.5 collective-permute-start.24
  250.5 6.8 %collective-permute-done.21 = bf16[4,64,576]{2,1,0:T(8,128)(2,1)S(1)} collective-permute-done((bf16[4,64,576]{2,1,0:T(8,128)(2,1)S(1)}, bf16[4,64,576]{2,1,0:T(8,128)(2,1)S(1)}, u32[]{:S(2)}, u32[]{:S(2)}) %collective-permute-start.21) | collective-permute-done | bytes 294944 | tf_op jit(solution)/shard_map/ppermute | solution.py:77
  257.4 7.3 %collective-permute-done.17 = bf16[4,4,24,576]{3,2,1,0:T(8,128)(2,1)S(1)} collective-permute-done((bf16[4,4,24,576]{3,2,1,0:T(8,128)(2,1)}, bf16[4,4,24,576]{3,2,1,0:T(8,128)(2,1)S(1)}, u32[]{:S(2)}, u32[]{:S(2)}) %collective-permute-start.17) | collective-permute-done | bytes 442400 | tf_op jit(solution)/shard_map/ppermute | solution.py:1307
  264.9 1.7 collective-permute-start.26
  268.0 8.2 %collective-permute-done.26 = bf16[2,160,576]{2,1,0:T(8,128)(2,1)S(1)} collective-permute-done((bf16[2,160,576]{2,1,0:T(8,128)(2,1)S(1)}, bf16[2,160,576]{2,1,0:T(8,128)(2,1)S(1)}, u32[]{:S(2)}, u32[]{:S(2)}) %collective-permute-start.26) | collective-permute-done | bytes 368672 | tf_op jit(solution)/shard_map/ppermute | solution.py:77
  277.2 1.6 collective-permute-start.32
  279.1 2.3 collective-permute-start.27
  282.2 9.5 %collective-permute-done.27 = bf16[1,160,576]{2,1,0:T(8,128)(2,1)S(1)} collective-permute-done((bf16[1,160,576]{2,1,0:T(8,128)(2,1)S(1)}, bf16[1,160,576]{2,1,0:T(8,128)(2,1)S(1)}, u32[]{:S(2)}, u32[]{:S(2)}) %collective-permute-start.27) | collective-permute-done | bytes 184352 | tf_op jit(solution)/shard_map/ppermute | solution.py:77
  292.0 1.6 collective-permute-start.29
  (279 shorter events, 40.0 us)
Async XLA Ops:
  13.3 16.6 %copy-start.14 = (bf16[3,64,768]{2,1,0:T(8,128)(2,1)}, bf16[3,64,768]{2,1,0:T(8,128)(2,1)S(1)}, u32[]{:S(2)}) copy-start(bf16[3,64,768]{2,1,0:T(8,128)(2,1)S(1)} %fusion.6.refs_0_) | copy-start | bytes 884740
  13.4 17.4 %copy-start.26 = (bf16[24,3072]{1,0:T(8,128)(2,1)S(1)}, bf16[24,3072]{1,0:T(8,128)(2,1)}, u32[]{:S(2)}) copy-start(bf16[24,3072]{1,0:T(8,128)(2,1)} %param.24) | copy-start | bytes 442372
  13.4 35.6 %collective-permute-start = (bf16[3,64,768]{2,1,0:T(8,128)(2,1)S(1)}, bf16[3,64,768]{2,1,0:T(8,128)(2,1)S(1)}, u32[]{:S(2)}, u32[]{:S(2)}) collective-permute-start(bf16[3,64,768]{2,1,0:T(8,128)(2,1)S(1)} %fusion.6.refs_0_), channel_id=1, source_target_pairs={{0,8},{8,0},{16,24},{24,16},{1,9},{9,1},{17,25},{25,17},{2,10},{10... | collective-permute-start | bytes 884744 | tf_op jit(solution)/shard_map/ppermute | solution.py:55
  13.9 35.1 %collective-permute-start.1 = (bf16[3,64,768]{2,1,0:T(8,128)(2,1)S(1)}, bf16[3,64,768]{2,1,0:T(8,128)(2,1)S(1)}, u32[]{:S(2)}, u32[]{:S(2)}) collective-permute-start(bf16[3,64,768]{2,1,0:T(8,128)(2,1)S(1)} %fusion.6.refs_0_), channel_id=1, source_target_pairs={{0,16},{8,24},{16,0},{24,8},{1,17},{9,25},{17,1},{25,9},{2,18},{10... | collective-permute-start | bytes 884744 | tf_op jit(solution)/shard_map/ppermute | solution.py:55
  16.5 32.5 %collective-permute-start.2 = (bf16[3,64,768]{2,1,0:T(8,128)(2,1)S(1)}, bf16[3,64,768]{2,1,0:T(8,128)(2,1)S(1)}, u32[]{:S(2)}, u32[]{:S(2)}) collective-permute-start(bf16[3,64,768]{2,1,0:T(8,128)(2,1)S(1)} %fusion.6.refs_0_), channel_id=1, source_target_pairs={{0,24},{8,16},{16,8},{24,0},{1,25},{9,17},{17,9},{25,1},{2,26},{10... | collective-permute-start | bytes 884744 | tf_op jit(solution)/shard_map/ppermute | solution.py:55
  16.5 32.2 %all-to-all-start = ((bf16[32,24,640]{2,1,0:T(8,128)(2,1)}), bf16[32,24,640]{2,1,0:T(8,128)(2,1)S(1)}, u32[]{:S(2)}, u32[]{:S(2)}) async-start(bf16[32,24,640]{2,1,0:T(8,128)(2,1)} %bitcast.9), calls=%async_computation | async-start | bytes 1966080 | tf_op jit(solution)/shard_map/all_to_all | solution.py:24
  22.6 128.9 %all-gather.3.cloned.1.call-start = ((), (), s32[]{:S(2)}) async-start(), calls=%async_computation.7 | async-start | bytes 10948608 | tf_op jit(solution)/shard_map/all_gather | solution.py:964
  55.0 46.6 %all-to-all-start.1 = ((bf16[8,400,128]{2,1,0:T(8,128)(2,1)}), bf16[8,400,128]{2,1,0:T(8,128)(2,1)S(1)}, u32[]{:S(2)}, u32[]{:S(2)}) async-start(bf16[8,400,128]{2,1,0:T(8,128)(2,1)} %get-tuple-element.109), calls=%async_computation.1 | async-start | bytes 1638400 | tf_op jit(solution)/shard_map/all_to_all | solution.py:1009
  58.7 20.4 %collective-permute-start.3 = (bf16[256,128]{1,0:T(8,128)(2,1)S(1)}, bf16[256,128]{1,0:T(8,128)(2,1)S(1)}, u32[]{:S(2)}, u32[]{:S(2)}) collective-permute-start(bf16[256,128]{1,0:T(8,128)(2,1)S(1)} %copy-done.29), channel_id=1, source_target_pairs={{0,2},{1,3},{2,0},{3,1},{4,6},{5,7},{6,4},{7,5},{8,10},{9,11},{10,... | collective-permute-start | bytes 196616 | tf_op jit(solution)/shard_map/ppermute | solution.py:1010
  60.6 39.2 %collective-permute-start.4 = (bf16[256,128]{1,0:T(8,128)(2,1)S(1)}, bf16[256,128]{1,0:T(8,128)(2,1)S(1)}, u32[]{:S(2)}, u32[]{:S(2)}) collective-permute-start(bf16[256,128]{1,0:T(8,128)(2,1)S(1)} %copy-done.29), channel_id=1, source_target_pairs={{0,4},{1,5},{2,6},{3,7},{4,0},{5,1},{6,2},{7,3},{8,12},{9,13},{10,... | collective-permute-start | bytes 196616 | tf_op jit(solution)/shard_map/ppermute | solution.py:1010
  63.0 36.8 %collective-permute-start.5 = (bf16[256,128]{1,0:T(8,128)(2,1)S(1)}, bf16[256,128]{1,0:T(8,128)(2,1)S(1)}, u32[]{:S(2)}, u32[]{:S(2)}) collective-permute-start(bf16[256,128]{1,0:T(8,128)(2,1)S(1)} %copy-done.29), channel_id=1, source_target_pairs={{0,6},{1,7},{2,4},{3,5},{4,2},{5,3},{6,0},{7,1},{8,14},{9,15},{10,... | collective-permute-start | bytes 196616 | tf_op jit(solution)/shard_map/ppermute | solution.py:1010
  99.8 15.8 %copy-start.9 = (bf16[4,256,128]{2,1,0:T(8,128)(2,1)}, bf16[4,256,128]{2,1,0:T(8,128)(2,1)S(1)}, u32[]{:S(2)}) copy-start(bf16[4,256,128]{2,1,0:T(8,128)(2,1)S(1)} %pad_maximum_fusion.2.refs_1_) | copy-start | bytes 786436
  99.8 15.8 %collective-permute-start.6 = (bf16[4,256,128]{2,1,0:T(8,128)(2,1)S(1)}, bf16[4,256,128]{2,1,0:T(8,128)(2,1)S(1)}, u32[]{:S(2)}, u32[]{:S(2)}) collective-permute-start(bf16[4,256,128]{2,1,0:T(8,128)(2,1)S(1)} %pad_maximum_fusion.2.refs_1_), channel_id=1, source_target_pairs={{0,1},{1,0},{2,3},{3,2},{4,5},{5,4},{6,7},{7,6},{8,9},{9,8},{10,11... | collective-permute-start | bytes 786440 | tf_op jit(solution)/shard_map/ppermute | solution.py:1010
  116.3 12.8 %copy-start.8 = (bf16[3,64,768]{2,1,0:T(8,128)(2,1)S(1)}, bf16[3,64,768]{2,1,0:T(8,128)(2,1)}, u32[]{:S(2)}) copy-start(bf16[3,64,768]{2,1,0:T(8,128)(2,1)} %param.15) | copy-start | bytes 884740
  124.7 23.1 %all-to-all-start.2 = ((bf16[32,40,128]{2,1,0:T(8,128)(2,1)}), bf16[32,40,128]{2,1,0:T(8,128)(2,1)S(1)}, u32[]{:S(2)}, u32[]{:S(2)}) async-start(bf16[32,40,128]{2,1,0:T(8,128)(2,1)} %get-tuple-element.115), calls=%async_computation.2 | async-start | bytes 655360 | tf_op jit(solution)/shard_map/all_to_all | solution.py:24
  129.2 27.1 %collective-permute-start.10 = (bf16[192,768]{1,0:T(8,128)(2,1)S(1)}, bf16[192,768]{1,0:T(8,128)(2,1)S(1)}, u32[]{:S(2)}, u32[]{:S(2)}) collective-permute-start(bf16[192,768]{1,0:T(8,128)(2,1)S(1)} %bitcast.182), channel_id=1, source_target_pairs={{0,8},{8,0},{16,24},{24,16},{1,9},{9,1},{17,25},{25,17},{2,10},{10... | collective-permute-start | bytes 884744 | tf_op jit(solution)/shard_map/ppermute | solution.py:55
  129.3 42.3 %collective-permute-start.11 = (bf16[192,768]{1,0:T(8,128)(2,1)S(1)}, bf16[192,768]{1,0:T(8,128)(2,1)S(1)}, u32[]{:S(2)}, u32[]{:S(2)}) collective-permute-start(bf16[192,768]{1,0:T(8,128)(2,1)S(1)} %bitcast.183), channel_id=1, source_target_pairs={{0,16},{8,24},{16,0},{24,8},{1,17},{9,25},{17,1},{25,9},{2,18},{10... | collective-permute-start | bytes 884744 | tf_op jit(solution)/shard_map/ppermute | solution.py:55
  131.0 40.7 %collective-permute-start.12 = (bf16[192,768]{1,0:T(8,128)(2,1)S(1)}, bf16[192,768]{1,0:T(8,128)(2,1)S(1)}, u32[]{:S(2)}, u32[]{:S(2)}) collective-permute-start(bf16[192,768]{1,0:T(8,128)(2,1)S(1)} %bitcast.184), channel_id=1, source_target_pairs={{0,24},{8,16},{16,8},{24,0},{1,25},{9,17},{17,9},{25,1},{2,26},{10... | collective-permute-start | bytes 884744 | tf_op jit(solution)/shard_map/ppermute | solution.py:55
  154.6 17.1 %collective-permute-start.7 = (bf16[192,768]{1,0:T(8,128)(2,1)}, bf16[192,768]{1,0:T(8,128)(2,1)S(1)}, u32[]{:S(2)}, u32[]{:S(2)}) collective-permute-start(bf16[192,768]{1,0:T(8,128)(2,1)} %get-tuple-element.116.second_ref.refs_0_), channel_id=1, source_target_pairs={{0,8},{8,0},{16,24},{24,16},{1,9},{9,1},{17,25},{25,17},{2,10},{10... | collective-permute-start | bytes 884744 | tf_op jit(solution)/shard_map/ppermute | solution.py:55
  154.8 16.9 %collective-permute-start.8 = (bf16[192,768]{1,0:T(8,128)(2,1)}, bf16[192,768]{1,0:T(8,128)(2,1)S(1)}, u32[]{:S(2)}, u32[]{:S(2)}) collective-permute-start(bf16[192,768]{1,0:T(8,128)(2,1)} %get-tuple-element.116.second_ref.refs_0_), channel_id=1, source_target_pairs={{0,16},{8,24},{16,0},{24,8},{1,17},{9,25},{17,1},{25,9},{2,18},{10... | collective-permute-start | bytes 884744 | tf_op jit(solution)/shard_map/ppermute | solution.py:55
  156.3 15.4 %collective-permute-start.9 = (bf16[192,768]{1,0:T(8,128)(2,1)}, bf16[192,768]{1,0:T(8,128)(2,1)S(1)}, u32[]{:S(2)}, u32[]{:S(2)}) collective-permute-start(bf16[192,768]{1,0:T(8,128)(2,1)} %get-tuple-element.116.second_ref.refs_0_), channel_id=1, source_target_pairs={{0,24},{8,16},{16,8},{24,0},{1,25},{9,17},{17,9},{25,1},{2,26},{10... | collective-permute-start | bytes 884744 | tf_op jit(solution)/shard_map/ppermute | solution.py:55
  167.9 15.9 %all-to-all-start.3 = ((bf16[32,40,128]{2,1,0:T(8,128)(2,1)}), bf16[32,40,128]{2,1,0:T(8,128)(2,1)S(1)}, u32[]{:S(2)}, u32[]{:S(2)}) async-start(bf16[32,40,128]{2,1,0:T(8,128)(2,1)} %get-tuple-element.121), calls=%async_computation.3 | async-start | bytes 655360 | tf_op jit(solution)/shard_map/all_to_all | solution.py:24
  191.5 15.3 %collective-permute-start.13 = (bf16[4,256,128]{2,1,0:T(8,128)(2,1)}, bf16[4,256,128]{2,1,0:T(8,128)(2,1)S(1)}, u32[]{:S(2)}, u32[]{:S(2)}) collective-permute-start(bf16[4,256,128]{2,1,0:T(8,128)(2,1)} %get-tuple-element.139), channel_id=1, source_target_pairs={{0,1},{1,0},{2,3},{3,2},{4,5},{5,4},{6,7},{7,6},{8,9},{9,8},{10,11... | collective-permute-start | bytes 786440 | tf_op jit(solution)/shard_map/ppermute | solution.py:1010
  192.5 39.8 %collective-permute-start.22 = (bf16[4,192,768]{2,1,0:T(8,128)(2,1)}, bf16[4,192,768]{2,1,0:T(8,128)(2,1)S(1)}, u32[]{:S(2)}, u32[]{:S(2)}) collective-permute-start(bf16[4,192,768]{2,1,0:T(8,128)(2,1)} %get-tuple-element.158), channel_id=1, source_target_pairs={{0,1},{1,0},{2,3},{3,2},{4,5},{5,4},{6,7},{7,6},{8,9},{9,8},{10,11... | collective-permute-start | bytes 3538952 | tf_op jit(solution)/shard_map/ppermute | solution.py:1173
  193.5 13.3 %copy-start.23 = (bf16[4,256,128]{2,1,0:T(8,128)(2,1)S(1)}, bf16[4,256,128]{2,1,0:T(8,128)(2,1)}, u32[]{:S(2)}) copy-start(bf16[4,256,128]{2,1,0:T(8,128)(2,1)} %get-tuple-element.138) | copy-start | bytes 786436
  207.0 31.0 %all-to-all-start.4 = ((bf16[8,400,128]{2,1,0:T(8,128)(2,1)}), bf16[8,400,128]{2,1,0:T(8,128)(2,1)}, u32[]{:S(2)}, u32[]{:S(2)}) async-start(bf16[8,400,128]{2,1,0:T(8,128)(2,1)} %attend_own_back.1), calls=%async_computation.4 | async-start | bytes 1638400 | tf_op jit(solution)/shard_map/all_to_all | solution.py:1227
  212.2 52.7 %reduce-scatter.2.cloned.1.call-start = ((), (), s32[]{:S(2)}) async-start(), calls=%async_computation.6 | async-start | bytes 1474560 | tf_op jit(solution)/shard_map/reduce_scatter | solution.py:1175
  213.2 4.6 %collective-permute-start.18 = (bf16[192,768]{1,0:T(8,128)(2,1)S(1)}, bf16[192,768]{1,0:T(8,128)(2,1)S(1)}, u32[]{:S(2)}, u32[]{:S(2)}) collective-permute-start(bf16[192,768]{1,0:T(8,128)(2,1)S(1)} %get-tuple-element.191), channel_id=1, source_target_pairs={{0,8},{8,0},{16,24},{24,16},{1,9},{9,1},{17,25},{25,17},{2,10},{10... | collective-permute-start | bytes 884744 | tf_op jit(solution)/shard_map/ppermute | solution.py:55
  213.3 9.9 %collective-permute-start.19 = (bf16[192,768]{1,0:T(8,128)(2,1)S(1)}, bf16[192,768]{1,0:T(8,128)(2,1)S(1)}, u32[]{:S(2)}, u32[]{:S(2)}) collective-permute-start(bf16[192,768]{1,0:T(8,128)(2,1)S(1)} %get-tuple-element.193), channel_id=1, source_target_pairs={{0,16},{8,24},{16,0},{24,8},{1,17},{9,25},{17,1},{25,9},{2,18},{10... | collective-permute-start | bytes 884744 | tf_op jit(solution)/shard_map/ppermute | solution.py:55
  214.8 13.7 %collective-permute-start.20 = (bf16[192,768]{1,0:T(8,128)(2,1)S(1)}, bf16[192,768]{1,0:T(8,128)(2,1)S(1)}, u32[]{:S(2)}, u32[]{:S(2)}) collective-permute-start(bf16[192,768]{1,0:T(8,128)(2,1)S(1)} %get-tuple-element.192), channel_id=1, source_target_pairs={{0,24},{8,16},{16,8},{24,0},{1,25},{9,17},{17,9},{25,1},{2,26},{10... | collective-permute-start | bytes 884744 | tf_op jit(solution)/shard_map/ppermute | solution.py:55
  215.9 16.5 %copy-start.7 = (bf16[4,192,768]{2,1,0:T(8,128)(2,1)S(1)}, bf16[4,192,768]{2,1,0:T(8,128)(2,1)}, u32[]{:S(2)}) copy-start(bf16[4,192,768]{2,1,0:T(8,128)(2,1)} %get-tuple-element.157) | copy-start | bytes 3538948
  215.9 17.9 %collective-permute-start.14 = (bf16[256,128]{1,0:T(8,128)(2,1)S(1)}, bf16[256,128]{1,0:T(8,128)(2,1)S(1)}, u32[]{:S(2)}, u32[]{:S(2)}) collective-permute-start(bf16[256,128]{1,0:T(8,128)(2,1)S(1)} %get-tuple-element.198), channel_id=1, source_target_pairs={{0,2},{1,3},{2,0},{3,1},{4,6},{5,7},{6,4},{7,5},{8,10},{9,11},{10,... | collective-permute-start | bytes 196616 | tf_op jit(solution)/shard_map/ppermute | solution.py:1010
  217.8 20.2 %collective-permute-start.15 = (bf16[256,128]{1,0:T(8,128)(2,1)S(1)}, bf16[256,128]{1,0:T(8,128)(2,1)}, u32[]{:S(2)}, u32[]{:S(2)}) collective-permute-start(bf16[256,128]{1,0:T(8,128)(2,1)S(1)} %get-tuple-element.197), channel_id=1, source_target_pairs={{0,4},{1,5},{2,6},{3,7},{4,0},{5,1},{6,2},{7,3},{8,12},{9,13},{10,... | collective-permute-start | bytes 196616 | tf_op jit(solution)/shard_map/ppermute | solution.py:1010
  223.1 14.8 %collective-permute-start.16 = (bf16[256,128]{1,0:T(8,128)(2,1)S(1)}, bf16[256,128]{1,0:T(8,128)(2,1)}, u32[]{:S(2)}, u32[]{:S(2)}) collective-permute-start(bf16[256,128]{1,0:T(8,128)(2,1)S(1)} %get-tuple-element.196), channel_id=1, source_target_pairs={{0,6},{1,7},{2,4},{3,5},{4,2},{5,3},{6,0},{7,1},{8,14},{9,15},{10,... | collective-permute-start | bytes 196616 | tf_op jit(solution)/shard_map/ppermute | solution.py:1010
  246.5 18.2 %copy-start.11 = (bf16[4,4,24,576]{3,2,1,0:T(8,128)(2,1)S(1)}, bf16[4,4,24,576]{3,2,1,0:T(8,128)(2,1)}, u32[]{:S(2)}) copy-start(bf16[4,4,24,576]{3,2,1,0:T(8,128)(2,1)} %get-tuple-element.142) | copy-start | bytes 1327108
  246.6 10.7 %collective-permute-start.21 = (bf16[4,64,576]{2,1,0:T(8,128)(2,1)S(1)}, bf16[4,64,576]{2,1,0:T(8,128)(2,1)S(1)}, u32[]{:S(2)}, u32[]{:S(2)}) collective-permute-start(bf16[4,64,576]{2,1,0:T(8,128)(2,1)S(1)} %fusion.22), channel_id=1, source_target_pairs={{0,1},{1,0},{2,3},{3,2},{4,5},{5,4},{6,7},{7,6},{8,9},{9,8},{10,11... | collective-permute-start | bytes 884744 | tf_op jit(solution)/shard_map/ppermute | solution.py:77
  247.9 16.8 %collective-permute-start.17 = (bf16[4,4,24,576]{3,2,1,0:T(8,128)(2,1)}, bf16[4,4,24,576]{3,2,1,0:T(8,128)(2,1)S(1)}, u32[]{:S(2)}, u32[]{:S(2)}) collective-permute-start(bf16[4,4,24,576]{3,2,1,0:T(8,128)(2,1)} %get-tuple-element.148), channel_id=1, source_target_pairs={{0,1},{1,0},{2,3},{3,2},{4,5},{5,4},{6,7},{7,6},{8,9},{9,8},{10,11... | collective-permute-start | bytes 1327112 | tf_op jit(solution)/shard_map/ppermute | solution.py:1307
  248.7 16.2 %collective-permute-start.23 = (bf16[3,64,768]{2,1,0:T(8,128)(2,1)}, bf16[3,64,768]{2,1,0:T(8,128)(2,1)S(1)}, u32[]{:S(2)}, u32[]{:S(2)}) collective-permute-start(bf16[3,64,768]{2,1,0:T(8,128)(2,1)} %get-tuple-element.160), channel_id=1, source_target_pairs={{0,8},{8,0},{16,24},{24,16},{1,9},{9,1},{17,25},{25,17},{2,10},{10... | collective-permute-start | bytes 884744 | tf_op jit(solution)/shard_map/ppermute | solution.py:55
  248.7 16.2 %collective-permute-start.24 = (bf16[3,64,768]{2,1,0:T(8,128)(2,1)}, bf16[3,64,768]{2,1,0:T(8,128)(2,1)S(1)}, u32[]{:S(2)}, u32[]{:S(2)}) collective-permute-start(bf16[3,64,768]{2,1,0:T(8,128)(2,1)} %get-tuple-element.161), channel_id=1, source_target_pairs={{0,16},{8,24},{16,0},{24,8},{1,17},{9,25},{17,1},{25,9},{2,18},{10... | collective-permute-start | bytes 884744 | tf_op jit(solution)/shard_map/ppermute | solution.py:55
  250.2 14.7 %collective-permute-start.25 = (bf16[3,64,768]{2,1,0:T(8,128)(2,1)}, bf16[3,64,768]{2,1,0:T(8,128)(2,1)S(1)}, u32[]{:S(2)}, u32[]{:S(2)}) collective-permute-start(bf16[3,64,768]{2,1,0:T(8,128)(2,1)} %get-tuple-element.162), channel_id=1, source_target_pairs={{0,24},{8,16},{16,8},{24,0},{1,25},{9,17},{17,9},{25,1},{2,26},{10... | collective-permute-start | bytes 884744 | tf_op jit(solution)/shard_map/ppermute | solution.py:55
  264.9 11.3 %collective-permute-start.26 = (bf16[2,160,576]{2,1,0:T(8,128)(2,1)S(1)}, bf16[2,160,576]{2,1,0:T(8,128)(2,1)S(1)}, u32[]{:S(2)}, u32[]{:S(2)}) collective-permute-start(bf16[2,160,576]{2,1,0:T(8,128)(2,1)S(1)} %fusion.18), channel_id=1, source_target_pairs={{0,2},{1,3},{2,0},{3,1},{4,6},{5,7},{6,4},{7,5},{8,10},{9,11},{10,... | collective-permute-start | bytes 1105928 | tf_op jit(solution)/shard_map/ppermute | solution.py:77
  277.1 4.3 %collective-permute-start.31 = (bf16[24,768]{1,0:T(8,128)(2,1)S(1)}, bf16[24,768]{1,0:T(8,128)(2,1)S(1)}, u32[]{:S(2)}, u32[]{:S(2)}) collective-permute-start(bf16[24,768]{1,0:T(8,128)(2,1)S(1)} %get-tuple-element.213), channel_id=1, source_target_pairs={{0,8},{8,0},{16,24},{24,16},{1,9},{9,1},{17,25},{25,17},{2,10},{10... | collective-permute-start | bytes 110600 | tf_op jit(solution)/shard_map/ppermute | solution.py:55
  277.2 4.2 %collective-permute-start.32 = (bf16[24,768]{1,0:T(8,128)(2,1)S(1)}, bf16[24,768]{1,0:T(8,128)(2,1)S(1)}, u32[]{:S(2)}, u32[]{:S(2)}) collective-permute-start(bf16[24,768]{1,0:T(8,128)(2,1)S(1)} %get-tuple-element.212), channel_id=1, source_target_pairs={{0,16},{8,24},{16,0},{24,8},{1,17},{9,25},{17,1},{25,9},{2,18},{10... | collective-permute-start | bytes 110600 | tf_op jit(solution)/shard_map/ppermute | solution.py:55
  278.8 3.4 %collective-permute-start.33 = (bf16[24,768]{1,0:T(8,128)(2,1)S(1)}, bf16[24,768]{1,0:T(8,128)(2,1)S(1)}, u32[]{:S(2)}, u32[]{:S(2)}) collective-permute-start(bf16[24,768]{1,0:T(8,128)(2,1)S(1)} %get-tuple-element.211), channel_id=1, source_target_pairs={{0,24},{8,16},{16,8},{24,0},{1,25},{9,17},{17,9},{25,1},{2,26},{10... | collective-permute-start | bytes 110600 | tf_op jit(solution)/shard_map/ppermute | solution.py:55
  279.1 12.7 %collective-permute-start.27 = (bf16[1,160,576]{2,1,0:T(8,128)(2,1)S(1)}, bf16[1,160,576]{2,1,0:T(8,128)(2,1)S(1)}, u32[]{:S(2)}, u32[]{:S(2)}) collective-permute-start(bf16[1,160,576]{2,1,0:T(8,128)(2,1)S(1)} %constant_dynamic-slice_fusion.1), channel_id=1, source_target_pairs={{0,4},{1,5},{2,6},{3,7},{4,0},{5,1},{6,2},{7,3},{8,12},{9,13},{10,... | collective-permute-start | bytes 552968 | tf_op jit(solution)/shard_map/ppermute | solution.py:77
  291.9 3.4 %collective-permute-start.28 = (bf16[32,576]{1,0:T(8,128)(2,1)S(1)}, bf16[32,576]{1,0:T(8,128)(2,1)S(1)}, u32[]{:S(2)}, u32[]{:S(2)}) collective-permute-start(bf16[32,576]{1,0:T(8,128)(2,1)S(1)} %get-tuple-element.203), channel_id=1, source_target_pairs={{0,8},{8,0},{16,24},{24,16},{1,9},{9,1},{17,25},{25,17},{2,10},{10... | collective-permute-start | bytes 110600 | tf_op jit(solution)/shard_map/ppermute | solution.py:55
  292.0 4.1 %collective-permute-start.29 = (bf16[32,576]{1,0:T(8,128)(2,1)S(1)}, bf16[32,576]{1,0:T(8,128)(2,1)S(1)}, u32[]{:S(2)}, u32[]{:S(2)}) collective-permute-start(bf16[32,576]{1,0:T(8,128)(2,1)S(1)} %get-tuple-element.204), channel_id=1, source_target_pairs={{0,16},{8,24},{16,0},{24,8},{1,17},{9,25},{17,1},{25,9},{2,18},{10... | collective-permute-start | bytes 110600 | tf_op jit(solution)/shard_map/ppermute | solution.py:55
  293.5 3.5 %collective-permute-start.30 = (bf16[32,576]{1,0:T(8,128)(2,1)S(1)}, bf16[32,576]{1,0:T(8,128)(2,1)S(1)}, u32[]{:S(2)}, u32[]{:S(2)}) collective-permute-start(bf16[32,576]{1,0:T(8,128)(2,1)S(1)} %get-tuple-element.205), channel_id=1, source_target_pairs={{0,24},{8,16},{16,8},{24,0},{1,25},{9,17},{17,9},{25,1},{2,26},{10... | collective-permute-start | bytes 110600 | tf_op jit(solution)/shard_map/ppermute | solution.py:55
  (34 other events, 122.6 us)
Sparse Core Ops, SparseCore 0:
  49.1 102.3 all-gather.2
  233.9 30.0 reduce-scatter.1
